TPU v7x, 32 devices: a whole 2x2x4 slice. The times are simulated.
32 devices in a mesh: fsdp: 32 (over z, y, x, core).
Axes of the slice: x: 2, y: 2, z: 4, core: 2. Of those that a mesh axis runs over, the one named last changes fastest.
Arguments:
- token_ids: int32 [16384], P('fsdp'), may hold values from 0 to 31999, as said below
- loss_rows: int32 [2048], P('fsdp'), may hold values from 256 to 511, as said below
- targets: int32 [2048], P('fsdp'), may hold values from 0 to 31999
- flat_master: float32 [9833280], P('fsdp'), may hold values from -3 to 3
- flat_m: float32 [9833280], P('fsdp'), may hold values from -1 to 1
- flat_v: float32 [9833280], P('fsdp'), may hold values from 0 to 1
- table_master: float32 [32000, 960], P('fsdp'), may hold values from -2 to 2
- table_m: float32 [32000, 960], P('fsdp'), may hold values from -1 to 1
- table_v: float32 [32000, 960], P('fsdp'), may hold values from 0 to 1
Outputs:
- loss: float32 [], replicated
- grad_norm: float32 [], replicated
- flat_m_new: float32 [9833280], P('fsdp')
- flat_v_new: float32 [9833280], P('fsdp')
- flat_update: float32 [9833280], P('fsdp')
- table_m_new: float32 [32000, 960], P('fsdp')
- table_v_new: float32 [32000, 960], P('fsdp')
- table_update: float32 [32000, 960], P('fsdp')
Inputs may be any that keep to these rules, and one draw needn't show every extreme that they name: `token_ids`: the owner of an id is id // 1000. Among the 512 tokens of one group no owner is named more than 32 times, and in every draw one owner is named exactly 32 times by every group. `loss_rows`: the 64 entries of one group are distinct indices into that group's own tokens, all in its continuations.
All inputs are finite; a program needn't handle non-finite values.
Results may differ from a plain program's by a relative error of at most 0.0051.
The roundings to bfloat16 on the way count: a program that leaves them out, or rounds other values in their place, can miss the bound.
Values may be sent and summed in bfloat16 or wider, within the bound.
No kernel may reach another device: no remote copies, remote signals or barrier semaphores. Data moves between devices by JAX's collectives and lax.ppermute only.
A program may use at most 256 MiB of HBM per device.

v0:
```python
import functools
import math

import jax
import jax.numpy as jnp
from jax import lax
from jax.sharding import PartitionSpec as P

D = 960
QUERY_HEADS = 15
KEY_VALUE_HEADS = 5
HEAD_SIZE = 64
FF = 2560
V = 32000
PL = 256
CL = 128
QBLK = 512
STEP = 10
QKV = 1600


EPS = 1e-05
SMOOTH = 0.1
ZCOEF = 0.0001
BETA1 = 0.9
BETA2 = 0.95
ADAM_EPS = 1e-08
DECAY = 0.1
RATE = 0.03
CLIP_C = 25.0
NEGATIVE = -1e30


def joined(x, axis, combine):
    everything = jax.tree.map(lambda part: lax.all_gather(part, axis), x)
    first = jax.tree.map(lambda part: part[0], everything)

    def lap(k, so_far):
        return combine(so_far, jax.tree.map(lambda part: part[k], everything))

    return lax.fori_loop(1, lax.axis_size(axis), lap, first)


def contract(left, right, left_dim, right_dim):
    return lax.dot_general(
        left, right, (((left_dim,), (right_dim,)), ((), ())), preferred_element_type=jnp.float32
    )


def norm_gain(value_rows, gain):
    return (
        value_rows
        * lax.rsqrt(jnp.mean(value_rows * value_rows, axis=-1, keepdims=True) + EPS)
        * gain
    )


def rotate_head_pairs(value_rows, cosine_table, sine_table):
    half_dim = value_rows.shape[-1] // 2
    turned = jnp.concatenate([-value_rows[..., half_dim:], value_rows[..., :half_dim]], axis=-1)
    return value_rows * cosine_table[:, None, :] + turned * sine_table[:, None, :]


def rope_tables(count, head_dim):
    index_row = jnp.arange(count, dtype=jnp.int32)
    position = jnp.where(index_row < PL, index_row, PL + (index_row - PL) % CL).astype(jnp.float32)
    freqs = 10000.0 ** (
        -(jnp.arange(head_dim // 2, dtype=jnp.int32).astype(jnp.float32) * 2.0 / head_dim)
    )
    angles = position[:, None] * freqs[None, :]
    angles = jnp.concatenate([angles, angles], axis=-1)
    return (jnp.cos(angles), jnp.sin(angles))


def allowed_mask(query_rows, count):
    query_pos = query_rows[:, None]
    key_pos = jnp.arange(count, dtype=jnp.int32)[None, :]
    query_seg = jnp.where(query_pos < PL, 0, 1 + (query_pos - PL) // CL)
    key_seg = jnp.where(key_pos < PL, 0, 1 + (key_pos - PL) // CL)
    return (key_pos <= query_pos) & ((key_seg == 0) | (key_seg == query_seg))


def block_scores(query_blk, key_head, first_row, count):
    scores = jnp.einsum(
        "qgd,kd->gqk", query_blk, key_head, preferred_element_type=jnp.float32
    ) * HEAD_SIZE ** (-0.5)
    allowed = allowed_mask(first_row + jnp.arange(query_blk.shape[0], dtype=jnp.int32), count)
    return jnp.where(allowed[None], scores, NEGATIVE)


def unpack(flat):
    edge_qkv = 3 * D
    edge_out = edge_qkv + D * QKV
    edge_gu = edge_out + QUERY_HEADS * HEAD_SIZE * D
    edge_down = edge_gu + 2 * D * FF
    edge_end = edge_down + FF * D
    gains = flat[:edge_qkv].reshape(3, D).astype(jnp.float32)
    w_qkv = flat[edge_qkv:edge_out].reshape(D, QKV)
    w_out = flat[edge_out:edge_gu].reshape(QUERY_HEADS * HEAD_SIZE, D)
    w_gu = flat[edge_gu:edge_down].reshape(D, 2 * FF)
    w_down = flat[edge_down:edge_end].reshape(FF, D)
    return (gains, w_qkv, w_out, w_gu, w_down)


def gated_unit(gate_up):
    gate = gate_up[:, :FF]
    return gate * jax.nn.sigmoid(gate) * gate_up[:, FF:]


def combine_stats(first, second):
    peak_one, total_one, target_one, sum_one = first
    peak_two, total_two, target_two, sum_two = second
    new_peak = jnp.maximum(peak_one, peak_two)
    new_total = total_one * jnp.exp(peak_one - new_peak) + total_two * jnp.exp(peak_two - new_peak)
    return (new_peak, new_total, target_one + target_two, sum_one + sum_two)


def adamw_step(param, gradient, moment_one, moment_two, clip_factor):
    gradient = gradient * clip_factor
    new_one = BETA1 * moment_one + (1.0 - BETA1) * gradient
    new_two = BETA2 * moment_two + (1.0 - BETA2) * gradient * gradient
    ratio = new_one / (1.0 - BETA1**STEP) / (jnp.sqrt(new_two / (1.0 - BETA2**STEP)) + ADAM_EPS)
    return (new_one, new_two, -RATE * (ratio + DECAY * param))


def local(
    token_ids, loss_rows, targets, flat_master, flat_m, flat_v, table_master, table_m, table_v
):
    devices = lax.axis_size("fsdp")
    my_index = lax.axis_index("fsdp")
    token_count = token_ids.shape[0]
    vocab_dev = table_master.shape[0]
    loss_dev = loss_rows.shape[0]
    loss_total = loss_dev * devices
    capacity = max(2, 2 * token_count // devices)
    query_groups = QUERY_HEADS // KEY_VALUE_HEADS
    emb_mult = math.sqrt(D) * 0.5
    block_count = token_count // QBLK
    brain_float_half = jnp.bfloat16
    f32 = jnp.float32
    flat_low = flat_master.astype(brain_float_half)
    table_low = table_master.astype(brain_float_half)
    gathered_w = lax.all_gather(flat_low, "fsdp", axis=0, tiled=True)
    gains, w_qkv, w_out, w_gu, w_down = unpack(gathered_w)
    owner_of = token_ids // vocab_dev
    owner_hot = (owner_of[:, None] == jnp.arange(devices, dtype=jnp.int32)[None, :]).astype(
        jnp.int32
    )
    slot_index = jnp.sum((jnp.cumsum(owner_hot, axis=0) - 1) * owner_hot, axis=1)
    destination = owner_of * capacity + slot_index
    requests = (
        jnp.full((devices * capacity,), -1, jnp.int32)
        .at[destination]
        .set(token_ids)
        .reshape(devices, capacity)
    )
    asked = lax.all_to_all(requests, "fsdp", split_axis=0, concat_axis=0, tiled=True)
    local_row = jnp.clip(asked - my_index * vocab_dev, 0, vocab_dev - 1)
    returned = lax.all_to_all(table_low[local_row], "fsdp", split_axis=0, concat_axis=0, tiled=True)
    x_embed = returned.reshape(devices * capacity, D)[destination].astype(f32) * emb_mult
    h_attn = norm_gain(x_embed, gains[0]).astype(brain_float_half)
    query_key_value = contract(h_attn, w_qkv, 1, 0)
    cosine_table, sine_table = rope_tables(token_count, HEAD_SIZE)
    rotary_function = functools.partial(
        rotate_head_pairs, cosine_table=cosine_table, sine_table=sine_table
    )
    unrotated_query = query_key_value[:, : QUERY_HEADS * HEAD_SIZE].reshape(
        token_count, QUERY_HEADS, HEAD_SIZE
    )
    unrotated_key = query_key_value[
        :, QUERY_HEADS * HEAD_SIZE : (QUERY_HEADS + KEY_VALUE_HEADS) * HEAD_SIZE
    ].reshape(token_count, KEY_VALUE_HEADS, HEAD_SIZE)
    unprojected_value = query_key_value[:, (QUERY_HEADS + KEY_VALUE_HEADS) * HEAD_SIZE :].reshape(
        token_count, KEY_VALUE_HEADS, HEAD_SIZE
    )
    query_low = (
        rotary_function(unrotated_query)
        .astype(brain_float_half)
        .reshape(token_count, KEY_VALUE_HEADS, query_groups, HEAD_SIZE)
        .transpose(1, 0, 2, 3)
    )
    key_low = rotary_function(unrotated_key).astype(brain_float_half).transpose(1, 0, 2)
    value_low = unprojected_value.astype(brain_float_half).transpose(1, 0, 2)

    def head_forward(operands):
        query_head, key_head, value_head = operands

        def block_forward(block_index):
            first_row = block_index * QBLK
            scores = block_scores(query_head, key_head, first_row, token_count)
            row_peak = jnp.max(scores, axis=-1, keepdims=True)
            exp_scores = jnp.exp(scores - row_peak)
            row_total = jnp.sum(exp_scores, axis=-1, keepdims=True)
            attn_probs = (exp_scores / row_total).astype(brain_float_half)
            mixed = jnp.einsum("gqk,kd->qgd", attn_probs, value_head, preferred_element_type=f32)
            return (mixed, (row_peak + jnp.log(row_total))[..., 0])

        mixed, log_totals = lax.map(block_forward, jnp.arange(block_count, dtype=jnp.int32))
        return (mixed.reshape(token_count, query_groups, HEAD_SIZE), log_totals)

    mixed_all, lse_all = lax.map(head_forward, (query_low, key_low, value_low))
    attended = (
        mixed_all.transpose(1, 0, 2, 3)
        .reshape(token_count, QUERY_HEADS * HEAD_SIZE)
        .astype(brain_float_half)
    )
    x_one = x_embed + contract(attended, w_out, 1, 0)
    h_mlp = norm_gain(x_one, gains[1]).astype(brain_float_half)
    gate_up = contract(h_mlp, w_gu, 1, 0)
    act = gated_unit(gate_up).astype(brain_float_half)
    x_two = x_one + contract(act, w_down, 1, 0)
    picked = x_two[loss_rows]
    hidden = norm_gain(picked, gains[2]).astype(brain_float_half)
    targets_all = lax.all_gather(targets, "fsdp", axis=0, tiled=True)
    logits = contract(lax.all_gather(hidden, "fsdp", axis=0, tiled=True), table_low, 1, 1)
    column = targets_all - my_index * vocab_dev
    target_hit = (column[:, None] == jnp.arange(vocab_dev, dtype=jnp.int32)[None, :]).astype(f32)
    local_peak = jnp.max(logits, axis=1)
    local_total = jnp.sum(jnp.exp(logits - local_peak[:, None]), axis=1)
    local_target = jnp.sum(target_hit * logits, axis=1)
    local_sum = jnp.sum(logits, axis=1)
    peak_all, total_all, target_all, sum_all = joined(
        (local_peak, local_total, local_target, local_sum), "fsdp", combine_stats
    )
    log_total = peak_all + jnp.log(total_all)
    row_loss = (
        log_total
        - (1.0 - SMOOTH) * target_all
        - SMOOTH * sum_all / V
        + ZCOEF * log_total * log_total
    )
    loss = jnp.mean(row_loss)
    soft_probs = jnp.exp(logits - log_total[:, None])
    d_logits = (
        (1.0 + 2.0 * ZCOEF * log_total)[:, None] * soft_probs
        - (1.0 - SMOOTH) * target_hit
        - SMOOTH / V
    ) / loss_total
    d_logits_low = d_logits.astype(brain_float_half)
    block = d_logits_low
    hidden_grad = lax.psum_scatter(
        contract(block, table_low, 1, 0), "fsdp", scatter_dimension=0, tiled=True
    )
    block = d_logits_low
    head_grad = contract(block, lax.all_gather(hidden, "fsdp", axis=0, tiled=True), 0, 0)
    back_w = lax.all_gather(flat_low, "fsdp", axis=0, tiled=True)
    gains_b, w_qkv_b, w_out_b, w_gu_b, w_down_b = unpack(back_w)
    _, final_pull = jax.vjp(norm_gain, picked, gains_b[2])
    d_picked, grad_final = final_pull(hidden_grad)
    d_x_two = jnp.zeros((token_count, D), f32).at[loss_rows].set(d_picked)
    d_down = d_x_two.astype(brain_float_half)
    grad_down = contract(act, d_down, 0, 0)
    d_act = contract(d_down, w_down_b, 1, 1)
    _, gate_pull = jax.vjp(gated_unit, gate_up)
    (d_gate_up,) = gate_pull(d_act)
    d_gate_low = d_gate_up.astype(brain_float_half)
    grad_gu = contract(h_mlp, d_gate_low, 0, 0)
    d_h_mlp = contract(d_gate_low, w_gu_b, 1, 1)
    _, mlp_pull = jax.vjp(norm_gain, x_one, gains_b[1])
    d_x_mlp, grad_mlp = mlp_pull(d_h_mlp)
    d_x_one = d_x_two + d_x_mlp
    d_branch = d_x_one.astype(brain_float_half)
    grad_out = contract(attended, d_branch, 0, 0)
    attended_gradient = contract(d_branch, w_out_b, 1, 1).astype(brain_float_half)
    attention_heads_gradient = attended_gradient.reshape(
        token_count, KEY_VALUE_HEADS, query_groups, HEAD_SIZE
    ).transpose(1, 0, 2, 3)

    def head_backward(operands):
        query_head, key_head, value_head, grad_head, lse_head = operands

        def block_backward(running, block_index):
            d_key, d_value = running
            first_row = block_index * QBLK
            scores = block_scores(query_head, key_head, first_row, token_count)
            attn_probs = jnp.exp(scores - lse_head[block_index][..., None])
            d_probs = jnp.einsum("qgd,kd->gqk", grad_head, value_head, preferred_element_type=f32)
            row_delta = jnp.sum(attn_probs * d_probs, axis=-1, keepdims=True)
            d_scores = (attn_probs * (d_probs - row_delta)).astype(brain_float_half)
            d_query = jnp.einsum(
                "gqk,kd->qgd", d_scores, key_head, preferred_element_type=f32
            ) * HEAD_SIZE ** (-0.5)
            d_key = d_key + jnp.einsum(
                "gqk,qgd->kd", d_scores, query_head, preferred_element_type=f32
            ) * HEAD_SIZE ** (-0.5)
            d_value = d_value + jnp.einsum(
                "gqk,qgd->kd",
                attn_probs.astype(brain_float_half),
                grad_head,
                preferred_element_type=f32,
            )
            return ((d_key, d_value), d_query)

        zero_rows = jnp.zeros((token_count, HEAD_SIZE), f32)
        (d_key, d_value), d_query = lax.scan(
            block_backward, (zero_rows, zero_rows), jnp.arange(block_count, dtype=jnp.int32)
        )
        return (d_query.reshape(token_count, query_groups, HEAD_SIZE), d_key, d_value)

    d_q_heads, d_k_heads, d_v_heads = lax.map(
        head_backward, (query_low, key_low, value_low, attention_heads_gradient, lse_all)
    )
    d_q_rot = d_q_heads.transpose(1, 0, 2, 3).reshape(token_count, QUERY_HEADS, HEAD_SIZE)
    d_k_rot = d_k_heads.transpose(1, 0, 2)
    value_gradient_full = d_v_heads.transpose(1, 0, 2)
    _, rope_pull_q = jax.vjp(rotary_function, unrotated_query)
    (d_q_raw,) = rope_pull_q(d_q_rot)
    _, rope_pull_k = jax.vjp(rotary_function, unrotated_key)
    (unrotated_key_gradient,) = rope_pull_k(d_k_rot)
    d_qkv = jnp.concatenate(
        [
            d_q_raw.reshape(token_count, QUERY_HEADS * HEAD_SIZE),
            unrotated_key_gradient.reshape(token_count, KEY_VALUE_HEADS * HEAD_SIZE),
            value_gradient_full.reshape(token_count, KEY_VALUE_HEADS * HEAD_SIZE),
        ],
        axis=1,
    ).astype(brain_float_half)
    grad_qkv = contract(h_attn, d_qkv, 0, 0)
    d_h_attn = contract(d_qkv, w_qkv_b, 1, 1)
    _, attn_pull = jax.vjp(norm_gain, x_embed, gains_b[0])
    d_x_attn, grad_attn = attn_pull(d_h_attn)
    d_x_embed = d_x_one + d_x_attn
    sending = (
        jnp.zeros((devices * capacity, D), f32)
        .at[destination]
        .set(d_x_embed * emb_mult)
        .reshape(devices, capacity, D)
    )
    arrived = lax.all_to_all(sending, "fsdp", split_axis=0, concat_axis=0, tiled=True)
    segment_row = jnp.where(asked >= 0, asked - my_index * vocab_dev, vocab_dev).reshape(-1)
    embed_grad = jax.ops.segment_sum(
        arrived.reshape(devices * capacity, D), segment_row, num_segments=vocab_dev + 1
    )[:vocab_dev]
    table_grad = head_grad + embed_grad
    pieces = [
        grad_attn,
        grad_mlp,
        grad_final,
        grad_qkv.reshape(-1),
        grad_out.reshape(-1),
        grad_gu.reshape(-1),
        grad_down.reshape(-1),
    ]
    used_count = 3 * D + D * QKV + QUERY_HEADS * HEAD_SIZE * D + 3 * D * FF
    padding = flat_master.shape[0] * devices - used_count
    flat_grad = jnp.concatenate(pieces + [jnp.zeros((padding,), f32)])
    layer_grad = lax.psum_scatter(flat_grad, "fsdp", scatter_dimension=0, tiled=True)
    squares = jnp.sum(layer_grad * layer_grad) + jnp.sum(table_grad * table_grad)
    grad_norm = jnp.sqrt(lax.psum(squares, "fsdp"))
    limit = CLIP_C / math.sqrt(loss_total)
    clip_factor = limit / jnp.maximum(grad_norm, limit)
    flat_one, flat_two, flat_update = adamw_step(
        flat_master, layer_grad, flat_m, flat_v, clip_factor
    )
    table_one, table_two, table_update = adamw_step(
        table_master, table_grad, table_m, table_v, clip_factor
    )
    return (loss, grad_norm, flat_one, flat_two, flat_update, table_one, table_two, table_update)


def solution(mesh):
    in_specs = (
        P("fsdp"),
        P("fsdp"),
        P("fsdp"),
        P("fsdp"),
        P("fsdp"),
        P("fsdp"),
        P("fsdp", None),
        P("fsdp", None),
        P("fsdp", None),
    )
    out_specs = (
        P(),
        P(),
        P("fsdp"),
        P("fsdp"),
        P("fsdp"),
        P("fsdp", None),
        P("fsdp", None),
        P("fsdp", None),
    )
    return jax.shard_map(local, mesh=mesh, in_specs=in_specs, out_specs=out_specs, check_vma=False)
```

profile of v0, /device:TPU:1, one launch (start us, length us, event | category | flops | bytes accessed | tf_op | source)
XLA Modules:
  0.0 2190.4 jit_solution(10914941979525049029)
XLA Ops:
  8.6 6.8 broadcast.1052
  15.4 10.2 dynamic-update-slice
  31.0 7.0 all-to-all-start
  38.1 3.4 copy.44
  41.5 3.6 all-to-all-done
  45.9 5.3 gather_fusion
  51.3 3.7 all-to-all-start.1
  57.3 68.8 %all-to-all-done.1 = bf16[32,32,960]{2,1,0:T(8,128)(2,1)} async-done(((bf16[32,32,960]{2,1,0:T(8,128)(2,1)}), bf16[32,32,960]{2,1,0:T(8,128)(2,1)}, u32[]{:S(2)}, u32[]{:S(2)}) %all-to-all-start.1) | async-done | bytes 1966112 | tf_op jit(solution)/shard_map/all_to_all | solution.py:159
  126.1 5.3 gather_fusion.1
  133.9 253.8 %all-reduce.12.cloned.1.call-done = bf16[9833280]{0:T(1024)(128)(2,1)} async-done(((bf16[9833280]{0:T(1024)(128)(2,1)}), bf16[9833280]{0:T(1024)(128)(2,1)}) %all-reduce.12.cloned.1.call-update) | async-done | bytes 19666576
  388.5 4.2 slice.147
  392.7 6.1 reshape.700
  398.8 4.0 fusion.120
  405.1 3.7 slice.155
  408.8 4.3 reshape.704
  415.9 24.9 %while.67 = (s32[]{:T(128)}, bf16[5,512,3,64]{1,3,2,0:T(8,128)(2,1)}, f32[5,1,3,512]{3,2,1,0:T(4,128)}, bf16[5,512,64]{1,2,0:T(8,128)(2,1)}, bf16[5,512,64]{1,2,...) while((s32[]{:T(128)}, bf16[5,512,3,64]{1,3,2,0:T(8,128)(2,1)}, f32[5,1,3,512]{3,2,1,0:T(4,128)}, ...), condition=%wide.region_8.9_spmd.clone, body=%wide.region_5.8_spmd.sunk.clone | while | flops 211830784 | bytes 11265105 | solution.py:201
  417.6 2.6 fusion.227
  422.5 2.6 fusion.227
  432.4 2.6 fusion.227
  437.4 2.6 fusion.227
  440.8 4.8 multiply_reduce_fusion.3
  445.6 11.6 slice.157
  457.2 14.9 reshape.705
  472.1 6.8 slice.160
  479.0 9.5 reshape.706
  488.5 9.2 fusion.150
  497.7 4.0 copy-done
  505.7 4.0 convolution_add_fusion.1
  509.7 2.9 copy.47
  516.2 39.7 %all-reduce.7 = s32[2048]{0:T(1024)S(1)} all-reduce(s32[2048]{0:T(1024)S(1)} %dynamic-update-slice.1), channel_id=1, replica_groups=mesh['fsdp'=32] {'fsdp'}, use_global_device_ids=true, to_apply=%add.7 | all-reduce | flops 2048 | bytes 16384
  555.9 21.6 all-gather.6.cloned.1.call-done
  577.5 6.3 fusion.158
  587.2 40.1 %all-gather.3 = f32[65536]{0:T(1024)S(1)} all-gather(f32[2048]{0:T(1024)S(1)} %get-tuple-element.544), channel_id=5, replica_groups=mesh['fsdp'=32] {'fsdp'}, dimensions={0}, use_global_device_ids=true | all-gather | bytes 270336 | tf_op jit(solution)/shard_map/all_gather | solution.py:35
  629.7 37.3 %all-gather = f32[65536]{0:T(1024)S(1)} all-gather(f32[2048]{0:T(1024)S(1)} %get-tuple-element.640), channel_id=2, replica_groups=mesh['fsdp'=32] {'fsdp'}, dimensions={0}, use_global_device_ids=true | all-gather | bytes 270336 | tf_op jit(solution)/shard_map/all_gather | solution.py:35
  669.5 38.7 %all-gather.2 = f32[65536]{0:T(1024)S(1)} all-gather(f32[2048]{0:T(1024)S(1)} %get-tuple-element.545), channel_id=4, replica_groups=mesh['fsdp'=32] {'fsdp'}, dimensions={0}, use_global_device_ids=true | all-gather | bytes 270336 | tf_op jit(solution)/shard_map/all_gather | solution.py:35
  710.5 37.3 %all-gather.1 = f32[65536]{0:T(1024)S(1)} all-gather(f32[2048]{0:T(1024)S(1)} %get-tuple-element.546), channel_id=3, replica_groups=mesh['fsdp'=32] {'fsdp'}, dimensions={0}, use_global_device_ids=true | all-gather | bytes 270336 | tf_op jit(solution)/shard_map/all_gather | solution.py:35
  750.3 57.4 %while.68 = (s32[]{:T(128)}, f32[2048]{0:T(1024)S(1)}, f32[2048]{0:T(1024)S(1)}, f32[2048]{0:T(1024)S(1)}, f32[2048]{0:T(1024)S(1)}, /*index=5*/f32[32,2048]{1,0...) while((s32[]{:T(128)}, f32[2048]{0:T(1024)S(1)}, f32[2048]{0:T(1024)S(1)}, ...), condition=%wide.region_16.17_spmd.clone, body=%wide.region_15.16_spmd.sunk.clone | while | flops 16389 | bytes 163975 | solution.py:41
  807.8 13.6 fusion.151
  821.5 141.7 %reduce-scatter.2.cloned.1.call-done = f32[64,960]{1,0:T(8,128)} async-done(((f32[2048,960]{1,0:T(8,128)}), f32[64,960]{1,0:T(8,128)}) %reduce-scatter.2.cloned.1.call-update) | async-done | bytes 245776 | tf_op jit(solution)/shard_map/reduce_scatter | solution.py:241
  966.2 11.1 fusion.110
  979.1 12.3 multiply_reduce_fusion.1
  995.1 3.2 fusion.115
  998.3 53.9 %while.69 = (s32[]{:T(128)}, f32[5,512,3,64]{1,3,2,0:T(8,128)}, f32[5,512,64]{1,2,0:T(8,128)}, bf16[5,512,64]{1,2,0:T(8,128)(2,1)}, bf16[5,512,64]{1,2,0:T(8,128...) while((s32[]{:T(128)}, f32[5,512,3,64]{1,3,2,0:T(8,128)}, ...), condition=%wide.region_24.25_spmd.clone, body=%wide.region_22.24_spmd.sunk.clone | while | flops 511592448 | bytes 25798760 | solution.py:300
  1057.4 3.4 fusion.90
  1060.8 4.7 fusion.104
  1065.5 5.5 fusion.111
  1071.0 12.1 convolution_bitcast_fusion.1
  1083.0 5.5 reshape.713
  1088.5 8.2 reshape.712
  1096.7 13.1 reshape.715
  1109.8 18.5 copy.59
  1128.3 327.8 %concatenate.35 = f32[9833280]{0:T(1024)} concatenate(f32[960]{0:T(1024)S(1)} %get-tuple-element.550, f32[960]{0:T(1024)S(1)} %get-tuple-element.547, f32[960]{0:T(1024)S(1)} %get-tuple-element.551, f32[1536000]{0:T(1024)} %reshape.712, f32[921600]{0:T(1024)} %reshape.713, f32[4915200]{0:T(1024)} %bitcast.278, f32[2457600]{0:T(1024)} %reshape.715), dimensions={0} | concatenate | bytes 78666240 | tf_op jit(solution)/shard_map/concatenate | solution.py:346
  1457.6 3.4 fusion.93
  1462.9 4.7 scatter_custom_fusion.2
  1467.6 9.8 all-to-all-start.2
  1478.2 137.9 %all-to-all-done.2 = f32[32,32,960]{2,1,0:T(8,128)} async-done(((f32[32,32,960]{2,1,0:T(8,128)}), f32[32,32,960]{2,1,0:T(8,128)}, u32[]{:S(2)}, u32[]{:S(2)}) %all-to-all-start.2) | async-done | bytes 3932192 | tf_op jit(solution)/shard_map/all_to_all | solution.py:329
  1616.1 12.6 scatter_custom_fusion.3
  1628.7 4.7 slice.166
  1633.4 5.4 copy.57
  1638.8 13.8 multiply_reduce_fusion
  1652.6 471.0 %all-reduce.14.cloned.1.call-done = f32[9833280]{0:T(1024)} async-done(((f32[9833280]{0:T(1024)}), f32[9833280]{0:T(1024)}) %all-reduce.14.cloned.1.call-update) | async-done | bytes 39333136
  2127.9 38.1 %psum.7 = f32[]{:T(128)} all-reduce(f32[]{:T(128)S(6)} %add.517), channel_id=1, replica_groups=mesh['fsdp'=32] {'fsdp'}, use_global_device_ids=true, to_apply=%region_34.35 | all-reduce | flops 1 | bytes 8 | tf_op jit(solution)/shard_map/psum | solution.py:349
  2166.8 10.3 add_multiply_fusion
  2177.1 4.3 add_multiply_fusion.1
  (433 shorter events, 182.4 us)
Async XLA Ops:
  7.2 380.6 %all-reduce.12.cloned.1.call-start = ((), (), s32[]{:S(2)}) async-start(), calls=%async_computation.6 | async-start | bytes 39333888
  25.6 0.7 copy-start.42
  27.9 27.4 %copy-start.46 = (s32[512]{0:T(512)}, s32[512]{0:T(512)S(1)}, u32[]{:S(2)}) copy-start(s32[512]{0:T(512)S(1)} %compare_select_fusion.3) | copy-start | bytes 6148
  31.0 14.2 all-to-all-start
  51.3 4.0 copy-start.52
  51.3 74.9 %all-to-all-start.1 = ((bf16[32,32,960]{2,1,0:T(8,128)(2,1)}), bf16[32,32,960]{2,1,0:T(8,128)(2,1)}, u32[]{:S(2)}, u32[]{:S(2)}) async-start(bf16[32,32,960]{2,1,0:T(8,128)(2,1)} %bitcast.282), calls=%async_computation.1 | async-start | bytes 4194304 | tf_op jit(solution)/shard_map/all_to_all | solution.py:159
  55.0 522.6 %all-gather.6.cloned.1.call-start = ((), (), s32[]{:S(2)}) async-start(), calls=%async_computation.4 | async-start | bytes 4325376 | tf_op jit(solution)/shard_map/all_gather | solution.py:215
  56.3 359.0 %copy-start.18 = (f32[512,64]{0,1:T(8,128)}, f32[512,64]{0,1:T(8,128)S(1)}, u32[]{:S(2)}) copy-start(f32[512,64]{0,1:T(8,128)S(1)} %get-tuple-element.629) | copy-start | bytes 393220
  133.0 265.8 %copy-start.6 = (bf16[512,960]{0,1:T(8,128)(2,1)}, bf16[512,960]{0,1:T(8,128)(2,1)S(1)}, u32[]{:S(2)}) copy-start(bf16[512,960]{0,1:T(8,128)(2,1)S(1)} %copy.46) | copy-start | bytes 2949124
  133.3 0.6 copy-start.40
  133.9 264.9 %copy-start.49 = (f32[512]{0:T(512)}, f32[512]{0:T(512)S(1)}, u32[]{:S(2)}) copy-start(f32[512]{0:T(512)S(1)} %get-tuple-element.637) | copy-start | bytes 6148
  388.5 10.3 copy-start.43
  413.1 2.0 copy-start.20
  413.1 2.2 copy-start.1
  440.8 4.8 copy-start.15
  497.7 4.0 copy-start
  501.6 3.1 copy-start.8
  501.6 4.0 copy-start.16
  503.3 1.5 copy-start.4
  509.7 6.2 copy-start.53
  515.9 447.3 %reduce-scatter.2.cloned.1.call-start = ((), (), s32[]{:S(2)}) async-start(), calls=%async_computation.5 | async-start | bytes 8650752 | tf_op jit(solution)/shard_map/reduce_scatter | solution.py:241
  555.9 251.9 %copy-start.36 = (s32[2048]{0:T(1024)}, s32[2048]{0:T(1024)S(1)}, u32[]{:S(2)}) copy-start(s32[2048]{0:T(1024)S(1)} %broadcast_subtract_fusion) | copy-start | bytes 24580
  583.8 3.3 copy-start.11
  627.3 0.7 copy-start.27
  667.1 0.7 copy-start.28
  708.2 0.7 copy-start.29
  747.9 0.7 copy-start.30
  807.7 13.6 copy-start.31
  807.7 13.6 copy-start.33
  807.7 13.6 copy-start.38
  807.8 13.6 copy-start.47
  821.4 1302.2 %all-reduce.14.cloned.1.call-start = ((), (), s32[]{:S(2)}) async-start(), calls=%async_computation.7 | async-start | bytes 78667776
  979.1 12.3 copy-start.9
  979.1 12.4 copy-start.14
  991.4 1.5 copy-start.24
  993.0 2.1 copy-start.2
  993.0 2.1 copy-start.12
  998.3 54.0 %copy-start.21 = (f32[512,64]{0,1:T(8,128)S(1)}, f32[512,64]{0,1:T(8,128)}, u32[]{:S(2)}) copy-start(f32[512,64]{0,1:T(8,128)} %get-tuple-element.630) | copy-start | bytes 393220
  1052.3 1.7 copy-start.13
  1054.0 0.9 copy-start.19
  1054.0 1.2 copy-start.23
  1055.2 1.2 copy-start.7
  1055.2 2.2 copy-start.22
  1055.2 2.2 copy-start.44
  1055.2 2.2 copy-start.50
  1055.2 2.2 copy-start.51
  1060.8 4.7 copy-start.5
  1060.8 10.2 slice-start
  1065.5 5.5 copy-start.10
  1065.5 5.5 slice-start.1
  1456.1 0.7 copy-start.41
  1456.1 1.5 copy-start.3
  1456.1 1.5 copy-start.45
  1467.6 9.9 copy-start.35
  1467.6 10.0 copy-start.32
  1467.6 10.0 copy-start.34
  1467.6 10.0 copy-start.39
  1467.6 148.4 %all-to-all-start.2 = ((f32[32,32,960]{2,1,0:T(8,128)}), f32[32,32,960]{2,1,0:T(8,128)}, u32[]{:S(2)}, u32[]{:S(2)}) async-start(f32[32,32,960]{2,1,0:T(8,128)} %bitcast.281), calls=%async_computation.3 | async-start | bytes 8388608 | tf_op jit(solution)/shard_map/all_to_all | solution.py:329
  1633.4 5.4 copy-start.37
  1633.4 5.4 copy-start.48
  2166.7 10.3 copy-start.17
  2166.8 10.3 copy-start.25
  2166.8 10.3 copy-start.26
Sparse Core Ops, SparseCore 0:
  25.7 361.9 all-reduce.11
  516.0 61.4 all-gather.5
  821.5 141.5 reduce-scatter.1
  1456.2 667.3 all-reduce.13
where the time goes:
time: 2220 us; the launch traced here: 2190 us
  waiting for transfers between devices  1100 us (50%)
  local copies, waits for them, and re-layouts  578 us (26%)
  blocking collectives  231 us (10%)
  matrix products  171 us (8%)
  other arithmetic  68.2 us (3%)
    unnamed x6, waiting for transfers between devices  725 us
    concatenate x1, local copies, waits for them, and re-layouts, local(): flat_grad = jnp.concatenate(pieces + [jnp.zeros((padding,), f32)])  328 us
    all_gather x4, blocking collectives, joined(): everything = jax.tree.map(lambda part: lax.all_gather(part, axis), x)  153 us
    reduce_scatter x1, waiting for transfers between devices, local(): lax.psum_scatter(contract(block, table_low, 1, 0), 'fsdp', scatter_dimens...  142 us
    all_to_all x1, waiting for transfers between devices, local(): lax.all_to_all(sending, 'fsdp', split_axis=0, concat_axis=0, tiled=True)  138 us
    dot_general x15, matrix products, contract(): lax.dot_general(left, right, (((left_dim,), (right_dim,)), ((), ())), pre...  110 us
    all_to_all x1, waiting for transfers between devices, local(): lax.all_to_all(table_low[local_row], 'fsdp', split_axis=0, concat_axis=0,...  68.8 us
    unnamed x119, local copies, waits for them, and re-layouts  60.6 us
  transfers between devices with their start and end apart: 7, of which 7 were waited for; matrix products, arithmetic and copies ran while one was open for 3% of the time, Pallas kernels for 0%

commit v1 on v0

v1 whole, which is shorter than its diff:
```python
import math

import jax
import jax.numpy as jnp
import numpy as np
from jax import lax
from jax.sharding import Mesh, PartitionSpec as P

D = 960
QUERY_HEADS = 15
KEY_VALUE_HEADS = 5
HEAD_SIZE = 64
FF = 2560
V = 32000
PL = 256
CL = 128
STEP = 10
QKV = 1600

EPS = 1e-05
SMOOTH = 0.1
ZCOEF = 0.0001
BETA1 = 0.9
BETA2 = 0.95
ADAM_EPS = 1e-08
DECAY = 0.1
RATE = 0.03
CLIP_C = 25.0
NEGATIVE = -1e30

UNIT = 320
GAINS = 3 * D
GAIN_UNITS = GAINS // UNIT
QKV_UNITS = D * QKV // UNIT
OUT_UNITS = D * D // UNIT
GU_UNITS = D * 2 * FF // UNIT
DOWN_UNITS = FF * D // UNIT
ALL_UNITS = QKV_UNITS + OUT_UNITS + GU_UNITS + DOWN_UNITS
PLANE = ("y", "x", "c")
ALL = ("q", "y", "x", "c")
SHARE = FF // 8

bf16 = jnp.bfloat16
f32 = jnp.float32


def dot(left, right, left_dim=1, right_dim=0):
    return lax.dot_general(
        left, right, (((left_dim,), (right_dim,)), ((), ())), preferred_element_type=f32
    )


def hot(index, count):
    return (index[:, None] == jnp.arange(count, dtype=jnp.int32)[None, :]).astype(bf16)


def scale_of(rows):
    return lax.rsqrt(jnp.mean(rows * rows, axis=-1, keepdims=True) + EPS)


def norm_back(rows, gain, grad):
    scale = scale_of(rows)
    normed = rows * scale
    grad_gain = jnp.sum(grad * normed, axis=0)
    scaled = grad * gain
    return scale * (scaled - normed * jnp.mean(scaled * normed, axis=-1, keepdims=True)), grad_gain


def flip(rows, axes, bits, size):
    return lax.ppermute(rows, axes, [(i, i ^ bits) for i in range(size)])


def rope_tables(count):
    row = np.arange(count)
    position = np.where(row < PL, row, PL + (row - PL) % CL).astype(np.float32)
    half = np.arange(HEAD_SIZE // 2, dtype=np.float32)
    freqs = np.float32(10000.0) ** (-(half * np.float32(2.0) / np.float32(HEAD_SIZE)))
    angles = (position[:, None] * freqs[None, :].astype(np.float32)).astype(np.float64)
    angles = np.concatenate([angles, angles], axis=-1)
    return np.cos(angles).astype(np.float32), np.sin(angles).astype(np.float32)


def rotate(rows, cosine, sine):
    heads = rows.reshape(rows.shape[0], -1, HEAD_SIZE)
    half = HEAD_SIZE // 2
    turned = jnp.concatenate([-heads[..., half:], heads[..., :half]], axis=-1)
    return (heads * cosine[:, None, :] + turned * sine[:, None, :]).reshape(rows.shape)


def rotate_back(grad, cosine, sine):
    heads = grad.reshape(grad.shape[0], -1, HEAD_SIZE)
    half = HEAD_SIZE // 2
    spun = heads * sine[:, None, :]
    turned = jnp.concatenate([spun[..., half:], -spun[..., :half]], axis=-1)
    return (heads * cosine[:, None, :] + turned).reshape(grad.shape)


def adamw_step(param, gradient, moment_one, moment_two, clip_factor):
    gradient = gradient * clip_factor
    new_one = BETA1 * moment_one + (1.0 - BETA1) * gradient
    new_two = BETA2 * moment_two + (1.0 - BETA2) * gradient * gradient
    ratio = new_one / (1.0 - BETA1**STEP) / (jnp.sqrt(new_two / (1.0 - BETA2**STEP)) + ADAM_EPS)
    return (new_one, new_two, -RATE * (ratio + DECAY * param))


def fold_plane(parts):
    got = flip(parts[1], "c", 1, 2)
    mine = parts[0].astype(f32) + got.astype(f32)
    low = mine.astype(parts[1].dtype)
    total = mine[0]
    for k in (1, 2, 3):
        total = total + flip(low[k], ("y", "x"), k, 4).astype(f32)
    return total


def spread_plane(rows):
    four = jnp.stack([rows] + [flip(rows, ("y", "x"), k, 4) for k in (1, 2, 3)])
    return jnp.stack([four, flip(four, "c", 1, 2)])


def local(
    token_ids, loss_rows, targets, flat_master, flat_m, flat_v, table_master, table_m, table_v
):
    devices = lax.axis_size(ALL)
    rows_q = lax.axis_size("q")
    me = lax.axis_index(ALL)
    q_index = lax.axis_index("q")
    p_index = lax.axis_index(PLANE)
    c_index = lax.axis_index("c")
    yx_index = lax.axis_index(("y", "x"))
    tokens = token_ids.shape[0]
    vocab_dev = table_master.shape[0]
    loss_dev = loss_rows.shape[0]
    loss_total = loss_dev * devices
    capacity = max(2, 2 * tokens // devices)
    slots = devices * capacity
    groups = QUERY_HEADS // KEY_VALUE_HEADS
    emb_mult = math.sqrt(D) * 0.5
    shard = flat_master.shape[0]
    units = ALL_UNITS // devices
    span = units * UNIT
    drift = shard - span
    aligned = devices == 32

    place = np.array([kq * 8 + kyx * 2 + kc for kc in range(2) for kyx in range(4) for kq in range(rows_q)])
    rank_of = np.argsort(place)
    source_of = me ^ jnp.asarray(place, jnp.int32)
    order_of = jnp.take(jnp.asarray(rank_of, jnp.int32), me ^ jnp.arange(devices, dtype=jnp.int32))

    flat_low = flat_master.astype(bf16)
    table_low = table_master.astype(bf16)
    ahead = lax.ppermute(flat_low[:GAINS], ALL, [(i + 1, i) for i in range(devices - 1)])
    back = max(0, drift * (devices - 1) - GAINS)
    pieces = [flat_low, ahead]
    if back:
        pieces = [lax.ppermute(flat_low[shard - back :], ALL, [(i, i + 1) for i in range(devices - 1)])] + pieces
    chunk = lax.dynamic_slice(jnp.concatenate(pieces), (back + GAINS - drift * me,), (span,)).reshape(units, UNIT)
    gain_rows = flat_low[:GAINS].reshape(GAIN_UNITS, UNIT)
    extra = jnp.concatenate([gain_rows, jnp.zeros((16 - GAIN_UNITS, UNIT), bf16)])
    if aligned:
        by_five = chunk.reshape(192, 5, UNIT).transpose(1, 0, 2).reshape(units, UNIT)
        by_three = chunk.reshape(320, 3, UNIT).transpose(1, 0, 2).reshape(units, UNIT)
        sent = chunk.reshape(60, 2, 8, UNIT).transpose(2, 1, 0, 3).reshape(8, 120, UNIT)
        got = lax.all_to_all(sent, PLANE, split_axis=0, concat_axis=0, tiled=True)
        by_share = got.reshape(8, 2, 60, UNIT).transpose(1, 0, 2, 3).reshape(units, UNIT)
        mixed = jnp.where((q_index == 0) & (p_index < 5), by_five, by_three)
        mixed = jnp.where((q_index == 1) | (q_index == 2), by_share, mixed)
        column = lax.all_gather(jnp.concatenate([mixed, extra]), "q")
        level = lax.all_gather(column[0], PLANE)
        gains = level[0, units : units + GAIN_UNITS].astype(f32).reshape(3, D)
        w_qkv = level[:5, :units].reshape(5, 5, 192, UNIT).transpose(1, 0, 2, 3).reshape(5, D, UNIT)
        w_out = level[5:, :units].reshape(3, 3, 320, UNIT).transpose(1, 0, 2, 3).reshape(3, D, UNIT)
        w_gate = jnp.concatenate([column[1, :480], column[2, :480]])
        w_up = jnp.concatenate([column[1, 480:units], column[2, 480:units]])
        w_down = column[3, :units].reshape(3, SHARE, UNIT)
    else:
        full = lax.all_gather(jnp.concatenate([chunk, extra]), ALL)
        gains = full[0, units : units + GAIN_UNITS].astype(f32).reshape(3, D)
        full = full[:, :units].reshape(ALL_UNITS, UNIT)
        edge = np.cumsum([QKV_UNITS, OUT_UNITS, GU_UNITS])
        w_qkv = full[: edge[0]].reshape(D, 5, UNIT).transpose(1, 0, 2)
        w_out = full[edge[0] : edge[1]].reshape(D, 3, UNIT).transpose(1, 0, 2)
        both = lax.dynamic_index_in_dim(full[edge[1] : edge[2]].reshape(D, 2, 8, UNIT), p_index, 2, False)
        w_gate, w_up = both[:, 0], both[:, 1]
        w_down = lax.dynamic_index_in_dim(full[edge[2] :].reshape(8, SHARE, 3, UNIT), p_index, 0, False).transpose(1, 0, 2)

    owner = token_ids // vocab_dev
    owner_hot = hot(owner, devices)
    before = (lax.broadcasted_iota(jnp.int32, (tokens, tokens), 0) > lax.broadcasted_iota(jnp.int32, (tokens, tokens), 1)).astype(bf16)
    slot = jnp.sum(dot(before, owner_hot) * owner_hot.astype(f32), axis=1).astype(jnp.int32)
    spot = hot(owner * capacity + slot, slots)
    marked = token_ids + 1
    halves = jnp.stack([marked // 256, marked % 256]).astype(bf16)
    found = dot(halves, spot).astype(jnp.int32)
    requests = (found[0] * 256 + found[1] - 1).reshape(devices, capacity)
    ask = jnp.concatenate([requests, jnp.broadcast_to(targets[None], (devices, loss_dev))], axis=1)
    asked = lax.all_to_all(ask, ALL, split_axis=0, concat_axis=0, tiled=True)
    row_hot = hot(asked[:, :capacity].reshape(-1) - me * vocab_dev, vocab_dev)
    answer = dot(row_hot, table_low).astype(bf16).reshape(devices, capacity, D)
    returned = lax.all_to_all(answer, ALL, split_axis=0, concat_axis=0, tiled=True).reshape(slots, D)
    x_low = dot(spot, returned).astype(bf16)
    x_embed = x_low.astype(f32) * emb_mult

    pick = hot(loss_rows, tokens)
    cosine, sine = (jnp.asarray(t) for t in rope_tables(tokens))
    cosine_pick, sine_pick = cosine[loss_rows], sine[loss_rows]
    h_attn = (x_embed * scale_of(x_embed) * gains[0]).astype(bf16)
    h_pick = dot(pick, h_attn).astype(bf16)
    x_pick = dot(pick, x_low) * emb_mult
    q_raw = jnp.concatenate([dot(h_pick, w_qkv[j]) for j in range(3)], axis=1)
    query = rotate(q_raw, cosine_pick, sine_pick).astype(bf16)
    key = rotate(dot(h_attn, w_qkv[3]), cosine, sine).astype(bf16)
    value = dot(h_attn, w_qkv[4]).astype(bf16)

    def heads_of(rows):
        return rows.reshape(loss_dev, KEY_VALUE_HEADS, groups, HEAD_SIZE).transpose(1, 2, 0, 3).reshape(KEY_VALUE_HEADS, groups * loss_dev, HEAD_SIZE)

    def heads_back(rows):
        return rows.reshape(KEY_VALUE_HEADS, groups, loss_dev, HEAD_SIZE).transpose(2, 0, 1, 3).reshape(loss_dev, D)

    query_h = heads_of(query)
    key_h = key.reshape(tokens, KEY_VALUE_HEADS, HEAD_SIZE).transpose(1, 0, 2)
    value_h = value.reshape(tokens, KEY_VALUE_HEADS, HEAD_SIZE).transpose(1, 0, 2)
    key_pos = jnp.arange(tokens, dtype=jnp.int32)[None, :]
    ask_pos = jnp.tile(loss_rows, groups)[:, None]
    key_seg = jnp.where(key_pos < PL, 0, 1 + (key_pos - PL) // CL)
    ask_seg = jnp.where(ask_pos < PL, 0, 1 + (ask_pos - PL) // CL)
    allowed = (key_pos <= ask_pos) & ((key_seg == 0) | (key_seg == ask_seg))
    scores = jnp.einsum("hqd,hkd->hqk", query_h, key_h, preferred_element_type=f32) * HEAD_SIZE**-0.5
    scores = jnp.where(allowed[None], scores, NEGATIVE)
    exp_scores = jnp.exp(scores - jnp.max(scores, axis=-1, keepdims=True))
    probs = exp_scores / jnp.sum(exp_scores, axis=-1, keepdims=True)
    probs_low = probs.astype(bf16)
    mixed_heads = jnp.einsum("hqk,hkd->hqd", probs_low, value_h, preferred_element_type=f32)
    attended = heads_back(mixed_heads.astype(bf16))
    x_one = x_pick + jnp.concatenate([dot(attended, w_out[j]) for j in range(3)], axis=1)

    h_mlp = (x_one * scale_of(x_one) * gains[1]).astype(bf16)
    plane_rows = 8 * loss_dev
    h_all = spread_plane(h_mlp).reshape(plane_rows, D)
    gate = dot(h_all, w_gate)
    up = dot(h_all, w_up)
    sig = jax.nn.sigmoid(gate)
    act = (gate * sig * up).astype(bf16)
    part = jnp.concatenate([dot(act, w_down[j]) for j in range(3)], axis=1)
    x_two = x_one + fold_plane(part.reshape(2, 4, loss_dev, D))

    hidden = (x_two * scale_of(x_two) * gains[2]).astype(bf16)
    across = jnp.stack([hidden] + [flip(hidden, "q", k, rows_q) for k in range(1, rows_q)])
    hidden_all = spread_plane(across).reshape(loss_total, D)
    logits = dot(hidden_all, table_low, 1, 1)
    targets_all = jnp.take(asked[:, capacity:], source_of, axis=0).reshape(loss_total)
    column_id = targets_all - me * vocab_dev
    hit = column_id[:, None] == jnp.arange(vocab_dev, dtype=jnp.int32)[None, :]
    local_peak = jnp.max(logits, axis=1)
    local_total = jnp.sum(jnp.exp(logits - local_peak[:, None]), axis=1)
    local_target = jnp.sum(jnp.where(hit, logits, 0.0), axis=1)
    local_sum = jnp.sum(logits, axis=1)
    stats = jnp.stack([local_peak, local_total, local_target, local_sum]).reshape(4, devices, loss_dev)
    stats = jnp.take(stats, order_of, axis=1).transpose(1, 0, 2)
    stats = lax.all_to_all(stats, ALL, split_axis=0, concat_axis=0, tiled=True)
    peak = jnp.max(stats[:, 0], axis=0)
    total = jnp.sum(stats[:, 1] * jnp.exp(stats[:, 0] - peak[None]), axis=0)
    my_log = peak + jnp.log(total)
    my_loss = jnp.sum(
        my_log
        - (1.0 - SMOOTH) * jnp.sum(stats[:, 2], axis=0)
        - SMOOTH / V * jnp.sum(stats[:, 3], axis=0)
        + ZCOEF * my_log * my_log
    )
    logs = lax.all_to_all(jnp.broadcast_to(my_log[None, None], (devices, 1, loss_dev)), ALL, split_axis=0, concat_axis=0, tiled=True)
    log_total = jnp.take(logs[:, 0], source_of, axis=0).reshape(loss_total, 1)
    d_logits = (
        (1.0 + 2.0 * ZCOEF * log_total) * jnp.exp(logits - log_total)
        - jnp.where(hit, 1.0 - SMOOTH, 0.0)
        - SMOOTH / V
    ) / loss_total
    d_logits = d_logits.astype(bf16)
    d_hidden = dot(d_logits, table_low).reshape(2, 4, rows_q, loss_dev, D)
    d_hidden = d_hidden.at[1].get().astype(bf16), d_hidden[0]
    d_hidden = fold_plane([d_hidden[1], d_hidden[0]])
    d_low = d_hidden.astype(bf16)
    total_hidden = d_hidden[0]
    for k in range(1, rows_q):
        total_hidden = total_hidden + flip(d_low[k], "q", k, rows_q).astype(f32)
    head_grad = dot(d_logits, hidden_all, 0, 0)

    d_x_two, grad_final = norm_back(x_two, gains[2], total_hidden)
    d_down = spread_plane(d_x_two.astype(bf16)).reshape(plane_rows, D)
    d_act = sum(dot(d_down[:, UNIT * j : UNIT * (j + 1)], w_down[j], 1, 1) for j in range(3))
    d_gate = (d_act * up * sig * (1.0 + gate * (1.0 - sig))).astype(bf16)
    d_up = (d_act * gate * sig).astype(bf16)
    grad_down = [dot(act, d_down[:, UNIT * j : UNIT * (j + 1)], 0, 0).astype(bf16) for j in range(3)]
    grad_gate = dot(h_all, d_gate, 0, 0).astype(bf16)
    grad_up = dot(h_all, d_up, 0, 0).astype(bf16)
    d_h = dot(d_gate, w_gate, 1, 1) + dot(d_up, w_up, 1, 1)
    d_h_mlp = fold_plane(d_h.reshape(2, 4, loss_dev, D))
    d_x_mlp, grad_mlp = norm_back(x_one, gains[1], d_h_mlp)
    d_x_one = d_x_two + d_x_mlp

    d_branch = d_x_one.astype(bf16)
    grad_out = [dot(attended, d_branch[:, UNIT * j : UNIT * (j + 1)], 0, 0).astype(bf16) for j in range(3)]
    d_attended = sum(dot(d_branch[:, UNIT * j : UNIT * (j + 1)], w_out[j], 1, 1) for j in range(3))
    d_mixed = heads_of(d_attended.astype(bf16))
    d_probs = jnp.einsum("hqd,hkd->hqk", d_mixed, value_h, preferred_element_type=f32)
    delta = jnp.sum(probs * d_probs, axis=-1, keepdims=True)
    d_scores = (probs * (d_probs - delta)).astype(bf16)
    d_query = jnp.einsum("hqk,hkd->hqd", d_scores, key_h, preferred_element_type=f32) * HEAD_SIZE**-0.5
    d_key = jnp.einsum("hqk,hqd->khd", d_scores, query_h, preferred_element_type=f32) * HEAD_SIZE**-0.5
    d_value = jnp.einsum("hqk,hqd->khd", probs_low, d_mixed, preferred_element_type=f32)
    d_q = rotate_back(heads_back(d_query), cosine_pick, sine_pick).astype(bf16)
    d_k = rotate_back(d_key.reshape(tokens, UNIT), cosine, sine).astype(bf16)
    d_v = d_value.reshape(tokens, UNIT).astype(bf16)
    grad_qkv = [dot(h_pick, d_q[:, UNIT * j : UNIT * (j + 1)], 0, 0).astype(bf16) for j in range(3)]
    grad_qkv += [dot(h_attn, d_k, 0, 0).astype(bf16), dot(h_attn, d_v, 0, 0).astype(bf16)]
    d_h_pick = sum(dot(d_q[:, UNIT * j : UNIT * (j + 1)], w_qkv[j], 1, 1) for j in range(3))
    high = d_h_pick.astype(bf16)
    rest = (d_h_pick - high.astype(f32)).astype(bf16)
    d_h_attn = dot(d_k, w_qkv[3], 1, 1) + dot(d_v, w_qkv[4], 1, 1) + dot(pick, high, 0, 0) + dot(pick, rest, 0, 0)
    d_x_attn, grad_attn = norm_back(x_embed, gains[0], d_h_attn)
    high = d_x_one.astype(bf16)
    rest = (d_x_one - high.astype(f32)).astype(bf16)
    d_x_embed = d_x_attn + dot(pick, high, 0, 0) + dot(pick, rest, 0, 0)

    sending = dot(spot, (d_x_embed * emb_mult).astype(bf16), 0, 0).astype(bf16).reshape(devices, capacity, D)
    arrived = lax.all_to_all(sending, ALL, split_axis=0, concat_axis=0, tiled=True).reshape(slots, D)
    table_grad = head_grad + dot(row_hot, arrived, 0, 0)

    gain_grads = jnp.concatenate([grad_attn, grad_mlp, grad_final]).reshape(GAIN_UNITS, UNIT)
    if aligned:
        lower = jnp.stack(grad_qkv).reshape(5, 5, 192, UNIT).transpose(1, 0, 2, 3).reshape(5, units, UNIT)
        upper = jnp.stack(grad_out).reshape(3, 3, 320, UNIT).transpose(1, 0, 2, 3).reshape(3, units, UNIT)
        room = jnp.zeros((8, 64, UNIT), bf16).at[0, :GAIN_UNITS].set(gain_grads.astype(bf16))
        level = jnp.concatenate([jnp.concatenate([lower, upper]), room], axis=1).reshape(4, 2, units + 64, UNIT)
        keep = lax.dynamic_index_in_dim(level, c_index, 1, False)
        give = lax.dynamic_index_in_dim(level, 1 - c_index, 1, False)
        level = keep.astype(f32) + flip(give, "c", 1, 2).astype(f32)
        own = lax.dynamic_index_in_dim(level, yx_index, 0, False)
        for k in (1, 2, 3):
            piece = lax.dynamic_index_in_dim(level, yx_index ^ k, 0, False).astype(bf16)
            own = own + flip(piece, ("y", "x"), k, 4).astype(f32)
        own = own.reshape(4, (units + 64) // 4, UNIT)
        quarter = lax.dynamic_index_in_dim(own, q_index, 0, False)
        for k in (1, 2, 3):
            piece = lax.dynamic_index_in_dim(own, q_index ^ k, 0, False).astype(bf16)
            quarter = quarter + flip(piece, "q", k, 4).astype(f32)
        quarter = quarter.astype(bf16)
        quarters = [quarter] + [lax.ppermute(quarter, "q", [(k, 0)]) for k in (1, 2, 3)]
        first = jnp.concatenate(quarters)
        gain_out = first[units : units + GAIN_UNITS]
        first = first[:units]
        blocks = jnp.concatenate(
            [jnp.zeros((units, UNIT), bf16)]
            + [grad_gate[:480], grad_up[:480], grad_gate[480:], grad_up[480:]]
            + grad_down
        )
        share = lax.psum_scatter(blocks, "q", scatter_dimension=0, tiled=True)
        sent = share.reshape(2, 8, 60, UNIT).transpose(1, 0, 2, 3).reshape(8, 120, UNIT)
        got = lax.all_to_all(sent, PLANE, split_axis=0, concat_axis=0, tiled=True)
        by_share = got.reshape(8, 2, 60, UNIT).transpose(2, 1, 0, 3).reshape(units, UNIT)
        by_five = first.reshape(5, 192, UNIT).transpose(1, 0, 2).reshape(units, UNIT)
        by_three = jnp.where(q_index == 0, first, share).reshape(3, 320, UNIT).transpose(1, 0, 2).reshape(units, UNIT)
        mixed = jnp.where((q_index == 0) & (p_index < 5), by_five, by_three)
        mine = jnp.where((q_index == 1) | (q_index == 2), by_share, mixed)
    else:
        zero = jnp.zeros((D, 2, 8, UNIT), bf16)
        both = lax.dynamic_update_index_in_dim(zero, jnp.stack([grad_gate, grad_up], axis=1), p_index, 2)
        downs = lax.dynamic_update_index_in_dim(jnp.zeros((8, SHARE, 3, UNIT), bf16), jnp.stack(grad_down, axis=1), p_index, 0)
        full = jnp.concatenate(
            [
                jnp.stack(grad_qkv, axis=1).reshape(-1, UNIT),
                jnp.stack(grad_out, axis=1).reshape(-1, UNIT),
                both.reshape(-1, UNIT),
                downs.reshape(-1, UNIT),
            ]
        ).reshape(devices, units, UNIT)
        room = jnp.zeros((devices, 16, UNIT), bf16).at[0, :GAIN_UNITS].set(gain_grads.astype(bf16))
        full = jnp.concatenate([full, room], axis=1)
        summed = lax.psum_scatter(full, ALL, scatter_dimension=0, tiled=False)
        mine, gain_out = summed[:units], summed[units : units + GAIN_UNITS]
    behind = lax.ppermute(mine[units - GAIN_UNITS :], ALL, [(i, i + 1) for i in range(devices - 1)])
    behind = jnp.where(me == 0, gain_out, behind)
    tail = max(0, drift * (devices - 1) + shard - GAINS - span)
    stream = jnp.concatenate([behind.reshape(-1), mine.reshape(-1), jnp.zeros((tail,), bf16)])
    layer_grad = lax.dynamic_slice(stream, (drift * me,), (shard,)).astype(f32)

    squares = jnp.sum(layer_grad * layer_grad) + jnp.sum(table_grad * table_grad)
    sums = jnp.broadcast_to(jnp.stack([squares, my_loss])[None], (devices, 2))
    sums = jnp.sum(lax.all_to_all(sums, ALL, split_axis=0, concat_axis=0, tiled=True), axis=0)
    grad_norm = jnp.sqrt(sums[0])
    loss = sums[1] / loss_total
    limit = CLIP_C / math.sqrt(loss_total)
    clip_factor = limit / jnp.maximum(grad_norm, limit)
    flat_one, flat_two, flat_update = adamw_step(flat_master, layer_grad, flat_m, flat_v, clip_factor)
    table_one, table_two, table_update = adamw_step(table_master, table_grad, table_m, table_v, clip_factor)
    return (loss, grad_norm, flat_one, flat_two, flat_update, table_one, table_two, table_update)


def solution(mesh):
    count = mesh.devices.size
    grid = Mesh(mesh.devices.reshape(count // 8, 2, 2, 2), ALL)
    rows, matrix = P(ALL), P(ALL, None)
    in_specs = (rows,) * 6 + (matrix,) * 3
    out_specs = (P(), P()) + (rows,) * 3 + (matrix,) * 3
    return jax.shard_map(local, mesh=grid, in_specs=in_specs, out_specs=out_specs, check_vma=False)
```

time: 2220 us -> 738 us (0.33)
  waiting for transfers between devices: 1100 us -> 277 us
  local copies, waits for them, and re-layouts: 578 us -> 155 us
  blocking collectives: 231 us -> 32 us
  matrix products: 171 us -> 101 us
  starting transfers between devices: 20.9 us -> 76 us
    unnamed x6 -> x3, waiting for transfers between devices: 725 us -> 0.05 us
    concatenate x1 -> x10, local copies, waits for them, and re-layouts: 328 us -> 14.7 us  [the longest x1 8.11 us: local(): jnp.concatenate([jnp.concatenate([lower, upper]), room], axis=1)]
    ppermute x0 -> x42, waiting for transfers between devices: none -> 163 us  [the longest x37 144 us: flip(): return lax.ppermute(rows, axes, [(i, i ^ bits) for i in range(size)])]
    all_gather x4 -> x0, blocking collectives: 153 us -> none  [joined(): everything = jax.tree.map(lambda part: lax.all_gather(part, axis), x)]
    all_to_all x3 -> x5, waiting for transfers between devices: 210 us -> 57.6 us  [the longest x1 45.8 us: local(): lax.all_to_all(answer, ALL, split_axis=0, concat_axis=0, tiled=True)]
    reduce_scatter x1, waiting for transfers between devices: 142 us -> 0.01 us  [local(): share = lax.psum_scatter(blocks, 'q', scatter_dimension=0, tiled=True)]
    dot_general x50 -> x58, matrix products: 171 us -> 97.7 us  [the longest x53 89.6 us: dot(): lax.dot_general(left, right, (((left_dim,), (right_dim,)), ((), ())), pre...]
    dynamic_slice x62 -> x0, local copies, waits for them, and re-layouts: 55.3 us -> none  [lap(): return combine(so_far, jax.tree.map(lambda part: part[k], everything))]
  transfers between devices with their start and end apart: 7 -> 50, of which waited for: 7 -> 37; matrix products, arithmetic and copies ran while one was open for 3% -> 24% of each run, Pallas kernels for 0% -> 0%
where the time goes in v1:
time: 738 us; the launch traced here: 727 us
  waiting for transfers between devices  277 us (38%)
  local copies, waits for them, and re-layouts  155 us (21%)
  matrix products  101 us (14%)
  starting transfers between devices  76 us (10%)
  other arithmetic  66.1 us (9%)
  blocking collectives  32 us (4%)
  between operations  20.8 us (3%)
    ppermute x37, waiting for transfers between devices, flip(): return lax.ppermute(rows, axes, [(i, i ^ bits) for i in range(size)])  144 us
    dot_general x53, matrix products, dot(): lax.dot_general(left, right, (((left_dim,), (right_dim,)), ((), ())), pre...  89.6 us
    all_gather x1, waiting for transfers between devices, local(): column = lax.all_gather(jnp.concatenate([mixed, extra]), 'q')  56.1 us
    all_to_all x1, waiting for transfers between devices, local(): lax.all_to_all(answer, ALL, split_axis=0, concat_axis=0, tiled=True)  45.8 us
    ppermute x37, starting transfers between devices, flip(): return lax.ppermute(rows, axes, [(i, i ^ bits) for i in range(size)])  44.8 us
    unnamed x208, local copies, waits for them, and re-layouts  33.8 us
    slice x4, local copies, waits for them, and re-layouts, local(): d_hidden = (d_hidden.at[1].get().astype(bf16), d_hidden[0])  15.4 us
  transfers between devices with their start and end apart: 50, of which 37 were waited for; matrix products, arithmetic and copies ran while one was open for 24% of the time, Pallas kernels for 0%

profile of v1, /device:TPU:1, one launch (start us, length us, event | category | flops | bytes accessed | tf_op | source)
XLA Modules:
  0.0 727.4 jit_solution(11717637219618602732)
XLA Ops:
  10.5 3.9 collective-permute-done
  17.9 5.6 all-to-all-start.2
  26.1 5.1 all-to-all-done.2
  34.9 56.1 %all-gather.7.cloned.1.call-done = bf16[4,976,320]{1,2,0:T(8,128)(2,1)} async-done(((bf16[1,976,320]{1,2,0:T(8,128)(2,1)}), bf16[4,976,320]{1,2,0:T(8,128)(2,1)}) %all-gather.7.cloned.1.call-update) | async-done | bytes 2498576 | tf_op jit(solution)/shard_map/all_gather | solution.py:168
  94.7 3.9 all-to-all-start
  98.7 6.7 all-to-all-done
  105.5 4.5 fusion.25
  110.0 2.5 copy.433
  112.6 3.1 all-to-all-start.1
  118.3 45.8 %all-to-all-done.1 = bf16[32,32,960]{2,1,0:T(8,128)(2,1)S(1)} async-done(((bf16[32,32,960]{2,1,0:T(8,128)(2,1)}), bf16[32,32,960]{2,1,0:T(8,128)(2,1)S(1)}, u32[]{:S(2)}, u32[]{:S(2)}) %all-to-all-start.1) | async-done | bytes 1966112 | tf_op jit(solution)/shard_map/all_to_all | solution.py:200
  171.3 3.6 copy.512
  189.1 3.2 fusion.206
  192.3 2.9 convolution_convert_fusion.15
  195.7 3.0 slice.423
  198.7 3.3 copy.513
  211.6 2.6 collective-permute-start.4
  234.5 5.2 collective-permute-done.6
  240.2 5.9 collective-permute-done.8
  253.6 4.5 collective-permute-done.11
  260.9 7.5 %collective-permute-done.12 = bf16[4,64,960]{2,1,0:T(8,128)(2,1)S(1)} collective-permute-done((bf16[4,64,960]{2,1,0:T(8,128)(2,1)S(1)}, bf16[4,64,960]{2,1,0:T(8,128)(2,1)S(1)}, u32[]{:S(2)}, u32[]{:S(2)}) %collective-permute-start.12) | collective-permute-done | bytes 491552 | tf_op jit(solution)/shard_map/ppermute | solution.py:70
  268.4 11.0 %collective-permute-done.14 = bf16[4,64,960]{2,1,0:T(8,128)(2,1)S(1)} collective-permute-done((bf16[4,64,960]{2,1,0:T(8,128)(2,1)S(1)}, bf16[4,64,960]{2,1,0:T(8,128)(2,1)S(1)}, u32[]{:S(2)}, u32[]{:S(2)}) %collective-permute-start.14) | collective-permute-done | bytes 491552 | tf_op jit(solution)/shard_map/ppermute | solution.py:70
  281.8 4.7 collective-permute-start.15
  290.6 2.8 pad_maximum_fusion.1
  294.0 6.6 fusion.207
  300.7 4.8 exponential_reduce_fusion
  306.6 12.9 %all_to_all.48 = f32[32,1,256]{2,1,0:T(1,128)S(1)} all-to-all(f32[32,1,256]{2,1,0:T(1,128)S(1)} %reshape.784), channel_id=1, replica_groups=mesh['q'=4,'y'=2,'x'=2,'c'=2] {'q','y','x','c'}, dimensions={0} | all-to-all | bytes 65536 | tf_op jit(solution)/shard_map/all_to_all | solution.py:261
  321.6 8.6 %all_to_all.49 = f32[32,1,64]{2,1,0:T(1,128)S(1)} all-to-all(f32[32,1,64]{2,1,0:T(1,128)S(1)} %broadcast_in_dim.143), channel_id=1, replica_groups=mesh['q'=4,'y'=2,'x'=2,'c'=2] {'q','y','x','c'}, dimensions={0} | all-to-all | bytes 16384 | tf_op jit(solution)/shard_map/all_to_all | solution.py:271
  331.0 8.6 %fusion.170 = f32[2048,960]{0,1:T(8,128)S(1)} fusion(f32[1000,960]{0,1:T(8,128)} %param.21, f32[2048,1000]{0,1:T(8,128)} %get-tuple-element.132, f32[2048]{0:T(1024)S(1)} %select_n.282, f32[2048]{0:T(1024)S(1)} %multiply_add_fusion.2, s32[2048]{0:T(1024)S(1)} %sub.159), kind=kOutput, calls=%fused_computation.397 | convolution fusion | flops 3949504000 | bytes 19920896 | tf_op jit(solution)/shard_map/dot_general | solution.py:48
  339.6 3.2 copy-done.22
  344.4 3.9 copy.462
  348.9 4.6 slice.445
  353.5 5.4 copy.461
  358.9 3.7 fusion.194
  365.5 10.8 %collective-permute-done.17 = bf16[4,64,960]{2,1,0:T(8,128)(2,1)S(1)} collective-permute-done((bf16[4,64,960]{2,1,0:T(8,128)(2,1)S(1)}, bf16[4,64,960]{2,1,0:T(8,128)(2,1)S(1)}, u32[]{:S(2)}, u32[]{:S(2)}) %collective-permute-start.17) | collective-permute-done | bytes 491552 | tf_op jit(solution)/shard_map/ppermute | solution.py:70
  376.4 11.3 %collective-permute-done.19 = bf16[4,64,960]{2,1,0:T(8,128)(2,1)S(1)} collective-permute-done((bf16[4,64,960]{2,1,0:T(8,128)(2,1)S(1)}, bf16[4,64,960]{2,1,0:T(8,128)(2,1)S(1)}, u32[]{:S(2)}, u32[]{:S(2)}) %collective-permute-start.19) | collective-permute-done | bytes 491552 | tf_op jit(solution)/shard_map/ppermute | solution.py:70
  388.6 3.0 collective-permute-start.22
  394.0 4.5 collective-permute-done.22
  402.8 2.6 collective-permute-done.24
  406.2 5.1 collective-permute-start.26
  459.5 2.7 collective-permute-done.28
  463.7 5.2 collective-permute-done.30
  473.4 3.9 convolution_convert_fusion.11
  515.3 4.4 copy.480
  525.0 3.5 fusion.15
  530.1 5.8 pad_maximum_fusion
  535.9 8.1 %copy.485 = bf16[8,1024,320]{1,2,0:T(8,128)(2,1)} copy(bf16[8,1024,320]{2,1,0:T(8,128)(2,1)} %pad_maximum_fusion) | data formatting | bytes 10485760 | tf_op jit(solution)/shard_map/concatenate | solution.py:334
  544.0 3.5 dynamic-slice_bitcast_fusion
  550.9 4.8 fusion.24
  555.6 3.9 copy.501
  559.5 3.7 all-to-all-start.6
  563.3 3.7 convert_add_fusion
  573.0 26.4 %collective-permute-done.32 = bf16[1024,320]{0,1:T(8,128)(2,1)S(1)} collective-permute-done((bf16[1024,320]{0,1:T(8,128)(2,1)}, bf16[1024,320]{0,1:T(8,128)(2,1)S(1)}, u32[]{:S(2)}, u32[]{:S(2)}) %collective-permute-start.32) | collective-permute-done | bytes 655392 | tf_op jit(solution)/shard_map/ppermute | solution.py:70
  599.5 6.3 collective-permute-done.33
  605.8 11.3 %collective-permute-done.34 = bf16[1024,320]{0,1:T(8,128)(2,1)S(1)} collective-permute-done((bf16[1024,320]{0,1:T(8,128)(2,1)S(1)}, bf16[1024,320]{0,1:T(8,128)(2,1)S(1)}, u32[]{:S(2)}, u32[]{:S(2)}) %collective-permute-start.34) | collective-permute-done | bytes 655392 | tf_op jit(solution)/shard_map/ppermute | solution.py:70
  623.1 4.6 collective-permute-done.35
  627.9 7.6 %collective-permute-done.37 = bf16[256,320]{1,0:T(8,128)(2,1)S(1)} collective-permute-done((bf16[256,320]{1,0:T(8,128)(2,1)S(1)}, bf16[256,320]{1,0:T(8,128)(2,1)S(1)}, u32[]{:S(2)}, u32[]{:S(2)}) %collective-permute-start.37) | collective-permute-done | bytes 163872 | tf_op jit(solution)/shard_map/ppermute | solution.py:70
  639.6 4.4 collective-permute-done.38
  644.0 9.6 %collective-permute-done.39 = bf16[256,320]{1,0:T(8,128)(2,1)S(1)} collective-permute-done((bf16[256,320]{1,0:T(8,128)(2,1)S(1)}, bf16[256,320]{1,0:T(8,128)(2,1)S(1)}, u32[]{:S(2)}, u32[]{:S(2)}) %collective-permute-start.39) | collective-permute-done | bytes 163872 | tf_op jit(solution)/shard_map/ppermute | solution.py:348
  661.8 5.0 all-to-all-start.5
  666.9 4.3 fusion.1
  671.2 11.1 %multiply_reduce_fusion = (f32[]{:T(128)}, f32[1000,960]{0,1:T(8,128)}) fusion(f32[1000,960]{0,1:T(8,128)S(1)} %fusion.1, bf16[2048,960]{1,0:T(8,128)(2,1)S(1)} %bitcast.394, f32[2048,1000]{0,1:T(8,128)} %get-tuple-element.132, f32[2048]{0:T(1024)S(1)} %select_n.282, f32[2048]{0:T(1024)S(1)} %copy-done.82, s32[2048]{0:T(1024)S(1)} %sub.159), kind=kOutput, calls=%fused_computation.23 | convolution fusion | flops 3951424000 | bytes 19828740 | tf_op jit(solution)/shard_map/dot_general | solution.py:48
  685.3 3.7 collective-permute-start.41
  693.1 10.4 %all_to_all.50 = f32[32,1,2]{2,1,0:T(1,128)S(1)} all-to-all(f32[32,1,2]{2,1,0:T(1,128)S(1)} %broadcast_in_dim.147), channel_id=1, replica_groups=mesh['q'=4,'y'=2,'x'=2,'c'=2] {'q','y','x','c'}, dimensions={0} | all-to-all | bytes 512 | tf_op jit(solution)/shard_map/all_to_all | solution.py:389
  705.5 10.3 %add_multiply_fusion = (f32[1000,960]{0,1:T(8,128)}, f32[1000,960]{0,1:T(8,128)}, f32[1000,960]{0,1:T(8,128)}) fusion(f32[1000,960]{0,1:T(8,128)} %param.21, f32[1000,960]{0,1:T(8,128)} %get-tuple-element.139, f32[]{:T(128)S(6)} %div.148, f32[1000,960]{0,1:T(8,128)} %param.23, f32[1000,960]{0,1:T(8,128)} %param.22), kind=kLoop, calls=%fused_computation.21 | loop fusion | flops 14400000 | bytes 26880004 | tf_op jit(solution)/shard_map/mul | solution.py:103
  (519 shorter events, 241.1 us)
Async XLA Ops:
  8.5 5.8 collective-permute-start
  17.9 13.3 %all-to-all-start.2 = ((bf16[8,120,320]{1,2,0:T(8,128)(2,1)}), bf16[8,120,320]{1,2,0:T(8,128)(2,1)}, u32[]{:S(2)}, u32[]{:S(2)}) async-start(bf16[8,120,320]{1,2,0:T(8,128)(2,1)} %copy.435), calls=%async_computation.2 | async-start | bytes 1310720 | tf_op jit(solution)/shard_map/all_to_all | solution.py:164
  23.5 67.6 %all-gather.7.cloned.1.call-start = ((), (), s32[]{:S(2)}) async-start(), calls=%async_computation.10 | async-start | bytes 3276800 | tf_op jit(solution)/shard_map/all_gather | solution.py:168
  33.7 59.3 %copy-start.88 = (s32[512]{0:T(512)S(1)}, s32[512]{0:T(512)}, u32[]{:S(2)}) copy-start(s32[512]{0:T(512)} %param.15) | copy-start | bytes 6148
  34.9 59.2 %copy-start.90 = (s32[64]{0:T(128)S(1)}, s32[64]{0:T(128)}, u32[]{:S(2)}) copy-start(s32[64]{0:T(128)} %param.17) | copy-start | bytes 772
  34.9 132.1 %all-gather.9.cloned.1.call-start = ((), (), s32[]{:S(2)}) async-start(), calls=%async_computation.11 | async-start | bytes 5898240 | tf_op jit(solution)/shard_map/all_gather | solution.py:169
  93.4 70.7 %copy-start.85 = (s32[512]{0:T(512)}, s32[512]{0:T(512)S(1)}, u32[]{:S(2)}) copy-start(s32[512]{0:T(512)S(1)} %convert_add_fusion.2) | copy-start | bytes 6148
  94.7 10.7 %all-to-all-start = ((s32[32,1,96]{2,1,0:T(1,128)}), s32[32,1,96]{2,1,0:T(1,128)S(1)}, u32[]{:S(2)}, u32[]{:S(2)}) async-start(s32[32,1,96]{2,1,0:T(1,128)} %bitcast), calls=%async_computation | async-start | bytes 32768 | tf_op jit(solution)/shard_map/all_to_all | solution.py:197
  112.6 51.5 %all-to-all-start.1 = ((bf16[32,32,960]{2,1,0:T(8,128)(2,1)}), bf16[32,32,960]{2,1,0:T(8,128)(2,1)S(1)}, u32[]{:S(2)}, u32[]{:S(2)}) async-start(bf16[32,32,960]{2,1,0:T(8,128)(2,1)} %bitcast.2), calls=%async_computation.1 | async-start | bytes 4194304 | tf_op jit(solution)/shard_map/all_to_all | solution.py:200
  115.7 537.8 %reduce-scatter.2.cloned.1.call-start = ((), (), s32[]{:S(2)}) async-start(), calls=%async_computation.9 | async-start | bytes 3686400 | tf_op jit(solution)/shard_map/reduce_scatter | solution.py:357
  116.7 68.7 %copy-start.62 = (f32[64,64]{0,1:T(8,128)}, f32[64,64]{0,1:T(8,128)S(1)}, u32[]{:S(2)}) copy-start(f32[64,64]{0,1:T(8,128)S(1)} %copy.445) | copy-start | bytes 49156
  117.3 49.1 %copy-start.64 = (f32[64,64]{1,0:T(8,128)}, f32[64,64]{1,0:T(8,128)S(1)}, u32[]{:S(2)}) copy-start(f32[64,64]{1,0:T(8,128)S(1)} %gather_fusion.1) | copy-start | bytes 49156
  167.0 20.5 %copy-start.78 = (f32[512]{0:T(512)}, f32[512]{0:T(512)S(1)}, u32[]{:S(2)}) copy-start(f32[512]{0:T(512)S(1)} %get-tuple-element.117) | copy-start | bytes 6148
  177.4 10.1 %copy-start.29 = (bf16[1,5,192,320]{3,2,0,1:T(8,128)(2,1)}, bf16[1,5,192,320]{3,2,0,1:T(8,128)(2,1)S(1)}, u32[]{:S(2)}) copy-start(bf16[1,5,192,320]{3,2,0,1:T(8,128)(2,1)S(1)} %get-tuple-element.59) | copy-start | bytes 1843204
  204.1 3.9 collective-permute-start.1
  205.0 4.1 collective-permute-start.2
  206.4 5.2 collective-permute-start.3
  211.6 4.3 collective-permute-start.4
  226.0 3.0 collective-permute-start.5
  231.7 8.0 %collective-permute-start.6 = (f32[64,960]{1,0:T(8,128)}, f32[64,960]{1,0:T(8,128)S(1)}, u32[]{:S(2)}, u32[]{:S(2)}) collective-permute-start(f32[64,960]{1,0:T(8,128)} %get-tuple-element.87), channel_id=1, source_target_pairs={{0,2},{2,0},{4,6},{6,4},{1,3},{3,1},{5,7},{7,5},{8,10},{10,8},{12,... | collective-permute-start | bytes 737288 | tf_op jit(solution)/shard_map/ppermute | solution.py:70
  232.4 7.8 %collective-permute-start.7 = (f32[64,960]{1,0:T(8,128)}, f32[64,960]{1,0:T(8,128)}, u32[]{:S(2)}, u32[]{:S(2)}) collective-permute-start(f32[64,960]{1,0:T(8,128)} %get-tuple-element.89), channel_id=1, source_target_pairs={{0,4},{2,6},{4,0},{6,2},{1,5},{3,7},{5,1},{7,3},{8,12},{10,14},{12... | collective-permute-start | bytes 737288 | tf_op jit(solution)/shard_map/ppermute | solution.py:70
  233.0 13.1 %collective-permute-start.8 = (f32[64,960]{1,0:T(8,128)}, f32[64,960]{1,0:T(8,128)}, u32[]{:S(2)}, u32[]{:S(2)}) collective-permute-start(f32[64,960]{1,0:T(8,128)} %get-tuple-element.88), channel_id=1, source_target_pairs={{0,6},{2,4},{4,2},{6,0},{1,7},{3,5},{5,3},{7,1},{8,14},{10,12},{12... | collective-permute-start | bytes 737288 | tf_op jit(solution)/shard_map/ppermute | solution.py:70
  247.5 6.1 collective-permute-start.9
  247.6 6.0 collective-permute-start.10
  249.9 8.2 %collective-permute-start.11 = (bf16[64,960]{1,0:T(8,128)(2,1)S(1)}, bf16[64,960]{1,0:T(8,128)(2,1)S(1)}, u32[]{:S(2)}, u32[]{:S(2)}) collective-permute-start(bf16[64,960]{1,0:T(8,128)(2,1)S(1)} %multiply_convert_fusion.5), channel_id=1, source_target_pairs={{0,24},{8,16},{16,8},{24,0},{1,25},{9,17},{17,9},{25,1},{2,26},{10... | collective-permute-start | bytes 368648 | tf_op jit(solution)/shard_map/ppermute | solution.py:70
  258.2 10.2 %collective-permute-start.12 = (bf16[4,64,960]{2,1,0:T(8,128)(2,1)S(1)}, bf16[4,64,960]{2,1,0:T(8,128)(2,1)S(1)}, u32[]{:S(2)}, u32[]{:S(2)}) collective-permute-start(bf16[4,64,960]{2,1,0:T(8,128)(2,1)S(1)} %get-tuple-element.104), channel_id=1, source_target_pairs={{0,2},{2,0},{4,6},{6,4},{1,3},{3,1},{5,7},{7,5},{8,10},{10,8},{12,... | collective-permute-start | bytes 1474568 | tf_op jit(solution)/shard_map/ppermute | solution.py:70
  258.5 9.9 %collective-permute-start.13 = (bf16[4,64,960]{2,1,0:T(8,128)(2,1)S(1)}, bf16[4,64,960]{2,1,0:T(8,128)(2,1)S(1)}, u32[]{:S(2)}, u32[]{:S(2)}) collective-permute-start(bf16[4,64,960]{2,1,0:T(8,128)(2,1)S(1)} %get-tuple-element.104), channel_id=1, source_target_pairs={{0,4},{2,6},{4,0},{6,2},{1,5},{3,7},{5,1},{7,3},{8,12},{10,14},{12... | collective-permute-start | bytes 1474568 | tf_op jit(solution)/shard_map/ppermute | solution.py:70
  258.9 20.6 %collective-permute-start.14 = (bf16[4,64,960]{2,1,0:T(8,128)(2,1)S(1)}, bf16[4,64,960]{2,1,0:T(8,128)(2,1)S(1)}, u32[]{:S(2)}, u32[]{:S(2)}) collective-permute-start(bf16[4,64,960]{2,1,0:T(8,128)(2,1)S(1)} %get-tuple-element.104), channel_id=1, source_target_pairs={{0,6},{2,4},{4,2},{6,0},{1,7},{3,5},{5,3},{7,1},{8,14},{10,12},{12... | collective-permute-start | bytes 1474568 | tf_op jit(solution)/shard_map/ppermute | solution.py:70
  279.5 7.8 %copy-start.89 = (s32[32]{0:T(128)S(1)}, s32[32]{0:T(128)}, u32[]{:S(2)}) copy-start(s32[32]{0:T(128)} %constant.301.clone) | copy-start | bytes 388
  281.8 8.8 %collective-permute-start.15 = (bf16[4,4,64,960]{3,2,1,0:T(8,128)(2,1)}, bf16[4,4,64,960]{3,2,1,0:T(8,128)(2,1)}, u32[]{:S(2)}, u32[]{:S(2)}) collective-permute-start(bf16[4,4,64,960]{3,2,1,0:T(8,128)(2,1)} %get-tuple-element.74), channel_id=1, source_target_pairs={{0,1},{1,0},{2,3},{3,2},{4,5},{5,4},{6,7},{7,6},{8,9},{9,8},{10,11... | collective-permute-start | bytes 5898248 | tf_op jit(solution)/shard_map/ppermute | solution.py:70
  331.0 8.6 %copy-start.81 = (f32[2048]{0:T(1024)}, f32[2048]{0:T(1024)S(1)}, u32[]{:S(2)}) copy-start(f32[2048]{0:T(1024)S(1)} %multiply_add_fusion.2) | copy-start | bytes 24580
  348.3 10.6 %collective-permute-start.16 = (bf16[4,4,64,960]{3,2,1,0:T(8,128)(2,1)}, bf16[4,4,64,960]{3,2,1,0:T(8,128)(2,1)}, u32[]{:S(2)}, u32[]{:S(2)}) collective-permute-start(bf16[4,4,64,960]{3,2,1,0:T(8,128)(2,1)} %bitcast.418), channel_id=1, source_target_pairs={{0,1},{1,0},{2,3},{3,2},{4,5},{5,4},{6,7},{7,6},{8,9},{9,8},{10,11... | collective-permute-start | bytes 5898248 | tf_op jit(solution)/shard_map/ppermute | solution.py:70
  362.8 13.5 %collective-permute-start.17 = (bf16[4,64,960]{2,1,0:T(8,128)(2,1)S(1)}, bf16[4,64,960]{2,1,0:T(8,128)(2,1)S(1)}, u32[]{:S(2)}, u32[]{:S(2)}) collective-permute-start(bf16[4,64,960]{2,1,0:T(8,128)(2,1)S(1)} %get-tuple-element.70), channel_id=1, source_target_pairs={{0,2},{2,0},{4,6},{6,4},{1,3},{3,1},{5,7},{7,5},{8,10},{10,8},{12,... | collective-permute-start | bytes 1474568 | tf_op jit(solution)/shard_map/ppermute | solution.py:70
  363.1 13.2 %collective-permute-start.18 = (bf16[4,64,960]{2,1,0:T(8,128)(2,1)S(1)}, bf16[4,64,960]{2,1,0:T(8,128)(2,1)S(1)}, u32[]{:S(2)}, u32[]{:S(2)}) collective-permute-start(bf16[4,64,960]{2,1,0:T(8,128)(2,1)S(1)} %get-tuple-element.72), channel_id=1, source_target_pairs={{0,4},{2,6},{4,0},{6,2},{1,5},{3,7},{5,1},{7,3},{8,12},{10,14},{12... | collective-permute-start | bytes 1474568 | tf_op jit(solution)/shard_map/ppermute | solution.py:70
  363.5 24.1 %collective-permute-start.19 = (bf16[4,64,960]{2,1,0:T(8,128)(2,1)S(1)}, bf16[4,64,960]{2,1,0:T(8,128)(2,1)S(1)}, u32[]{:S(2)}, u32[]{:S(2)}) collective-permute-start(bf16[4,64,960]{2,1,0:T(8,128)(2,1)S(1)} %get-tuple-element.71), channel_id=1, source_target_pairs={{0,6},{2,4},{4,2},{6,0},{1,7},{3,5},{5,3},{7,1},{8,14},{10,12},{12... | collective-permute-start | bytes 1474568 | tf_op jit(solution)/shard_map/ppermute | solution.py:70
  388.0 5.5 collective-permute-start.20
  388.4 5.6 collective-permute-start.21
  388.6 9.9 %collective-permute-start.22 = (bf16[64,960]{1,0:T(8,128)(2,1)S(1)}, bf16[64,960]{1,0:T(8,128)(2,1)S(1)}, u32[]{:S(2)}, u32[]{:S(2)}) collective-permute-start(bf16[64,960]{1,0:T(8,128)(2,1)S(1)} %get-tuple-element.101), channel_id=1, source_target_pairs={{0,24},{8,16},{16,8},{24,0},{1,25},{9,17},{17,9},{25,1},{2,26},{10... | collective-permute-start | bytes 368648 | tf_op jit(solution)/shard_map/ppermute | solution.py:70
  398.9 3.9 collective-permute-start.23
  400.1 5.2 collective-permute-start.24
  400.4 4.9 collective-permute-start.25
  406.2 6.7 collective-permute-start.26
  427.8 24.1 %collective-permute-start.27 = (f32[4,64,960]{2,1,0:T(8,128)}, f32[4,64,960]{2,1,0:T(8,128)}, u32[]{:S(2)}, u32[]{:S(2)}) collective-permute-start(f32[4,64,960]{2,1,0:T(8,128)} %bitcast.424), channel_id=1, source_target_pairs={{0,1},{1,0},{2,3},{3,2},{4,5},{5,4},{6,7},{7,6},{8,9},{9,8},{10,11... | collective-permute-start | bytes 2949128 | tf_op jit(solution)/shard_map/ppermute | solution.py:70
  454.3 7.9 %collective-permute-start.28 = (f32[64,960]{1,0:T(8,128)}, f32[64,960]{1,0:T(8,128)S(1)}, u32[]{:S(2)}, u32[]{:S(2)}) collective-permute-start(f32[64,960]{1,0:T(8,128)} %get-tuple-element.84), channel_id=1, source_target_pairs={{0,2},{2,0},{4,6},{6,4},{1,3},{3,1},{5,7},{7,5},{8,10},{10,8},{12,... | collective-permute-start | bytes 737288 | tf_op jit(solution)/shard_map/ppermute | solution.py:70
  455.3 7.7 %collective-permute-start.29 = (f32[64,960]{1,0:T(8,128)}, f32[64,960]{1,0:T(8,128)S(1)}, u32[]{:S(2)}, u32[]{:S(2)}) collective-permute-start(f32[64,960]{1,0:T(8,128)} %get-tuple-element.86), channel_id=1, source_target_pairs={{0,4},{2,6},{4,0},{6,2},{1,5},{3,7},{5,1},{7,3},{8,12},{10,14},{12... | collective-permute-start | bytes 737288 | tf_op jit(solution)/shard_map/ppermute | solution.py:70
  455.7 13.1 %collective-permute-start.30 = (f32[64,960]{1,0:T(8,128)}, f32[64,960]{1,0:T(8,128)}, u32[]{:S(2)}, u32[]{:S(2)}) collective-permute-start(f32[64,960]{1,0:T(8,128)} %get-tuple-element.85), channel_id=1, source_target_pairs={{0,6},{2,4},{4,2},{6,0},{1,7},{3,5},{5,3},{7,1},{8,14},{10,12},{12... | collective-permute-start | bytes 737288 | tf_op jit(solution)/shard_map/ppermute | solution.py:70
  459.5 12.1 %copy-start.18 = (bf16[1,3,320,320]{3,2,0,1:T(8,128)(2,1)S(1)}, bf16[1,3,320,320]{3,2,0,1:T(8,128)(2,1)}, u32[]{:S(2)}) copy-start(bf16[1,3,320,320]{3,2,0,1:T(8,128)(2,1)} %copy-done.17) | copy-start | bytes 1843204
  459.5 12.5 %copy-start.14 = (bf16[1,3,320,320]{3,2,0,1:T(8,128)(2,1)S(1)}, bf16[1,3,320,320]{3,2,0,1:T(8,128)(2,1)}, u32[]{:S(2)}) copy-start(bf16[1,3,320,320]{3,2,0,1:T(8,128)(2,1)} %copy-done.13) | copy-start | bytes 1843204
  547.5 15.8 %collective-permute-start.31 = (bf16[4,1024,320]{1,2,0:T(8,128)(2,1)}, bf16[4,1024,320]{1,2,0:T(8,128)(2,1)}, u32[]{:S(2)}, u32[]{:S(2)}) collective-permute-start(bf16[4,1024,320]{1,2,0:T(8,128)(2,1)} %dynamic-slice_bitcast_fusion), channel_id=1, source_target_pairs={{0,1},{1,0},{2,3},{3,2},{4,5},{5,4},{6,7},{7,6},{8,9},{9,8},{10,11... | collective-permute-start | bytes 7864328 | tf_op jit(solution)/shard_map/ppermute | solution.py:70
  559.5 102.3 %all-to-all-start.6 = ((bf16[32,32,960]{2,1,0:T(8,128)(2,1)}), bf16[32,32,960]{2,1,0:T(8,128)(2,1)}, u32[]{:S(2)}, u32[]{:S(2)}) async-start(bf16[32,32,960]{2,1,0:T(8,128)(2,1)} %bitcast.150), calls=%async_computation.7 | async-start | bytes 4194304 | tf_op jit(solution)/shard_map/all_to_all | solution.py:326
  570.4 29.1 %collective-permute-start.32 = (bf16[1024,320]{0,1:T(8,128)(2,1)}, bf16[1024,320]{0,1:T(8,128)(2,1)S(1)}, u32[]{:S(2)}, u32[]{:S(2)}) collective-permute-start(bf16[1024,320]{0,1:T(8,128)(2,1)} %get-tuple-element.55), channel_id=1, source_target_pairs={{0,2},{2,0},{4,6},{6,4},{1,3},{3,1},{5,7},{7,5},{8,10},{10,8},{12,... | collective-permute-start | bytes 1966088 | tf_op jit(solution)/shard_map/ppermute | solution.py:70
  571.7 34.0 %collective-permute-start.33 = (bf16[1024,320]{0,1:T(8,128)(2,1)S(1)}, bf16[1024,320]{0,1:T(8,128)(2,1)S(1)}, u32[]{:S(2)}, u32[]{:S(2)}) collective-permute-start(bf16[1024,320]{0,1:T(8,128)(2,1)S(1)} %get-tuple-element.57), channel_id=1, source_target_pairs={{0,4},{2,6},{4,0},{6,2},{1,5},{3,7},{5,1},{7,3},{8,12},{10,14},{12... | collective-permute-start | bytes 1966088 | tf_op jit(solution)/shard_map/ppermute | solution.py:70
  572.9 44.2 %collective-permute-start.34 = (bf16[1024,320]{0,1:T(8,128)(2,1)S(1)}, bf16[1024,320]{0,1:T(8,128)(2,1)S(1)}, u32[]{:S(2)}, u32[]{:S(2)}) collective-permute-start(bf16[1024,320]{0,1:T(8,128)(2,1)S(1)} %get-tuple-element.56), channel_id=1, source_target_pairs={{0,6},{2,4},{4,2},{6,0},{1,7},{3,5},{5,3},{7,1},{8,14},{10,12},{12... | collective-permute-start | bytes 1966088 | tf_op jit(solution)/shard_map/ppermute | solution.py:70
  619.4 8.4 %collective-permute-start.35 = (bf16[256,320]{1,0:T(8,128)(2,1)S(1)}, bf16[256,320]{1,0:T(8,128)(2,1)S(1)}, u32[]{:S(2)}, u32[]{:S(2)}) collective-permute-start(bf16[256,320]{1,0:T(8,128)(2,1)S(1)} %get-tuple-element.79), channel_id=1, source_target_pairs={{0,8},{8,0},{16,24},{24,16},{1,9},{9,1},{17,25},{25,17},{2,10},{10... | collective-permute-start | bytes 491528 | tf_op jit(solution)/shard_map/ppermute | solution.py:70
  620.5 7.5 %collective-permute-start.36 = (bf16[256,320]{1,0:T(8,128)(2,1)S(1)}, bf16[256,320]{1,0:T(8,128)(2,1)S(1)}, u32[]{:S(2)}, u32[]{:S(2)}) collective-permute-start(bf16[256,320]{1,0:T(8,128)(2,1)S(1)} %get-tuple-element.81), channel_id=1, source_target_pairs={{0,16},{8,24},{16,0},{24,8},{1,17},{9,25},{17,1},{25,9},{2,18},{10... | collective-permute-start | bytes 491528 | tf_op jit(solution)/shard_map/ppermute | solution.py:70
  622.9 12.7 %collective-permute-start.37 = (bf16[256,320]{1,0:T(8,128)(2,1)S(1)}, bf16[256,320]{1,0:T(8,128)(2,1)S(1)}, u32[]{:S(2)}, u32[]{:S(2)}) collective-permute-start(bf16[256,320]{1,0:T(8,128)(2,1)S(1)} %get-tuple-element.80), channel_id=1, source_target_pairs={{0,24},{8,16},{16,8},{24,0},{1,25},{9,17},{17,9},{25,1},{2,26},{10... | collective-permute-start | bytes 491528 | tf_op jit(solution)/shard_map/ppermute | solution.py:70
  635.7 8.3 %collective-permute-start.38 = (bf16[256,320]{1,0:T(8,128)(2,1)S(1)}, bf16[256,320]{1,0:T(8,128)(2,1)S(1)}, u32[]{:S(2)}, u32[]{:S(2)}) collective-permute-start(bf16[256,320]{1,0:T(8,128)(2,1)S(1)} %fusion.80), channel_id=1, source_target_pairs={{24,0},{25,1},{26,2},{27,3},{28,4},{29,5},{30,6},{31,7}} | collective-permute-start | bytes 491528 | tf_op jit(solution)/shard_map/ppermute | solution.py:348
  637.0 16.6 %collective-permute-start.39 = (bf16[256,320]{1,0:T(8,128)(2,1)S(1)}, bf16[256,320]{1,0:T(8,128)(2,1)S(1)}, u32[]{:S(2)}, u32[]{:S(2)}) collective-permute-start(bf16[256,320]{1,0:T(8,128)(2,1)S(1)} %fusion.80), channel_id=1, source_target_pairs={{8,0},{9,1},{10,2},{11,3},{12,4},{13,5},{14,6},{15,7}} | collective-permute-start | bytes 491528 | tf_op jit(solution)/shard_map/ppermute | solution.py:348
  638.3 15.3 %collective-permute-start.40 = (bf16[256,320]{1,0:T(8,128)(2,1)S(1)}, bf16[256,320]{1,0:T(8,128)(2,1)S(1)}, u32[]{:S(2)}, u32[]{:S(2)}) collective-permute-start(bf16[256,320]{1,0:T(8,128)(2,1)S(1)} %fusion.80), channel_id=1, source_target_pairs={{16,0},{17,1},{18,2},{19,3},{20,4},{21,5},{22,6},{23,7}} | collective-permute-start | bytes 491528 | tf_op jit(solution)/shard_map/ppermute | solution.py:348
  661.8 20.4 %all-to-all-start.5 = ((bf16[8,120,320]{1,2,0:T(8,128)(2,1)}), bf16[8,120,320]{1,2,0:T(8,128)(2,1)S(1)}, u32[]{:S(2)}, u32[]{:S(2)}) async-start(bf16[8,120,320]{1,2,0:T(8,128)(2,1)} %copy.495), calls=%async_computation.6 | async-start | bytes 1310720 | tf_op jit(solution)/shard_map/all_to_all | solution.py:359
  685.3 4.6 collective-permute-start.41
  705.5 10.3 %copy-start.19 = (f32[307290]{0:T(1024)S(1)}, f32[307290]{0:T(1024)}, u32[]{:S(2)}) copy-start(f32[307290]{0:T(1024)} %param.18) | copy-start | bytes 3687484
  705.5 10.3 %copy-start.51 = (f32[307290]{0:T(1024)S(1)}, f32[307290]{0:T(1024)}, u32[]{:S(2)}) copy-start(f32[307290]{0:T(1024)} %param.20) | copy-start | bytes 3687484
  705.5 10.3 %copy-start.52 = (f32[307290]{0:T(1024)S(1)}, f32[307290]{0:T(1024)}, u32[]{:S(2)}) copy-start(f32[307290]{0:T(1024)} %param.19) | copy-start | bytes 3687484
  (82 other events, 251.6 us)
Sparse Core Ops, SparseCore 0:
  35.0 56.0 all-gather.6
  93.5 59.7 all-gather.8
  459.6 56.3 reduce-scatter.1

commit v2 on v1

--- a/solution.py
+++ b/solution.py
@@ -147,8 +147,22 @@
     source_of = me ^ jnp.asarray(place, jnp.int32)
     order_of = jnp.take(jnp.asarray(rank_of, jnp.int32), me ^ jnp.arange(devices, dtype=jnp.int32))
 
+    table_low = table_master.astype(bf16)
+    owner = token_ids // vocab_dev
+    owner_hot = hot(owner, devices)
+    before = (lax.broadcasted_iota(jnp.int32, (tokens, tokens), 0) > lax.broadcasted_iota(jnp.int32, (tokens, tokens), 1)).astype(bf16)
+    slot = jnp.sum(dot(before, owner_hot) * owner_hot.astype(f32), axis=1).astype(jnp.int32)
+    spot = hot(owner * capacity + slot, slots)
+    marked = token_ids + 1
+    halves = jnp.stack([marked // 256, marked % 256]).astype(bf16)
+    found = dot(halves, spot).astype(jnp.int32)
+    requests = (found[0] * 256 + found[1] - 1).reshape(devices, capacity)
+    ask = jnp.concatenate([requests, jnp.broadcast_to(targets[None], (devices, loss_dev))], axis=1)
+    asked = lax.all_to_all(ask, ALL, split_axis=0, concat_axis=0, tiled=True)
+    row_hot = hot(asked[:, :capacity].reshape(-1) - me * vocab_dev, vocab_dev)
+    answer = dot(row_hot, table_low).astype(bf16).reshape(devices, capacity, D)
+
     flat_low = flat_master.astype(bf16)
-    table_low = table_master.astype(bf16)
     ahead = lax.ppermute(flat_low[:GAINS], ALL, [(i + 1, i) for i in range(devices - 1)])
     back = max(0, drift * (devices - 1) - GAINS)
     pieces = [flat_low, ahead]
@@ -162,18 +176,26 @@
         by_three = chunk.reshape(320, 3, UNIT).transpose(1, 0, 2).reshape(units, UNIT)
         sent = chunk.reshape(60, 2, 8, UNIT).transpose(2, 1, 0, 3).reshape(8, 120, UNIT)
         got = lax.all_to_all(sent, PLANE, split_axis=0, concat_axis=0, tiled=True)
-        by_share = got.reshape(8, 2, 60, UNIT).transpose(1, 0, 2, 3).reshape(units, UNIT)
-        mixed = jnp.where((q_index == 0) & (p_index < 5), by_five, by_three)
-        mixed = jnp.where((q_index == 1) | (q_index == 2), by_share, mixed)
-        column = lax.all_gather(jnp.concatenate([mixed, extra]), "q")
-        level = lax.all_gather(column[0], PLANE)
+        first = jnp.concatenate([jnp.where(p_index < 5, by_five, by_three), extra])
+        jumped = lax.ppermute(first, "q", [(0, 2)])
+        first = jnp.where(q_index == 2, jumped, first)
+        stepped = lax.ppermute(first, "q", [(0, 1), (2, 3)])
+        first = jnp.where((q_index == 1) | (q_index == 3), stepped, first)
+        answer, first, got = lax.optimization_barrier((answer, first, got))
+        returned = lax.all_to_all(answer, ALL, split_axis=0, concat_axis=0, tiled=True).reshape(slots, D)
+        level = lax.all_gather(first, PLANE)
         gains = level[0, units : units + GAIN_UNITS].astype(f32).reshape(3, D)
         w_qkv = level[:5, :units].reshape(5, 5, 192, UNIT).transpose(1, 0, 2, 3).reshape(5, D, UNIT)
         w_out = level[5:, :units].reshape(3, 3, 320, UNIT).transpose(1, 0, 2, 3).reshape(3, D, UNIT)
+        by_share = got.reshape(8, 2, 60, UNIT).transpose(1, 0, 2, 3).reshape(units, UNIT)
+        mixed = jnp.where(q_index == 3, by_three, by_share)
+        mixed, returned = lax.optimization_barrier((mixed, returned))
+        column = lax.all_gather(mixed, "q")
         w_gate = jnp.concatenate([column[1, :480], column[2, :480]])
-        w_up = jnp.concatenate([column[1, 480:units], column[2, 480:units]])
-        w_down = column[3, :units].reshape(3, SHARE, UNIT)
+        w_up = jnp.concatenate([column[1, 480:], column[2, 480:]])
+        w_down = column[3].reshape(3, SHARE, UNIT)
     else:
+        returned = lax.all_to_all(answer, ALL, split_axis=0, concat_axis=0, tiled=True).reshape(slots, D)
         full = lax.all_gather(jnp.concatenate([chunk, extra]), ALL)
         gains = full[0, units : units + GAIN_UNITS].astype(f32).reshape(3, D)
         full = full[:, :units].reshape(ALL_UNITS, UNIT)
@@ -183,21 +205,6 @@
         both = lax.dynamic_index_in_dim(full[edge[1] : edge[2]].reshape(D, 2, 8, UNIT), p_index, 2, False)
         w_gate, w_up = both[:, 0], both[:, 1]
         w_down = lax.dynamic_index_in_dim(full[edge[2] :].reshape(8, SHARE, 3, UNIT), p_index, 0, False).transpose(1, 0, 2)
-
-    owner = token_ids // vocab_dev
-    owner_hot = hot(owner, devices)
-    before = (lax.broadcasted_iota(jnp.int32, (tokens, tokens), 0) > lax.broadcasted_iota(jnp.int32, (tokens, tokens), 1)).astype(bf16)
-    slot = jnp.sum(dot(before, owner_hot) * owner_hot.astype(f32), axis=1).astype(jnp.int32)
-    spot = hot(owner * capacity + slot, slots)
-    marked = token_ids + 1
-    halves = jnp.stack([marked // 256, marked % 256]).astype(bf16)
-    found = dot(halves, spot).astype(jnp.int32)
-    requests = (found[0] * 256 + found[1] - 1).reshape(devices, capacity)
-    ask = jnp.concatenate([requests, jnp.broadcast_to(targets[None], (devices, loss_dev))], axis=1)
-    asked = lax.all_to_all(ask, ALL, split_axis=0, concat_axis=0, tiled=True)
-    row_hot = hot(asked[:, :capacity].reshape(-1) - me * vocab_dev, vocab_dev)
-    answer = dot(row_hot, table_low).astype(bf16).reshape(devices, capacity, D)
-    returned = lax.all_to_all(answer, ALL, split_axis=0, concat_axis=0, tiled=True).reshape(slots, D)
     x_low = dot(spot, returned).astype(bf16)
     x_embed = x_low.astype(f32) * emb_mult
 
@@ -299,7 +306,6 @@
     d_x_one = d_x_two + d_x_mlp
 
     d_branch = d_x_one.astype(bf16)
-    grad_out = [dot(attended, d_branch[:, UNIT * j : UNIT * (j + 1)], 0, 0).astype(bf16) for j in range(3)]
     d_attended = sum(dot(d_branch[:, UNIT * j : UNIT * (j + 1)], w_out[j], 1, 1) for j in range(3))
     d_mixed = heads_of(d_attended.astype(bf16))
     d_probs = jnp.einsum("hqd,hkd->hqk", d_mixed, value_h, preferred_element_type=f32)
@@ -311,8 +317,6 @@
     d_q = rotate_back(heads_back(d_query), cosine_pick, sine_pick).astype(bf16)
     d_k = rotate_back(d_key.reshape(tokens, UNIT), cosine, sine).astype(bf16)
     d_v = d_value.reshape(tokens, UNIT).astype(bf16)
-    grad_qkv = [dot(h_pick, d_q[:, UNIT * j : UNIT * (j + 1)], 0, 0).astype(bf16) for j in range(3)]
-    grad_qkv += [dot(h_attn, d_k, 0, 0).astype(bf16), dot(h_attn, d_v, 0, 0).astype(bf16)]
     d_h_pick = sum(dot(d_q[:, UNIT * j : UNIT * (j + 1)], w_qkv[j], 1, 1) for j in range(3))
     high = d_h_pick.astype(bf16)
     rest = (d_h_pick - high.astype(f32)).astype(bf16)
@@ -323,8 +327,19 @@
     d_x_embed = d_x_attn + dot(pick, high, 0, 0) + dot(pick, rest, 0, 0)
 
     sending = dot(spot, (d_x_embed * emb_mult).astype(bf16), 0, 0).astype(bf16).reshape(devices, capacity, D)
+    if aligned:
+        blocks = jnp.concatenate(
+            [jnp.zeros((units, UNIT), bf16)]
+            + [grad_gate[:480], grad_up[:480], grad_gate[480:], grad_up[480:]]
+            + grad_down
+        )
+        share = lax.psum_scatter(blocks, "q", scatter_dimension=0, tiled=True)
+        sending, share = lax.optimization_barrier((sending, share))
+    sending, d_q, d_k, d_v, attended = lax.optimization_barrier((sending, d_q, d_k, d_v, attended))
     arrived = lax.all_to_all(sending, ALL, split_axis=0, concat_axis=0, tiled=True).reshape(slots, D)
-    table_grad = head_grad + dot(row_hot, arrived, 0, 0)
+    grad_out = [dot(attended, d_branch[:, UNIT * j : UNIT * (j + 1)], 0, 0).astype(bf16) for j in range(3)]
+    grad_qkv = [dot(h_pick, d_q[:, UNIT * j : UNIT * (j + 1)], 0, 0).astype(bf16) for j in range(3)]
+    grad_qkv += [dot(h_attn, d_k, 0, 0).astype(bf16), dot(h_attn, d_v, 0, 0).astype(bf16)]
 
     gain_grads = jnp.concatenate([grad_attn, grad_mlp, grad_final]).reshape(GAIN_UNITS, UNIT)
     if aligned:
@@ -332,6 +347,7 @@
         upper = jnp.stack(grad_out).reshape(3, 3, 320, UNIT).transpose(1, 0, 2, 3).reshape(3, units, UNIT)
         room = jnp.zeros((8, 64, UNIT), bf16).at[0, :GAIN_UNITS].set(gain_grads.astype(bf16))
         level = jnp.concatenate([jnp.concatenate([lower, upper]), room], axis=1).reshape(4, 2, units + 64, UNIT)
+        level, arrived = lax.optimization_barrier((level, arrived))
         keep = lax.dynamic_index_in_dim(level, c_index, 1, False)
         give = lax.dynamic_index_in_dim(level, 1 - c_index, 1, False)
         level = keep.astype(f32) + flip(give, "c", 1, 2).astype(f32)
@@ -349,12 +365,6 @@
         first = jnp.concatenate(quarters)
         gain_out = first[units : units + GAIN_UNITS]
         first = first[:units]
-        blocks = jnp.concatenate(
-            [jnp.zeros((units, UNIT), bf16)]
-            + [grad_gate[:480], grad_up[:480], grad_gate[480:], grad_up[480:]]
-            + grad_down
-        )
-        share = lax.psum_scatter(blocks, "q", scatter_dimension=0, tiled=True)
         sent = share.reshape(2, 8, 60, UNIT).transpose(1, 0, 2, 3).reshape(8, 120, UNIT)
         got = lax.all_to_all(sent, PLANE, split_axis=0, concat_axis=0, tiled=True)
         by_share = got.reshape(8, 2, 60, UNIT).transpose(2, 1, 0, 3).reshape(units, UNIT)
@@ -384,6 +394,7 @@
     stream = jnp.concatenate([behind.reshape(-1), mine.reshape(-1), jnp.zeros((tail,), bf16)])
     layer_grad = lax.dynamic_slice(stream, (drift * me,), (shard,)).astype(f32)
 
+    table_grad = head_grad + dot(row_hot, arrived, 0, 0)
     squares = jnp.sum(layer_grad * layer_grad) + jnp.sum(table_grad * table_grad)
     sums = jnp.broadcast_to(jnp.stack([squares, my_loss])[None], (devices, 2))
     sums = jnp.sum(lax.all_to_all(sums, ALL, split_axis=0, concat_axis=0, tiled=True), axis=0)

time: 738 us -> 695 us (0.942)
  waiting for transfers between devices: 277 us -> 216 us
  starting transfers between devices: 76 us -> 85.2 us
    all_gather x2, waiting for transfers between devices: 56.1 us -> 9.57 us  [the longest x1 8.77 us: local(): column = lax.all_gather(mixed, 'q')]
    ppermute x37, waiting for transfers between devices: 144 us -> 111 us  [flip(): return lax.ppermute(rows, axes, [(i, i ^ bits) for i in range(size)])]
    all_to_all x2, waiting for transfers between devices: 5.07 us -> 28 us  [local(): got = lax.all_to_all(sent, PLANE, split_axis=0, concat_axis=0, tiled=True)]
    reduce_scatter x1, waiting for transfers between devices: 0.01 us -> 12.9 us  [local(): share = lax.psum_scatter(blocks, 'q', scatter_dimension=0, tiled=True)]
    ppermute x3, waiting for transfers between devices: 14 us -> 1.68 us  [local(): lax.ppermute(quarter, 'q', [(k, 0)])]
    ppermute x37, starting transfers between devices: 44.8 us -> 36.8 us  [flip(): return lax.ppermute(rows, axes, [(i, i ^ bits) for i in range(size)])]
    unnamed x208 -> x214, local copies, waits for them, and re-layouts: 33.8 us -> 34.2 us
  transfers between devices with their start and end apart: 50 -> 52, of which waited for: 37 -> 32; matrix products, arithmetic and copies ran while one was open for 24% -> 30% of each run, Pallas kernels for 0% -> 0%
where the time goes in v2:
time: 695 us; the launch traced here: 684 us
  waiting for transfers between devices  216 us (31%)
  local copies, waits for them, and re-layouts  158 us (23%)
  matrix products  106 us (15%)
  starting transfers between devices  85.2 us (12%)
  other arithmetic  64.4 us (9%)
  blocking collectives  31.6 us (5%)
  between operations  21.2 us (3%)
    ppermute x37, waiting for transfers between devices, flip(): return lax.ppermute(rows, axes, [(i, i ^ bits) for i in range(size)])  111 us
    dot_general x53, matrix products, dot(): lax.dot_general(left, right, (((left_dim,), (right_dim,)), ((), ())), pre...  95.2 us
    all_to_all x1, waiting for transfers between devices, local(): lax.all_to_all(answer, ALL, split_axis=0, concat_axis=0, tiled=True)  42.8 us
    ppermute x37, starting transfers between devices, flip(): return lax.ppermute(rows, axes, [(i, i ^ bits) for i in range(size)])  36.8 us
    unnamed x214, local copies, waits for them, and re-layouts  34.2 us
    all_to_all x2, waiting for transfers between devices, local(): got = lax.all_to_all(sent, PLANE, split_axis=0, concat_axis=0, tiled=True)  28 us
    slice x4, local copies, waits for them, and re-layouts, local(): d_hidden = (d_hidden.at[1].get().astype(bf16), d_hidden[0])  15.4 us
  transfers between devices with their start and end apart: 52, of which 32 were waited for; matrix products, arithmetic and copies ran while one was open for 30% of the time, Pallas kernels for 0%

profile of v2, /device:TPU:1, one launch (start us, length us, event | category | flops | bytes accessed | tf_op | source)
XLA Modules:
  0.0 683.6 jit_solution(6236428479156338761)
XLA Ops:
  11.6 2.7 collective-permute-done
  20.0 5.0 collective-permute-start.1
  26.3 4.4 all-to-all-start
  32.8 5.1 collective-permute-done.1
  42.9 5.8 all-to-all-start.1
  48.8 4.5 fusion.25
  53.3 2.5 copy.469
  58.7 8.8 %all-to-all-start.2 = ((bf16[32,32,960]{2,1,0:T(8,128)(2,1)}), bf16[32,32,960]{2,1,0:T(8,128)(2,1)}, u32[]{:S(2)}, u32[]{:S(2)}) async-start(bf16[32,32,960]{2,1,0:T(8,128)(2,1)} %bitcast.4), calls=%async_computation.2 | async-start | bytes 4194304 | tf_op jit(solution)/shard_map/all_to_all | solution.py:185
  72.9 42.8 %all-to-all-done.2 = bf16[32,32,960]{2,1,0:T(8,128)(2,1)} async-done(((bf16[32,32,960]{2,1,0:T(8,128)(2,1)}), bf16[32,32,960]{2,1,0:T(8,128)(2,1)}, u32[]{:S(2)}, u32[]{:S(2)}) %all-to-all-start.2) | async-done | bytes 1966112 | tf_op jit(solution)/shard_map/all_to_all | solution.py:185
  116.7 3.9 fusion.23
  124.4 3.6 copy.555
  128.0 3.3 fusion.192
  149.9 3.0 slice.425
  153.0 3.4 copy.556
  162.3 3.1 collective-permute-done.5
  165.4 3.4 collective-permute-done.4
  169.3 8.8 %all-gather.9.cloned.1.call-done = bf16[4,960,320]{1,2,0:T(8,128)(2,1)} async-done(((bf16[1,960,320]{1,2,0:T(8,128)(2,1)}), bf16[4,960,320]{1,2,0:T(8,128)(2,1)}) %all-gather.9.cloned.1.call-update) | async-done | bytes 2457616 | tf_op jit(solution)/shard_map/all_gather | solution.py:193
  189.0 2.5 copy.498
  200.4 5.8 collective-permute-done.10
  206.3 6.4 collective-permute-done.9
  215.2 2.6 collective-permute-start.11
  217.9 2.8 collective-permute-done.13
  220.6 6.3 collective-permute-done.12
  229.7 10.6 %collective-permute-done.16 = bf16[4,64,960]{2,1,0:T(8,128)(2,1)S(1)} collective-permute-done((bf16[4,64,960]{2,1,0:T(8,128)(2,1)S(1)}, bf16[4,64,960]{2,1,0:T(8,128)(2,1)S(1)}, u32[]{:S(2)}, u32[]{:S(2)}) %collective-permute-start.16) | collective-permute-done | bytes 491552 | tf_op jit(solution)/shard_map/ppermute | solution.py:70
  240.3 12.7 %collective-permute-done.15 = bf16[4,64,960]{2,1,0:T(8,128)(2,1)S(1)} collective-permute-done((bf16[4,64,960]{2,1,0:T(8,128)(2,1)S(1)}, bf16[4,64,960]{2,1,0:T(8,128)(2,1)S(1)}, u32[]{:S(2)}, u32[]{:S(2)}) %collective-permute-start.15) | collective-permute-done | bytes 491552 | tf_op jit(solution)/shard_map/ppermute | solution.py:70
  257.7 2.5 collective-permute-done.17
  260.3 2.8 pad_maximum_fusion.1
  263.6 6.7 fusion.203
  270.5 4.8 exponential_reduce_fusion
  276.4 10.6 %all_to_all.48 = f32[32,1,256]{2,1,0:T(1,128)S(1)} all-to-all(f32[32,1,256]{2,1,0:T(1,128)S(1)} %reshape.781), channel_id=1, replica_groups=mesh['q'=4,'y'=2,'x'=2,'c'=2] {'q','y','x','c'}, dimensions={0} | all-to-all | bytes 65536 | tf_op jit(solution)/shard_map/all_to_all | solution.py:268
  289.1 8.6 %all_to_all.49 = f32[32,1,64]{2,1,0:T(1,128)S(1)} all-to-all(f32[32,1,64]{2,1,0:T(1,128)S(1)} %broadcast_in_dim.143), channel_id=1, replica_groups=mesh['q'=4,'y'=2,'x'=2,'c'=2] {'q','y','x','c'}, dimensions={0} | all-to-all | bytes 16384 | tf_op jit(solution)/shard_map/all_to_all | solution.py:278
  298.4 8.6 %fusion.166 = f32[2048,960]{0,1:T(8,128)S(1)} fusion(f32[1000,960]{0,1:T(8,128)} %param.21, f32[2048,1000]{0,1:T(8,128)} %get-tuple-element.160, f32[2048]{0:T(1024)S(1)} %select_n.304, f32[2048]{0:T(1024)S(1)} %multiply_add_fusion.2, s32[2048]{0:T(1024)S(1)} %sub.159), kind=kOutput, calls=%fused_computation.400 | convolution fusion | flops 3949504000 | bytes 19920896 | tf_op jit(solution)/shard_map/dot_general | solution.py:48
  307.1 3.1 copy-done.17
  311.8 3.9 copy.502
  316.3 4.6 slice.447
  320.9 5.4 copy.501
  326.3 3.7 fusion.190
  332.9 11.8 %collective-permute-done.21 = bf16[4,64,960]{2,1,0:T(8,128)(2,1)S(1)} collective-permute-done((bf16[4,64,960]{2,1,0:T(8,128)(2,1)S(1)}, bf16[4,64,960]{2,1,0:T(8,128)(2,1)S(1)}, u32[]{:S(2)}, u32[]{:S(2)}) %collective-permute-start.21) | collective-permute-done | bytes 491552 | tf_op jit(solution)/shard_map/ppermute | solution.py:70
  344.7 10.4 %collective-permute-done.20 = bf16[4,64,960]{2,1,0:T(8,128)(2,1)S(1)} collective-permute-done((bf16[4,64,960]{2,1,0:T(8,128)(2,1)S(1)}, bf16[4,64,960]{2,1,0:T(8,128)(2,1)S(1)}, u32[]{:S(2)}, u32[]{:S(2)}) %collective-permute-start.20) | collective-permute-done | bytes 491552 | tf_op jit(solution)/shard_map/ppermute | solution.py:70
  361.4 6.3 collective-permute-done.23
  368.0 2.5 collective-permute-start.27
  372.9 3.7 collective-permute-done.26
  425.4 3.6 collective-permute-done.32
  429.0 6.2 collective-permute-done.31
  445.3 3.9 convolution_convert_fusion.11
  454.6 2.4 fusion.21
  458.8 5.3 fusion.24
  464.2 3.9 copy.515
  468.1 12.9 %reduce-scatter.2.cloned.1.call-done = bf16[960,320]{1,0:T(8,128)(2,1)} async-done(((bf16[3840,320]{1,0:T(8,128)(2,1)}), bf16[960,320]{1,0:T(8,128)(2,1)}) %reduce-scatter.2.cloned.1.call-update) | async-done | bytes 614416 | tf_op jit(solution)/shard_map/reduce_scatter | solution.py:336
  480.9 5.8 all-to-all-start.5
  509.5 2.5 convolution_convert_fusion.9
  521.6 3.6 pad_maximum_fusion
  525.3 8.1 %copy.533 = bf16[8,1024,320]{1,2,0:T(8,128)(2,1)} copy(bf16[8,1024,320]{2,1,0:T(8,128)(2,1)} %pad_maximum_fusion) | data formatting | bytes 10485760 | tf_op jit(solution)/shard_map/concatenate | solution.py:349
  537.7 4.7 collective-permute-done.33
  542.3 3.7 convert_add_fusion
  554.3 5.1 all-to-all-start.6
  559.5 28.0 %all-to-all-done.6 = bf16[8,120,320]{1,2,0:T(8,128)(2,1)S(1)} async-done(((bf16[8,120,320]{1,2,0:T(8,128)(2,1)}), bf16[8,120,320]{1,2,0:T(8,128)(2,1)S(1)}, u32[]{:S(2)}, u32[]{:S(2)}) %all-to-all-start.6) | async-done | bytes 614432 | tf_op jit(solution)/shard_map/all_to_all | solution.py:369
  599.0 6.0 fusion.1
  605.5 5.5 collective-permute-done.38
  615.3 13.1 %multiply_reduce_fusion = (f32[]{:T(128)}, f32[1000,960]{0,1:T(8,128)}) fusion(f32[1000,960]{0,1:T(8,128)} %fusion.1, bf16[2048,960]{1,0:T(8,128)(2,1)} %bitcast.397, f32[2048,1000]{0,1:T(8,128)} %get-tuple-element.160, f32[2048]{0:T(1024)} %copy-done.75, f32[2048]{0:T(1024)} %copy-done.86, s32[2048]{0:T(1024)} %copy-done.74), kind=kOutput, calls=%fused_computation.23 | convolution fusion | flops 3951424000 | bytes 19828740 | tf_op jit(solution)/shard_map/dot_general | solution.py:48
  638.0 4.9 collective-permute-start.43
  646.9 12.4 %all_to_all.50 = f32[32,1,2]{2,1,0:T(1,128)S(1)} all-to-all(f32[32,1,2]{2,1,0:T(1,128)S(1)} %broadcast_in_dim.147), channel_id=1, replica_groups=mesh['q'=4,'y'=2,'x'=2,'c'=2] {'q','y','x','c'}, dimensions={0} | all-to-all | bytes 512 | tf_op jit(solution)/shard_map/all_to_all | solution.py:400
  661.4 4.2 add_multiply_fusion.1
  666.7 7.8 %add_multiply_fusion = (f32[1000,960]{0,1:T(8,128)}, f32[1000,960]{0,1:T(8,128)}, f32[1000,960]{0,1:T(8,128)}) fusion(f32[1000,960]{0,1:T(8,128)S(1)} %copy-done.20, f32[1000,960]{0,1:T(8,128)} %get-tuple-element.167, f32[]{:T(128)S(6)} %div.148, f32[1000,960]{0,1:T(8,128)S(1)} %copy-done.21, f32[1000,960]{0,1:T(8,128)} %param.22), kind=kLoop, calls=%fused_computation.21 | loop fusion | flops 14400000 | bytes 26880004 | tf_op jit(solution)/shard_map/mul | solution.py:103
  (537 shorter events, 244.8 us)
Async XLA Ops:
  8.5 5.8 collective-permute-start
  20.0 17.9 %collective-permute-start.1 = (bf16[976,320]{0,1:T(8,128)(2,1)}, bf16[976,320]{0,1:T(8,128)(2,1)}, u32[]{:S(2)}, u32[]{:S(2)}) collective-permute-start(bf16[976,320]{0,1:T(8,128)(2,1)} %copy.471), channel_id=1, source_target_pairs={{0,16},{1,17},{2,18},{3,19},{4,20},{5,21},{6,22},{7,23}} | collective-permute-start | bytes 1873928 | tf_op jit(solution)/shard_map/ppermute | solution.py:180
  25.0 91.7 %copy-start.88 = (s32[512]{0:T(512)}, s32[512]{0:T(512)S(1)}, u32[]{:S(2)}) copy-start(s32[512]{0:T(512)S(1)} %convert_add_fusion.2) | copy-start | bytes 6148
  26.3 16.6 %all-to-all-start = ((s32[32,1,96]{2,1,0:T(1,128)}), s32[32,1,96]{2,1,0:T(1,128)S(1)}, u32[]{:S(2)}, u32[]{:S(2)}) async-start(s32[32,1,96]{2,1,0:T(1,128)} %bitcast.2), calls=%async_computation | async-start | bytes 32768 | tf_op jit(solution)/shard_map/all_to_all | solution.py:161
  40.8 15.1 %collective-permute-start.2 = (bf16[976,320]{0,1:T(8,128)(2,1)}, bf16[976,320]{0,1:T(8,128)(2,1)}, u32[]{:S(2)}, u32[]{:S(2)}) collective-permute-start(bf16[976,320]{0,1:T(8,128)(2,1)} %copy.473), channel_id=1, source_target_pairs={{0,8},{16,24},{1,9},{17,25},{2,10},{18,26},{3,11},{19,27},{4,12},{... | collective-permute-start | bytes 1873928 | tf_op jit(solution)/shard_map/ppermute | solution.py:182
  42.9 14.5 %all-to-all-start.1 = ((bf16[8,120,320]{1,2,0:T(8,128)(2,1)}), bf16[8,120,320]{1,2,0:T(8,128)(2,1)}, u32[]{:S(2)}, u32[]{:S(2)}) async-start(bf16[8,120,320]{1,2,0:T(8,128)(2,1)} %copy.476), calls=%async_computation.1 | async-start | bytes 1310720 | tf_op jit(solution)/shard_map/all_to_all | solution.py:178
  48.7 73.4 %all-gather.7.cloned.1.call-start = ((), (), s32[]{:S(2)}) async-start(), calls=%async_computation.10 | async-start | bytes 5898240 | tf_op jit(solution)/shard_map/all_gather | solution.py:186
  58.7 10.4 %copy-start.65 = (f32[512,64]{1,0:T(8,128)S(1)}, f32[512,64]{1,0:T(8,128)}, u32[]{:S(2)}) copy-start(f32[512,64]{1,0:T(8,128)} %constant.315) | copy-start | bytes 393220
  58.7 57.0 %all-to-all-start.2 = ((bf16[32,32,960]{2,1,0:T(8,128)(2,1)}), bf16[32,32,960]{2,1,0:T(8,128)(2,1)}, u32[]{:S(2)}, u32[]{:S(2)}) async-start(bf16[32,32,960]{2,1,0:T(8,128)(2,1)} %bitcast.4), calls=%async_computation.2 | async-start | bytes 4194304 | tf_op jit(solution)/shard_map/all_to_all | solution.py:185
  67.4 110.7 %all-gather.9.cloned.1.call-start = ((), (), s32[]{:S(2)}) async-start(), calls=%async_computation.11 | async-start | bytes 3276800 | tf_op jit(solution)/shard_map/all_gather | solution.py:193
  121.3 23.2 %copy-start.84 = (f32[512]{0:T(512)}, f32[512]{0:T(512)S(1)}, u32[]{:S(2)}) copy-start(f32[512]{0:T(512)S(1)} %get-tuple-element.145) | copy-start | bytes 6148
  121.3 359.6 %reduce-scatter.2.cloned.1.call-start = ((), (), s32[]{:S(2)}) async-start(), calls=%async_computation.9 | async-start | bytes 3686400 | tf_op jit(solution)/shard_map/reduce_scatter | solution.py:336
  133.4 11.1 %copy-start.76 = (f32[960]{0:T(1024)}, f32[960]{0:T(1024)S(1)}, u32[]{:S(2)}) copy-start(f32[960]{0:T(1024)S(1)} %mul.477) | copy-start | bytes 11524
  159.5 5.9 collective-permute-start.5
  160.9 7.9 %collective-permute-start.4 = (bf16[64,960]{1,0:T(8,128)(2,1)S(1)}, bf16[64,960]{1,0:T(8,128)(2,1)S(1)}, u32[]{:S(2)}, u32[]{:S(2)}) collective-permute-start(bf16[64,960]{1,0:T(8,128)(2,1)S(1)} %multiply_convert_fusion.6), channel_id=1, source_target_pairs={{0,4},{2,6},{4,0},{6,2},{1,5},{3,7},{5,1},{7,3},{8,12},{10,14},{12... | collective-permute-start | bytes 368648 | tf_op jit(solution)/shard_map/ppermute | solution.py:70
  161.3 7.5 %collective-permute-start.3 = (bf16[64,960]{1,0:T(8,128)(2,1)S(1)}, bf16[64,960]{1,0:T(8,128)(2,1)S(1)}, u32[]{:S(2)}, u32[]{:S(2)}) collective-permute-start(bf16[64,960]{1,0:T(8,128)(2,1)S(1)} %multiply_convert_fusion.6), channel_id=1, source_target_pairs={{0,2},{2,0},{4,6},{6,4},{1,3},{3,1},{5,7},{7,5},{8,10},{10,8},{12,... | collective-permute-start | bytes 368648 | tf_op jit(solution)/shard_map/ppermute | solution.py:70
  168.9 10.9 %collective-permute-start.6 = (bf16[4,64,960]{2,1,0:T(8,128)(2,1)S(1)}, bf16[4,64,960]{2,1,0:T(8,128)(2,1)S(1)}, u32[]{:S(2)}, u32[]{:S(2)}) collective-permute-start(bf16[4,64,960]{2,1,0:T(8,128)(2,1)S(1)} %get-tuple-element.134), channel_id=1, source_target_pairs={{0,1},{1,0},{2,3},{3,2},{4,5},{5,4},{6,7},{7,6},{8,9},{9,8},{10,11... | collective-permute-start | bytes 1474568 | tf_op jit(solution)/shard_map/ppermute | solution.py:70
  191.6 3.5 collective-permute-start.7
  197.6 8.6 %collective-permute-start.10 = (f32[64,960]{1,0:T(8,128)}, f32[64,960]{1,0:T(8,128)S(1)}, u32[]{:S(2)}, u32[]{:S(2)}) collective-permute-start(f32[64,960]{1,0:T(8,128)} %get-tuple-element.116), channel_id=1, source_target_pairs={{0,6},{2,4},{4,2},{6,0},{1,7},{3,5},{5,3},{7,1},{8,14},{10,12},{12... | collective-permute-start | bytes 737288 | tf_op jit(solution)/shard_map/ppermute | solution.py:70
  199.7 12.9 %collective-permute-start.9 = (f32[64,960]{1,0:T(8,128)}, f32[64,960]{1,0:T(8,128)}, u32[]{:S(2)}, u32[]{:S(2)}) collective-permute-start(f32[64,960]{1,0:T(8,128)} %get-tuple-element.117), channel_id=1, source_target_pairs={{0,4},{2,6},{4,0},{6,2},{1,5},{3,7},{5,1},{7,3},{8,12},{10,14},{12... | collective-permute-start | bytes 737288 | tf_op jit(solution)/shard_map/ppermute | solution.py:70
  200.0 12.7 %collective-permute-start.8 = (f32[64,960]{1,0:T(8,128)}, f32[64,960]{1,0:T(8,128)}, u32[]{:S(2)}, u32[]{:S(2)}) collective-permute-start(f32[64,960]{1,0:T(8,128)} %get-tuple-element.115), channel_id=1, source_target_pairs={{0,2},{2,0},{4,6},{6,4},{1,3},{3,1},{5,7},{7,5},{8,10},{10,8},{12,... | collective-permute-start | bytes 737288 | tf_op jit(solution)/shard_map/ppermute | solution.py:70
  214.1 6.5 collective-permute-start.13
  214.8 12.1 %collective-permute-start.12 = (bf16[64,960]{1,0:T(8,128)(2,1)S(1)}, bf16[64,960]{1,0:T(8,128)(2,1)S(1)}, u32[]{:S(2)}, u32[]{:S(2)}) collective-permute-start(bf16[64,960]{1,0:T(8,128)(2,1)S(1)} %multiply_convert_fusion.5), channel_id=1, source_target_pairs={{0,16},{8,24},{16,0},{24,8},{1,17},{9,25},{17,1},{25,9},{2,18},{10... | collective-permute-start | bytes 368648 | tf_op jit(solution)/shard_map/ppermute | solution.py:70
  215.2 11.7 %collective-permute-start.11 = (bf16[64,960]{1,0:T(8,128)(2,1)S(1)}, bf16[64,960]{1,0:T(8,128)(2,1)S(1)}, u32[]{:S(2)}, u32[]{:S(2)}) collective-permute-start(bf16[64,960]{1,0:T(8,128)(2,1)S(1)} %multiply_convert_fusion.5), channel_id=1, source_target_pairs={{0,8},{8,0},{16,24},{24,16},{1,9},{9,1},{17,25},{25,17},{2,10},{10... | collective-permute-start | bytes 368648 | tf_op jit(solution)/shard_map/ppermute | solution.py:70
  227.0 13.3 %collective-permute-start.16 = (bf16[4,64,960]{2,1,0:T(8,128)(2,1)S(1)}, bf16[4,64,960]{2,1,0:T(8,128)(2,1)S(1)}, u32[]{:S(2)}, u32[]{:S(2)}) collective-permute-start(bf16[4,64,960]{2,1,0:T(8,128)(2,1)S(1)} %get-tuple-element.132), channel_id=1, source_target_pairs={{0,6},{2,4},{4,2},{6,0},{1,7},{3,5},{5,3},{7,1},{8,14},{10,12},{12... | collective-permute-start | bytes 1474568 | tf_op jit(solution)/shard_map/ppermute | solution.py:70
  227.7 25.3 %collective-permute-start.15 = (bf16[4,64,960]{2,1,0:T(8,128)(2,1)S(1)}, bf16[4,64,960]{2,1,0:T(8,128)(2,1)S(1)}, u32[]{:S(2)}, u32[]{:S(2)}) collective-permute-start(bf16[4,64,960]{2,1,0:T(8,128)(2,1)S(1)} %get-tuple-element.132), channel_id=1, source_target_pairs={{0,4},{2,6},{4,0},{6,2},{1,5},{3,7},{5,1},{7,3},{8,12},{10,14},{12... | collective-permute-start | bytes 1474568 | tf_op jit(solution)/shard_map/ppermute | solution.py:70
  229.6 23.4 %collective-permute-start.14 = (bf16[4,64,960]{2,1,0:T(8,128)(2,1)S(1)}, bf16[4,64,960]{2,1,0:T(8,128)(2,1)S(1)}, u32[]{:S(2)}, u32[]{:S(2)}) collective-permute-start(bf16[4,64,960]{2,1,0:T(8,128)(2,1)S(1)} %get-tuple-element.132), channel_id=1, source_target_pairs={{0,2},{2,0},{4,6},{6,4},{1,3},{3,1},{5,7},{7,5},{8,10},{10,8},{12,... | collective-permute-start | bytes 1474568 | tf_op jit(solution)/shard_map/ppermute | solution.py:70
  255.4 4.9 collective-permute-start.17
  257.7 40.7 %copy-start.74 = (s32[2048]{0:T(1024)}, s32[2048]{0:T(1024)S(1)}, u32[]{:S(2)}) copy-start(s32[2048]{0:T(1024)S(1)} %sub.159) | copy-start | bytes 24580
  315.6 10.6 %collective-permute-start.18 = (bf16[4,4,64,960]{3,2,1,0:T(8,128)(2,1)}, bf16[4,4,64,960]{3,2,1,0:T(8,128)(2,1)}, u32[]{:S(2)}, u32[]{:S(2)}) collective-permute-start(bf16[4,4,64,960]{3,2,1,0:T(8,128)(2,1)} %bitcast.420), channel_id=1, source_target_pairs={{0,1},{1,0},{2,3},{3,2},{4,5},{5,4},{6,7},{7,6},{8,9},{9,8},{10,11... | collective-permute-start | bytes 5898248 | tf_op jit(solution)/shard_map/ppermute | solution.py:70
  330.2 14.5 %collective-permute-start.21 = (bf16[4,64,960]{2,1,0:T(8,128)(2,1)S(1)}, bf16[4,64,960]{2,1,0:T(8,128)(2,1)S(1)}, u32[]{:S(2)}, u32[]{:S(2)}) collective-permute-start(bf16[4,64,960]{2,1,0:T(8,128)(2,1)S(1)} %get-tuple-element.99), channel_id=1, source_target_pairs={{0,6},{2,4},{4,2},{6,0},{1,7},{3,5},{5,3},{7,1},{8,14},{10,12},{12... | collective-permute-start | bytes 1474568 | tf_op jit(solution)/shard_map/ppermute | solution.py:70
  330.6 24.5 %collective-permute-start.20 = (bf16[4,64,960]{2,1,0:T(8,128)(2,1)S(1)}, bf16[4,64,960]{2,1,0:T(8,128)(2,1)S(1)}, u32[]{:S(2)}, u32[]{:S(2)}) collective-permute-start(bf16[4,64,960]{2,1,0:T(8,128)(2,1)S(1)} %get-tuple-element.100), channel_id=1, source_target_pairs={{0,4},{2,6},{4,0},{6,2},{1,5},{3,7},{5,1},{7,3},{8,12},{10,14},{12... | collective-permute-start | bytes 1474568 | tf_op jit(solution)/shard_map/ppermute | solution.py:70
  331.7 23.4 %collective-permute-start.19 = (bf16[4,64,960]{2,1,0:T(8,128)(2,1)S(1)}, bf16[4,64,960]{2,1,0:T(8,128)(2,1)S(1)}, u32[]{:S(2)}, u32[]{:S(2)}) collective-permute-start(bf16[4,64,960]{2,1,0:T(8,128)(2,1)S(1)} %get-tuple-element.98), channel_id=1, source_target_pairs={{0,2},{2,0},{4,6},{6,4},{1,3},{3,1},{5,7},{7,5},{8,10},{10,8},{12,... | collective-permute-start | bytes 1474568 | tf_op jit(solution)/shard_map/ppermute | solution.py:70
  355.5 5.9 collective-permute-start.24
  355.7 12.0 %collective-permute-start.23 = (bf16[64,960]{1,0:T(8,128)(2,1)S(1)}, bf16[64,960]{1,0:T(8,128)(2,1)S(1)}, u32[]{:S(2)}, u32[]{:S(2)}) collective-permute-start(bf16[64,960]{1,0:T(8,128)(2,1)S(1)} %get-tuple-element.130), channel_id=1, source_target_pairs={{0,16},{8,24},{16,0},{24,8},{1,17},{9,25},{17,1},{25,9},{2,18},{10... | collective-permute-start | bytes 368648 | tf_op jit(solution)/shard_map/ppermute | solution.py:70
  357.0 10.7 %collective-permute-start.22 = (bf16[64,960]{1,0:T(8,128)(2,1)S(1)}, bf16[64,960]{1,0:T(8,128)(2,1)S(1)}, u32[]{:S(2)}, u32[]{:S(2)}) collective-permute-start(bf16[64,960]{1,0:T(8,128)(2,1)S(1)} %get-tuple-element.128), channel_id=1, source_target_pairs={{0,8},{8,0},{16,24},{24,16},{1,9},{9,1},{17,25},{25,17},{2,10},{10... | collective-permute-start | bytes 368648 | tf_op jit(solution)/shard_map/ppermute | solution.py:70
  367.9 12.7 %copy-start.34 = (f32[64,960]{1,0:T(8,128)}, f32[64,960]{1,0:T(8,128)S(1)}, u32[]{:S(2)}) copy-start(f32[64,960]{1,0:T(8,128)S(1)} %get-tuple-element.72) | copy-start | bytes 737284
  368.0 4.8 collective-permute-start.27
  370.5 6.1 collective-permute-start.26
  371.6 5.2 collective-permute-start.25
  376.9 3.7 collective-permute-start.28
  393.6 24.1 %collective-permute-start.29 = (f32[4,64,960]{2,1,0:T(8,128)}, f32[4,64,960]{2,1,0:T(8,128)}, u32[]{:S(2)}, u32[]{:S(2)}) collective-permute-start(f32[4,64,960]{2,1,0:T(8,128)} %bitcast.426), channel_id=1, source_target_pairs={{0,1},{1,0},{2,3},{3,2},{4,5},{5,4},{6,7},{7,6},{8,9},{9,8},{10,11... | collective-permute-start | bytes 2949128 | tf_op jit(solution)/shard_map/ppermute | solution.py:70
  420.1 8.9 %collective-permute-start.32 = (f32[64,960]{1,0:T(8,128)}, f32[64,960]{1,0:T(8,128)S(1)}, u32[]{:S(2)}, u32[]{:S(2)}) collective-permute-start(f32[64,960]{1,0:T(8,128)} %get-tuple-element.113), channel_id=1, source_target_pairs={{0,6},{2,4},{4,2},{6,0},{1,7},{3,5},{5,3},{7,1},{8,14},{10,12},{12... | collective-permute-start | bytes 737288 | tf_op jit(solution)/shard_map/ppermute | solution.py:70
  421.3 13.9 %collective-permute-start.31 = (f32[64,960]{1,0:T(8,128)}, f32[64,960]{1,0:T(8,128)}, u32[]{:S(2)}, u32[]{:S(2)}) collective-permute-start(f32[64,960]{1,0:T(8,128)} %get-tuple-element.114), channel_id=1, source_target_pairs={{0,4},{2,6},{4,0},{6,2},{1,5},{3,7},{5,1},{7,3},{8,12},{10,14},{12... | collective-permute-start | bytes 737288 | tf_op jit(solution)/shard_map/ppermute | solution.py:70
  422.4 12.8 %collective-permute-start.30 = (f32[64,960]{1,0:T(8,128)}, f32[64,960]{1,0:T(8,128)}, u32[]{:S(2)}, u32[]{:S(2)}) collective-permute-start(f32[64,960]{1,0:T(8,128)} %get-tuple-element.112), channel_id=1, source_target_pairs={{0,2},{2,0},{4,6},{6,4},{1,3},{3,1},{5,7},{7,5},{8,10},{10,8},{12,... | collective-permute-start | bytes 737288 | tf_op jit(solution)/shard_map/ppermute | solution.py:70
  423.7 11.5 %copy-start.83 = (f32[64]{0:T(128)S(1)}, f32[64]{0:T(128)}, u32[]{:S(2)}) copy-start(f32[64]{0:T(128)} %copy-done.82) | copy-start | bytes 772
  425.3 11.2 %copy-start.35 = (f32[64,960]{1,0:T(8,128)S(1)}, f32[64,960]{1,0:T(8,128)}, u32[]{:S(2)}) copy-start(f32[64,960]{1,0:T(8,128)} %copy-done.34) | copy-start | bytes 737284
  425.4 12.1 %copy-start.15 = (bf16[1,3,320,320]{3,2,0,1:T(8,128)(2,1)S(1)}, bf16[1,3,320,320]{3,2,0,1:T(8,128)(2,1)}, u32[]{:S(2)}) copy-start(bf16[1,3,320,320]{3,2,0,1:T(8,128)(2,1)} %copy-done.14) | copy-start | bytes 1843204
  425.4 12.5 %copy-start.11 = (bf16[1,3,320,320]{3,2,0,1:T(8,128)(2,1)S(1)}, bf16[1,3,320,320]{3,2,0,1:T(8,128)(2,1)}, u32[]{:S(2)}) copy-start(bf16[1,3,320,320]{3,2,0,1:T(8,128)(2,1)} %copy-done.10) | copy-start | bytes 1843204
  480.9 53.7 %all-to-all-start.5 = ((bf16[32,32,960]{2,1,0:T(8,128)(2,1)}), bf16[32,32,960]{2,1,0:T(8,128)(2,1)}, u32[]{:S(2)}, u32[]{:S(2)}) async-start(bf16[32,32,960]{2,1,0:T(8,128)(2,1)} %bitcast.116), calls=%async_computation.6 | async-start | bytes 4194304 | tf_op jit(solution)/shard_map/all_to_all | solution.py:339
  536.6 5.7 collective-permute-start.33
  549.8 40.1 %collective-permute-start.36 = (bf16[1024,320]{0,1:T(8,128)(2,1)}, bf16[1024,320]{0,1:T(8,128)(2,1)S(1)}, u32[]{:S(2)}, u32[]{:S(2)}) collective-permute-start(bf16[1024,320]{0,1:T(8,128)(2,1)} %get-tuple-element.84), channel_id=1, source_target_pairs={{0,6},{2,4},{4,2},{6,0},{1,7},{3,5},{5,3},{7,1},{8,14},{10,12},{12... | collective-permute-start | bytes 1966088 | tf_op jit(solution)/shard_map/ppermute | solution.py:70
  551.9 37.9 %collective-permute-start.35 = (bf16[1024,320]{0,1:T(8,128)(2,1)}, bf16[1024,320]{0,1:T(8,128)(2,1)}, u32[]{:S(2)}, u32[]{:S(2)}) collective-permute-start(bf16[1024,320]{0,1:T(8,128)(2,1)} %get-tuple-element.85), channel_id=1, source_target_pairs={{0,4},{2,6},{4,0},{6,2},{1,5},{3,7},{5,1},{7,3},{8,12},{10,14},{12... | collective-permute-start | bytes 1966088 | tf_op jit(solution)/shard_map/ppermute | solution.py:70
  552.3 37.6 %collective-permute-start.34 = (bf16[1024,320]{0,1:T(8,128)(2,1)}, bf16[1024,320]{0,1:T(8,128)(2,1)}, u32[]{:S(2)}, u32[]{:S(2)}) collective-permute-start(bf16[1024,320]{0,1:T(8,128)(2,1)} %get-tuple-element.83), channel_id=1, source_target_pairs={{0,2},{2,0},{4,6},{6,4},{1,3},{3,1},{5,7},{7,5},{8,10},{10,8},{12,... | collective-permute-start | bytes 1966088 | tf_op jit(solution)/shard_map/ppermute | solution.py:70
  554.3 33.2 %all-to-all-start.6 = ((bf16[8,120,320]{1,2,0:T(8,128)(2,1)}), bf16[8,120,320]{1,2,0:T(8,128)(2,1)S(1)}, u32[]{:S(2)}, u32[]{:S(2)}) async-start(bf16[8,120,320]{1,2,0:T(8,128)(2,1)} %copy.539), calls=%async_computation.7 | async-start | bytes 1310720 | tf_op jit(solution)/shard_map/all_to_all | solution.py:369
  593.7 11.8 %collective-permute-start.39 = (bf16[256,320]{1,0:T(8,128)(2,1)S(1)}, bf16[256,320]{1,0:T(8,128)(2,1)S(1)}, u32[]{:S(2)}, u32[]{:S(2)}) collective-permute-start(bf16[256,320]{1,0:T(8,128)(2,1)S(1)} %bitcast.445), channel_id=1, source_target_pairs={{0,24},{8,16},{16,8},{24,0},{1,25},{9,17},{17,9},{25,1},{2,26},{10... | collective-permute-start | bytes 491528 | tf_op jit(solution)/shard_map/ppermute | solution.py:70
  596.2 14.8 %collective-permute-start.38 = (bf16[256,320]{1,0:T(8,128)(2,1)}, bf16[256,320]{1,0:T(8,128)(2,1)S(1)}, u32[]{:S(2)}, u32[]{:S(2)}) collective-permute-start(bf16[256,320]{1,0:T(8,128)(2,1)} %bitcast.272), channel_id=1, source_target_pairs={{0,16},{8,24},{16,0},{24,8},{1,17},{9,25},{17,1},{25,9},{2,18},{10... | collective-permute-start | bytes 491528 | tf_op jit(solution)/shard_map/ppermute | solution.py:70
  597.1 13.9 %collective-permute-start.37 = (bf16[256,320]{1,0:T(8,128)(2,1)}, bf16[256,320]{1,0:T(8,128)(2,1)S(1)}, u32[]{:S(2)}, u32[]{:S(2)}) collective-permute-start(bf16[256,320]{1,0:T(8,128)(2,1)} %bitcast.273), channel_id=1, source_target_pairs={{0,8},{8,0},{16,24},{24,16},{1,9},{9,1},{17,25},{25,17},{2,10},{10... | collective-permute-start | bytes 491528 | tf_op jit(solution)/shard_map/ppermute | solution.py:70
  611.1 19.1 %copy-start.28 = (bf16[960,320]{1,0:T(8,128)(2,1)S(1)}, bf16[960,320]{1,0:T(8,128)(2,1)}, u32[]{:S(2)}) copy-start(bf16[960,320]{1,0:T(8,128)(2,1)} %reduce-scatter.2.cloned.1.call-done) | copy-start | bytes 1843204
  611.1 17.4 %collective-permute-start.40 = (bf16[256,320]{1,0:T(8,128)(2,1)S(1)}, bf16[256,320]{1,0:T(8,128)(2,1)S(1)}, u32[]{:S(2)}, u32[]{:S(2)}) collective-permute-start(bf16[256,320]{1,0:T(8,128)(2,1)S(1)} %fusion.79), channel_id=1, source_target_pairs={{24,0},{25,1},{26,2},{27,3},{28,4},{29,5},{30,6},{31,7}} | collective-permute-start | bytes 491528 | tf_op jit(solution)/shard_map/ppermute | solution.py:364
  612.5 16.0 %collective-permute-start.42 = (bf16[256,320]{1,0:T(8,128)(2,1)S(1)}, bf16[256,320]{1,0:T(8,128)(2,1)S(1)}, u32[]{:S(2)}, u32[]{:S(2)}) collective-permute-start(bf16[256,320]{1,0:T(8,128)(2,1)S(1)} %fusion.79), channel_id=1, source_target_pairs={{16,0},{17,1},{18,2},{19,3},{20,4},{21,5},{22,6},{23,7}} | collective-permute-start | bytes 491528 | tf_op jit(solution)/shard_map/ppermute | solution.py:364
  613.8 16.3 %collective-permute-start.41 = (bf16[256,320]{1,0:T(8,128)(2,1)S(1)}, bf16[256,320]{1,0:T(8,128)(2,1)S(1)}, u32[]{:S(2)}, u32[]{:S(2)}) collective-permute-start(bf16[256,320]{1,0:T(8,128)(2,1)S(1)} %fusion.79), channel_id=1, source_target_pairs={{8,0},{9,1},{10,2},{11,3},{12,4},{13,5},{14,6},{15,7}} | collective-permute-start | bytes 491528 | tf_op jit(solution)/shard_map/ppermute | solution.py:364
  637.2 24.2 %copy-start.16 = (f32[307290]{0:T(1024)S(1)}, f32[307290]{0:T(1024)}, u32[]{:S(2)}) copy-start(f32[307290]{0:T(1024)} %param.18) | copy-start | bytes 3687484
  638.0 5.8 collective-permute-start.43
  (85 other events, 276.6 us)
Sparse Core Ops, SparseCore 0:
  58.7 63.3 all-gather.6
  124.3 53.7 all-gather.8
  425.5 55.3 reduce-scatter.1

commit v3 on v2

--- a/solution.py
+++ b/solution.py
@@ -39,6 +39,8 @@
 PLANE = ("y", "x", "c")
 ALL = ("q", "y", "x", "c")
 SHARE = FF // 8
+LINES = D * (QKV + D + 3 * FF) // 32 // 128
+EXTRA = 32
 
 bf16 = jnp.bfloat16
 f32 = jnp.float32
@@ -103,14 +105,25 @@
     return (new_one, new_two, -RATE * (ratio + DECAY * param))
 
 
-def fold_plane(parts):
-    got = flip(parts[1], "c", 1, 2)
-    mine = parts[0].astype(f32) + got.astype(f32)
-    low = mine.astype(parts[1].dtype)
+def fold_plane(left, right, right_dim):
+    half = left.shape[0] // 2
+    got = flip(dot(left[half:], right, 1, right_dim).astype(bf16), "c", 1, 2)
+    mine = (dot(left[:half], right, 1, right_dim) + got.astype(f32)).reshape(4, half // 4, D)
+    low = mine.astype(bf16)
     total = mine[0]
     for k in (1, 2, 3):
         total = total + flip(low[k], ("y", "x"), k, 4).astype(f32)
     return total
+
+
+def down_pack(rows):
+    side = jnp.concatenate([rows[: SHARE // 2, 640:], rows[SHARE // 2 :, 640:]], axis=1)
+    return jnp.concatenate([rows[:, :640], side])
+
+
+def down_unpack(rows):
+    side = jnp.concatenate([rows[SHARE:, :UNIT], rows[SHARE:, UNIT:]])
+    return jnp.concatenate([rows[:SHARE], side], axis=1)
 
 
 def spread_plane(rows):
@@ -168,15 +181,11 @@
     pieces = [flat_low, ahead]
     if back:
         pieces = [lax.ppermute(flat_low[shard - back :], ALL, [(i, i + 1) for i in range(devices - 1)])] + pieces
-    chunk = lax.dynamic_slice(jnp.concatenate(pieces), (back + GAINS - drift * me,), (span,)).reshape(units, UNIT)
-    gain_rows = flat_low[:GAINS].reshape(GAIN_UNITS, UNIT)
-    extra = jnp.concatenate([gain_rows, jnp.zeros((16 - GAIN_UNITS, UNIT), bf16)])
+    chunk = lax.dynamic_slice(jnp.concatenate(pieces), (back + GAINS - drift * me,), (span,))
     if aligned:
-        by_five = chunk.reshape(192, 5, UNIT).transpose(1, 0, 2).reshape(units, UNIT)
-        by_three = chunk.reshape(320, 3, UNIT).transpose(1, 0, 2).reshape(units, UNIT)
-        sent = chunk.reshape(60, 2, 8, UNIT).transpose(2, 1, 0, 3).reshape(8, 120, UNIT)
+        sent = chunk.reshape(60, 2, 8, UNIT).transpose(2, 0, 1, 3).reshape(8, 60, 2 * UNIT)
         got = lax.all_to_all(sent, PLANE, split_axis=0, concat_axis=0, tiled=True)
-        first = jnp.concatenate([jnp.where(p_index < 5, by_five, by_three), extra])
+        first = jnp.concatenate([chunk, flat_low[:GAINS], jnp.zeros((EXTRA * 128 - GAINS,), bf16)]).reshape(LINES + EXTRA, 128)
         jumped = lax.ppermute(first, "q", [(0, 2)])
         first = jnp.where(q_index == 2, jumped, first)
         stepped = lax.ppermute(first, "q", [(0, 1), (2, 3)])
@@ -184,27 +193,26 @@
         answer, first, got = lax.optimization_barrier((answer, first, got))
         returned = lax.all_to_all(answer, ALL, split_axis=0, concat_axis=0, tiled=True).reshape(slots, D)
         level = lax.all_gather(first, PLANE)
-        gains = level[0, units : units + GAIN_UNITS].astype(f32).reshape(3, D)
-        w_qkv = level[:5, :units].reshape(5, 5, 192, UNIT).transpose(1, 0, 2, 3).reshape(5, D, UNIT)
-        w_out = level[5:, :units].reshape(3, 3, 320, UNIT).transpose(1, 0, 2, 3).reshape(3, D, UNIT)
-        by_share = got.reshape(8, 2, 60, UNIT).transpose(1, 0, 2, 3).reshape(units, UNIT)
-        mixed = jnp.where(q_index == 3, by_three, by_share)
+        gains = level[0, LINES:].reshape(-1)[:GAINS].astype(f32).reshape(3, D)
+        w_qkv = level[:5, :LINES].reshape(D, QKV)
+        w_out = level[5:, :LINES].reshape(D, D)
+        mixed = jnp.where(q_index == 3, down_pack(chunk.reshape(SHARE, D)), got.reshape(480, 2 * UNIT))
         mixed, returned = lax.optimization_barrier((mixed, returned))
         column = lax.all_gather(mixed, "q")
-        w_gate = jnp.concatenate([column[1, :480], column[2, :480]])
-        w_up = jnp.concatenate([column[1, 480:], column[2, 480:]])
-        w_down = column[3].reshape(3, SHARE, UNIT)
+        w_gu = column[1:3].reshape(D, 2 * SHARE)
+        w_down = down_unpack(column[3])
     else:
         returned = lax.all_to_all(answer, ALL, split_axis=0, concat_axis=0, tiled=True).reshape(slots, D)
-        full = lax.all_gather(jnp.concatenate([chunk, extra]), ALL)
+        extra = jnp.zeros((16 * UNIT,), bf16).at[:GAINS].set(flat_low[:GAINS])
+        full = lax.all_gather(jnp.concatenate([chunk, extra]).reshape(units + 16, UNIT), ALL)
         gains = full[0, units : units + GAIN_UNITS].astype(f32).reshape(3, D)
         full = full[:, :units].reshape(ALL_UNITS, UNIT)
         edge = np.cumsum([QKV_UNITS, OUT_UNITS, GU_UNITS])
-        w_qkv = full[: edge[0]].reshape(D, 5, UNIT).transpose(1, 0, 2)
-        w_out = full[edge[0] : edge[1]].reshape(D, 3, UNIT).transpose(1, 0, 2)
+        w_qkv = full[: edge[0]].reshape(D, QKV)
+        w_out = full[edge[0] : edge[1]].reshape(D, D)
         both = lax.dynamic_index_in_dim(full[edge[1] : edge[2]].reshape(D, 2, 8, UNIT), p_index, 2, False)
-        w_gate, w_up = both[:, 0], both[:, 1]
-        w_down = lax.dynamic_index_in_dim(full[edge[2] :].reshape(8, SHARE, 3, UNIT), p_index, 0, False).transpose(1, 0, 2)
+        w_gu = both.reshape(D, 2 * SHARE)
+        w_down = lax.dynamic_index_in_dim(full[edge[2] :].reshape(8, SHARE, D), p_index, 0, False)
     x_low = dot(spot, returned).astype(bf16)
     x_embed = x_low.astype(f32) * emb_mult
 
@@ -214,10 +222,11 @@
     h_attn = (x_embed * scale_of(x_embed) * gains[0]).astype(bf16)
     h_pick = dot(pick, h_attn).astype(bf16)
     x_pick = dot(pick, x_low) * emb_mult
-    q_raw = jnp.concatenate([dot(h_pick, w_qkv[j]) for j in range(3)], axis=1)
-    query = rotate(q_raw, cosine_pick, sine_pick).astype(bf16)
-    key = rotate(dot(h_attn, w_qkv[3]), cosine, sine).astype(bf16)
-    value = dot(h_attn, w_qkv[4]).astype(bf16)
+    query = rotate(dot(h_pick, w_qkv[:, :D]), cosine_pick, sine_pick).astype(bf16)
+    w_kv = w_qkv[:, D:]
+    key_value = dot(h_attn, w_kv)
+    key = rotate(key_value[:, :UNIT], cosine, sine).astype(bf16)
+    value = key_value[:, UNIT:].astype(bf16)
 
     def heads_of(rows):
         return rows.reshape(loss_dev, KEY_VALUE_HEADS, groups, HEAD_SIZE).transpose(1, 2, 0, 3).reshape(KEY_VALUE_HEADS, groups * loss_dev, HEAD_SIZE)
@@ -240,30 +249,38 @@
     probs_low = probs.astype(bf16)
     mixed_heads = jnp.einsum("hqk,hkd->hqd", probs_low, value_h, preferred_element_type=f32)
     attended = heads_back(mixed_heads.astype(bf16))
-    x_one = x_pick + jnp.concatenate([dot(attended, w_out[j]) for j in range(3)], axis=1)
+    x_one = x_pick + dot(attended, w_out)
 
     h_mlp = (x_one * scale_of(x_one) * gains[1]).astype(bf16)
     plane_rows = 8 * loss_dev
     h_all = spread_plane(h_mlp).reshape(plane_rows, D)
-    gate = dot(h_all, w_gate)
-    up = dot(h_all, w_up)
+    gate_up = dot(h_all, w_gu)
+    gate, up = gate_up[:, :SHARE], gate_up[:, SHARE:]
     sig = jax.nn.sigmoid(gate)
     act = (gate * sig * up).astype(bf16)
-    part = jnp.concatenate([dot(act, w_down[j]) for j in range(3)], axis=1)
-    x_two = x_one + fold_plane(part.reshape(2, 4, loss_dev, D))
+    x_two = x_one + fold_plane(act, w_down, 0)
 
     hidden = (x_two * scale_of(x_two) * gains[2]).astype(bf16)
     across = jnp.stack([hidden] + [flip(hidden, "q", k, rows_q) for k in range(1, rows_q)])
-    hidden_all = spread_plane(across).reshape(loss_total, D)
-    logits = dot(hidden_all, table_low, 1, 1)
-    targets_all = jnp.take(asked[:, capacity:], source_of, axis=0).reshape(loss_total)
-    column_id = targets_all - me * vocab_dev
-    hit = column_id[:, None] == jnp.arange(vocab_dev, dtype=jnp.int32)[None, :]
-    local_peak = jnp.max(logits, axis=1)
-    local_total = jnp.sum(jnp.exp(logits - local_peak[:, None]), axis=1)
-    local_target = jnp.sum(jnp.where(hit, logits, 0.0), axis=1)
-    local_sum = jnp.sum(logits, axis=1)
-    stats = jnp.stack([local_peak, local_total, local_target, local_sum]).reshape(4, devices, loss_dev)
+    by_x, by_y = flip(across, "x", 1, 2), flip(across, "y", 1, 2)
+    cut = rows_q // 2
+    corner = [flip(by_x[:cut], "y", 1, 2), flip(by_y[cut:], "x", 1, 2)]
+    near = jnp.stack([across, by_x, by_y, jnp.concatenate(corner)]).reshape(loss_total // 2, D)
+    sides = [near, flip(near, "c", 1, 2)]
+    targets_all = jnp.take(asked[:, capacity:], source_of, axis=0).reshape(2, loss_total // 2)
+    logits, hits, stats = [], [], []
+    for side, rows in enumerate(sides):
+        z = dot(rows, table_low, 1, 1)
+        column_id = targets_all[side] - me * vocab_dev
+        hit = column_id[:, None] == jnp.arange(vocab_dev, dtype=jnp.int32)[None, :]
+        local_peak = jnp.max(z, axis=1)
+        local_total = jnp.sum(jnp.exp(z - local_peak[:, None]), axis=1)
+        local_target = jnp.sum(jnp.where(hit, z, 0.0), axis=1)
+        local_sum = jnp.sum(z, axis=1)
+        logits.append(z)
+        hits.append(hit)
+        stats.append(jnp.stack([local_peak, local_total, local_target, local_sum]))
+    stats = jnp.concatenate(stats, axis=1).reshape(4, devices, loss_dev)
     stats = jnp.take(stats, order_of, axis=1).transpose(1, 0, 2)
     stats = lax.all_to_all(stats, ALL, split_axis=0, concat_axis=0, tiled=True)
     peak = jnp.max(stats[:, 0], axis=0)
@@ -276,37 +293,44 @@
         + ZCOEF * my_log * my_log
     )
     logs = lax.all_to_all(jnp.broadcast_to(my_log[None, None], (devices, 1, loss_dev)), ALL, split_axis=0, concat_axis=0, tiled=True)
-    log_total = jnp.take(logs[:, 0], source_of, axis=0).reshape(loss_total, 1)
-    d_logits = (
-        (1.0 + 2.0 * ZCOEF * log_total) * jnp.exp(logits - log_total)
-        - jnp.where(hit, 1.0 - SMOOTH, 0.0)
-        - SMOOTH / V
-    ) / loss_total
-    d_logits = d_logits.astype(bf16)
-    d_hidden = dot(d_logits, table_low).reshape(2, 4, rows_q, loss_dev, D)
-    d_hidden = d_hidden.at[1].get().astype(bf16), d_hidden[0]
-    d_hidden = fold_plane([d_hidden[1], d_hidden[0]])
+    log_total = jnp.take(logs[:, 0], source_of, axis=0).reshape(2, loss_total // 2, 1)
+    d_logits = [
+        (
+            (
+                (1.0 + 2.0 * ZCOEF * log_total[side]) * jnp.exp(logits[side] - log_total[side])
+                - jnp.where(hits[side], 1.0 - SMOOTH, 0.0)
+                - SMOOTH / V
+            )
+            / loss_total
+        ).astype(bf16)
+        for side in (1, 0)
+    ]
+    got = flip(dot(d_logits[0], table_low).astype(bf16), "c", 1, 2)
+    d_hidden = (dot(d_logits[1], table_low) + got.astype(f32)).reshape(4, rows_q, loss_dev, D)
+    d_low = d_hidden.astype(bf16)
+    d_hidden = d_hidden[0]
+    for k in (1, 2, 3):
+        d_hidden = d_hidden + flip(d_low[k], ("y", "x"), k, 4).astype(f32)
     d_low = d_hidden.astype(bf16)
     total_hidden = d_hidden[0]
     for k in range(1, rows_q):
         total_hidden = total_hidden + flip(d_low[k], "q", k, rows_q).astype(f32)
-    head_grad = dot(d_logits, hidden_all, 0, 0)
+    head_grad = dot(d_logits[1], sides[0], 0, 0) + dot(d_logits[0], sides[1], 0, 0)
+    head_grad, total_hidden = lax.optimization_barrier((head_grad, total_hidden))
 
     d_x_two, grad_final = norm_back(x_two, gains[2], total_hidden)
     d_down = spread_plane(d_x_two.astype(bf16)).reshape(plane_rows, D)
-    d_act = sum(dot(d_down[:, UNIT * j : UNIT * (j + 1)], w_down[j], 1, 1) for j in range(3))
-    d_gate = (d_act * up * sig * (1.0 + gate * (1.0 - sig))).astype(bf16)
-    d_up = (d_act * gate * sig).astype(bf16)
-    grad_down = [dot(act, d_down[:, UNIT * j : UNIT * (j + 1)], 0, 0).astype(bf16) for j in range(3)]
-    grad_gate = dot(h_all, d_gate, 0, 0).astype(bf16)
-    grad_up = dot(h_all, d_up, 0, 0).astype(bf16)
-    d_h = dot(d_gate, w_gate, 1, 1) + dot(d_up, w_up, 1, 1)
-    d_h_mlp = fold_plane(d_h.reshape(2, 4, loss_dev, D))
+    d_act = dot(d_down, w_down, 1, 1)
+    d_gate = d_act * up * sig * (1.0 + gate * (1.0 - sig))
+    d_gu = jnp.concatenate([d_gate, d_act * gate * sig], axis=1).astype(bf16)
+    d_h_mlp = fold_plane(d_gu, w_gu, 1)
+    grad_down = dot(act, d_down, 0, 0).astype(bf16)
+    grad_gu = dot(h_all, d_gu, 0, 0).astype(bf16)
     d_x_mlp, grad_mlp = norm_back(x_one, gains[1], d_h_mlp)
     d_x_one = d_x_two + d_x_mlp
 
     d_branch = d_x_one.astype(bf16)
-    d_attended = sum(dot(d_branch[:, UNIT * j : UNIT * (j + 1)], w_out[j], 1, 1) for j in range(3))
+    d_attended = dot(d_branch, w_out, 1, 1)
     d_mixed = heads_of(d_attended.astype(bf16))
     d_probs = jnp.einsum("hqd,hkd->hqk", d_mixed, value_h, preferred_element_type=f32)
     delta = jnp.sum(probs * d_probs, axis=-1, keepdims=True)
@@ -315,12 +339,12 @@
     d_key = jnp.einsum("hqk,hqd->khd", d_scores, query_h, preferred_element_type=f32) * HEAD_SIZE**-0.5
     d_value = jnp.einsum("hqk,hqd->khd", probs_low, d_mixed, preferred_element_type=f32)
     d_q = rotate_back(heads_back(d_query), cosine_pick, sine_pick).astype(bf16)
-    d_k = rotate_back(d_key.reshape(tokens, UNIT), cosine, sine).astype(bf16)
-    d_v = d_value.reshape(tokens, UNIT).astype(bf16)
-    d_h_pick = sum(dot(d_q[:, UNIT * j : UNIT * (j + 1)], w_qkv[j], 1, 1) for j in range(3))
+    d_k = rotate_back(d_key.reshape(tokens, UNIT), cosine, sine)
+    d_kv = jnp.concatenate([d_k, d_value.reshape(tokens, UNIT)], axis=1).astype(bf16)
+    d_h_pick = dot(d_q, w_qkv[:, :D], 1, 1)
     high = d_h_pick.astype(bf16)
     rest = (d_h_pick - high.astype(f32)).astype(bf16)
-    d_h_attn = dot(d_k, w_qkv[3], 1, 1) + dot(d_v, w_qkv[4], 1, 1) + dot(pick, high, 0, 0) + dot(pick, rest, 0, 0)
+    d_h_attn = dot(d_kv, w_kv, 1, 1) + dot(pick, high, 0, 0) + dot(pick, rest, 0, 0)
     d_x_attn, grad_attn = norm_back(x_embed, gains[0], d_h_attn)
     high = d_x_one.astype(bf16)
     rest = (d_x_one - high.astype(f32)).astype(bf16)
@@ -328,25 +352,19 @@
 
     sending = dot(spot, (d_x_embed * emb_mult).astype(bf16), 0, 0).astype(bf16).reshape(devices, capacity, D)
     if aligned:
-        blocks = jnp.concatenate(
-            [jnp.zeros((units, UNIT), bf16)]
-            + [grad_gate[:480], grad_up[:480], grad_gate[480:], grad_up[480:]]
-            + grad_down
-        )
-        share = lax.psum_scatter(blocks, "q", scatter_dimension=0, tiled=True)
-        sending, share = lax.optimization_barrier((sending, share))
-    sending, d_q, d_k, d_v, attended = lax.optimization_barrier((sending, d_q, d_k, d_v, attended))
+        blocks = jnp.concatenate([jnp.zeros((1, 480, 640), bf16), grad_gu.reshape(2, 480, 640), down_pack(grad_down)[None]])
+        share = lax.psum_scatter(blocks, "q", scatter_dimension=0, tiled=False)
+        sending, d_q, d_kv, attended = lax.optimization_barrier((sending, d_q, d_kv, attended))
+        share, d_q, d_kv, attended = lax.optimization_barrier((share, d_q, d_kv, attended))
     arrived = lax.all_to_all(sending, ALL, split_axis=0, concat_axis=0, tiled=True).reshape(slots, D)
-    grad_out = [dot(attended, d_branch[:, UNIT * j : UNIT * (j + 1)], 0, 0).astype(bf16) for j in range(3)]
-    grad_qkv = [dot(h_pick, d_q[:, UNIT * j : UNIT * (j + 1)], 0, 0).astype(bf16) for j in range(3)]
-    grad_qkv += [dot(h_attn, d_k, 0, 0).astype(bf16), dot(h_attn, d_v, 0, 0).astype(bf16)]
-
-    gain_grads = jnp.concatenate([grad_attn, grad_mlp, grad_final]).reshape(GAIN_UNITS, UNIT)
+    grad_out = dot(attended, d_branch, 0, 0).astype(bf16)
+    grad_qkv = jnp.concatenate([dot(h_pick, d_q, 0, 0), dot(h_attn, d_kv, 0, 0)], axis=1).astype(bf16)
+
+    gain_grads = jnp.concatenate([grad_attn, grad_mlp, grad_final]).astype(bf16)
     if aligned:
-        lower = jnp.stack(grad_qkv).reshape(5, 5, 192, UNIT).transpose(1, 0, 2, 3).reshape(5, units, UNIT)
-        upper = jnp.stack(grad_out).reshape(3, 3, 320, UNIT).transpose(1, 0, 2, 3).reshape(3, units, UNIT)
-        room = jnp.zeros((8, 64, UNIT), bf16).at[0, :GAIN_UNITS].set(gain_grads.astype(bf16))
-        level = jnp.concatenate([jnp.concatenate([lower, upper]), room], axis=1).reshape(4, 2, units + 64, UNIT)
+        level = jnp.concatenate([grad_qkv.reshape(5, LINES, 128), grad_out.reshape(3, LINES, 128)])
+        room = jnp.zeros((8, EXTRA * 128), bf16).at[0, :GAINS].set(gain_grads).reshape(8, EXTRA, 128)
+        level = jnp.concatenate([level, room], axis=1).reshape(4, 2, LINES + EXTRA, 128)
         level, arrived = lax.optimization_barrier((level, arrived))
         keep = lax.dynamic_index_in_dim(level, c_index, 1, False)
         give = lax.dynamic_index_in_dim(level, 1 - c_index, 1, False)
@@ -355,7 +373,9 @@
         for k in (1, 2, 3):
             piece = lax.dynamic_index_in_dim(level, yx_index ^ k, 0, False).astype(bf16)
             own = own + flip(piece, ("y", "x"), k, 4).astype(f32)
-        own = own.reshape(4, (units + 64) // 4, UNIT)
+        own = own.reshape(4, (LINES + EXTRA) // 4, 128)
+        own, share = lax.optimization_barrier((own, share))
+        got = lax.all_to_all(share.reshape(8, 60, 640), PLANE, split_axis=0, concat_axis=0, tiled=True)
         quarter = lax.dynamic_index_in_dim(own, q_index, 0, False)
         for k in (1, 2, 3):
             piece = lax.dynamic_index_in_dim(own, q_index ^ k, 0, False).astype(bf16)
@@ -363,35 +383,23 @@
         quarter = quarter.astype(bf16)
         quarters = [quarter] + [lax.ppermute(quarter, "q", [(k, 0)]) for k in (1, 2, 3)]
         first = jnp.concatenate(quarters)
-        gain_out = first[units : units + GAIN_UNITS]
-        first = first[:units]
-        sent = share.reshape(2, 8, 60, UNIT).transpose(1, 0, 2, 3).reshape(8, 120, UNIT)
-        got = lax.all_to_all(sent, PLANE, split_axis=0, concat_axis=0, tiled=True)
-        by_share = got.reshape(8, 2, 60, UNIT).transpose(2, 1, 0, 3).reshape(units, UNIT)
-        by_five = first.reshape(5, 192, UNIT).transpose(1, 0, 2).reshape(units, UNIT)
-        by_three = jnp.where(q_index == 0, first, share).reshape(3, 320, UNIT).transpose(1, 0, 2).reshape(units, UNIT)
-        mixed = jnp.where((q_index == 0) & (p_index < 5), by_five, by_three)
-        mine = jnp.where((q_index == 1) | (q_index == 2), by_share, mixed)
+        gain_out = first[LINES:].reshape(-1)[:GAINS]
+        first = first[:LINES].reshape(-1)
+        by_share = got.reshape(8, 60, 2, UNIT).transpose(1, 2, 0, 3).reshape(-1)
+        mine = jnp.where(q_index == 3, down_unpack(share).reshape(-1), by_share)
+        mine = jnp.where(q_index == 0, first, mine)
     else:
-        zero = jnp.zeros((D, 2, 8, UNIT), bf16)
-        both = lax.dynamic_update_index_in_dim(zero, jnp.stack([grad_gate, grad_up], axis=1), p_index, 2)
-        downs = lax.dynamic_update_index_in_dim(jnp.zeros((8, SHARE, 3, UNIT), bf16), jnp.stack(grad_down, axis=1), p_index, 0)
-        full = jnp.concatenate(
-            [
-                jnp.stack(grad_qkv, axis=1).reshape(-1, UNIT),
-                jnp.stack(grad_out, axis=1).reshape(-1, UNIT),
-                both.reshape(-1, UNIT),
-                downs.reshape(-1, UNIT),
-            ]
-        ).reshape(devices, units, UNIT)
-        room = jnp.zeros((devices, 16, UNIT), bf16).at[0, :GAIN_UNITS].set(gain_grads.astype(bf16))
+        both = lax.dynamic_update_index_in_dim(jnp.zeros((D, 2, 8, UNIT), bf16), grad_gu.reshape(D, 2, UNIT), p_index, 2)
+        downs = lax.dynamic_update_index_in_dim(jnp.zeros((8, SHARE, D), bf16), grad_down, p_index, 0)
+        full = jnp.concatenate([part.reshape(-1, UNIT) for part in (grad_qkv, grad_out, both, downs)]).reshape(devices, units, UNIT)
+        room = jnp.zeros((devices, 16, UNIT), bf16).at[0, :GAIN_UNITS].set(gain_grads.reshape(GAIN_UNITS, UNIT))
         full = jnp.concatenate([full, room], axis=1)
         summed = lax.psum_scatter(full, ALL, scatter_dimension=0, tiled=False)
-        mine, gain_out = summed[:units], summed[units : units + GAIN_UNITS]
-    behind = lax.ppermute(mine[units - GAIN_UNITS :], ALL, [(i, i + 1) for i in range(devices - 1)])
+        mine, gain_out = summed[:units].reshape(-1), summed[units : units + GAIN_UNITS].reshape(-1)
+    behind = lax.ppermute(mine[span - GAINS :], ALL, [(i, i + 1) for i in range(devices - 1)])
     behind = jnp.where(me == 0, gain_out, behind)
     tail = max(0, drift * (devices - 1) + shard - GAINS - span)
-    stream = jnp.concatenate([behind.reshape(-1), mine.reshape(-1), jnp.zeros((tail,), bf16)])
+    stream = jnp.concatenate([behind, mine, jnp.zeros((tail,), bf16)])
     layer_grad = lax.dynamic_slice(stream, (drift * me,), (shard,)).astype(f32)
 
     table_grad = head_grad + dot(row_hot, arrived, 0, 0)

time: 695 us -> 657 us (0.945)
  local copies, waits for them, and re-layouts: 158 us -> 127 us
  matrix products: 106 us -> 92.6 us
  waiting for transfers between devices: 216 us -> 226 us
  other arithmetic: 64.4 us -> 72.7 us
  starting transfers between devices: 85.2 us -> 78.2 us
    all_to_all x2 -> x1, waiting for transfers between devices: 28 us -> 0.01 us  [local(): got = lax.all_to_all(sent, PLANE, split_axis=0, concat_axis=0, tiled=True)]
    all_to_all x1, waiting for transfers between devices: 1.23 us -> 29.1 us  [local(): lax.all_to_all(sending, ALL, split_axis=0, concat_axis=0, tiled=True)]
    ppermute x37 -> x38, waiting for transfers between devices: 111 us -> 137 us  [flip(): return lax.ppermute(rows, axes, [(i, i ^ bits) for i in range(size)])]
    unnamed x214 -> x157, local copies, waits for them, and re-layouts: 34.2 us -> 13.7 us
    slice x22 -> x25, local copies, waits for them, and re-layouts: 45 us -> 29.3 us  [the longest x4 6.1 us: local(): d_hidden = d_hidden + flip(d_low[k], ('y', 'x'), k, 4).astype(f32)]
    dot_general x53 -> x34, matrix products: 95.2 us -> 82.6 us  [dot(): lax.dot_general(left, right, (((left_dim,), (right_dim,)), ((), ())), pre...]
    convert_element_type x11 -> x3, local copies, waits for them, and re-layouts: 17.5 us -> 5.11 us  [the longest x1 4.85 us: local(): jnp.concatenate([dot(h_pick, d_q, 0, 0), dot(h_attn, d_kv, 0, 0)], axis=1)]
    ppermute x2 -> x7, local copies, waits for them, and re-layouts: 2.94 us -> 15.3 us  [flip(): return lax.ppermute(rows, axes, [(i, i ^ bits) for i in range(size)])]
  transfers between devices with their start and end apart: 52 -> 53, of which waited for: 32 -> 32; matrix products, arithmetic and copies ran while one was open for 30% -> 27% of each run, Pallas kernels for 0% -> 0%
where the time goes in v3:
time: 657 us; the launch traced here: 646 us
  waiting for transfers between devices  226 us (34%)
  local copies, waits for them, and re-layouts  127 us (19%)
  matrix products  92.6 us (14%)
  starting transfers between devices  78.2 us (12%)
  other arithmetic  72.7 us (11%)
  blocking collectives  28.6 us (4%)
  between operations  20.4 us (3%)
    ppermute x38, waiting for transfers between devices, flip(): return lax.ppermute(rows, axes, [(i, i ^ bits) for i in range(size)])  137 us
    dot_general x34, matrix products, dot(): lax.dot_general(left, right, (((left_dim,), (right_dim,)), ((), ())), pre...  82.6 us
    all_to_all x1, waiting for transfers between devices, local(): lax.all_to_all(answer, ALL, split_axis=0, concat_axis=0, tiled=True)  44 us
    ppermute x38, starting transfers between devices, flip(): return lax.ppermute(rows, axes, [(i, i ^ bits) for i in range(size)])  36.9 us
    all_to_all x1, waiting for transfers between devices, local(): lax.all_to_all(sending, ALL, split_axis=0, concat_axis=0, tiled=True)  29.1 us
    ppermute x7, local copies, waits for them, and re-layouts, flip(): return lax.ppermute(rows, axes, [(i, i ^ bits) for i in range(size)])  15.3 us
    unnamed x157, local copies, waits for them, and re-layouts  13.7 us
  transfers between devices with their start and end apart: 53, of which 32 were waited for; matrix products, arithmetic and copies ran while one was open for 27% of the time, Pallas kernels for 0%

profile of v3, /device:TPU:1, one launch (start us, length us, event | category | flops | bytes accessed | tf_op | source)
XLA Modules:
  0.0 645.5 jit_solution(9972117572694406310)
XLA Ops:
  18.8 4.2 collective-permute-start.1
  24.4 4.4 all-to-all-start
  28.9 3.7 convert_element_type.271
  39.4 4.3 all-to-all-start.1
  43.9 5.2 fusion.25
  49.1 3.9 copy.309
  53.9 7.4 %all-to-all-start.2 = ((bf16[32,32,960]{2,1,0:T(8,128)(2,1)}), bf16[32,32,960]{2,1,0:T(8,128)(2,1)}, u32[]{:S(2)}, u32[]{:S(2)}) async-start(bf16[32,32,960]{2,1,0:T(8,128)(2,1)} %bitcast.2), calls=%async_computation.2 | async-start | bytes 4194304 | tf_op jit(solution)/shard_map/all_to_all | solution.py:194
  65.6 44.0 %all-to-all-done.2 = bf16[32,32,960]{2,1,0:T(8,128)(2,1)} async-done(((bf16[32,32,960]{2,1,0:T(8,128)(2,1)}), bf16[32,32,960]{2,1,0:T(8,128)(2,1)}, u32[]{:S(2)}, u32[]{:S(2)}) %all-to-all-start.2) | async-done | bytes 1966112 | tf_op jit(solution)/shard_map/all_to_all | solution.py:194
  109.6 3.0 fusion.23
  115.3 3.7 slice.379
  119.7 4.9 reshape.619
  124.7 3.3 fusion.41
  146.4 3.5 reshape.628
  153.9 4.8 collective-permute-done.5
  158.6 6.5 %collective-permute-done.4 = bf16[64,960]{0,1:T(8,128)(2,1)S(1)} collective-permute-done((bf16[64,960]{0,1:T(8,128)(2,1)S(1)}, bf16[64,960]{0,1:T(8,128)(2,1)S(1)}, u32[]{:S(2)}, u32[]{:S(2)}) %collective-permute-start.4) | collective-permute-done | bytes 122912 | tf_op jit(solution)/shard_map/ppermute | solution.py:72
  189.3 5.4 collective-permute-done.10
  194.7 6.0 collective-permute-done.9
  204.9 5.2 collective-permute-done.13
  210.0 14.7 %collective-permute-done.12 = bf16[64,960]{0,1:T(8,128)(2,1)S(1)} collective-permute-done((bf16[64,960]{0,1:T(8,128)(2,1)S(1)}, bf16[64,960]{0,1:T(8,128)(2,1)S(1)}, u32[]{:S(2)}, u32[]{:S(2)}) %collective-permute-start.12) | collective-permute-done | bytes 122912 | tf_op jit(solution)/shard_map/ppermute | solution.py:72
  229.8 10.4 %collective-permute-done.15 = bf16[4,64,960]{2,1,0:T(8,128)(2,1)} collective-permute-done((bf16[4,64,960]{2,1,0:T(8,128)(2,1)S(1)}, bf16[4,64,960]{2,1,0:T(8,128)(2,1)}, u32[]{:S(2)}, u32[]{:S(2)}) %collective-permute-start.15) | collective-permute-done | bytes 491552 | tf_op jit(solution)/shard_map/ppermute | solution.py:72
  249.1 6.1 collective-permute-done.17
  255.2 3.7 collective-permute-done.16
  262.6 4.8 copy.332
  267.4 4.1 copy.333
  271.5 3.4 collective-permute-start.18
  275.8 4.5 fusion.174
  283.3 4.0 fusion.173
  290.3 9.9 %all_to_all.48 = f32[32,1,256]{2,1,0:T(1,128)S(1)} all-to-all(f32[32,1,256]{2,1,0:T(1,128)S(1)} %reshape.720), channel_id=1, replica_groups=mesh['q'=4,'y'=2,'x'=2,'c'=2] {'q','y','x','c'}, dimensions={0} | all-to-all | bytes 65536 | tf_op jit(solution)/shard_map/all_to_all | solution.py:285
  302.3 8.6 %all_to_all.49 = f32[32,1,64]{2,1,0:T(1,128)S(1)} all-to-all(f32[32,1,64]{2,1,0:T(1,128)S(1)} %broadcast_in_dim.153), channel_id=1, replica_groups=mesh['q'=4,'y'=2,'x'=2,'c'=2] {'q','y','x','c'}, dimensions={0} | all-to-all | bytes 16384 | tf_op jit(solution)/shard_map/all_to_all | solution.py:295
  311.7 6.5 %convolution_convert_fusion.1 = bf16[1024,960]{0,1:T(8,128)(2,1)} fusion(bf16[1000,960]{0,1:T(8,128)(2,1)} %convert_element_type.271, f32[1024,1000]{0,1:T(8,128)} %copy-done.10, f32[1024]{0:T(1024)S(1)} %squeeze.85, f32[1024]{0:T(1024)S(1)} %multiply_add_fusion.2, s32[1024]{0:T(1024)S(1)} %sub.195), kind=kOutput, calls=%fused_computation.67 | convolution fusion | flops 1975255040 | bytes 7994368 | tf_op jit(solution)/shard_map/dot_general | solution.py:50
  318.9 3.9 collective-permute-done.19
  322.8 7.8 %fusion.175 = (bf16[1024,960]{0,1:T(8,128)(2,1)S(1)}, f32[1024,960]{0,1:T(8,128)}) fusion(bf16[1024,960]{0,1:T(8,128)(2,1)} %collective-permute-done.19, bf16[1000,960]{0,1:T(8,128)(2,1)} %convert_element_type.271, f32[1024,1000]{0,1:T(8,128)} %copy-done.12, f32[1024]{0:T(1024)S(1)} %squeeze.84, f32[1024]{0:T(1024)S(1)} %multiply_add_fusion.3, ...), kind=kOutput, calls=%fused_computation.362 | convolution fusion | flops 1977221120 | bytes 13892608 | tf_op jit(solution)/shard_map/dot_general | solution.py:50
  339.3 7.2 %fusion.150 = f32[1000,960]{0,1:T(8,128)} fusion(bf16[1024,960]{1,0:T(8,128)(2,1)} %bitcast.226, f32[1024,1000]{0,1:T(8,128)} %copy-done.12, f32[1024]{0:T(1024)S(1)} %squeeze.84, f32[1024]{0:T(1024)S(1)} %multiply_add_fusion.3, s32[1024]{0:T(1024)S(1)} %sub.191), kind=kOutput, calls=%fused_computation.343 | convolution fusion | flops 1974272000 | bytes 9914368 | tf_op jit(solution)/shard_map/dot_general | solution.py:50
  351.2 3.1 copy.339
  356.6 3.3 collective-permute-done.21
  363.5 3.0 fusion.157
  370.2 6.0 convolution_add_fusion
  376.2 13.2 %collective-permute-done.24 = bf16[64,960]{0,1:T(8,128)(2,1)S(1)} collective-permute-done((bf16[64,960]{0,1:T(8,128)(2,1)S(1)}, bf16[64,960]{0,1:T(8,128)(2,1)S(1)}, u32[]{:S(2)}, u32[]{:S(2)}) %collective-permute-start.24) | collective-permute-done | bytes 122912 | tf_op jit(solution)/shard_map/ppermute | solution.py:72
  392.9 4.5 collective-permute-done.28
  397.4 5.7 collective-permute-done.27
  412.3 3.2 pad_maximum_fusion.6
  431.6 4.0 collective-permute-done.33
  435.6 6.0 collective-permute-done.32
  451.8 3.0 convolution_convert_fusion.8
  458.8 3.1 fusion.14
  463.6 5.3 fusion.24
  468.9 3.9 copy.358
  473.7 3.6 all-to-all-start.5
  480.2 3.1 reshape.641
  486.2 4.8 convert_element_type.323
  496.5 29.1 %all-to-all-done.5 = bf16[32,32,960]{2,1,0:T(8,128)(2,1)} async-done(((bf16[32,32,960]{2,1,0:T(8,128)(2,1)}), bf16[32,32,960]{2,1,0:T(8,128)(2,1)}, u32[]{:S(2)}, u32[]{:S(2)}) %all-to-all-start.5) | async-done | bytes 1966112 | tf_op jit(solution)/shard_map/all_to_all | solution.py:359
  525.7 3.3 dynamic-slice_bitcast_fusion
  529.9 4.6 collective-permute-done.34
  541.9 4.1 fusion.1
  546.1 9.4 %collective-permute-done.37 = bf16[2432,128]{1,0:T(8,128)(2,1)S(1)} collective-permute-done((bf16[2432,128]{1,0:T(8,128)(2,1)S(1)}, bf16[2432,128]{1,0:T(8,128)(2,1)S(1)}, u32[]{:S(2)}, u32[]{:S(2)}) %collective-permute-start.37) | collective-permute-done | bytes 622624 | tf_op jit(solution)/shard_map/ppermute | solution.py:72
  555.4 14.1 %collective-permute-done.36 = bf16[2432,128]{1,0:T(8,128)(2,1)S(1)} collective-permute-done((bf16[2432,128]{1,0:T(8,128)(2,1)S(1)}, bf16[2432,128]{1,0:T(8,128)(2,1)S(1)}, u32[]{:S(2)}, u32[]{:S(2)}) %collective-permute-start.36) | collective-permute-done | bytes 622624 | tf_op jit(solution)/shard_map/ppermute | solution.py:72
  575.0 3.6 multiply_reduce_fusion
  579.5 4.7 all-to-all-start.6
  594.2 5.1 collective-permute-done.43
  599.3 3.3 collective-permute-done.42
  603.9 3.4 collective-permute-start.44
  611.2 10.1 %all_to_all.50 = f32[32,1,2]{2,1,0:T(1,128)S(1)} all-to-all(f32[32,1,2]{2,1,0:T(1,128)S(1)} %broadcast_in_dim.157), channel_id=1, replica_groups=mesh['q'=4,'y'=2,'x'=2,'c'=2] {'q','y','x','c'}, dimensions={0} | all-to-all | bytes 512 | tf_op jit(solution)/shard_map/all_to_all | solution.py:408
  623.3 4.2 add_multiply_fusion.1
  628.7 7.8 %add_multiply_fusion = (f32[1000,960]{0,1:T(8,128)}, f32[1000,960]{0,1:T(8,128)}, f32[1000,960]{0,1:T(8,128)}) fusion(f32[1000,960]{0,1:T(8,128)S(1)} %copy-done.1, f32[1000,960]{0,1:T(8,128)S(1)} %copy-done.2, f32[]{:T(128)S(6)} %div.148, f32[1000,960]{0,1:T(8,128)} %param.23, f32[1000,960]{0,1:T(8,128)} %param.22), kind=kLoop, calls=%fused_computation.24 | loop fusion | flops 14400000 | bytes 26880004 | tf_op jit(solution)/shard_map/mul | solution.py:105
  (448 shorter events, 216.5 us)
Async XLA Ops:
  8.5 15.2 %copy-start.74 = (s32[64]{0:T(128)S(1)}, s32[64]{0:T(128)}, u32[]{:S(2)}) copy-start(s32[64]{0:T(128)} %param.17) | copy-start | bytes 772
  8.5 5.8 collective-permute-start
  18.8 16.9 %collective-permute-start.1 = (bf16[2432,128]{1,0:T(8,128)(2,1)S(1)}, bf16[2432,128]{1,0:T(8,128)(2,1)S(1)}, u32[]{:S(2)}, u32[]{:S(2)}) collective-permute-start(bf16[2432,128]{1,0:T(8,128)(2,1)S(1)} %bitcast.230), channel_id=1, source_target_pairs={{0,16},{1,17},{2,18},{3,19},{4,20},{5,21},{6,22},{7,23}} | collective-permute-start | bytes 1867784 | tf_op jit(solution)/shard_map/ppermute | solution.py:189
  23.1 86.5 %copy-start.70 = (s32[512]{0:T(512)}, s32[512]{0:T(512)S(1)}, u32[]{:S(2)}) copy-start(s32[512]{0:T(512)S(1)} %convert_add_fusion.5) | copy-start | bytes 6148
  24.4 15.0 %all-to-all-start = ((s32[32,1,96]{2,1,0:T(1,128)}), s32[32,1,96]{2,1,0:T(1,128)S(1)}, u32[]{:S(2)}, u32[]{:S(2)}) async-start(s32[32,1,96]{2,1,0:T(1,128)} %bitcast), calls=%async_computation | async-start | bytes 32768 | tf_op jit(solution)/shard_map/all_to_all | solution.py:174
  36.6 16.3 %collective-permute-start.2 = (bf16[2432,128]{1,0:T(8,128)(2,1)}, bf16[2432,128]{1,0:T(8,128)(2,1)S(1)}, u32[]{:S(2)}, u32[]{:S(2)}) collective-permute-start(bf16[2432,128]{1,0:T(8,128)(2,1)} %broadcast_select_fusion), channel_id=1, source_target_pairs={{0,8},{16,24},{1,9},{17,25},{2,10},{18,26},{3,11},{19,27},{4,12},{... | collective-permute-start | bytes 1867784 | tf_op jit(solution)/shard_map/ppermute | solution.py:191
  39.4 14.4 %all-to-all-start.1 = ((bf16[8,60,640]{2,1,0:T(8,128)(2,1)}), bf16[8,60,640]{2,1,0:T(8,128)(2,1)S(1)}, u32[]{:S(2)}, u32[]{:S(2)}) async-start(bf16[8,60,640]{2,1,0:T(8,128)(2,1)} %reshape.709), calls=%async_computation.1 | async-start | bytes 1310720 | tf_op jit(solution)/shard_map/all_to_all | solution.py:187
  43.8 71.5 %all-gather.5.cloned.1.call-start = ((), (), s32[]{:S(2)}) async-start(), calls=%async_computation.10 | async-start | bytes 5603328 | tf_op jit(solution)/shard_map/all_gather | solution.py:195
  53.9 55.6 %all-to-all-start.2 = ((bf16[32,32,960]{2,1,0:T(8,128)(2,1)}), bf16[32,32,960]{2,1,0:T(8,128)(2,1)}, u32[]{:S(2)}, u32[]{:S(2)}) async-start(bf16[32,32,960]{2,1,0:T(8,128)(2,1)} %bitcast.2), calls=%async_computation.2 | async-start | bytes 4194304 | tf_op jit(solution)/shard_map/all_to_all | solution.py:194
  61.4 106.5 %all-gather.7.cloned.1.call-start = ((), (), s32[]{:S(2)}) async-start(), calls=%async_computation.11 | async-start | bytes 3072000 | tf_op jit(solution)/shard_map/all_gather | solution.py:201
  63.0 77.0 %copy-start.24 = (f32[64,960]{1,0:T(8,128)}, f32[64,960]{1,0:T(8,128)S(1)}, u32[]{:S(2)}) copy-start(f32[64,960]{1,0:T(8,128)S(1)} %mul.492) | copy-start | bytes 737284
  113.2 21.4 %copy-start.66 = (f32[512]{0:T(512)}, f32[512]{0:T(512)S(1)}, u32[]{:S(2)}) copy-start(f32[512]{0:T(512)S(1)} %get-tuple-element.145) | copy-start | bytes 6148
  114.9 364.6 %reduce-scatter.2.cloned.1.call-start = ((), (), s32[]{:S(2)}) async-start(), calls=%async_computation.9 | async-start | bytes 3072000 | tf_op jit(solution)/shard_map/reduce_scatter | solution.py:356
  124.6 11.7 %copy-start.4 = (bf16[960,1600]{1,0:T(8,128)(2,1)}, bf16[960,1600]{1,0:T(8,128)(2,1)S(1)}, u32[]{:S(2)}) copy-start(bf16[960,1600]{1,0:T(8,128)(2,1)S(1)} %reshape.619) | copy-start | bytes 9216004
  150.7 14.4 %copy-start.64 = (f32[64]{0:T(128)}, f32[64]{0:T(128)S(1)}, u32[]{:S(2)}) copy-start(f32[64]{0:T(128)S(1)} %add_rsqrt_fusion.2) | copy-start | bytes 772
  151.0 7.7 %collective-permute-start.5 = (bf16[64,960]{0,1:T(8,128)(2,1)S(1)}, bf16[64,960]{0,1:T(8,128)(2,1)S(1)}, u32[]{:S(2)}, u32[]{:S(2)}) collective-permute-start(bf16[64,960]{0,1:T(8,128)(2,1)S(1)} %multiply_convert_fusion.7), channel_id=1, source_target_pairs={{0,6},{2,4},{4,2},{6,0},{1,7},{3,5},{5,3},{7,1},{8,14},{10,12},{12... | collective-permute-start | bytes 368648 | tf_op jit(solution)/shard_map/ppermute | solution.py:72
  153.0 12.1 %collective-permute-start.4 = (bf16[64,960]{0,1:T(8,128)(2,1)S(1)}, bf16[64,960]{0,1:T(8,128)(2,1)S(1)}, u32[]{:S(2)}, u32[]{:S(2)}) collective-permute-start(bf16[64,960]{0,1:T(8,128)(2,1)S(1)} %multiply_convert_fusion.7), channel_id=1, source_target_pairs={{0,4},{2,6},{4,0},{6,2},{1,5},{3,7},{5,1},{7,3},{8,12},{10,14},{12... | collective-permute-start | bytes 368648 | tf_op jit(solution)/shard_map/ppermute | solution.py:72
  153.2 12.0 %collective-permute-start.3 = (bf16[64,960]{0,1:T(8,128)(2,1)S(1)}, bf16[64,960]{0,1:T(8,128)(2,1)S(1)}, u32[]{:S(2)}, u32[]{:S(2)}) collective-permute-start(bf16[64,960]{0,1:T(8,128)(2,1)S(1)} %multiply_convert_fusion.7), channel_id=1, source_target_pairs={{0,2},{2,0},{4,6},{6,4},{1,3},{3,1},{5,7},{7,5},{8,10},{10,8},{12,... | collective-permute-start | bytes 368648 | tf_op jit(solution)/shard_map/ppermute | solution.py:72
  167.5 3.9 collective-permute-start.6
  183.8 2.0 collective-permute-start.7
  186.6 8.1 %collective-permute-start.10 = (bf16[64,960]{0,1:T(8,128)(2,1)S(1)}, bf16[64,960]{0,1:T(8,128)(2,1)S(1)}, u32[]{:S(2)}, u32[]{:S(2)}) collective-permute-start(bf16[64,960]{0,1:T(8,128)(2,1)S(1)} %get-tuple-element.133), channel_id=1, source_target_pairs={{0,6},{2,4},{4,2},{6,0},{1,7},{3,5},{5,3},{7,1},{8,14},{10,12},{12... | collective-permute-start | bytes 368648 | tf_op jit(solution)/shard_map/ppermute | solution.py:72
  188.7 11.9 %collective-permute-start.9 = (bf16[64,960]{0,1:T(8,128)(2,1)S(1)}, bf16[64,960]{0,1:T(8,128)(2,1)S(1)}, u32[]{:S(2)}, u32[]{:S(2)}) collective-permute-start(bf16[64,960]{0,1:T(8,128)(2,1)S(1)} %get-tuple-element.134), channel_id=1, source_target_pairs={{0,4},{2,6},{4,0},{6,2},{1,5},{3,7},{5,1},{7,3},{8,12},{10,14},{12... | collective-permute-start | bytes 368648 | tf_op jit(solution)/shard_map/ppermute | solution.py:72
  189.0 11.7 %collective-permute-start.8 = (bf16[64,960]{0,1:T(8,128)(2,1)S(1)}, bf16[64,960]{0,1:T(8,128)(2,1)S(1)}, u32[]{:S(2)}, u32[]{:S(2)}) collective-permute-start(bf16[64,960]{0,1:T(8,128)(2,1)S(1)} %get-tuple-element.132), channel_id=1, source_target_pairs={{0,2},{2,0},{4,6},{6,4},{1,3},{3,1},{5,7},{7,5},{8,10},{10,8},{12,... | collective-permute-start | bytes 368648 | tf_op jit(solution)/shard_map/ppermute | solution.py:72
  201.1 9.0 %collective-permute-start.13 = (bf16[64,960]{0,1:T(8,128)(2,1)S(1)}, bf16[64,960]{0,1:T(8,128)(2,1)S(1)}, u32[]{:S(2)}, u32[]{:S(2)}) collective-permute-start(bf16[64,960]{0,1:T(8,128)(2,1)S(1)} %multiply_convert_fusion.6), channel_id=1, source_target_pairs={{0,24},{8,16},{16,8},{24,0},{1,25},{9,17},{17,9},{25,1},{2,26},{10... | collective-permute-start | bytes 368648 | tf_op jit(solution)/shard_map/ppermute | solution.py:72
  203.1 21.6 %collective-permute-start.12 = (bf16[64,960]{0,1:T(8,128)(2,1)S(1)}, bf16[64,960]{0,1:T(8,128)(2,1)S(1)}, u32[]{:S(2)}, u32[]{:S(2)}) collective-permute-start(bf16[64,960]{0,1:T(8,128)(2,1)S(1)} %multiply_convert_fusion.6), channel_id=1, source_target_pairs={{0,16},{8,24},{16,0},{24,8},{1,17},{9,25},{17,1},{25,9},{2,18},{10... | collective-permute-start | bytes 368648 | tf_op jit(solution)/shard_map/ppermute | solution.py:72
  203.3 21.4 %collective-permute-start.11 = (bf16[64,960]{0,1:T(8,128)(2,1)S(1)}, bf16[64,960]{0,1:T(8,128)(2,1)S(1)}, u32[]{:S(2)}, u32[]{:S(2)}) collective-permute-start(bf16[64,960]{0,1:T(8,128)(2,1)S(1)} %multiply_convert_fusion.6), channel_id=1, source_target_pairs={{0,8},{8,0},{16,24},{24,16},{1,9},{9,1},{17,25},{25,17},{2,10},{10... | collective-permute-start | bytes 368648 | tf_op jit(solution)/shard_map/ppermute | solution.py:72
  227.8 12.3 %collective-permute-start.15 = (bf16[4,64,960]{2,1,0:T(8,128)(2,1)S(1)}, bf16[4,64,960]{2,1,0:T(8,128)(2,1)}, u32[]{:S(2)}, u32[]{:S(2)}) collective-permute-start(bf16[4,64,960]{2,1,0:T(8,128)(2,1)S(1)} %copy.326), channel_id=1, source_target_pairs={{0,4},{4,0},{1,5},{5,1},{2,6},{6,2},{3,7},{7,3},{8,12},{12,8},{9,1... | collective-permute-start | bytes 1474568 | tf_op jit(solution)/shard_map/ppermute | solution.py:72
  228.3 16.6 %collective-permute-start.14 = (bf16[4,64,960]{2,1,0:T(8,128)(2,1)S(1)}, bf16[4,64,960]{2,1,0:T(8,128)(2,1)}, u32[]{:S(2)}, u32[]{:S(2)}) collective-permute-start(bf16[4,64,960]{2,1,0:T(8,128)(2,1)S(1)} %copy.326), channel_id=1, source_target_pairs={{0,2},{2,0},{1,3},{3,1},{4,6},{6,4},{5,7},{7,5},{8,10},{10,8},{9,1... | collective-permute-start | bytes 1474568 | tf_op jit(solution)/shard_map/ppermute | solution.py:72
  244.3 10.9 %collective-permute-start.17 = (bf16[2,64,960]{1,2,0:T(8,128)(2,1)}, bf16[2,64,960]{1,2,0:T(8,128)(2,1)}, u32[]{:S(2)}, u32[]{:S(2)}) collective-permute-start(bf16[2,64,960]{1,2,0:T(8,128)(2,1)} %slice.404), channel_id=1, source_target_pairs={{0,2},{2,0},{1,3},{3,1},{4,6},{6,4},{5,7},{7,5},{8,10},{10,8},{9,1... | collective-permute-start | bytes 737288 | tf_op jit(solution)/shard_map/ppermute | solution.py:72
  247.3 12.8 %copy-start.6 = (bf16[4,64,960]{1,2,0:T(8,128)(2,1)S(1)}, bf16[4,64,960]{1,2,0:T(8,128)(2,1)}, u32[]{:S(2)}) copy-start(bf16[4,64,960]{1,2,0:T(8,128)(2,1)} %copy.329) | copy-start | bytes 1474564
  247.3 12.8 %copy-start.7 = (bf16[4,64,960]{1,2,0:T(8,128)(2,1)S(1)}, bf16[4,64,960]{1,2,0:T(8,128)(2,1)}, u32[]{:S(2)}) copy-start(bf16[4,64,960]{1,2,0:T(8,128)(2,1)} %copy.327) | copy-start | bytes 1474564
  247.3 12.8 %copy-start.14 = (bf16[1,4,64,960]{2,3,1,0:T(8,128)(2,1)S(1)}, bf16[1,4,64,960]{2,3,1,0:T(8,128)(2,1)}, u32[]{:S(2)}) copy-start(bf16[1,4,64,960]{2,3,1,0:T(8,128)(2,1)} %get-tuple-element.111) | copy-start | bytes 1474564
  248.5 10.4 %collective-permute-start.16 = (bf16[2,64,960]{1,2,0:T(8,128)(2,1)S(1)}, bf16[2,64,960]{1,2,0:T(8,128)(2,1)S(1)}, u32[]{:S(2)}, u32[]{:S(2)}) collective-permute-start(bf16[2,64,960]{1,2,0:T(8,128)(2,1)S(1)} %slice.403), channel_id=1, source_target_pairs={{0,4},{4,0},{1,5},{5,1},{2,6},{6,2},{3,7},{7,3},{8,12},{12,8},{9,1... | collective-permute-start | bytes 737288 | tf_op jit(solution)/shard_map/ppermute | solution.py:72
  271.5 10.9 %collective-permute-start.18 = (bf16[1024,960]{0,1:T(8,128)(2,1)}, bf16[1024,960]{0,1:T(8,128)(2,1)}, u32[]{:S(2)}, u32[]{:S(2)}) collective-permute-start(bf16[1024,960]{0,1:T(8,128)(2,1)} %copy.333), channel_id=1, source_target_pairs={{0,1},{1,0},{2,3},{3,2},{4,5},{5,4},{6,7},{7,6},{8,9},{9,8},{10,11... | collective-permute-start | bytes 5898248 | tf_op jit(solution)/shard_map/ppermute | solution.py:72
  318.2 4.6 collective-permute-start.19
  333.6 20.7 %collective-permute-start.22 = (bf16[4,64,960]{2,1,0:T(8,128)(2,1)}, bf16[4,64,960]{2,1,0:T(8,128)(2,1)}, u32[]{:S(2)}, u32[]{:S(2)}) collective-permute-start(bf16[4,64,960]{2,1,0:T(8,128)(2,1)} %bitcast.272), channel_id=1, source_target_pairs={{0,6},{2,4},{4,2},{6,0},{1,7},{3,5},{5,3},{7,1},{8,14},{10,12},{12... | collective-permute-start | bytes 1474568 | tf_op jit(solution)/shard_map/ppermute | solution.py:72
  335.9 23.9 %collective-permute-start.21 = (bf16[4,64,960]{2,1,0:T(8,128)(2,1)}, bf16[4,64,960]{2,1,0:T(8,128)(2,1)}, u32[]{:S(2)}, u32[]{:S(2)}) collective-permute-start(bf16[4,64,960]{2,1,0:T(8,128)(2,1)} %bitcast.273), channel_id=1, source_target_pairs={{0,4},{2,6},{4,0},{6,2},{1,5},{3,7},{5,1},{7,3},{8,12},{10,14},{12... | collective-permute-start | bytes 1474568 | tf_op jit(solution)/shard_map/ppermute | solution.py:72
  338.0 24.2 %collective-permute-start.20 = (bf16[4,64,960]{2,1,0:T(8,128)(2,1)}, bf16[4,64,960]{2,1,0:T(8,128)(2,1)S(1)}, u32[]{:S(2)}, u32[]{:S(2)}) collective-permute-start(bf16[4,64,960]{2,1,0:T(8,128)(2,1)} %bitcast.274), channel_id=1, source_target_pairs={{0,2},{2,0},{4,6},{6,4},{1,3},{3,1},{5,7},{7,5},{8,10},{10,8},{12,... | collective-permute-start | bytes 1474568 | tf_op jit(solution)/shard_map/ppermute | solution.py:72
  366.6 9.7 %collective-permute-start.25 = (bf16[64,960]{0,1:T(8,128)(2,1)S(1)}, bf16[64,960]{0,1:T(8,128)(2,1)S(1)}, u32[]{:S(2)}, u32[]{:S(2)}) collective-permute-start(bf16[64,960]{0,1:T(8,128)(2,1)S(1)} %get-tuple-element.109), channel_id=1, source_target_pairs={{0,24},{8,16},{16,8},{24,0},{1,25},{9,17},{17,9},{25,1},{2,26},{10... | collective-permute-start | bytes 368648 | tf_op jit(solution)/shard_map/ppermute | solution.py:72
  366.9 22.5 %collective-permute-start.24 = (bf16[64,960]{0,1:T(8,128)(2,1)S(1)}, bf16[64,960]{0,1:T(8,128)(2,1)S(1)}, u32[]{:S(2)}, u32[]{:S(2)}) collective-permute-start(bf16[64,960]{0,1:T(8,128)(2,1)S(1)} %get-tuple-element.110), channel_id=1, source_target_pairs={{0,16},{8,24},{16,0},{24,8},{1,17},{9,25},{17,1},{25,9},{2,18},{10... | collective-permute-start | bytes 368648 | tf_op jit(solution)/shard_map/ppermute | solution.py:72
  368.1 21.4 %collective-permute-start.23 = (bf16[64,960]{0,1:T(8,128)(2,1)S(1)}, bf16[64,960]{0,1:T(8,128)(2,1)S(1)}, u32[]{:S(2)}, u32[]{:S(2)}) collective-permute-start(bf16[64,960]{0,1:T(8,128)(2,1)S(1)} %get-tuple-element.108), channel_id=1, source_target_pairs={{0,8},{8,0},{16,24},{24,16},{1,9},{9,1},{17,25},{25,17},{2,10},{10... | collective-permute-start | bytes 368648 | tf_op jit(solution)/shard_map/ppermute | solution.py:72
  390.2 7.2 %collective-permute-start.28 = (bf16[64,960]{0,1:T(8,128)(2,1)S(1)}, bf16[64,960]{0,1:T(8,128)(2,1)S(1)}, u32[]{:S(2)}, u32[]{:S(2)}) collective-permute-start(bf16[64,960]{0,1:T(8,128)(2,1)S(1)} %fusion.101), channel_id=1, source_target_pairs={{0,6},{2,4},{4,2},{6,0},{1,7},{3,5},{5,3},{7,1},{8,14},{10,12},{12... | collective-permute-start | bytes 368648 | tf_op jit(solution)/shard_map/ppermute | solution.py:72
  390.6 12.6 %collective-permute-start.27 = (bf16[64,960]{0,1:T(8,128)(2,1)S(1)}, bf16[64,960]{0,1:T(8,128)(2,1)S(1)}, u32[]{:S(2)}, u32[]{:S(2)}) collective-permute-start(bf16[64,960]{0,1:T(8,128)(2,1)S(1)} %fusion.101), channel_id=1, source_target_pairs={{0,4},{2,6},{4,0},{6,2},{1,5},{3,7},{5,1},{7,3},{8,12},{10,14},{12... | collective-permute-start | bytes 368648 | tf_op jit(solution)/shard_map/ppermute | solution.py:72
  391.7 11.5 %collective-permute-start.26 = (bf16[64,960]{0,1:T(8,128)(2,1)S(1)}, bf16[64,960]{0,1:T(8,128)(2,1)S(1)}, u32[]{:S(2)}, u32[]{:S(2)}) collective-permute-start(bf16[64,960]{0,1:T(8,128)(2,1)S(1)} %fusion.101), channel_id=1, source_target_pairs={{0,2},{2,0},{4,6},{6,4},{1,3},{3,1},{5,7},{7,5},{8,10},{10,8},{12,... | collective-permute-start | bytes 368648 | tf_op jit(solution)/shard_map/ppermute | solution.py:72
  407.0 2.9 collective-permute-start.29
  422.3 2.2 collective-permute-start.30
  427.2 8.4 %collective-permute-start.33 = (bf16[64,960]{0,1:T(8,128)(2,1)}, bf16[64,960]{0,1:T(8,128)(2,1)}, u32[]{:S(2)}, u32[]{:S(2)}) collective-permute-start(bf16[64,960]{0,1:T(8,128)(2,1)} %get-tuple-element.130), channel_id=1, source_target_pairs={{0,6},{2,4},{4,2},{6,0},{1,7},{3,5},{5,3},{7,1},{8,14},{10,12},{12... | collective-permute-start | bytes 368648 | tf_op jit(solution)/shard_map/ppermute | solution.py:72
  428.1 13.5 %collective-permute-start.32 = (bf16[64,960]{0,1:T(8,128)(2,1)}, bf16[64,960]{0,1:T(8,128)(2,1)}, u32[]{:S(2)}, u32[]{:S(2)}) collective-permute-start(bf16[64,960]{0,1:T(8,128)(2,1)} %get-tuple-element.131), channel_id=1, source_target_pairs={{0,4},{2,6},{4,0},{6,2},{1,5},{3,7},{5,1},{7,3},{8,12},{10,14},{12... | collective-permute-start | bytes 368648 | tf_op jit(solution)/shard_map/ppermute | solution.py:72
  429.2 12.4 %collective-permute-start.31 = (bf16[64,960]{0,1:T(8,128)(2,1)}, bf16[64,960]{0,1:T(8,128)(2,1)}, u32[]{:S(2)}, u32[]{:S(2)}) collective-permute-start(bf16[64,960]{0,1:T(8,128)(2,1)} %get-tuple-element.129), channel_id=1, source_target_pairs={{0,2},{2,0},{4,6},{6,4},{1,3},{3,1},{5,7},{7,5},{8,10},{10,8},{12,... | collective-permute-start | bytes 368648 | tf_op jit(solution)/shard_map/ppermute | solution.py:72
  473.7 52.0 %all-to-all-start.5 = ((bf16[32,32,960]{2,1,0:T(8,128)(2,1)}), bf16[32,32,960]{2,1,0:T(8,128)(2,1)}, u32[]{:S(2)}, u32[]{:S(2)}) async-start(bf16[32,32,960]{2,1,0:T(8,128)(2,1)} %bitcast.85), calls=%async_computation.6 | async-start | bytes 4194304 | tf_op jit(solution)/shard_map/all_to_all | solution.py:359
  529.0 5.5 collective-permute-start.34
  539.2 16.2 %collective-permute-start.37 = (bf16[2432,128]{1,0:T(8,128)(2,1)S(1)}, bf16[2432,128]{1,0:T(8,128)(2,1)S(1)}, u32[]{:S(2)}, u32[]{:S(2)}) collective-permute-start(bf16[2432,128]{1,0:T(8,128)(2,1)S(1)} %get-tuple-element.94), channel_id=1, source_target_pairs={{0,6},{2,4},{4,2},{6,0},{1,7},{3,5},{5,3},{7,1},{8,14},{10,12},{12... | collective-permute-start | bytes 1867784 | tf_op jit(solution)/shard_map/ppermute | solution.py:72
  541.3 28.2 %collective-permute-start.36 = (bf16[2432,128]{1,0:T(8,128)(2,1)S(1)}, bf16[2432,128]{1,0:T(8,128)(2,1)S(1)}, u32[]{:S(2)}, u32[]{:S(2)}) collective-permute-start(bf16[2432,128]{1,0:T(8,128)(2,1)S(1)} %get-tuple-element.95), channel_id=1, source_target_pairs={{0,4},{2,6},{4,0},{6,2},{1,5},{3,7},{5,1},{7,3},{8,12},{10,14},{12... | collective-permute-start | bytes 1867784 | tf_op jit(solution)/shard_map/ppermute | solution.py:72
  541.6 28.0 %collective-permute-start.35 = (bf16[2432,128]{1,0:T(8,128)(2,1)S(1)}, bf16[2432,128]{1,0:T(8,128)(2,1)}, u32[]{:S(2)}, u32[]{:S(2)}) collective-permute-start(bf16[2432,128]{1,0:T(8,128)(2,1)S(1)} %get-tuple-element.93), channel_id=1, source_target_pairs={{0,2},{2,0},{4,6},{6,4},{1,3},{3,1},{5,7},{7,5},{8,10},{10,8},{12,... | collective-permute-start | bytes 1867784 | tf_op jit(solution)/shard_map/ppermute | solution.py:72
  546.0 29.0 %copy-start.13 = (f32[1000,960]{0,1:T(8,128)S(1)}, f32[1000,960]{0,1:T(8,128)}, u32[]{:S(2)}) copy-start(f32[1000,960]{0,1:T(8,128)} %convolution_add_fusion) | copy-start | bytes 11520004
  571.4 12.8 %collective-permute-start.40 = (bf16[608,128]{1,0:T(8,128)(2,1)S(1)}, bf16[608,128]{1,0:T(8,128)(2,1)S(1)}, u32[]{:S(2)}, u32[]{:S(2)}) collective-permute-start(bf16[608,128]{1,0:T(8,128)(2,1)S(1)} %get-tuple-element.104), channel_id=1, source_target_pairs={{0,24},{8,16},{16,8},{24,0},{1,25},{9,17},{17,9},{25,1},{2,26},{10... | collective-permute-start | bytes 466952 | tf_op jit(solution)/shard_map/ppermute | solution.py:72
  572.7 13.4 %collective-permute-start.39 = (bf16[608,128]{1,0:T(8,128)(2,1)S(1)}, bf16[608,128]{1,0:T(8,128)(2,1)S(1)}, u32[]{:S(2)}, u32[]{:S(2)}) collective-permute-start(bf16[608,128]{1,0:T(8,128)(2,1)S(1)} %get-tuple-element.105), channel_id=1, source_target_pairs={{0,16},{8,24},{16,0},{24,8},{1,17},{9,25},{17,1},{25,9},{2,18},{10... | collective-permute-start | bytes 466952 | tf_op jit(solution)/shard_map/ppermute | solution.py:72
  572.7 13.4 %collective-permute-start.38 = (bf16[608,128]{1,0:T(8,128)(2,1)S(1)}, bf16[608,128]{1,0:T(8,128)(2,1)S(1)}, u32[]{:S(2)}, u32[]{:S(2)}) collective-permute-start(bf16[608,128]{1,0:T(8,128)(2,1)S(1)} %get-tuple-element.103), channel_id=1, source_target_pairs={{0,8},{8,0},{16,24},{24,16},{1,9},{9,1},{17,25},{25,17},{2,10},{10... | collective-permute-start | bytes 466952 | tf_op jit(solution)/shard_map/ppermute | solution.py:72
  579.5 12.3 %all-to-all-start.6 = ((bf16[8,60,640]{2,1,0:T(8,128)(2,1)}), bf16[8,60,640]{2,1,0:T(8,128)(2,1)S(1)}, u32[]{:S(2)}, u32[]{:S(2)}) async-start(bf16[8,60,640]{2,1,0:T(8,128)(2,1)} %reshape.647), calls=%async_computation.7 | async-start | bytes 1310720 | tf_op jit(solution)/shard_map/all_to_all | solution.py:378
  586.2 8.0 %collective-permute-start.41 = (bf16[608,128]{1,0:T(8,128)(2,1)S(1)}, bf16[608,128]{1,0:T(8,128)(2,1)S(1)}, u32[]{:S(2)}, u32[]{:S(2)}) collective-permute-start(bf16[608,128]{1,0:T(8,128)(2,1)S(1)} %fusion.87), channel_id=1, source_target_pairs={{24,0},{25,1},{26,2},{27,3},{28,4},{29,5},{30,6},{31,7}} | collective-permute-start | bytes 466952 | tf_op jit(solution)/shard_map/ppermute | solution.py:384
  587.5 11.8 %collective-permute-start.43 = (bf16[608,128]{1,0:T(8,128)(2,1)S(1)}, bf16[608,128]{1,0:T(8,128)(2,1)}, u32[]{:S(2)}, u32[]{:S(2)}) collective-permute-start(bf16[608,128]{1,0:T(8,128)(2,1)S(1)} %fusion.87), channel_id=1, source_target_pairs={{16,0},{17,1},{18,2},{19,3},{20,4},{21,5},{22,6},{23,7}} | collective-permute-start | bytes 466952 | tf_op jit(solution)/shard_map/ppermute | solution.py:384
  588.8 13.8 %collective-permute-start.42 = (bf16[608,128]{1,0:T(8,128)(2,1)S(1)}, bf16[608,128]{1,0:T(8,128)(2,1)}, u32[]{:S(2)}, u32[]{:S(2)}) collective-permute-start(bf16[608,128]{1,0:T(8,128)(2,1)S(1)} %fusion.87), channel_id=1, source_target_pairs={{8,0},{9,1},{10,2},{11,3},{12,4},{13,5},{14,6},{15,7}} | collective-permute-start | bytes 466952 | tf_op jit(solution)/shard_map/ppermute | solution.py:384
  593.5 29.8 %copy-start.8 = (f32[307290]{0:T(1024)S(1)}, f32[307290]{0:T(1024)}, u32[]{:S(2)}) copy-start(f32[307290]{0:T(1024)} %param.18) | copy-start | bytes 3687484
  603.9 4.2 collective-permute-start.44
  (65 other events, 209.1 us)
Sparse Core Ops, SparseCore 0:
  54.0 60.9 all-gather.4
  116.6 50.9 all-gather.6
  431.7 47.7 reduce-scatter.1

commit v4 on v3

--- a/solution.py
+++ b/solution.py
@@ -41,6 +41,7 @@
 SHARE = FF // 8
 LINES = D * (QKV + D + 3 * FF) // 32 // 128
 EXTRA = 32
+WIDE = 1024
 
 bf16 = jnp.bfloat16
 f32 = jnp.float32
@@ -105,15 +106,26 @@
     return (new_one, new_two, -RATE * (ratio + DECAY * param))
 
 
+def pick_block(blocks, index, axis=0):
+    return lax.dynamic_index_in_dim(blocks, index, axis, False)
+
+
+def widen(rows):
+    return jnp.pad(rows, ((0, 0), (0, WIDE - D)))
+
+
 def fold_plane(left, right, right_dim):
-    half = left.shape[0] // 2
-    got = flip(dot(left[half:], right, 1, right_dim).astype(bf16), "c", 1, 2)
-    mine = (dot(left[:half], right, 1, right_dim) + got.astype(f32)).reshape(4, half // 4, D)
+    c_index, yx_index = lax.axis_index("c"), lax.axis_index(("y", "x"))
+    rows = left.reshape(4, 2, left.shape[0] // 8, left.shape[1])
+    far = pick_block(rows, 1 - c_index, 1).reshape(-1, left.shape[1])
+    near = pick_block(rows, c_index, 1).reshape(-1, left.shape[1])
+    got = flip(dot(far, right, 1, right_dim).astype(bf16), "c", 1, 2)
+    mine = (dot(near, right, 1, right_dim) + got.astype(f32)).reshape(4, -1, WIDE)
     low = mine.astype(bf16)
-    total = mine[0]
+    total = pick_block(mine, yx_index)
     for k in (1, 2, 3):
-        total = total + flip(low[k], ("y", "x"), k, 4).astype(f32)
-    return total
+        total = total + flip(pick_block(low, yx_index ^ k), ("y", "x"), k, 4).astype(f32)
+    return total[:, :D]
 
 
 def down_pack(rows):
@@ -127,8 +139,7 @@
 
 
 def spread_plane(rows):
-    four = jnp.stack([rows] + [flip(rows, ("y", "x"), k, 4) for k in (1, 2, 3)])
-    return jnp.stack([four, flip(four, "c", 1, 2)])
+    return widen(lax.all_gather(rows, PLANE).reshape(-1, D))
 
 
 def local(
@@ -155,10 +166,10 @@
     drift = shard - span
     aligned = devices == 32
 
-    place = np.array([kq * 8 + kyx * 2 + kc for kc in range(2) for kyx in range(4) for kq in range(rows_q)])
+    place = np.array([q * 8 + kyx * 2 + kc for kc in range(2) for kyx in range(4) for q in range(rows_q)])
     rank_of = np.argsort(place)
-    source_of = me ^ jnp.asarray(place, jnp.int32)
-    order_of = jnp.take(jnp.asarray(rank_of, jnp.int32), me ^ jnp.arange(devices, dtype=jnp.int32))
+    source_of = p_index ^ jnp.asarray(place, jnp.int32)
+    order_of = jnp.take(jnp.asarray(rank_of, jnp.int32), p_index ^ jnp.arange(devices, dtype=jnp.int32))
 
     table_low = table_master.astype(bf16)
     owner = token_ids // vocab_dev
@@ -197,7 +208,8 @@
         w_qkv = level[:5, :LINES].reshape(D, QKV)
         w_out = level[5:, :LINES].reshape(D, D)
         mixed = jnp.where(q_index == 3, down_pack(chunk.reshape(SHARE, D)), got.reshape(480, 2 * UNIT))
-        mixed, returned = lax.optimization_barrier((mixed, returned))
+        mixed, w_qkv, w_out = lax.optimization_barrier((mixed, w_qkv, w_out))
+        returned, w_qkv, w_out = lax.optimization_barrier((returned, w_qkv, w_out))
         column = lax.all_gather(mixed, "q")
         w_gu = column[1:3].reshape(D, 2 * SHARE)
         w_down = down_unpack(column[3])
@@ -213,6 +225,8 @@
         both = lax.dynamic_index_in_dim(full[edge[1] : edge[2]].reshape(D, 2, 8, UNIT), p_index, 2, False)
         w_gu = both.reshape(D, 2 * SHARE)
         w_down = lax.dynamic_index_in_dim(full[edge[2] :].reshape(8, SHARE, D), p_index, 0, False)
+    w_gu = jnp.pad(w_gu, ((0, WIDE - D), (0, 0)))
+    w_down = widen(w_down)
     x_low = dot(spot, returned).astype(bf16)
     x_embed = x_low.astype(f32) * emb_mult
 
@@ -252,8 +266,7 @@
     x_one = x_pick + dot(attended, w_out)
 
     h_mlp = (x_one * scale_of(x_one) * gains[1]).astype(bf16)
-    plane_rows = 8 * loss_dev
-    h_all = spread_plane(h_mlp).reshape(plane_rows, D)
+    h_all = spread_plane(h_mlp)
     gate_up = dot(h_all, w_gu)
     gate, up = gate_up[:, :SHARE], gate_up[:, SHARE:]
     sig = jax.nn.sigmoid(gate)
@@ -261,16 +274,17 @@
     x_two = x_one + fold_plane(act, w_down, 0)
 
     hidden = (x_two * scale_of(x_two) * gains[2]).astype(bf16)
-    across = jnp.stack([hidden] + [flip(hidden, "q", k, rows_q) for k in range(1, rows_q)])
+    wide_table = widen(table_low)
+    across = lax.all_gather(widen(hidden), "q")
     by_x, by_y = flip(across, "x", 1, 2), flip(across, "y", 1, 2)
     cut = rows_q // 2
     corner = [flip(by_x[:cut], "y", 1, 2), flip(by_y[cut:], "x", 1, 2)]
-    near = jnp.stack([across, by_x, by_y, jnp.concatenate(corner)]).reshape(loss_total // 2, D)
+    near = jnp.concatenate([across, by_x, by_y] + corner).reshape(loss_total // 2, WIDE)
     sides = [near, flip(near, "c", 1, 2)]
     targets_all = jnp.take(asked[:, capacity:], source_of, axis=0).reshape(2, loss_total // 2)
     logits, hits, stats = [], [], []
     for side, rows in enumerate(sides):
-        z = dot(rows, table_low, 1, 1)
+        z = dot(rows, wide_table, 1, 1)
         column_id = targets_all[side] - me * vocab_dev
         hit = column_id[:, None] == jnp.arange(vocab_dev, dtype=jnp.int32)[None, :]
         local_peak = jnp.max(z, axis=1)
@@ -305,27 +319,28 @@
         ).astype(bf16)
         for side in (1, 0)
     ]
-    got = flip(dot(d_logits[0], table_low).astype(bf16), "c", 1, 2)
-    d_hidden = (dot(d_logits[1], table_low) + got.astype(f32)).reshape(4, rows_q, loss_dev, D)
+    got = flip(dot(d_logits[0], wide_table).astype(bf16), "c", 1, 2)
+    d_hidden = (dot(d_logits[1], wide_table) + got.astype(f32)).reshape(4, rows_q, loss_dev, WIDE)
     d_low = d_hidden.astype(bf16)
     d_hidden = d_hidden[0]
     for k in (1, 2, 3):
         d_hidden = d_hidden + flip(d_low[k], ("y", "x"), k, 4).astype(f32)
     d_low = d_hidden.astype(bf16)
-    total_hidden = d_hidden[0]
+    total_hidden = pick_block(d_hidden, q_index)
     for k in range(1, rows_q):
-        total_hidden = total_hidden + flip(d_low[k], "q", k, rows_q).astype(f32)
+        total_hidden = total_hidden + flip(pick_block(d_low, q_index ^ k), "q", k, rows_q).astype(f32)
+    total_hidden = total_hidden[:, :D]
     head_grad = dot(d_logits[1], sides[0], 0, 0) + dot(d_logits[0], sides[1], 0, 0)
     head_grad, total_hidden = lax.optimization_barrier((head_grad, total_hidden))
 
     d_x_two, grad_final = norm_back(x_two, gains[2], total_hidden)
-    d_down = spread_plane(d_x_two.astype(bf16)).reshape(plane_rows, D)
+    d_down = spread_plane(d_x_two.astype(bf16))
     d_act = dot(d_down, w_down, 1, 1)
     d_gate = d_act * up * sig * (1.0 + gate * (1.0 - sig))
     d_gu = jnp.concatenate([d_gate, d_act * gate * sig], axis=1).astype(bf16)
     d_h_mlp = fold_plane(d_gu, w_gu, 1)
-    grad_down = dot(act, d_down, 0, 0).astype(bf16)
-    grad_gu = dot(h_all, d_gu, 0, 0).astype(bf16)
+    grad_down = dot(act, d_down, 0, 0)[:, :D].astype(bf16)
+    grad_gu = dot(h_all, d_gu, 0, 0)[:D].astype(bf16)
     d_x_mlp, grad_mlp = norm_back(x_one, gains[1], d_h_mlp)
     d_x_one = d_x_two + d_x_mlp
 
@@ -350,13 +365,19 @@
     rest = (d_x_one - high.astype(f32)).astype(bf16)
     d_x_embed = d_x_attn + dot(pick, high, 0, 0) + dot(pick, rest, 0, 0)
 
-    sending = dot(spot, (d_x_embed * emb_mult).astype(bf16), 0, 0).astype(bf16).reshape(devices, capacity, D)
+    part = capacity // 2
+    scaled = (d_x_embed * emb_mult).astype(bf16)
+    sending = []
+    for side in range(2):
+        inside = (slot >= side * part) & (slot < (side + 1) * part)
+        place_of = jnp.where(inside, owner * part + slot - side * part, -1)
+        sending.append(dot(hot(place_of, devices * part), scaled, 0, 0).astype(bf16).reshape(devices, part, D))
     if aligned:
         blocks = jnp.concatenate([jnp.zeros((1, 480, 640), bf16), grad_gu.reshape(2, 480, 640), down_pack(grad_down)[None]])
         share = lax.psum_scatter(blocks, "q", scatter_dimension=0, tiled=False)
         sending, d_q, d_kv, attended = lax.optimization_barrier((sending, d_q, d_kv, attended))
         share, d_q, d_kv, attended = lax.optimization_barrier((share, d_q, d_kv, attended))
-    arrived = lax.all_to_all(sending, ALL, split_axis=0, concat_axis=0, tiled=True).reshape(slots, D)
+    arrived = [lax.all_to_all(rows, ALL, split_axis=0, concat_axis=0, tiled=True).reshape(-1, D) for rows in sending]
     grad_out = dot(attended, d_branch, 0, 0).astype(bf16)
     grad_qkv = jnp.concatenate([dot(h_pick, d_q, 0, 0), dot(h_attn, d_kv, 0, 0)], axis=1).astype(bf16)
 
@@ -365,7 +386,7 @@
         level = jnp.concatenate([grad_qkv.reshape(5, LINES, 128), grad_out.reshape(3, LINES, 128)])
         room = jnp.zeros((8, EXTRA * 128), bf16).at[0, :GAINS].set(gain_grads).reshape(8, EXTRA, 128)
         level = jnp.concatenate([level, room], axis=1).reshape(4, 2, LINES + EXTRA, 128)
-        level, arrived = lax.optimization_barrier((level, arrived))
+        level, arrived[0] = lax.optimization_barrier((level, arrived[0]))
         keep = lax.dynamic_index_in_dim(level, c_index, 1, False)
         give = lax.dynamic_index_in_dim(level, 1 - c_index, 1, False)
         level = keep.astype(f32) + flip(give, "c", 1, 2).astype(f32)
@@ -374,7 +395,7 @@
             piece = lax.dynamic_index_in_dim(level, yx_index ^ k, 0, False).astype(bf16)
             own = own + flip(piece, ("y", "x"), k, 4).astype(f32)
         own = own.reshape(4, (LINES + EXTRA) // 4, 128)
-        own, share = lax.optimization_barrier((own, share))
+        own, share, arrived[1] = lax.optimization_barrier((own, share, arrived[1]))
         got = lax.all_to_all(share.reshape(8, 60, 640), PLANE, split_axis=0, concat_axis=0, tiled=True)
         quarter = lax.dynamic_index_in_dim(own, q_index, 0, False)
         for k in (1, 2, 3):
@@ -402,7 +423,10 @@
     stream = jnp.concatenate([behind, mine, jnp.zeros((tail,), bf16)])
     layer_grad = lax.dynamic_slice(stream, (drift * me,), (shard,)).astype(f32)
 
-    table_grad = head_grad + dot(row_hot, arrived, 0, 0)
+    table_grad = head_grad[:, :D]
+    for side in range(2):
+        rows = asked[:, side * part : (side + 1) * part].reshape(-1) - me * vocab_dev
+        table_grad = table_grad + dot(hot(rows, vocab_dev), arrived[side], 0, 0)
     squares = jnp.sum(layer_grad * layer_grad) + jnp.sum(table_grad * table_grad)
     sums = jnp.broadcast_to(jnp.stack([squares, my_loss])[None], (devices, 2))
     sums = jnp.sum(lax.all_to_all(sums, ALL, split_axis=0, concat_axis=0, tiled=True), axis=0)

time: 657 us -> 614 us (0.935)
  waiting for transfers between devices: 226 us -> 153 us
  blocking collectives: 28.6 us -> 58.4 us
    ppermute x38 -> x27, waiting for transfers between devices: 137 us -> 73.1 us  [flip(): return lax.ppermute(rows, axes, [(i, i ^ bits) for i in range(size)])]
    all_gather x1, waiting for transfers between devices: 0.02 us -> 48.2 us  [local(): level = lax.all_gather(first, PLANE)]
    all_to_all x1, waiting for transfers between devices: 44 us -> 0.01 us  [local(): lax.all_to_all(answer, ALL, split_axis=0, concat_axis=0, tiled=True)]
    unnamed x157 -> x191, local copies, waits for them, and re-layouts: 13.7 us -> 57 us
    all_gather x0 -> x3, blocking collectives: none -> 39.1 us  [the longest x2 25.4 us: spread_plane(): return widen(lax.all_gather(rows, PLANE).reshape(-1, D))]
    all_to_all x1 -> x3, waiting for transfers between devices: 29.1 us -> 4.31 us  [the longest x2 4.31 us: local(): lax.all_to_all(rows, ALL, split_axis=0, concat_axis=0, tiled=True)]
    ppermute x7 -> x0, local copies, waits for them, and re-layouts: 15.3 us -> none  [flip(): return lax.ppermute(rows, axes, [(i, i ^ bits) for i in range(size)])]
    another operation x6 -> x0, local copies, waits for them, and re-layouts: 14.8 us -> none  [the longest x2 5.06 us: spread_plane(): return jnp.stack([four, flip(four, 'c', 1, 2)])]
  transfers between devices with their start and end apart: 53 -> 44, of which waited for: 32 -> 21; matrix products, arithmetic and copies ran while one was open for 27% -> 31% of each run, Pallas kernels for 0% -> 0%
where the time goes in v4:
time: 614 us; the launch traced here: 604 us
  waiting for transfers between devices  153 us (25%)
  local copies, waits for them, and re-layouts  132 us (21%)
  matrix products  94.5 us (15%)
  starting transfers between devices  78.9 us (13%)
  other arithmetic  66.2 us (11%)
  blocking collectives  58.4 us (10%)
  between operations  20.5 us (3%)
    dot_general x37, matrix products, dot(): lax.dot_general(left, right, (((left_dim,), (right_dim,)), ((), ())), pre...  80.4 us
    ppermute x27, waiting for transfers between devices, flip(): return lax.ppermute(rows, axes, [(i, i ^ bits) for i in range(size)])  73.1 us
    unnamed x191, local copies, waits for them, and re-layouts  57 us
    all_gather x1, waiting for transfers between devices, local(): level = lax.all_gather(first, PLANE)  48.2 us
    ppermute x27, starting transfers between devices, flip(): return lax.ppermute(rows, axes, [(i, i ^ bits) for i in range(size)])  28.2 us
    all_gather x2, blocking collectives, spread_plane(): return widen(lax.all_gather(rows, PLANE).reshape(-1, D))  25.4 us
    mul x2, other arithmetic, adamw_step(): return (new_one, new_two, -RATE * (ratio + DECAY * param))  14.8 us
    all_gather x1, blocking collectives, local(): across = lax.all_gather(widen(hidden), 'q')  13.7 us
  transfers between devices with their start and end apart: 44, of which 21 were waited for; matrix products, arithmetic and copies ran while one was open for 31% of the time, Pallas kernels for 0%

profile of v4, /device:TPU:1, one launch (start us, length us, event | category | flops | bytes accessed | tf_op | source)
XLA Modules:
  0.0 604.2 jit_solution(2061353725554449491)
XLA Ops:
  11.5 2.9 collective-permute-done
  15.9 2.9 concatenate.112
  18.8 4.2 collective-permute-start.1
  25.0 4.4 all-to-all-start
  29.4 3.7 convert_element_type.283
  36.7 3.3 collective-permute-start.2
  40.0 4.3 all-to-all-start.1
  44.4 5.2 fusion.22
  49.6 3.9 copy.236
  54.5 7.2 %all-to-all-start.2 = ((bf16[32,32,960]{2,1,0:T(8,128)(2,1)}), bf16[32,32,960]{2,1,0:T(8,128)(2,1)}, u32[]{:S(2)}, u32[]{:S(2)}) async-start(bf16[32,32,960]{2,1,0:T(8,128)(2,1)} %bitcast.2), calls=%async_computation.2 | async-start | bytes 4194304 | tf_op jit(solution)/shard_map/all_to_all | solution.py:205
  67.1 48.2 %all-gather.8.cloned.1.call-done = bf16[19456,128]{1,0:T(8,128)(2,1)} async-done(((bf16[2432,128]{1,0:T(8,128)(2,1)}), bf16[19456,128]{1,0:T(8,128)(2,1)}) %all-gather.8.cloned.1.call-update) | async-done | bytes 4980752 | tf_op jit(solution)/shard_map/all_gather | solution.py:206
  117.4 2.9 slice.339
  120.3 4.0 reshape.653
  124.2 3.3 reshape.654
  128.3 3.0 fusion.21
  138.1 2.8 fusion.26
  152.0 3.7 fusion.189
  155.6 3.6 convolution_convert_fusion.10
  162.4 12.1 %all-gather.1 = bf16[512,960]{1,0:T(8,128)(2,1)} all-gather(bf16[64,960]{1,0:T(8,128)(2,1)S(1)} %multiply_convert_fusion.7), channel_id=3, replica_groups=mesh['q'=4,'y'=2,'x'=2,'c'=2] {'y','x','c'}, dimensions={0}, use_global_device_ids=true | all-gather | bytes 1105920 | tf_op jit(solution)/shard_map/all_gather | solution.py:142
  174.5 8.7 %all-gather.10.cloned.1.call-done = bf16[1920,640]{1,0:T(8,128)(2,1)} async-done(((bf16[480,640]{1,0:T(8,128)(2,1)}), bf16[1920,640]{1,0:T(8,128)(2,1)}) %all-gather.10.cloned.1.call-update) | async-done | bytes 2457616 | tf_op jit(solution)/shard_map/all_gather | solution.py:213
  201.9 3.7 collective-permute-done.5
  207.7 13.7 %all-gather.3 = bf16[256,1024]{1,0:T(8,128)(2,1)} all-gather(bf16[64,1024]{1,0:T(8,128)(2,1)S(1)} %pad.31), channel_id=5, replica_groups=mesh['q'=4,'y'=2,'x'=2,'c'=2] {'q'}, dimensions={0}, use_global_device_ids=true | all-gather | bytes 655360 | tf_op jit(solution)/shard_map/all_gather | solution.py:278
  223.3 8.5 %collective-permute-done.7 = bf16[4,64,1024]{2,1,0:T(8,128)(2,1)} collective-permute-done((bf16[4,64,1024]{2,1,0:T(8,128)(2,1)}, bf16[4,64,1024]{2,1,0:T(8,128)(2,1)}, u32[]{:S(2)}, u32[]{:S(2)}) %collective-permute-start.7) | collective-permute-done | bytes 524320 | tf_op jit(solution)/shard_map/ppermute | solution.py:73
  242.2 5.7 collective-permute-start.11
  249.9 4.5 fusion.191
  257.5 3.9 fusion.190
  268.1 10.2 %all_to_all.53 = f32[32,1,256]{2,1,0:T(1,128)S(1)} all-to-all(f32[32,1,256]{2,1,0:T(1,128)} %reshape.768), channel_id=1, replica_groups=mesh['q'=4,'y'=2,'x'=2,'c'=2] {'q','y','x','c'}, dimensions={0} | all-to-all | bytes 65536 | tf_op jit(solution)/shard_map/all_to_all | solution.py:299
  285.1 9.1 %all_to_all.54 = f32[32,1,64]{2,1,0:T(1,128)S(1)} all-to-all(f32[32,1,64]{2,1,0:T(1,128)S(1)} %broadcast_in_dim.101), channel_id=1, replica_groups=mesh['q'=4,'y'=2,'x'=2,'c'=2] {'q','y','x','c'}, dimensions={0} | all-to-all | bytes 16384 | tf_op jit(solution)/shard_map/all_to_all | solution.py:309
  295.7 7.1 %convolution_convert_fusion = bf16[1024,1024]{1,0:T(8,128)(2,1)} fusion(bf16[1000,960]{0,1:T(8,128)(2,1)} %convert_element_type.283, f32[1024,1000]{0,1:T(8,128)} %copy-done.15, f32[1024]{0:T(1024)S(1)} %squeeze.113, f32[1024]{0:T(1024)S(1)} %multiply_add_fusion.2, s32[1024]{0:T(1024)S(1)} %sub.225), kind=kOutput, calls=%fused_computation.60 | convolution fusion | flops 2106392576 | bytes 8125440 | tf_op jit(solution)/shard_map/dot_general | solution.py:51
  303.5 4.0 collective-permute-done.12
  307.5 6.6 %fusion.192 = (bf16[1024,1024]{1,0:T(8,128)(2,1)S(1)}, f32[1024,1024]{1,0:T(8,128)S(1)}) fusion(bf16[1024,1024]{1,0:T(8,128)(2,1)} %collective-permute-done.12, bf16[1000,960]{0,1:T(8,128)(2,1)} %convert_element_type.283, f32[1024,1000]{0,1:T(8,128)} %copy-done.13, f32[1024]{0:T(1024)S(1)} %squeeze.112, f32[1024]{0:T(1024)S(1)} %multiply_add_fusion.3, ...), kind=kOutput, calls=%fused_computation.400 | convolution fusion | flops 2108489728 | bytes 14416896 | tf_op jit(solution)/shard_map/dot_general | solution.py:51
  317.0 4.3 fusion.164
  321.4 7.1 %collective-permute-done.15 = bf16[4,64,1024]{2,1,0:T(8,128)(2,1)S(1)} collective-permute-done((bf16[4,64,1024]{2,1,0:T(8,128)(2,1)S(1)}, bf16[4,64,1024]{2,1,0:T(8,128)(2,1)S(1)}, u32[]{:S(2)}, u32[]{:S(2)}) %collective-permute-start.15) | collective-permute-done | bytes 524320 | tf_op jit(solution)/shard_map/ppermute | solution.py:73
  328.4 10.9 %collective-permute-done.14 = bf16[4,64,1024]{2,1,0:T(8,128)(2,1)S(1)} collective-permute-done((bf16[4,64,1024]{2,1,0:T(8,128)(2,1)S(1)}, bf16[4,64,1024]{2,1,0:T(8,128)(2,1)S(1)}, u32[]{:S(2)}, u32[]{:S(2)}) %collective-permute-start.14) | collective-permute-done | bytes 524320 | tf_op jit(solution)/shard_map/ppermute | solution.py:73
  343.3 6.4 %convolution_add_fusion = f32[1000,1024]{1,0:T(8,128)} fusion(f32[1000,1024]{1,0:T(8,128)S(1)} %fusion.164, bf16[1024,1024]{1,0:T(8,128)(2,1)} %bitcast.33, f32[1024,1000]{0,1:T(8,128)S(1)} %copy-done.14, f32[1024]{0:T(1024)S(1)} %squeeze.112, f32[1024]{0:T(1024)S(1)} %multiply_add_fusion.3, s32[1024]{0:T(1024)S(1)} %sub.221), kind=kOutput, calls=%fused_computation.61 | convolution fusion | flops 2106368000 | bytes 14397440 | tf_op jit(solution)/shard_map/dot_general | solution.py:51
  352.9 13.3 %all-gather.4 = bf16[512,960]{1,0:T(8,128)(2,1)S(1)} all-gather(bf16[64,960]{1,0:T(8,128)(2,1)S(1)} %fusion.160), channel_id=6, replica_groups=mesh['q'=4,'y'=2,'x'=2,'c'=2] {'y','x','c'}, dimensions={0}, use_global_device_ids=true | all-gather | bytes 1105920 | tf_op jit(solution)/shard_map/all_gather | solution.py:142
  378.7 3.2 collective-permute-done.21
  391.1 3.8 convolution_convert_fusion.9
  415.5 3.6 all-to-all-start.5
  419.1 7.3 %reduce-scatter.2.cloned.1.call-done = bf16[1,480,640]{2,1,0:T(8,128)(2,1)} async-done(((bf16[4,480,640]{2,1,0:T(8,128)(2,1)}), bf16[1,480,640]{2,1,0:T(8,128)(2,1)}) %reduce-scatter.2.cloned.1.call-update) | async-done | bytes 614416 | tf_op jit(solution)/shard_map/reduce_scatter | solution.py:377
  427.0 3.1 reshape.683
  433.0 4.8 convert_element_type.335
  437.9 2.9 pad_maximum_fusion.1
  443.3 4.3 all-to-all-done.5
  447.6 3.3 dynamic-slice_bitcast_fusion
  451.4 4.0 all-to-all-start.6
  464.4 4.6 fusion.10
  469.0 15.3 %collective-permute-done.26 = bf16[2432,128]{1,0:T(8,128)(2,1)S(1)} collective-permute-done((bf16[2432,128]{1,0:T(8,128)(2,1)}, bf16[2432,128]{1,0:T(8,128)(2,1)S(1)}, u32[]{:S(2)}, u32[]{:S(2)}) %collective-permute-start.26) | collective-permute-done | bytes 622624 | tf_op jit(solution)/shard_map/ppermute | solution.py:73
  484.3 13.5 %collective-permute-done.25 = bf16[2432,128]{1,0:T(8,128)(2,1)} collective-permute-done((bf16[2432,128]{1,0:T(8,128)(2,1)S(1)}, bf16[2432,128]{1,0:T(8,128)(2,1)}, u32[]{:S(2)}, u32[]{:S(2)}) %collective-permute-start.25) | collective-permute-done | bytes 622624 | tf_op jit(solution)/shard_map/ppermute | solution.py:73
  500.6 2.8 collective-permute-start.29
  505.1 5.6 all-to-all-start.7
  510.6 7.5 %multiply_reduce_fusion = (f32[]{:T(128)}, f32[1000,960]{1,0:T(8,128)}) fusion(bf16[512,960]{1,0:T(8,128)(2,1)S(1)} %bitcast.227, s32[512]{0:T(512)S(1)} %sub.249, f32[1000,960]{1,0:T(8,128)} %fusion.10, f32[1000,1024]{1,0:T(8,128)} %convolution_add_fusion), kind=kOutput, calls=%fused_computation.17 | convolution fusion | flops 987392000 | bytes 12505092 | tf_op jit(solution)/shard_map/dot_general | solution.py:51
  527.3 4.0 collective-permute-done.32
  531.3 3.3 collective-permute-done.31
  534.9 3.6 collective-permute-start.33
  543.0 4.0 all-to-all-start.8
  547.0 5.3 copy.270
  552.3 5.3 copy.269
  557.6 5.2 copy.268
  564.2 11.0 %add_multiply_fusion = (f32[1000,960]{1,0:T(8,128)}, f32[1000,960]{1,0:T(8,128)}, f32[1000,960]{1,0:T(8,128)}) fusion(f32[1000,960]{1,0:T(8,128)} %copy.270, f32[1000,960]{1,0:T(8,128)} %get-tuple-element.238, f32[]{:T(128)S(6)} %div.148, f32[1000,960]{1,0:T(8,128)} %copy.269, f32[1000,960]{1,0:T(8,128)} %copy.268), kind=kLoop, calls=%fused_computation.15 | loop fusion | flops 14400000 | bytes 26880004 | tf_op jit(solution)/shard_map/mul | solution.py:106
  575.2 5.2 copy.271
  580.4 5.2 copy.272
  585.5 5.3 copy.273
  591.5 3.7 add_multiply_fusion.1
  (455 shorter events, 179.6 us)
Async XLA Ops:
  8.5 15.8 %copy-start.87 = (s32[64]{0:T(128)S(1)}, s32[64]{0:T(128)}, u32[]{:S(2)}) copy-start(s32[64]{0:T(128)} %param.17) | copy-start | bytes 772
  8.5 5.8 collective-permute-start
  18.8 17.0 %collective-permute-start.1 = (bf16[2432,128]{1,0:T(8,128)(2,1)S(1)}, bf16[2432,128]{1,0:T(8,128)(2,1)S(1)}, u32[]{:S(2)}, u32[]{:S(2)}) collective-permute-start(bf16[2432,128]{1,0:T(8,128)(2,1)S(1)} %bitcast.218), channel_id=1, source_target_pairs={{0,16},{1,17},{2,18},{3,19},{4,20},{5,21},{6,22},{7,23}} | collective-permute-start | bytes 1867784 | tf_op jit(solution)/shard_map/ppermute | solution.py:200
  25.0 15.0 %all-to-all-start = ((s32[32,1,96]{2,1,0:T(1,128)}), s32[32,1,96]{2,1,0:T(1,128)S(1)}, u32[]{:S(2)}, u32[]{:S(2)}) async-start(s32[32,1,96]{2,1,0:T(1,128)} %bitcast), calls=%async_computation | async-start | bytes 32768 | tf_op jit(solution)/shard_map/all_to_all | solution.py:185
  36.7 16.8 %collective-permute-start.2 = (bf16[2432,128]{1,0:T(8,128)(2,1)}, bf16[2432,128]{1,0:T(8,128)(2,1)S(1)}, u32[]{:S(2)}, u32[]{:S(2)}) collective-permute-start(bf16[2432,128]{1,0:T(8,128)(2,1)} %broadcast_select_fusion), channel_id=1, source_target_pairs={{0,8},{16,24},{1,9},{17,25},{2,10},{18,26},{3,11},{19,27},{4,12},{... | collective-permute-start | bytes 1867784 | tf_op jit(solution)/shard_map/ppermute | solution.py:202
  40.0 14.4 %all-to-all-start.1 = ((bf16[8,60,640]{2,1,0:T(8,128)(2,1)}), bf16[8,60,640]{2,1,0:T(8,128)(2,1)S(1)}, u32[]{:S(2)}, u32[]{:S(2)}) async-start(bf16[8,60,640]{2,1,0:T(8,128)(2,1)} %reshape.757), calls=%async_computation.1 | async-start | bytes 1310720 | tf_op jit(solution)/shard_map/all_to_all | solution.py:198
  44.3 71.0 %all-gather.8.cloned.1.call-start = ((), (), s32[]{:S(2)}) async-start(), calls=%async_computation.11 | async-start | bytes 5603328 | tf_op jit(solution)/shard_map/all_gather | solution.py:206
  54.4 7.8 %copy-start.67 = (s32[64]{0:T(128)S(1)}, s32[64]{0:T(128)}, u32[]{:S(2)}) copy-start(s32[64]{0:T(128)} %param.16) | copy-start | bytes 772
  54.4 7.9 %copy-start.49 = (f32[512,64]{1,0:T(8,128)S(1)}, f32[512,64]{1,0:T(8,128)}, u32[]{:S(2)}) copy-start(f32[512,64]{1,0:T(8,128)} %constant.372) | copy-start | bytes 393220
  54.5 8.5 %copy-start.48 = (f32[512,64]{1,0:T(8,128)S(1)}, f32[512,64]{1,0:T(8,128)}, u32[]{:S(2)}) copy-start(f32[512,64]{1,0:T(8,128)} %constant.371) | copy-start | bytes 393220
  54.5 73.8 %all-to-all-start.2 = ((bf16[32,32,960]{2,1,0:T(8,128)(2,1)}), bf16[32,32,960]{2,1,0:T(8,128)(2,1)}, u32[]{:S(2)}, u32[]{:S(2)}) async-start(bf16[32,32,960]{2,1,0:T(8,128)(2,1)} %bitcast.2), calls=%async_computation.2 | async-start | bytes 4194304 | tf_op jit(solution)/shard_map/all_to_all | solution.py:205
  61.7 121.5 %all-gather.10.cloned.1.call-start = ((), (), s32[]{:S(2)}) async-start(), calls=%async_computation.12 | async-start | bytes 3072000 | tf_op jit(solution)/shard_map/all_gather | solution.py:213
  63.0 79.3 %copy-start.45 = (f32[64,64]{1,0:T(8,128)}, f32[64,64]{1,0:T(8,128)S(1)}, u32[]{:S(2)}) copy-start(f32[64,64]{1,0:T(8,128)S(1)} %gather_fusion.1) | copy-start | bytes 49156
  131.3 29.3 %copy-start.3 = (bf16[512,960]{0,1:T(8,128)(2,1)}, bf16[512,960]{0,1:T(8,128)(2,1)S(1)}, u32[]{:S(2)}) copy-start(bf16[512,960]{0,1:T(8,128)(2,1)S(1)} %get-tuple-element.221) | copy-start | bytes 2949124
  132.1 294.2 %reduce-scatter.2.cloned.1.call-start = ((), (), s32[]{:S(2)}) async-start(), calls=%async_computation.10 | async-start | bytes 3072000 | tf_op jit(solution)/shard_map/reduce_scatter | solution.py:377
  148.1 7.5 %copy-start.39 = (bf16[5,3,64,64]{3,2,1,0:T(8,128)(2,1)}, bf16[5,3,64,64]{3,2,1,0:T(8,128)(2,1)S(1)}, u32[]{:S(2)}) copy-start(bf16[5,3,64,64]{3,2,1,0:T(8,128)(2,1)S(1)} %copy.242) | copy-start | bytes 368644
  152.0 7.3 %copy-start.31 = (bf16[512,320]{0,1:T(8,128)(2,1)}, bf16[512,320]{0,1:T(8,128)(2,1)S(1)}, u32[]{:S(2)}) copy-start(bf16[512,320]{0,1:T(8,128)(2,1)S(1)} %fusion.76) | copy-start | bytes 983044
  161.6 24.1 %copy-start.81 = (f32[64]{0:T(128)}, f32[64]{0:T(128)S(1)}, u32[]{:S(2)}) copy-start(f32[64]{0:T(128)S(1)} %add_rsqrt_fusion.2) | copy-start | bytes 772
  189.9 2.8 collective-permute-start.3
  195.4 27.2 %copy-start = (s32[32]{0:T(128)S(1)}, s32[32]{0:T(128)}, u32[]{:S(2)}) copy-start(s32[32]{0:T(128)} %constant.346.clone) | copy-start | bytes 388
  196.2 5.8 collective-permute-start.6
  198.3 7.3 %collective-permute-start.5 = (bf16[64,1024]{1,0:T(8,128)(2,1)}, bf16[64,1024]{1,0:T(8,128)(2,1)S(1)}, u32[]{:S(2)}, u32[]{:S(2)}) collective-permute-start(bf16[64,1024]{1,0:T(8,128)(2,1)} %get-tuple-element.194), channel_id=1, source_target_pairs={{0,4},{2,6},{4,0},{6,2},{1,5},{3,7},{5,1},{7,3},{8,12},{10,14},{12... | collective-permute-start | bytes 393224 | tf_op jit(solution)/shard_map/ppermute | solution.py:73
  198.5 7.7 %collective-permute-start.4 = (bf16[64,1024]{1,0:T(8,128)(2,1)}, bf16[64,1024]{1,0:T(8,128)(2,1)}, u32[]{:S(2)}, u32[]{:S(2)}) collective-permute-start(bf16[64,1024]{1,0:T(8,128)(2,1)} %get-tuple-element.192), channel_id=1, source_target_pairs={{0,2},{2,0},{4,6},{6,4},{1,3},{3,1},{5,7},{7,5},{8,10},{10,8},{12,... | collective-permute-start | bytes 393224 | tf_op jit(solution)/shard_map/ppermute | solution.py:73
  207.6 31.3 %copy-start.78 = (f32[64]{0:T(128)}, f32[64]{0:T(128)S(1)}, u32[]{:S(2)}) copy-start(f32[64]{0:T(128)S(1)} %add_rsqrt_fusion.1) | copy-start | bytes 772
  221.4 10.4 %collective-permute-start.7 = (bf16[4,64,1024]{2,1,0:T(8,128)(2,1)}, bf16[4,64,1024]{2,1,0:T(8,128)(2,1)}, u32[]{:S(2)}, u32[]{:S(2)}) collective-permute-start(bf16[4,64,1024]{2,1,0:T(8,128)(2,1)} %bitcast.32), channel_id=1, source_target_pairs={{0,2},{2,0},{1,3},{3,1},{4,6},{6,4},{5,7},{7,5},{8,10},{10,8},{9,1... | collective-permute-start | bytes 1572872 | tf_op jit(solution)/shard_map/ppermute | solution.py:73
  222.6 12.2 %collective-permute-start.8 = (bf16[4,64,1024]{2,1,0:T(8,128)(2,1)}, bf16[4,64,1024]{2,1,0:T(8,128)(2,1)}, u32[]{:S(2)}, u32[]{:S(2)}) collective-permute-start(bf16[4,64,1024]{2,1,0:T(8,128)(2,1)} %bitcast.32), channel_id=1, source_target_pairs={{0,4},{4,0},{1,5},{5,1},{2,6},{6,2},{3,7},{7,3},{8,12},{12,8},{9,1... | collective-permute-start | bytes 1572872 | tf_op jit(solution)/shard_map/ppermute | solution.py:73
  232.8 7.9 %collective-permute-start.9 = (bf16[2,64,1024]{2,1,0:T(8,128)(2,1)S(1)}, bf16[2,64,1024]{2,1,0:T(8,128)(2,1)S(1)}, u32[]{:S(2)}, u32[]{:S(2)}) collective-permute-start(bf16[2,64,1024]{2,1,0:T(8,128)(2,1)S(1)} %slice.361), channel_id=1, source_target_pairs={{0,4},{4,0},{1,5},{5,1},{2,6},{6,2},{3,7},{7,3},{8,12},{12,8},{9,1... | collective-permute-start | bytes 786440 | tf_op jit(solution)/shard_map/ppermute | solution.py:73
  234.8 13.1 %copy-start.86 = (s32[32]{0:T(128)S(1)}, s32[32]{0:T(128)}, u32[]{:S(2)}) copy-start(s32[32]{0:T(128)} %constant.345.clone) | copy-start | bytes 388
  235.8 5.7 collective-permute-start.10
  242.2 14.4 %collective-permute-start.11 = (bf16[1024,1024]{1,0:T(8,128)(2,1)}, bf16[1024,1024]{1,0:T(8,128)(2,1)}, u32[]{:S(2)}, u32[]{:S(2)}) collective-permute-start(bf16[1024,1024]{1,0:T(8,128)(2,1)} %bitcast.33), channel_id=1, source_target_pairs={{0,1},{1,0},{2,3},{3,2},{4,5},{5,4},{6,7},{7,6},{8,9},{9,8},{10,11... | collective-permute-start | bytes 6291464 | tf_op jit(solution)/shard_map/ppermute | solution.py:73
  302.8 4.7 collective-permute-start.12
  307.5 9.5 %copy-start.16 = (f32[1024,1000]{0,1:T(8,128)S(1)}, f32[1024,1000]{0,1:T(8,128)}, u32[]{:S(2)}) copy-start(f32[1024,1000]{0,1:T(8,128)} %copy-done.15) | copy-start | bytes 12288004
  314.3 14.1 %collective-permute-start.15 = (bf16[4,64,1024]{2,1,0:T(8,128)(2,1)S(1)}, bf16[4,64,1024]{2,1,0:T(8,128)(2,1)S(1)}, u32[]{:S(2)}, u32[]{:S(2)}) collective-permute-start(bf16[4,64,1024]{2,1,0:T(8,128)(2,1)S(1)} %bitcast.263), channel_id=1, source_target_pairs={{0,6},{2,4},{4,2},{6,0},{1,7},{3,5},{5,3},{7,1},{8,14},{10,12},{12... | collective-permute-start | bytes 1572872 | tf_op jit(solution)/shard_map/ppermute | solution.py:73
  314.7 24.5 %collective-permute-start.14 = (bf16[4,64,1024]{2,1,0:T(8,128)(2,1)S(1)}, bf16[4,64,1024]{2,1,0:T(8,128)(2,1)S(1)}, u32[]{:S(2)}, u32[]{:S(2)}) collective-permute-start(bf16[4,64,1024]{2,1,0:T(8,128)(2,1)S(1)} %bitcast.262), channel_id=1, source_target_pairs={{0,4},{2,6},{4,0},{6,2},{1,5},{3,7},{5,1},{7,3},{8,12},{10,14},{12... | collective-permute-start | bytes 1572872 | tf_op jit(solution)/shard_map/ppermute | solution.py:73
  315.8 23.5 %collective-permute-start.13 = (bf16[4,64,1024]{2,1,0:T(8,128)(2,1)S(1)}, bf16[4,64,1024]{2,1,0:T(8,128)(2,1)S(1)}, u32[]{:S(2)}, u32[]{:S(2)}) collective-permute-start(bf16[4,64,1024]{2,1,0:T(8,128)(2,1)S(1)} %bitcast.261), channel_id=1, source_target_pairs={{0,2},{2,0},{4,6},{6,4},{1,3},{3,1},{5,7},{7,5},{8,10},{10,8},{12,... | collective-permute-start | bytes 1572872 | tf_op jit(solution)/shard_map/ppermute | solution.py:73
  339.7 10.0 %collective-permute-start.18 = (bf16[64,1024]{1,0:T(8,128)(2,1)S(1)}, bf16[64,1024]{1,0:T(8,128)(2,1)S(1)}, u32[]{:S(2)}, u32[]{:S(2)}) collective-permute-start(bf16[64,1024]{1,0:T(8,128)(2,1)S(1)} %get-tuple-element.190), channel_id=1, source_target_pairs={{0,24},{8,16},{16,8},{24,0},{1,25},{9,17},{17,9},{25,1},{2,26},{10... | collective-permute-start | bytes 393224 | tf_op jit(solution)/shard_map/ppermute | solution.py:73
  339.8 12.1 %collective-permute-start.17 = (bf16[64,1024]{1,0:T(8,128)(2,1)S(1)}, bf16[64,1024]{1,0:T(8,128)(2,1)S(1)}, u32[]{:S(2)}, u32[]{:S(2)}) collective-permute-start(bf16[64,1024]{1,0:T(8,128)(2,1)S(1)} %get-tuple-element.191), channel_id=1, source_target_pairs={{0,16},{8,24},{16,0},{24,8},{1,17},{9,25},{17,1},{25,9},{2,18},{10... | collective-permute-start | bytes 393224 | tf_op jit(solution)/shard_map/ppermute | solution.py:73
  341.3 10.8 %copy-start.79 = (f32[64]{0:T(128)S(1)}, f32[64]{0:T(128)}, u32[]{:S(2)}) copy-start(f32[64]{0:T(128)} %copy-done.78) | copy-start | bytes 772
  341.3 10.7 %collective-permute-start.16 = (bf16[64,1024]{1,0:T(8,128)(2,1)S(1)}, bf16[64,1024]{1,0:T(8,128)(2,1)S(1)}, u32[]{:S(2)}, u32[]{:S(2)}) collective-permute-start(bf16[64,1024]{1,0:T(8,128)(2,1)S(1)} %get-tuple-element.189), channel_id=1, source_target_pairs={{0,8},{8,0},{16,24},{24,16},{1,9},{9,1},{17,25},{25,17},{2,10},{10... | collective-permute-start | bytes 393224 | tf_op jit(solution)/shard_map/ppermute | solution.py:73
  349.7 16.5 %copy-start.27 = (f32[512,640]{1,0:T(8,128)S(1)}, f32[512,640]{1,0:T(8,128)}, u32[]{:S(2)}) copy-start(f32[512,640]{1,0:T(8,128)} %copy-done.26) | copy-start | bytes 3932164
  349.7 16.5 %copy-start.43 = (bf16[320,640]{1,0:T(8,128)(2,1)S(1)}, bf16[320,640]{1,0:T(8,128)(2,1)}, u32[]{:S(2)}) copy-start(bf16[320,640]{1,0:T(8,128)(2,1)} %copy-done.42) | copy-start | bytes 1228804
  349.7 16.5 %copy-start.60 = (bf16[160,320]{1,0:T(8,128)(2,1)S(1)}, bf16[160,320]{1,0:T(8,128)(2,1)}, u32[]{:S(2)}) copy-start(bf16[160,320]{1,0:T(8,128)(2,1)} %copy-done.59) | copy-start | bytes 307204
  349.7 16.5 %copy-start.62 = (bf16[160,320]{1,0:T(8,128)(2,1)S(1)}, bf16[160,320]{1,0:T(8,128)(2,1)}, u32[]{:S(2)}) copy-start(bf16[160,320]{1,0:T(8,128)(2,1)} %copy-done.61) | copy-start | bytes 307204
  367.9 2.9 collective-permute-start.19
  372.6 6.1 %collective-permute-start.22 = (bf16[64,1024]{1,0:T(8,128)(2,1)S(1)}, bf16[64,1024]{1,0:T(8,128)(2,1)}, u32[]{:S(2)}, u32[]{:S(2)}) collective-permute-start(bf16[64,1024]{1,0:T(8,128)(2,1)S(1)} %get-tuple-element.187), channel_id=1, source_target_pairs={{0,6},{2,4},{4,2},{6,0},{1,7},{3,5},{5,3},{7,1},{8,14},{10,12},{12... | collective-permute-start | bytes 393224 | tf_op jit(solution)/shard_map/ppermute | solution.py:73
  373.8 8.0 %collective-permute-start.21 = (bf16[64,1024]{1,0:T(8,128)(2,1)S(1)}, bf16[64,1024]{1,0:T(8,128)(2,1)}, u32[]{:S(2)}, u32[]{:S(2)}) collective-permute-start(bf16[64,1024]{1,0:T(8,128)(2,1)S(1)} %get-tuple-element.188), channel_id=1, source_target_pairs={{0,4},{2,6},{4,0},{6,2},{1,5},{3,7},{5,1},{7,3},{8,12},{10,14},{12... | collective-permute-start | bytes 393224 | tf_op jit(solution)/shard_map/ppermute | solution.py:73
  374.2 7.7 %collective-permute-start.20 = (bf16[64,1024]{1,0:T(8,128)(2,1)S(1)}, bf16[64,1024]{1,0:T(8,128)(2,1)}, u32[]{:S(2)}, u32[]{:S(2)}) collective-permute-start(bf16[64,1024]{1,0:T(8,128)(2,1)S(1)} %get-tuple-element.186), channel_id=1, source_target_pairs={{0,2},{2,0},{4,6},{6,4},{1,3},{3,1},{5,7},{7,5},{8,10},{10,8},{12,... | collective-permute-start | bytes 393224 | tf_op jit(solution)/shard_map/ppermute | solution.py:73
  415.5 10.9 %copy-start.23 = (bf16[64,5,3,64]{0,3,2,1:T(8,128)(2,1)S(1)}, bf16[64,5,3,64]{0,3,2,1:T(8,128)(2,1)}, u32[]{:S(2)}) copy-start(bf16[64,5,3,64]{0,3,2,1:T(8,128)(2,1)} %copy-done.22) | copy-start | bytes 368644
  415.5 32.2 %all-to-all-start.5 = ((bf16[32,16,960]{2,1,0:T(8,128)(2,1)}), bf16[32,16,960]{2,1,0:T(8,128)(2,1)}, u32[]{:S(2)}, u32[]{:S(2)}) async-start(bf16[32,16,960]{2,1,0:T(8,128)(2,1)} %bitcast.81), calls=%async_computation.6 | async-start | bytes 2097152 | tf_op jit(solution)/shard_map/all_to_all | solution.py:380
  450.9 5.0 collective-permute-start.23
  451.4 48.4 %all-to-all-start.6 = ((bf16[32,16,960]{2,1,0:T(8,128)(2,1)}), bf16[32,16,960]{2,1,0:T(8,128)(2,1)S(1)}, u32[]{:S(2)}, u32[]{:S(2)}) async-start(bf16[32,16,960]{2,1,0:T(8,128)(2,1)} %bitcast.82), calls=%async_computation.7 | async-start | bytes 2097152 | tf_op jit(solution)/shard_map/all_to_all | solution.py:380
  461.5 22.8 %collective-permute-start.26 = (bf16[2432,128]{1,0:T(8,128)(2,1)}, bf16[2432,128]{1,0:T(8,128)(2,1)S(1)}, u32[]{:S(2)}, u32[]{:S(2)}) collective-permute-start(bf16[2432,128]{1,0:T(8,128)(2,1)} %get-tuple-element.160), channel_id=1, source_target_pairs={{0,6},{2,4},{4,2},{6,0},{1,7},{3,5},{5,3},{7,1},{8,14},{10,12},{12... | collective-permute-start | bytes 1867784 | tf_op jit(solution)/shard_map/ppermute | solution.py:73
  463.6 34.3 %collective-permute-start.25 = (bf16[2432,128]{1,0:T(8,128)(2,1)S(1)}, bf16[2432,128]{1,0:T(8,128)(2,1)}, u32[]{:S(2)}, u32[]{:S(2)}) collective-permute-start(bf16[2432,128]{1,0:T(8,128)(2,1)S(1)} %get-tuple-element.161), channel_id=1, source_target_pairs={{0,4},{2,6},{4,0},{6,2},{1,5},{3,7},{5,1},{7,3},{8,12},{10,14},{12... | collective-permute-start | bytes 1867784 | tf_op jit(solution)/shard_map/ppermute | solution.py:73
  463.9 34.0 %collective-permute-start.24 = (bf16[2432,128]{1,0:T(8,128)(2,1)S(1)}, bf16[2432,128]{1,0:T(8,128)(2,1)}, u32[]{:S(2)}, u32[]{:S(2)}) collective-permute-start(bf16[2432,128]{1,0:T(8,128)(2,1)S(1)} %get-tuple-element.159), channel_id=1, source_target_pairs={{0,2},{2,0},{4,6},{6,4},{1,3},{3,1},{5,7},{7,5},{8,10},{10,8},{12,... | collective-permute-start | bytes 1867784 | tf_op jit(solution)/shard_map/ppermute | solution.py:73
  469.0 35.1 %copy-start.19 = (bf16[1,480,640]{2,1,0:T(8,128)(2,1)S(1)}, bf16[1,480,640]{2,1,0:T(8,128)(2,1)}, u32[]{:S(2)}) copy-start(bf16[1,480,640]{2,1,0:T(8,128)(2,1)} %reduce-scatter.2.cloned.1.call-done) | copy-start | bytes 1843204
  500.6 17.6 %collective-permute-start.29 = (bf16[608,128]{1,0:T(8,128)(2,1)}, bf16[608,128]{1,0:T(8,128)(2,1)S(1)}, u32[]{:S(2)}, u32[]{:S(2)}) collective-permute-start(bf16[608,128]{1,0:T(8,128)(2,1)} %get-tuple-element.170), channel_id=1, source_target_pairs={{0,24},{8,16},{16,8},{24,0},{1,25},{9,17},{17,9},{25,1},{2,26},{10... | collective-permute-start | bytes 466952 | tf_op jit(solution)/shard_map/ppermute | solution.py:73
  503.4 14.8 %collective-permute-start.28 = (bf16[608,128]{1,0:T(8,128)(2,1)}, bf16[608,128]{1,0:T(8,128)(2,1)S(1)}, u32[]{:S(2)}, u32[]{:S(2)}) collective-permute-start(bf16[608,128]{1,0:T(8,128)(2,1)} %get-tuple-element.171), channel_id=1, source_target_pairs={{0,16},{8,24},{16,0},{24,8},{1,17},{9,25},{17,1},{25,9},{2,18},{10... | collective-permute-start | bytes 466952 | tf_op jit(solution)/shard_map/ppermute | solution.py:73
  503.4 14.8 %collective-permute-start.27 = (bf16[608,128]{1,0:T(8,128)(2,1)S(1)}, bf16[608,128]{1,0:T(8,128)(2,1)S(1)}, u32[]{:S(2)}, u32[]{:S(2)}) collective-permute-start(bf16[608,128]{1,0:T(8,128)(2,1)S(1)} %get-tuple-element.169), channel_id=1, source_target_pairs={{0,8},{8,0},{16,24},{24,16},{1,9},{9,1},{17,25},{25,17},{2,10},{10... | collective-permute-start | bytes 466952 | tf_op jit(solution)/shard_map/ppermute | solution.py:73
  505.1 18.1 %all-to-all-start.7 = ((bf16[8,60,640]{2,1,0:T(8,128)(2,1)}), bf16[8,60,640]{2,1,0:T(8,128)(2,1)}, u32[]{:S(2)}, u32[]{:S(2)}) async-start(bf16[8,60,640]{2,1,0:T(8,128)(2,1)} %reshape.690), calls=%async_computation.8 | async-start | bytes 1310720 | tf_op jit(solution)/shard_map/all_to_all | solution.py:399
  518.3 9.0 %collective-permute-start.30 = (bf16[608,128]{1,0:T(8,128)(2,1)S(1)}, bf16[608,128]{1,0:T(8,128)(2,1)S(1)}, u32[]{:S(2)}, u32[]{:S(2)}) collective-permute-start(bf16[608,128]{1,0:T(8,128)(2,1)S(1)} %fusion.93), channel_id=1, source_target_pairs={{24,0},{25,1},{26,2},{27,3},{28,4},{29,5},{30,6},{31,7}} | collective-permute-start | bytes 466952 | tf_op jit(solution)/shard_map/ppermute | solution.py:405
  519.6 11.7 %collective-permute-start.32 = (bf16[608,128]{1,0:T(8,128)(2,1)S(1)}, bf16[608,128]{1,0:T(8,128)(2,1)S(1)}, u32[]{:S(2)}, u32[]{:S(2)}) collective-permute-start(bf16[608,128]{1,0:T(8,128)(2,1)S(1)} %fusion.93), channel_id=1, source_target_pairs={{16,0},{17,1},{18,2},{19,3},{20,4},{21,5},{22,6},{23,7}} | collective-permute-start | bytes 466952 | tf_op jit(solution)/shard_map/ppermute | solution.py:405
  520.9 13.7 %collective-permute-start.31 = (bf16[608,128]{1,0:T(8,128)(2,1)S(1)}, bf16[608,128]{1,0:T(8,128)(2,1)S(1)}, u32[]{:S(2)}, u32[]{:S(2)}) collective-permute-start(bf16[608,128]{1,0:T(8,128)(2,1)S(1)} %fusion.93), channel_id=1, source_target_pairs={{8,0},{9,1},{10,2},{11,3},{12,4},{13,5},{14,6},{15,7}} | collective-permute-start | bytes 466952 | tf_op jit(solution)/shard_map/ppermute | solution.py:405
  534.9 4.4 collective-permute-start.33
  543.0 19.8 %all-to-all-start.8 = ((f32[32,1,2]{2,1,0:T(1,128)}), f32[32,1,2]{2,1,0:T(1,128)S(1)}, u32[]{:S(2)}, u32[]{:S(2)}) async-start(f32[32,1,2]{2,1,0:T(1,128)} %broadcast_in_dim.168), calls=%async_computation.9 | async-start | bytes 32768 | tf_op jit(solution)/shard_map/all_to_all | solution.py:432
  (69 other events, 171.6 us)
Sparse Core Ops, SparseCore 0:
  54.5 60.7 all-gather.7
  132.2 50.9 all-gather.9
  377.8 48.5 reduce-scatter.1

commit v5 on v4

--- a/solution.py
+++ b/solution.py
@@ -39,8 +39,9 @@
 PLANE = ("y", "x", "c")
 ALL = ("q", "y", "x", "c")
 SHARE = FF // 8
-LINES = D * (QKV + D + 3 * FF) // 32 // 128
-EXTRA = 32
+TOP = D // 5
+KV = QKV - D
+ROOM = 32
 WIDE = 1024
 
 bf16 = jnp.bfloat16
@@ -182,9 +183,6 @@
     found = dot(halves, spot).astype(jnp.int32)
     requests = (found[0] * 256 + found[1] - 1).reshape(devices, capacity)
     ask = jnp.concatenate([requests, jnp.broadcast_to(targets[None], (devices, loss_dev))], axis=1)
-    asked = lax.all_to_all(ask, ALL, split_axis=0, concat_axis=0, tiled=True)
-    row_hot = hot(asked[:, :capacity].reshape(-1) - me * vocab_dev, vocab_dev)
-    answer = dot(row_hot, table_low).astype(bf16).reshape(devices, capacity, D)
 
     flat_low = flat_master.astype(bf16)
     ahead = lax.ppermute(flat_low[:GAINS], ALL, [(i + 1, i) for i in range(devices - 1)])
@@ -196,7 +194,14 @@
     if aligned:
         sent = chunk.reshape(60, 2, 8, UNIT).transpose(2, 0, 1, 3).reshape(8, 60, 2 * UNIT)
         got = lax.all_to_all(sent, PLANE, split_axis=0, concat_axis=0, tiled=True)
-        first = jnp.concatenate([chunk, flat_low[:GAINS], jnp.zeros((EXTRA * 128 - GAINS,), bf16)]).reshape(LINES + EXTRA, 128)
+        both = chunk.reshape(TOP, QKV)
+        both = jnp.concatenate([both[:, :D], both[:, D:].reshape(SHARE - TOP, D)])
+        first = jnp.where(p_index < 5, both, chunk.reshape(SHARE, D))
+        first = jnp.concatenate([first, flat_low[:GAINS].reshape(3, D), jnp.zeros((5, D), bf16)])
+        first, ask = lax.optimization_barrier((first, ask))
+        asked = lax.all_to_all(ask, ALL, split_axis=0, concat_axis=0, tiled=True)
+        row_hot = hot(asked[:, :capacity].reshape(-1) - me * vocab_dev, vocab_dev)
+        answer = dot(row_hot, table_low).astype(bf16).reshape(devices, capacity, D)
         jumped = lax.ppermute(first, "q", [(0, 2)])
         first = jnp.where(q_index == 2, jumped, first)
         stepped = lax.ppermute(first, "q", [(0, 1), (2, 3)])
@@ -204,16 +209,18 @@
         answer, first, got = lax.optimization_barrier((answer, first, got))
         returned = lax.all_to_all(answer, ALL, split_axis=0, concat_axis=0, tiled=True).reshape(slots, D)
         level = lax.all_gather(first, PLANE)
-        gains = level[0, LINES:].reshape(-1)[:GAINS].astype(f32).reshape(3, D)
-        w_qkv = level[:5, :LINES].reshape(D, QKV)
-        w_out = level[5:, :LINES].reshape(D, D)
         mixed = jnp.where(q_index == 3, down_pack(chunk.reshape(SHARE, D)), got.reshape(480, 2 * UNIT))
-        mixed, w_qkv, w_out = lax.optimization_barrier((mixed, w_qkv, w_out))
-        returned, w_qkv, w_out = lax.optimization_barrier((returned, w_qkv, w_out))
+        mixed, level = lax.optimization_barrier((mixed, level))
+        gains = level[0, SHARE : SHARE + 3].astype(f32)
+        w_q = level[:5, :TOP].reshape(D, D)
+        w_kv = level[:5, TOP:SHARE].reshape(D, KV)
+        w_out = level[5:, :SHARE].reshape(D, D)
+        returned, w_q, w_kv, w_out = lax.optimization_barrier((returned, w_q, w_kv, w_out))
         column = lax.all_gather(mixed, "q")
-        w_gu = column[1:3].reshape(D, 2 * SHARE)
-        w_down = down_unpack(column[3])
     else:
+        asked = lax.all_to_all(ask, ALL, split_axis=0, concat_axis=0, tiled=True)
+        row_hot = hot(asked[:, :capacity].reshape(-1) - me * vocab_dev, vocab_dev)
+        answer = dot(row_hot, table_low).astype(bf16).reshape(devices, capacity, D)
         returned = lax.all_to_all(answer, ALL, split_axis=0, concat_axis=0, tiled=True).reshape(slots, D)
         extra = jnp.zeros((16 * UNIT,), bf16).at[:GAINS].set(flat_low[:GAINS])
         full = lax.all_gather(jnp.concatenate([chunk, extra]).reshape(units + 16, UNIT), ALL)
@@ -221,12 +228,11 @@
         full = full[:, :units].reshape(ALL_UNITS, UNIT)
         edge = np.cumsum([QKV_UNITS, OUT_UNITS, GU_UNITS])
         w_qkv = full[: edge[0]].reshape(D, QKV)
+        w_q, w_kv = w_qkv[:, :D], w_qkv[:, D:]
         w_out = full[edge[0] : edge[1]].reshape(D, D)
         both = lax.dynamic_index_in_dim(full[edge[1] : edge[2]].reshape(D, 2, 8, UNIT), p_index, 2, False)
         w_gu = both.reshape(D, 2 * SHARE)
         w_down = lax.dynamic_index_in_dim(full[edge[2] :].reshape(8, SHARE, D), p_index, 0, False)
-    w_gu = jnp.pad(w_gu, ((0, WIDE - D), (0, 0)))
-    w_down = widen(w_down)
     x_low = dot(spot, returned).astype(bf16)
     x_embed = x_low.astype(f32) * emb_mult
 
@@ -236,8 +242,7 @@
     h_attn = (x_embed * scale_of(x_embed) * gains[0]).astype(bf16)
     h_pick = dot(pick, h_attn).astype(bf16)
     x_pick = dot(pick, x_low) * emb_mult
-    query = rotate(dot(h_pick, w_qkv[:, :D]), cosine_pick, sine_pick).astype(bf16)
-    w_kv = w_qkv[:, D:]
+    query = rotate(dot(h_pick, w_q), cosine_pick, sine_pick).astype(bf16)
     key_value = dot(h_attn, w_kv)
     key = rotate(key_value[:, :UNIT], cosine, sine).astype(bf16)
     value = key_value[:, UNIT:].astype(bf16)
@@ -265,6 +270,12 @@
     attended = heads_back(mixed_heads.astype(bf16))
     x_one = x_pick + dot(attended, w_out)
 
+    if aligned:
+        column, x_one = lax.optimization_barrier((column, x_one))
+        w_gu = column[1:3].reshape(D, 2 * SHARE)
+        w_down = down_unpack(column[3])
+    w_gu = jnp.pad(w_gu, ((0, WIDE - D), (0, 0)))
+    w_down = widen(w_down)
     h_mlp = (x_one * scale_of(x_one) * gains[1]).astype(bf16)
     h_all = spread_plane(h_mlp)
     gate_up = dot(h_all, w_gu)
@@ -330,7 +341,7 @@
     for k in range(1, rows_q):
         total_hidden = total_hidden + flip(pick_block(d_low, q_index ^ k), "q", k, rows_q).astype(f32)
     total_hidden = total_hidden[:, :D]
-    head_grad = dot(d_logits[1], sides[0], 0, 0) + dot(d_logits[0], sides[1], 0, 0)
+    head_grad = (dot(d_logits[1], sides[0], 0, 0) + dot(d_logits[0], sides[1], 0, 0))[:, :D]
     head_grad, total_hidden = lax.optimization_barrier((head_grad, total_hidden))
 
     d_x_two, grad_final = norm_back(x_two, gains[2], total_hidden)
@@ -356,7 +367,7 @@
     d_q = rotate_back(heads_back(d_query), cosine_pick, sine_pick).astype(bf16)
     d_k = rotate_back(d_key.reshape(tokens, UNIT), cosine, sine)
     d_kv = jnp.concatenate([d_k, d_value.reshape(tokens, UNIT)], axis=1).astype(bf16)
-    d_h_pick = dot(d_q, w_qkv[:, :D], 1, 1)
+    d_h_pick = dot(d_q, w_q, 1, 1)
     high = d_h_pick.astype(bf16)
     rest = (d_h_pick - high.astype(f32)).astype(bf16)
     d_h_attn = dot(d_kv, w_kv, 1, 1) + dot(pick, high, 0, 0) + dot(pick, rest, 0, 0)
@@ -379,13 +390,15 @@
         share, d_q, d_kv, attended = lax.optimization_barrier((share, d_q, d_kv, attended))
     arrived = [lax.all_to_all(rows, ALL, split_axis=0, concat_axis=0, tiled=True).reshape(-1, D) for rows in sending]
     grad_out = dot(attended, d_branch, 0, 0).astype(bf16)
-    grad_qkv = jnp.concatenate([dot(h_pick, d_q, 0, 0), dot(h_attn, d_kv, 0, 0)], axis=1).astype(bf16)
+    grad_q = dot(h_pick, d_q, 0, 0).astype(bf16)
+    grad_kv = dot(h_attn, d_kv, 0, 0).astype(bf16)
 
     gain_grads = jnp.concatenate([grad_attn, grad_mlp, grad_final]).astype(bf16)
     if aligned:
-        level = jnp.concatenate([grad_qkv.reshape(5, LINES, 128), grad_out.reshape(3, LINES, 128)])
-        room = jnp.zeros((8, EXTRA * 128), bf16).at[0, :GAINS].set(gain_grads).reshape(8, EXTRA, 128)
-        level = jnp.concatenate([level, room], axis=1).reshape(4, 2, LINES + EXTRA, 128)
+        lower = jnp.concatenate([grad_q.reshape(5, TOP, D), grad_kv.reshape(5, SHARE - TOP, D)], axis=1)
+        level = jnp.concatenate([lower, grad_out.reshape(3, SHARE, D)])
+        room = jnp.zeros((8, ROOM, D), bf16).at[0, :3].set(gain_grads.reshape(3, D))
+        level = jnp.concatenate([level, room], axis=1).reshape(4, 2, SHARE + ROOM, D)
         level, arrived[0] = lax.optimization_barrier((level, arrived[0]))
         keep = lax.dynamic_index_in_dim(level, c_index, 1, False)
         give = lax.dynamic_index_in_dim(level, 1 - c_index, 1, False)
@@ -394,7 +407,7 @@
         for k in (1, 2, 3):
             piece = lax.dynamic_index_in_dim(level, yx_index ^ k, 0, False).astype(bf16)
             own = own + flip(piece, ("y", "x"), k, 4).astype(f32)
-        own = own.reshape(4, (LINES + EXTRA) // 4, 128)
+        own = own.reshape(4, (SHARE + ROOM) // 4, D)
         own, share, arrived[1] = lax.optimization_barrier((own, share, arrived[1]))
         got = lax.all_to_all(share.reshape(8, 60, 640), PLANE, split_axis=0, concat_axis=0, tiled=True)
         quarter = lax.dynamic_index_in_dim(own, q_index, 0, False)
@@ -404,15 +417,16 @@
         quarter = quarter.astype(bf16)
         quarters = [quarter] + [lax.ppermute(quarter, "q", [(k, 0)]) for k in (1, 2, 3)]
         first = jnp.concatenate(quarters)
-        gain_out = first[LINES:].reshape(-1)[:GAINS]
-        first = first[:LINES].reshape(-1)
+        gain_out = first[SHARE : SHARE + 3].reshape(-1)
+        both = jnp.concatenate([first[:TOP], first[TOP:SHARE].reshape(TOP, KV)], axis=1)
+        first = jnp.where(p_index < 5, both.reshape(-1), first[:SHARE].reshape(-1))
         by_share = got.reshape(8, 60, 2, UNIT).transpose(1, 2, 0, 3).reshape(-1)
         mine = jnp.where(q_index == 3, down_unpack(share).reshape(-1), by_share)
         mine = jnp.where(q_index == 0, first, mine)
     else:
         both = lax.dynamic_update_index_in_dim(jnp.zeros((D, 2, 8, UNIT), bf16), grad_gu.reshape(D, 2, UNIT), p_index, 2)
         downs = lax.dynamic_update_index_in_dim(jnp.zeros((8, SHARE, D), bf16), grad_down, p_index, 0)
-        full = jnp.concatenate([part.reshape(-1, UNIT) for part in (grad_qkv, grad_out, both, downs)]).reshape(devices, units, UNIT)
+        full = jnp.concatenate([part.reshape(-1, UNIT) for part in (jnp.concatenate([grad_q, grad_kv], axis=1), grad_out, both, downs)]).reshape(devices, units, UNIT)
         room = jnp.zeros((devices, 16, UNIT), bf16).at[0, :GAIN_UNITS].set(gain_grads.reshape(GAIN_UNITS, UNIT))
         full = jnp.concatenate([full, room], axis=1)
         summed = lax.psum_scatter(full, ALL, scatter_dimension=0, tiled=False)
@@ -423,7 +437,7 @@
     stream = jnp.concatenate([behind, mine, jnp.zeros((tail,), bf16)])
     layer_grad = lax.dynamic_slice(stream, (drift * me,), (shard,)).astype(f32)
 
-    table_grad = head_grad[:, :D]
+    table_grad = head_grad
     for side in range(2):
         rows = asked[:, side * part : (side + 1) * part].reshape(-1) - me * vocab_dev
         table_grad = table_grad + dot(hot(rows, vocab_dev), arrived[side], 0, 0)

time: 614 us -> 614 us (level)
  local copies, waits for them, and re-layouts: 132 us -> 87.5 us
  waiting for transfers between devices: 153 us -> 182 us
  other arithmetic: 66.2 us -> 79.6 us
    unnamed x191 -> x205, local copies, waits for them, and re-layouts: 57 us -> 18.9 us
    ppermute x27, waiting for transfers between devices: 73.1 us -> 91.4 us  [flip(): return lax.ppermute(rows, axes, [(i, i ^ bits) for i in range(size)])]
    reduce_sum x0 -> x1, other arithmetic: none -> 8.96 us  [local(): jnp.sum(table_grad * table_grad)]
    all_to_all x0 -> x1, blocking collectives: none -> 8.3 us  [local(): lax.all_to_all(sums, ALL, split_axis=0, concat_axis=0, tiled=True)]
    all_gather x1, waiting for transfers between devices: 8.68 us -> 15.6 us  [local(): column = lax.all_gather(mixed, 'q')]
  transfers between devices with their start and end apart: 44 -> 43, of which waited for: 21 -> 24; matrix products, arithmetic and copies ran while one was open for 31% -> 29% of each run, Pallas kernels for 0% -> 0%
where the time goes in v5:
time: 614 us; the launch traced here: 603 us
  waiting for transfers between devices  182 us (30%)
  matrix products  91.3 us (15%)
  local copies, waits for them, and re-layouts  87.5 us (14%)
  other arithmetic  79.6 us (13%)
  starting transfers between devices  78.9 us (13%)
  blocking collectives  63.5 us (10%)
  between operations  20.7 us (3%)
    ppermute x27, waiting for transfers between devices, flip(): return lax.ppermute(rows, axes, [(i, i ^ bits) for i in range(size)])  91.4 us
    dot_general x37, matrix products, dot(): lax.dot_general(left, right, (((left_dim,), (right_dim,)), ((), ())), pre...  75.2 us
    all_gather x1, waiting for transfers between devices, local(): level = lax.all_gather(first, PLANE)  49.5 us
    ppermute x27, starting transfers between devices, flip(): return lax.ppermute(rows, axes, [(i, i ^ bits) for i in range(size)])  30.2 us
    all_gather x2, blocking collectives, spread_plane(): return widen(lax.all_gather(rows, PLANE).reshape(-1, D))  24.9 us
    unnamed x205, local copies, waits for them, and re-layouts  18.9 us
    all_gather x1, waiting for transfers between devices, local(): column = lax.all_gather(mixed, 'q')  15.6 us
  transfers between devices with their start and end apart: 43, of which 24 were waited for; matrix products, arithmetic and copies ran while one was open for 29% of the time, Pallas kernels for 0%

profile of v5, /device:TPU:1, one launch (start us, length us, event | category | flops | bytes accessed | tf_op | source)
XLA Modules:
  0.0 602.9 jit_solution(3829471848238583419)
XLA Ops:
  17.9 5.7 collective-permute-start.1
  23.6 3.7 convert_element_type.292
  28.0 4.2 all-to-all-start
  39.0 5.6 all-to-all-start.1
  44.7 5.2 fusion.25
  50.0 3.9 copy.194
  54.8 9.4 %all-to-all-start.2 = ((bf16[32,32,960]{2,1,0:T(8,128)(2,1)}), bf16[32,32,960]{2,1,0:T(8,128)(2,1)}, u32[]{:S(2)}, u32[]{:S(2)}) async-start(bf16[32,32,960]{2,1,0:T(8,128)(2,1)} %bitcast.223), calls=%async_computation.2 | async-start | bytes 4194304 | tf_op jit(solution)/shard_map/all_to_all | solution.py:210
  70.0 49.5 %all-gather.8.cloned.1.call-done = bf16[2624,960]{1,0:T(8,128)(2,1)} async-done(((bf16[328,960]{1,0:T(8,128)(2,1)}), bf16[2624,960]{1,0:T(8,128)(2,1)}) %all-gather.8.cloned.1.call-update) | async-done | bytes 5038096 | tf_op jit(solution)/shard_map/all_gather | solution.py:211
  122.7 3.0 slice.269
  126.2 2.8 reshape.663
  129.0 3.1 fusion.24
  146.2 2.3 copy.235
  150.0 3.7 fusion.186
  153.7 3.6 convolution_convert_fusion.10
  161.2 15.6 %all-gather.10.cloned.1.call-done = bf16[1920,640]{1,0:T(8,128)(2,1)} async-done(((bf16[480,640]{1,0:T(8,128)(2,1)}), bf16[1920,640]{1,0:T(8,128)(2,1)}) %all-gather.10.cloned.1.call-update) | async-done | bytes 2457616 | tf_op jit(solution)/shard_map/all_gather | solution.py:219
  180.8 11.8 %all-gather.2 = bf16[512,960]{1,0:T(8,128)(2,1)S(1)} all-gather(bf16[64,960]{1,0:T(8,128)(2,1)S(1)} %multiply_convert_fusion.7), channel_id=4, replica_groups=mesh['q'=4,'y'=2,'x'=2,'c'=2] {'y','x','c'}, dimensions={0}, use_global_device_ids=true | all-gather | bytes 1105920 | tf_op jit(solution)/shard_map/all_gather | solution.py:143
  205.6 2.5 collective-permute-done.6
  208.2 3.3 collective-permute-done.5
  212.9 12.2 %all-gather.3 = bf16[256,1024]{1,0:T(8,128)(2,1)S(1)} all-gather(bf16[64,1024]{1,0:T(8,128)(2,1)S(1)} %pad.31), channel_id=5, replica_groups=mesh['q'=4,'y'=2,'x'=2,'c'=2] {'q'}, dimensions={0}, use_global_device_ids=true | all-gather | bytes 655360 | tf_op jit(solution)/shard_map/all_gather | solution.py:289
  226.5 7.6 %collective-permute-done.7 = bf16[4,64,1024]{2,1,0:T(8,128)(2,1)S(1)} collective-permute-done((bf16[4,64,1024]{2,1,0:T(8,128)(2,1)S(1)}, bf16[4,64,1024]{2,1,0:T(8,128)(2,1)S(1)}, u32[]{:S(2)}, u32[]{:S(2)}) %collective-permute-start.7) | collective-permute-done | bytes 524320 | tf_op jit(solution)/shard_map/ppermute | solution.py:74
  238.2 4.3 collective-permute-done.9
  243.9 6.6 %collective-permute-start.11 = (bf16[1024,1024]{1,0:T(8,128)(2,1)}, bf16[1024,1024]{1,0:T(8,128)(2,1)}, u32[]{:S(2)}, u32[]{:S(2)}) collective-permute-start(bf16[1024,1024]{1,0:T(8,128)(2,1)} %bitcast.38), channel_id=1, source_target_pairs={{0,1},{1,0},{2,3},{3,2},{4,5},{5,4},{6,7},{7,6},{8,9},{9,8},{10,11... | collective-permute-start | bytes 6291464 | tf_op jit(solution)/shard_map/ppermute | solution.py:74
  251.5 4.5 fusion.188
  259.1 3.9 fusion.187
  269.7 9.4 %all_to_all.53 = f32[32,1,256]{2,1,0:T(1,128)S(1)} all-to-all(f32[32,1,256]{2,1,0:T(1,128)} %reshape.779), channel_id=1, replica_groups=mesh['q'=4,'y'=2,'x'=2,'c'=2] {'q','y','x','c'}, dimensions={0} | all-to-all | bytes 65536 | tf_op jit(solution)/shard_map/all_to_all | solution.py:310
  285.0 8.6 %all_to_all.54 = f32[32,1,64]{2,1,0:T(1,128)S(1)} all-to-all(f32[32,1,64]{2,1,0:T(1,128)S(1)} %broadcast_in_dim.101), channel_id=1, replica_groups=mesh['q'=4,'y'=2,'x'=2,'c'=2] {'q','y','x','c'}, dimensions={0} | all-to-all | bytes 16384 | tf_op jit(solution)/shard_map/all_to_all | solution.py:320
  295.1 7.1 %convolution_convert_fusion = bf16[1024,1024]{1,0:T(8,128)(2,1)} fusion(bf16[1000,960]{0,1:T(8,128)(2,1)} %convert_element_type.292, f32[1024,1000]{0,1:T(8,128)} %copy-done.18, f32[1024]{0:T(1024)S(1)} %squeeze.114, f32[1024]{0:T(1024)S(1)} %multiply_add_fusion.2, s32[1024]{0:T(1024)} %copy-done.78), kind=kOutput, calls=%fused_computation.62 | convolution fusion | flops 2106392576 | bytes 8125440 | tf_op jit(solution)/shard_map/dot_general | solution.py:52
  303.0 5.6 fusion.160
  308.6 4.8 fusion.189
  316.3 4.3 fusion.161
  320.7 7.4 %collective-permute-done.15 = bf16[4,64,1024]{2,1,0:T(8,128)(2,1)S(1)} collective-permute-done((bf16[4,64,1024]{2,1,0:T(8,128)(2,1)S(1)}, bf16[4,64,1024]{2,1,0:T(8,128)(2,1)S(1)}, u32[]{:S(2)}, u32[]{:S(2)}) %collective-permute-start.15) | collective-permute-done | bytes 524320 | tf_op jit(solution)/shard_map/ppermute | solution.py:74
  328.1 10.4 %collective-permute-done.14 = bf16[4,64,1024]{2,1,0:T(8,128)(2,1)S(1)} collective-permute-done((bf16[4,64,1024]{2,1,0:T(8,128)(2,1)S(1)}, bf16[4,64,1024]{2,1,0:T(8,128)(2,1)S(1)}, u32[]{:S(2)}, u32[]{:S(2)}) %collective-permute-start.14) | collective-permute-done | bytes 524320 | tf_op jit(solution)/shard_map/ppermute | solution.py:74
  342.7 2.9 slice_add_fusion
  345.6 5.7 collective-permute-done.17
  352.3 13.2 %all-gather.4 = bf16[512,960]{1,0:T(8,128)(2,1)S(1)} all-gather(bf16[64,960]{1,0:T(8,128)(2,1)S(1)} %fusion.155), channel_id=6, replica_groups=mesh['q'=4,'y'=2,'x'=2,'c'=2] {'y','x','c'}, dimensions={0}, use_global_device_ids=true | all-gather | bytes 1105920 | tf_op jit(solution)/shard_map/all_gather | solution.py:143
  378.4 3.3 collective-permute-done.21
  385.6 2.2 multiply_reduce_fusion.1
  397.4 4.0 convolution_convert_fusion.9
  406.6 2.2 fusion.15
  412.5 2.3 copy.219
  416.5 2.3 copy.220
  418.8 3.3 all-to-all-start.5
  426.8 3.1 reshape.694
  432.2 6.2 %fusion.2 = bf16[8,352,960]{2,1,0:T(8,128)(2,1)} fusion(bf16[1,3,960]{2,1,0:T(4,128)(2,1)S(1)} %copy-done.71, bf16[3,320,960]{2,1,0:T(8,128)(2,1)S(1)} %bitcast.225, bf16[5,128,960]{2,1,0:T(8,128)(2,1)S(1)} %reshape.694, bf16[5,192,960]{2,1,0:T(8,128)(2,1)S(1)} %bitcast.224), kind=kLoop, calls=%fused_computation.10 | loop fusion | flops 27033600 | bytes 10327680 | tf_op jit(solution)/shard_map/concatenate | solution.py:401
  438.4 9.1 %all-to-all-done.5 = bf16[32,16,960]{2,1,0:T(8,128)(2,1)} async-done(((bf16[32,16,960]{2,1,0:T(8,128)(2,1)}), bf16[32,16,960]{2,1,0:T(8,128)(2,1)}, u32[]{:S(2)}, u32[]{:S(2)}) %all-to-all-start.5) | async-done | bytes 983072 | tf_op jit(solution)/shard_map/all_to_all | solution.py:391
  447.5 3.7 dynamic-slice_bitcast_fusion
  452.4 4.0 all-to-all-start.6
  457.7 4.0 convert_add_fusion
  461.7 2.5 copy-done.4
  464.5 2.2 collective-permute-start.26
  467.5 4.5 fusion.12
  472.0 16.7 %collective-permute-done.26 = bf16[352,960]{1,0:T(8,128)(2,1)} collective-permute-done((bf16[352,960]{1,0:T(8,128)(2,1)S(1)}, bf16[352,960]{1,0:T(8,128)(2,1)}, u32[]{:S(2)}, u32[]{:S(2)}) %collective-permute-start.26) | collective-permute-done | bytes 675872 | tf_op jit(solution)/shard_map/ppermute | solution.py:74
  488.7 15.2 %collective-permute-done.25 = bf16[352,960]{1,0:T(8,128)(2,1)} collective-permute-done((bf16[352,960]{1,0:T(8,128)(2,1)S(1)}, bf16[352,960]{1,0:T(8,128)(2,1)}, u32[]{:S(2)}, u32[]{:S(2)}) %collective-permute-start.25) | collective-permute-done | bytes 675872 | tf_op jit(solution)/shard_map/ppermute | solution.py:74
  504.1 2.5 fusion.39
  507.5 4.1 all-to-all-start.7
  515.3 4.5 fusion.13
  519.8 11.2 %collective-permute-done.28 = bf16[88,960]{1,0:T(8,128)(2,1)S(1)} collective-permute-done((bf16[88,960]{1,0:T(8,128)(2,1)S(1)}, bf16[88,960]{1,0:T(8,128)(2,1)S(1)}, u32[]{:S(2)}, u32[]{:S(2)}) %collective-permute-start.28) | collective-permute-done | bytes 168992 | tf_op jit(solution)/shard_map/ppermute | solution.py:74
  536.0 7.1 %collective-permute-done.32 = bf16[88,960]{1,0:T(8,128)(2,1)S(1)} collective-permute-done((bf16[88,960]{1,0:T(8,128)(2,1)S(1)}, bf16[88,960]{1,0:T(8,128)(2,1)S(1)}, u32[]{:S(2)}, u32[]{:S(2)}) %collective-permute-start.32) | collective-permute-done | bytes 168992 | tf_op jit(solution)/shard_map/ppermute | solution.py:418
  543.6 4.5 collective-permute-done.31
  554.5 3.8 collective-permute-start.33
  558.3 9.0 %multiply_reduce_fusion = (f32[]{:T(128)}, f32[1000,960]{0,1:T(8,128)}) fusion(f32[1000,960]{0,1:T(8,128)} %fusion.13, f32[1000,960]{0,1:T(8,128)} %slice_add_fusion, f32[1000,960]{0,1:T(8,128)} %fusion.12), kind=kLoop, calls=%fused_computation.27 | loop fusion | flops 3839999 | bytes 15360004 | tf_op jit(solution)/shard_map/reduce_sum | solution.py:444
  570.4 8.3 %all_to_all.55 = f32[32,1,2]{2,1,0:T(1,128)S(1)} all-to-all(f32[32,1,2]{2,1,0:T(1,128)S(1)} %broadcast_in_dim.168), channel_id=1, replica_groups=mesh['q'=4,'y'=2,'x'=2,'c'=2] {'q','y','x','c'}, dimensions={0} | all-to-all | bytes 512 | tf_op jit(solution)/shard_map/all_to_all | solution.py:446
  580.8 4.2 add_multiply_fusion.1
  586.1 7.8 %add_multiply_fusion = (f32[1000,960]{0,1:T(8,128)}, f32[1000,960]{0,1:T(8,128)}, f32[1000,960]{0,1:T(8,128)}) fusion(f32[1000,960]{0,1:T(8,128)S(1)} %copy-done.2, f32[1000,960]{0,1:T(8,128)S(1)} %copy-done.3, f32[]{:T(128)S(6)} %div.148, f32[1000,960]{0,1:T(8,128)} %param.23, f32[1000,960]{0,1:T(8,128)} %param.22), kind=kLoop, calls=%fused_computation.25 | loop fusion | flops 14400000 | bytes 26880004 | tf_op jit(solution)/shard_map/mul | solution.py:107
  (480 shorter events, 167.0 us)
Async XLA Ops:
  8.5 5.8 collective-permute-start
  17.9 17.6 %collective-permute-start.1 = (bf16[328,960]{1,0:T(8,128)(2,1)S(1)}, bf16[328,960]{1,0:T(8,128)(2,1)}, u32[]{:S(2)}, u32[]{:S(2)}) collective-permute-start(bf16[328,960]{1,0:T(8,128)(2,1)S(1)} %maximum_maximum_fusion), channel_id=1, source_target_pairs={{0,16},{1,17},{2,18},{3,19},{4,20},{5,21},{6,22},{7,23}} | collective-permute-start | bytes 1889288 | tf_op jit(solution)/shard_map/ppermute | solution.py:205
  28.0 11.1 %all-to-all-start = ((s32[32,1,96]{2,1,0:T(1,128)}), s32[32,1,96]{2,1,0:T(1,128)S(1)}, u32[]{:S(2)}, u32[]{:S(2)}) async-start(s32[32,1,96]{2,1,0:T(1,128)} %bitcast), calls=%async_computation | async-start | bytes 32768 | tf_op jit(solution)/shard_map/all_to_all | solution.py:202
  36.6 17.2 %collective-permute-start.2 = (bf16[328,960]{1,0:T(8,128)(2,1)S(1)}, bf16[328,960]{1,0:T(8,128)(2,1)S(1)}, u32[]{:S(2)}, u32[]{:S(2)}) collective-permute-start(bf16[328,960]{1,0:T(8,128)(2,1)S(1)} %broadcast_select_fusion), channel_id=1, source_target_pairs={{0,8},{16,24},{1,9},{17,25},{2,10},{18,26},{3,11},{19,27},{4,12},{... | collective-permute-start | bytes 1889288 | tf_op jit(solution)/shard_map/ppermute | solution.py:207
  39.0 15.7 %all-to-all-start.1 = ((bf16[8,60,640]{2,1,0:T(8,128)(2,1)}), bf16[8,60,640]{2,1,0:T(8,128)(2,1)S(1)}, u32[]{:S(2)}, u32[]{:S(2)}) async-start(bf16[8,60,640]{2,1,0:T(8,128)(2,1)} %reshape.768), calls=%async_computation.1 | async-start | bytes 1310720 | tf_op jit(solution)/shard_map/all_to_all | solution.py:196
  44.7 74.8 %all-gather.8.cloned.1.call-start = ((), (), s32[]{:S(2)}) async-start(), calls=%async_computation.11 | async-start | bytes 6045696 | tf_op jit(solution)/shard_map/all_gather | solution.py:211
  54.8 10.9 %copy-start.54 = (f32[512,64]{1,0:T(8,128)S(1)}, f32[512,64]{1,0:T(8,128)}, u32[]{:S(2)}) copy-start(f32[512,64]{1,0:T(8,128)} %constant.377) | copy-start | bytes 393220
  54.8 11.5 %copy-start.53 = (f32[512,64]{1,0:T(8,128)S(1)}, f32[512,64]{1,0:T(8,128)}, u32[]{:S(2)}) copy-start(f32[512,64]{1,0:T(8,128)} %constant.376) | copy-start | bytes 393220
  54.8 74.2 %all-to-all-start.2 = ((bf16[32,32,960]{2,1,0:T(8,128)(2,1)}), bf16[32,32,960]{2,1,0:T(8,128)(2,1)}, u32[]{:S(2)}, u32[]{:S(2)}) async-start(bf16[32,32,960]{2,1,0:T(8,128)(2,1)} %bitcast.223), calls=%async_computation.2 | async-start | bytes 4194304 | tf_op jit(solution)/shard_map/all_to_all | solution.py:210
  64.2 112.5 %all-gather.10.cloned.1.call-start = ((), (), s32[]{:S(2)}) async-start(), calls=%async_computation.12 | async-start | bytes 3072000 | tf_op jit(solution)/shard_map/all_gather | solution.py:219
  66.3 74.0 %copy-start.51 = (f32[64,64]{1,0:T(8,128)}, f32[64,64]{1,0:T(8,128)S(1)}, u32[]{:S(2)}) copy-start(f32[64,64]{1,0:T(8,128)S(1)} %gather_fusion.1) | copy-start | bytes 49156
  125.7 299.1 %reduce-scatter.2.cloned.1.call-start = ((), (), s32[]{:S(2)}) async-start(), calls=%async_computation.10 | async-start | bytes 3072000 | tf_op jit(solution)/shard_map/reduce_scatter | solution.py:388
  132.1 26.6 %copy-start.5 = (bf16[512,960]{0,1:T(8,128)(2,1)}, bf16[512,960]{0,1:T(8,128)(2,1)S(1)}, u32[]{:S(2)}) copy-start(bf16[512,960]{0,1:T(8,128)(2,1)S(1)} %get-tuple-element.175) | copy-start | bytes 2949124
  133.5 47.2 %copy-start.66 = (f32[1,1,960]{2,1,0:T(1,128)}, f32[1,1,960]{2,1,0:T(1,128)S(1)}, u32[]{:S(2)}) copy-start(f32[1,1,960]{2,1,0:T(1,128)S(1)} %get-tuple-element.162) | copy-start | bytes 11524
  133.5 79.2 %copy-start.64 = (f32[1,1,960]{2,1,0:T(1,128)}, f32[1,1,960]{2,1,0:T(1,128)S(1)}, u32[]{:S(2)}) copy-start(f32[1,1,960]{2,1,0:T(1,128)S(1)} %get-tuple-element.161) | copy-start | bytes 11524
  179.2 15.6 %copy-start.48 = (bf16[320,640]{1,0:T(8,128)(2,1)}, bf16[320,640]{1,0:T(8,128)(2,1)S(1)}, u32[]{:S(2)}) copy-start(bf16[320,640]{1,0:T(8,128)(2,1)S(1)} %slice_bitcast_fusion.1) | copy-start | bytes 1228804
  180.6 12.9 %copy-start.90 = (f32[64]{0:T(128)}, f32[64]{0:T(128)S(1)}, u32[]{:S(2)}) copy-start(f32[64]{0:T(128)S(1)} %add_rsqrt_fusion.2) | copy-start | bytes 772
  196.1 2.3 collective-permute-start.3
  202.0 6.2 %collective-permute-start.6 = (bf16[64,1024]{1,0:T(8,128)(2,1)}, bf16[64,1024]{1,0:T(8,128)(2,1)}, u32[]{:S(2)}, u32[]{:S(2)}) collective-permute-start(bf16[64,1024]{1,0:T(8,128)(2,1)} %get-tuple-element.147), channel_id=1, source_target_pairs={{0,6},{2,4},{4,2},{6,0},{1,7},{3,5},{5,3},{7,1},{8,14},{10,12},{12... | collective-permute-start | bytes 393224 | tf_op jit(solution)/shard_map/ppermute | solution.py:74
  203.2 8.3 %collective-permute-start.5 = (bf16[64,1024]{1,0:T(8,128)(2,1)}, bf16[64,1024]{1,0:T(8,128)(2,1)}, u32[]{:S(2)}, u32[]{:S(2)}) collective-permute-start(bf16[64,1024]{1,0:T(8,128)(2,1)} %get-tuple-element.148), channel_id=1, source_target_pairs={{0,4},{2,6},{4,0},{6,2},{1,5},{3,7},{5,1},{7,3},{8,12},{10,14},{12... | collective-permute-start | bytes 393224 | tf_op jit(solution)/shard_map/ppermute | solution.py:74
  204.4 7.1 %collective-permute-start.4 = (bf16[64,1024]{1,0:T(8,128)(2,1)}, bf16[64,1024]{1,0:T(8,128)(2,1)}, u32[]{:S(2)}, u32[]{:S(2)}) collective-permute-start(bf16[64,1024]{1,0:T(8,128)(2,1)} %get-tuple-element.146), channel_id=1, source_target_pairs={{0,2},{2,0},{4,6},{6,4},{1,3},{3,1},{5,7},{7,5},{8,10},{10,8},{12,... | collective-permute-start | bytes 393224 | tf_op jit(solution)/shard_map/ppermute | solution.py:74
  212.7 24.7 %copy-start.7 = (f32[64,960]{1,0:T(8,128)}, f32[64,960]{1,0:T(8,128)S(1)}, u32[]{:S(2)}) copy-start(f32[64,960]{1,0:T(8,128)S(1)} %get-tuple-element.112) | copy-start | bytes 737284
  212.7 24.7 %copy-start.86 = (f32[64]{0:T(128)}, f32[64]{0:T(128)S(1)}, u32[]{:S(2)}) copy-start(f32[64]{0:T(128)S(1)} %add_rsqrt_fusion.1) | copy-start | bytes 772
  225.0 9.0 %collective-permute-start.7 = (bf16[4,64,1024]{2,1,0:T(8,128)(2,1)S(1)}, bf16[4,64,1024]{2,1,0:T(8,128)(2,1)S(1)}, u32[]{:S(2)}, u32[]{:S(2)}) collective-permute-start(bf16[4,64,1024]{2,1,0:T(8,128)(2,1)S(1)} %bitcast.249), channel_id=1, source_target_pairs={{0,2},{2,0},{1,3},{3,1},{4,6},{6,4},{5,7},{7,5},{8,10},{10,8},{9,1... | collective-permute-start | bytes 1572872 | tf_op jit(solution)/shard_map/ppermute | solution.py:74
  226.2 9.9 %collective-permute-start.8 = (bf16[4,64,1024]{2,1,0:T(8,128)(2,1)S(1)}, bf16[4,64,1024]{2,1,0:T(8,128)(2,1)S(1)}, u32[]{:S(2)}, u32[]{:S(2)}) collective-permute-start(bf16[4,64,1024]{2,1,0:T(8,128)(2,1)S(1)} %bitcast.250), channel_id=1, source_target_pairs={{0,4},{4,0},{1,5},{5,1},{2,6},{6,2},{3,7},{7,3},{8,12},{12,8},{9,1... | collective-permute-start | bytes 1572872 | tf_op jit(solution)/shard_map/ppermute | solution.py:74
  234.1 8.4 %collective-permute-start.9 = (bf16[2,64,1024]{2,1,0:T(8,128)(2,1)S(1)}, bf16[2,64,1024]{2,1,0:T(8,128)(2,1)S(1)}, u32[]{:S(2)}, u32[]{:S(2)}) collective-permute-start(bf16[2,64,1024]{2,1,0:T(8,128)(2,1)S(1)} %slice.365), channel_id=1, source_target_pairs={{0,4},{4,0},{1,5},{5,1},{2,6},{6,2},{3,7},{7,3},{8,12},{12,8},{9,1... | collective-permute-start | bytes 786440 | tf_op jit(solution)/shard_map/ppermute | solution.py:74
  236.1 14.4 %copy-start.95 = (s32[32]{0:T(128)S(1)}, s32[32]{0:T(128)}, u32[]{:S(2)}) copy-start(s32[32]{0:T(128)} %constant.350.clone) | copy-start | bytes 388
  236.1 14.5 %copy-start.97 = (s32[32]{0:T(128)S(1)}, s32[32]{0:T(128)}, u32[]{:S(2)}) copy-start(s32[32]{0:T(128)} %copy-done.96) | copy-start | bytes 388
  236.1 7.1 %collective-permute-start.10 = (bf16[2,64,1024]{2,1,0:T(8,128)(2,1)S(1)}, bf16[2,64,1024]{2,1,0:T(8,128)(2,1)S(1)}, u32[]{:S(2)}, u32[]{:S(2)}) collective-permute-start(bf16[2,64,1024]{2,1,0:T(8,128)(2,1)S(1)} %slice.366), channel_id=1, source_target_pairs={{0,2},{2,0},{1,3},{3,1},{4,6},{6,4},{5,7},{7,5},{8,10},{10,8},{9,1... | collective-permute-start | bytes 786440 | tf_op jit(solution)/shard_map/ppermute | solution.py:74
  243.9 14.2 %collective-permute-start.11 = (bf16[1024,1024]{1,0:T(8,128)(2,1)}, bf16[1024,1024]{1,0:T(8,128)(2,1)}, u32[]{:S(2)}, u32[]{:S(2)}) collective-permute-start(bf16[1024,1024]{1,0:T(8,128)(2,1)} %bitcast.38), channel_id=1, source_target_pairs={{0,1},{1,0},{2,3},{3,2},{4,5},{5,4},{6,7},{7,6},{8,9},{9,8},{10,11... | collective-permute-start | bytes 6291464 | tf_op jit(solution)/shard_map/ppermute | solution.py:74
  251.4 11.6 %copy-start.78 = (s32[1024]{0:T(1024)}, s32[1024]{0:T(1024)S(1)}, u32[]{:S(2)}) copy-start(s32[1024]{0:T(1024)S(1)} %sub.225) | copy-start | bytes 12292
  302.2 6.4 %collective-permute-start.12 = (bf16[1024,1024]{1,0:T(8,128)(2,1)}, bf16[1024,1024]{1,0:T(8,128)(2,1)}, u32[]{:S(2)}, u32[]{:S(2)}) collective-permute-start(bf16[1024,1024]{1,0:T(8,128)(2,1)} %convolution_convert_fusion), channel_id=1, source_target_pairs={{0,1},{1,0},{2,3},{3,2},{4,5},{5,4},{6,7},{7,6},{8,9},{9,8},{10,11... | collective-permute-start | bytes 6291464 | tf_op jit(solution)/shard_map/ppermute | solution.py:74
  313.6 14.5 %collective-permute-start.15 = (bf16[4,64,1024]{2,1,0:T(8,128)(2,1)S(1)}, bf16[4,64,1024]{2,1,0:T(8,128)(2,1)S(1)}, u32[]{:S(2)}, u32[]{:S(2)}) collective-permute-start(bf16[4,64,1024]{2,1,0:T(8,128)(2,1)S(1)} %bitcast.276), channel_id=1, source_target_pairs={{0,6},{2,4},{4,2},{6,0},{1,7},{3,5},{5,3},{7,1},{8,14},{10,12},{12... | collective-permute-start | bytes 1572872 | tf_op jit(solution)/shard_map/ppermute | solution.py:74
  314.0 24.5 %collective-permute-start.14 = (bf16[4,64,1024]{2,1,0:T(8,128)(2,1)S(1)}, bf16[4,64,1024]{2,1,0:T(8,128)(2,1)S(1)}, u32[]{:S(2)}, u32[]{:S(2)}) collective-permute-start(bf16[4,64,1024]{2,1,0:T(8,128)(2,1)S(1)} %bitcast.275), channel_id=1, source_target_pairs={{0,4},{2,6},{4,0},{6,2},{1,5},{3,7},{5,1},{7,3},{8,12},{10,14},{12... | collective-permute-start | bytes 1572872 | tf_op jit(solution)/shard_map/ppermute | solution.py:74
  315.1 23.4 %collective-permute-start.13 = (bf16[4,64,1024]{2,1,0:T(8,128)(2,1)S(1)}, bf16[4,64,1024]{2,1,0:T(8,128)(2,1)S(1)}, u32[]{:S(2)}, u32[]{:S(2)}) collective-permute-start(bf16[4,64,1024]{2,1,0:T(8,128)(2,1)S(1)} %bitcast.274), channel_id=1, source_target_pairs={{0,2},{2,0},{4,6},{6,4},{1,3},{3,1},{5,7},{7,5},{8,10},{10,8},{12,... | collective-permute-start | bytes 1572872 | tf_op jit(solution)/shard_map/ppermute | solution.py:74
  338.9 6.7 %collective-permute-start.18 = (bf16[64,1024]{1,0:T(8,128)(2,1)S(1)}, bf16[64,1024]{1,0:T(8,128)(2,1)S(1)}, u32[]{:S(2)}, u32[]{:S(2)}) collective-permute-start(bf16[64,1024]{1,0:T(8,128)(2,1)S(1)} %get-tuple-element.144), channel_id=1, source_target_pairs={{0,24},{8,16},{16,8},{24,0},{1,25},{9,17},{17,9},{25,1},{2,26},{10... | collective-permute-start | bytes 393224 | tf_op jit(solution)/shard_map/ppermute | solution.py:74
  339.3 12.0 %collective-permute-start.17 = (bf16[64,1024]{1,0:T(8,128)(2,1)S(1)}, bf16[64,1024]{1,0:T(8,128)(2,1)S(1)}, u32[]{:S(2)}, u32[]{:S(2)}) collective-permute-start(bf16[64,1024]{1,0:T(8,128)(2,1)S(1)} %get-tuple-element.145), channel_id=1, source_target_pairs={{0,16},{8,24},{16,0},{24,8},{1,17},{9,25},{17,1},{25,9},{2,18},{10... | collective-permute-start | bytes 393224 | tf_op jit(solution)/shard_map/ppermute | solution.py:74
  340.7 10.7 %copy-start.65 = (f32[1,1,960]{2,1,0:T(1,128)S(1)}, f32[1,1,960]{2,1,0:T(1,128)}, u32[]{:S(2)}) copy-start(f32[1,1,960]{2,1,0:T(1,128)} %copy-done.64) | copy-start | bytes 11524
  340.7 10.8 %copy-start.87 = (f32[64]{0:T(128)S(1)}, f32[64]{0:T(128)}, u32[]{:S(2)}) copy-start(f32[64]{0:T(128)} %copy-done.86) | copy-start | bytes 772
  340.7 10.7 %collective-permute-start.16 = (bf16[64,1024]{1,0:T(8,128)(2,1)S(1)}, bf16[64,1024]{1,0:T(8,128)(2,1)S(1)}, u32[]{:S(2)}, u32[]{:S(2)}) collective-permute-start(bf16[64,1024]{1,0:T(8,128)(2,1)S(1)} %get-tuple-element.143), channel_id=1, source_target_pairs={{0,8},{8,0},{16,24},{24,16},{1,9},{9,1},{17,25},{25,17},{2,10},{10... | collective-permute-start | bytes 393224 | tf_op jit(solution)/shard_map/ppermute | solution.py:74
  345.6 19.9 %copy-start.38 = (f32[512,640]{1,0:T(8,128)S(1)}, f32[512,640]{1,0:T(8,128)}, u32[]{:S(2)}) copy-start(f32[512,640]{1,0:T(8,128)} %copy-done.37) | copy-start | bytes 3932164
  345.6 19.9 %copy-start.49 = (bf16[320,640]{1,0:T(8,128)(2,1)S(1)}, bf16[320,640]{1,0:T(8,128)(2,1)}, u32[]{:S(2)}) copy-start(bf16[320,640]{1,0:T(8,128)(2,1)} %copy-done.48) | copy-start | bytes 1228804
  345.6 19.9 %copy-start.61 = (bf16[160,320]{1,0:T(8,128)(2,1)S(1)}, bf16[160,320]{1,0:T(8,128)(2,1)}, u32[]{:S(2)}) copy-start(bf16[160,320]{1,0:T(8,128)(2,1)} %copy-done.60) | copy-start | bytes 307204
  345.6 19.9 %copy-start.63 = (bf16[160,320]{1,0:T(8,128)(2,1)S(1)}, bf16[160,320]{1,0:T(8,128)(2,1)}, u32[]{:S(2)}) copy-start(bf16[160,320]{1,0:T(8,128)(2,1)} %copy-done.62) | copy-start | bytes 307204
  367.3 3.4 collective-permute-start.19
  372.3 6.0 %collective-permute-start.22 = (bf16[64,1024]{1,0:T(8,128)(2,1)S(1)}, bf16[64,1024]{1,0:T(8,128)(2,1)}, u32[]{:S(2)}, u32[]{:S(2)}) collective-permute-start(bf16[64,1024]{1,0:T(8,128)(2,1)S(1)} %get-tuple-element.141), channel_id=1, source_target_pairs={{0,6},{2,4},{4,2},{6,0},{1,7},{3,5},{5,3},{7,1},{8,14},{10,12},{12... | collective-permute-start | bytes 393224 | tf_op jit(solution)/shard_map/ppermute | solution.py:74
  373.6 8.1 %collective-permute-start.21 = (bf16[64,1024]{1,0:T(8,128)(2,1)S(1)}, bf16[64,1024]{1,0:T(8,128)(2,1)}, u32[]{:S(2)}, u32[]{:S(2)}) collective-permute-start(bf16[64,1024]{1,0:T(8,128)(2,1)S(1)} %get-tuple-element.142), channel_id=1, source_target_pairs={{0,4},{2,6},{4,0},{6,2},{1,5},{3,7},{5,1},{7,3},{8,12},{10,14},{12... | collective-permute-start | bytes 393224 | tf_op jit(solution)/shard_map/ppermute | solution.py:74
  374.0 7.7 %collective-permute-start.20 = (bf16[64,1024]{1,0:T(8,128)(2,1)S(1)}, bf16[64,1024]{1,0:T(8,128)(2,1)}, u32[]{:S(2)}, u32[]{:S(2)}) collective-permute-start(bf16[64,1024]{1,0:T(8,128)(2,1)S(1)} %get-tuple-element.140), channel_id=1, source_target_pairs={{0,2},{2,0},{4,6},{6,4},{1,3},{3,1},{5,7},{7,5},{8,10},{10,8},{12,... | collective-permute-start | bytes 393224 | tf_op jit(solution)/shard_map/ppermute | solution.py:74
  418.8 28.7 %all-to-all-start.5 = ((bf16[32,16,960]{2,1,0:T(8,128)(2,1)}), bf16[32,16,960]{2,1,0:T(8,128)(2,1)}, u32[]{:S(2)}, u32[]{:S(2)}) async-start(bf16[32,16,960]{2,1,0:T(8,128)(2,1)} %bitcast.86), calls=%async_computation.6 | async-start | bytes 2097152 | tf_op jit(solution)/shard_map/all_to_all | solution.py:391
  451.2 6.5 %collective-permute-start.23 = (bf16[4,352,960]{2,1,0:T(8,128)(2,1)}, bf16[4,352,960]{2,1,0:T(8,128)(2,1)}, u32[]{:S(2)}, u32[]{:S(2)}) collective-permute-start(bf16[4,352,960]{2,1,0:T(8,128)(2,1)} %dynamic-slice_bitcast_fusion), channel_id=1, source_target_pairs={{0,1},{1,0},{2,3},{3,2},{4,5},{5,4},{6,7},{7,6},{8,9},{9,8},{10,11... | collective-permute-start | bytes 8110088 | tf_op jit(solution)/shard_map/ppermute | solution.py:74
  452.4 54.1 %all-to-all-start.6 = ((bf16[32,16,960]{2,1,0:T(8,128)(2,1)}), bf16[32,16,960]{2,1,0:T(8,128)(2,1)}, u32[]{:S(2)}, u32[]{:S(2)}) async-start(bf16[32,16,960]{2,1,0:T(8,128)(2,1)} %bitcast.87), calls=%async_computation.7 | async-start | bytes 2097152 | tf_op jit(solution)/shard_map/all_to_all | solution.py:391
  464.5 24.2 %collective-permute-start.26 = (bf16[352,960]{1,0:T(8,128)(2,1)S(1)}, bf16[352,960]{1,0:T(8,128)(2,1)}, u32[]{:S(2)}, u32[]{:S(2)}) collective-permute-start(bf16[352,960]{1,0:T(8,128)(2,1)S(1)} %get-tuple-element.114), channel_id=1, source_target_pairs={{0,6},{2,4},{4,2},{6,0},{1,7},{3,5},{5,3},{7,1},{8,14},{10,12},{12... | collective-permute-start | bytes 2027528 | tf_op jit(solution)/shard_map/ppermute | solution.py:74
  466.7 37.1 %collective-permute-start.25 = (bf16[352,960]{1,0:T(8,128)(2,1)S(1)}, bf16[352,960]{1,0:T(8,128)(2,1)}, u32[]{:S(2)}, u32[]{:S(2)}) collective-permute-start(bf16[352,960]{1,0:T(8,128)(2,1)S(1)} %get-tuple-element.115), channel_id=1, source_target_pairs={{0,4},{2,6},{4,0},{6,2},{1,5},{3,7},{5,1},{7,3},{8,12},{10,14},{12... | collective-permute-start | bytes 2027528 | tf_op jit(solution)/shard_map/ppermute | solution.py:74
  467.0 37.1 %collective-permute-start.24 = (bf16[352,960]{1,0:T(8,128)(2,1)S(1)}, bf16[352,960]{1,0:T(8,128)(2,1)}, u32[]{:S(2)}, u32[]{:S(2)}) collective-permute-start(bf16[352,960]{1,0:T(8,128)(2,1)S(1)} %get-tuple-element.113), channel_id=1, source_target_pairs={{0,2},{2,0},{4,6},{6,4},{1,3},{3,1},{5,7},{7,5},{8,10},{10,8},{12,... | collective-permute-start | bytes 2027528 | tf_op jit(solution)/shard_map/ppermute | solution.py:74
  472.0 34.6 %copy-start.27 = (bf16[1,480,640]{2,1,0:T(8,128)(2,1)S(1)}, bf16[1,480,640]{2,1,0:T(8,128)(2,1)}, u32[]{:S(2)}) copy-start(bf16[1,480,640]{2,1,0:T(8,128)(2,1)} %reduce-scatter.2.cloned.1.call-done) | copy-start | bytes 1843204
  507.5 43.9 %all-to-all-start.7 = ((bf16[8,60,640]{2,1,0:T(8,128)(2,1)}), bf16[8,60,640]{2,1,0:T(8,128)(2,1)S(1)}, u32[]{:S(2)}, u32[]{:S(2)}) async-start(bf16[8,60,640]{2,1,0:T(8,128)(2,1)} %reshape.705), calls=%async_computation.8 | async-start | bytes 1310720 | tf_op jit(solution)/shard_map/all_to_all | solution.py:412
  511.7 8.1 %collective-permute-start.29 = (bf16[88,960]{1,0:T(8,128)(2,1)S(1)}, bf16[88,960]{1,0:T(8,128)(2,1)S(1)}, u32[]{:S(2)}, u32[]{:S(2)}) collective-permute-start(bf16[88,960]{1,0:T(8,128)(2,1)S(1)} %get-tuple-element.122), channel_id=1, source_target_pairs={{0,24},{8,16},{16,8},{24,0},{1,25},{9,17},{17,9},{25,1},{2,26},{10... | collective-permute-start | bytes 506888 | tf_op jit(solution)/shard_map/ppermute | solution.py:74
  513.5 17.5 %collective-permute-start.28 = (bf16[88,960]{1,0:T(8,128)(2,1)S(1)}, bf16[88,960]{1,0:T(8,128)(2,1)S(1)}, u32[]{:S(2)}, u32[]{:S(2)}) collective-permute-start(bf16[88,960]{1,0:T(8,128)(2,1)S(1)} %get-tuple-element.123), channel_id=1, source_target_pairs={{0,16},{8,24},{16,0},{24,8},{1,17},{9,25},{17,1},{25,9},{2,18},{10... | collective-permute-start | bytes 506888 | tf_op jit(solution)/shard_map/ppermute | solution.py:74
  514.7 16.3 %collective-permute-start.27 = (bf16[88,960]{1,0:T(8,128)(2,1)S(1)}, bf16[88,960]{1,0:T(8,128)(2,1)S(1)}, u32[]{:S(2)}, u32[]{:S(2)}) collective-permute-start(bf16[88,960]{1,0:T(8,128)(2,1)S(1)} %get-tuple-element.121), channel_id=1, source_target_pairs={{0,8},{8,0},{16,24},{24,16},{1,9},{9,1},{17,25},{25,17},{2,10},{10... | collective-permute-start | bytes 506888 | tf_op jit(solution)/shard_map/ppermute | solution.py:74
  531.1 12.0 %collective-permute-start.32 = (bf16[88,960]{1,0:T(8,128)(2,1)S(1)}, bf16[88,960]{1,0:T(8,128)(2,1)S(1)}, u32[]{:S(2)}, u32[]{:S(2)}) collective-permute-start(bf16[88,960]{1,0:T(8,128)(2,1)S(1)} %fusion.86), channel_id=1, source_target_pairs={{16,0},{17,1},{18,2},{19,3},{20,4},{21,5},{22,6},{23,7}} | collective-permute-start | bytes 506888 | tf_op jit(solution)/shard_map/ppermute | solution.py:418
  532.4 10.7 %collective-permute-start.30 = (bf16[88,960]{1,0:T(8,128)(2,1)S(1)}, bf16[88,960]{1,0:T(8,128)(2,1)S(1)}, u32[]{:S(2)}, u32[]{:S(2)}) collective-permute-start(bf16[88,960]{1,0:T(8,128)(2,1)S(1)} %fusion.86), channel_id=1, source_target_pairs={{24,0},{25,1},{26,2},{27,3},{28,4},{29,5},{30,6},{31,7}} | collective-permute-start | bytes 506888 | tf_op jit(solution)/shard_map/ppermute | solution.py:418
  533.9 14.2 %collective-permute-start.31 = (bf16[88,960]{1,0:T(8,128)(2,1)S(1)}, bf16[88,960]{1,0:T(8,128)(2,1)S(1)}, u32[]{:S(2)}, u32[]{:S(2)}) collective-permute-start(bf16[88,960]{1,0:T(8,128)(2,1)S(1)} %fusion.86), channel_id=1, source_target_pairs={{8,0},{9,1},{10,2},{11,3},{12,4},{13,5},{14,6},{15,7}} | collective-permute-start | bytes 506888 | tf_op jit(solution)/shard_map/ppermute | solution.py:418
  554.5 12.9 %collective-permute-start.33 = (bf16[2880]{0:T(1024)(128)(2,1)S(1)}, bf16[2880]{0:T(1024)(128)(2,1)S(1)}, u32[]{:S(2)}, u32[]{:S(2)}) collective-permute-start(bf16[2880]{0:T(1024)(128)(2,1)S(1)} %slice.397), channel_id=1, source_target_pairs={{0,1},{1,2},{2,3},{3,4},{4,5},{5,6},{6,7},{7,8},{8,9},{9,10},{10,1... | collective-permute-start | bytes 17288 | tf_op jit(solution)/shard_map/ppermute | solution.py:434
  567.3 13.4 %copy-start.12 = (f32[307290]{0:T(1024)S(1)}, f32[307290]{0:T(1024)}, u32[]{:S(2)}) copy-start(f32[307290]{0:T(1024)} %param.18) | copy-start | bytes 3687484
  (79 other events, 275.9 us)
Sparse Core Ops, SparseCore 0:
  54.9 64.5 all-gather.7
  125.8 50.9 all-gather.9
  377.0 47.7 reduce-scatter.1

commit v6 on v5

--- a/solution.py
+++ b/solution.py
@@ -178,6 +178,19 @@
     before = (lax.broadcasted_iota(jnp.int32, (tokens, tokens), 0) > lax.broadcasted_iota(jnp.int32, (tokens, tokens), 1)).astype(bf16)
     slot = jnp.sum(dot(before, owner_hot) * owner_hot.astype(f32), axis=1).astype(jnp.int32)
     spot = hot(owner * capacity + slot, slots)
+
+    def spot_between(low, high):
+        inside = (slot >= low) & (slot < high)
+        return hot(jnp.where(inside, owner * (high - low) + slot - low, -1), devices * (high - low))
+
+    def rows_between(low, high):
+        return hot(asked[:, low:high].reshape(-1) - me * vocab_dev, vocab_dev)
+
+    def exchange(blocks):
+        return lax.all_to_all(blocks, ALL, split_axis=0, concat_axis=0, tiled=True).reshape(-1, D)
+
+    cuts = (0, 3 * capacity // 4, capacity)
+    cuts_back = (0, capacity // 4, capacity)
     marked = token_ids + 1
     halves = jnp.stack([marked // 256, marked % 256]).astype(bf16)
     found = dot(halves, spot).astype(jnp.int32)
@@ -200,28 +213,32 @@
         first = jnp.concatenate([first, flat_low[:GAINS].reshape(3, D), jnp.zeros((5, D), bf16)])
         first, ask = lax.optimization_barrier((first, ask))
         asked = lax.all_to_all(ask, ALL, split_axis=0, concat_axis=0, tiled=True)
-        row_hot = hot(asked[:, :capacity].reshape(-1) - me * vocab_dev, vocab_dev)
-        answer = dot(row_hot, table_low).astype(bf16).reshape(devices, capacity, D)
+        answer = [dot(rows_between(low, high), table_low).astype(bf16).reshape(devices, high - low, D) for low, high in zip(cuts, cuts[1:])]
         jumped = lax.ppermute(first, "q", [(0, 2)])
         first = jnp.where(q_index == 2, jumped, first)
         stepped = lax.ppermute(first, "q", [(0, 1), (2, 3)])
         first = jnp.where((q_index == 1) | (q_index == 3), stepped, first)
         answer, first, got = lax.optimization_barrier((answer, first, got))
-        returned = lax.all_to_all(answer, ALL, split_axis=0, concat_axis=0, tiled=True).reshape(slots, D)
-        level = lax.all_gather(first, PLANE)
+        returned = [exchange(blocks) for blocks in answer]
+        level = jnp.stack([first] + [flip(first, ("y", "x"), k, 4) for k in (1, 2, 3)])
         mixed = jnp.where(q_index == 3, down_pack(chunk.reshape(SHARE, D)), got.reshape(480, 2 * UNIT))
-        mixed, level = lax.optimization_barrier((mixed, level))
-        gains = level[0, SHARE : SHARE + 3].astype(f32)
-        w_q = level[:5, :TOP].reshape(D, D)
-        w_kv = level[:5, TOP:SHARE].reshape(D, KV)
-        w_out = level[5:, :SHARE].reshape(D, D)
-        returned, w_q, w_kv, w_out = lax.optimization_barrier((returned, w_q, w_kv, w_out))
+        level, returned[0] = lax.optimization_barrier((level, returned[0]))
+        level = jnp.concatenate([level, flip(level, "c", 1, 2)])
+
+        def from_place(p):
+            k = p_index ^ p
+            return pick_block(level, (k & 1) * 4 + (k >> 1))
+
+        gains = from_place(0)[SHARE : SHARE + 3].astype(f32)
+        w_q = jnp.concatenate([from_place(p)[:TOP] for p in range(5)])
+        w_kv = jnp.concatenate([from_place(p)[TOP:SHARE] for p in range(5)]).reshape(D, KV)
+        w_out = jnp.concatenate([from_place(p)[:SHARE] for p in range(5, 8)])
+        returned[1], w_q, w_kv, w_out = lax.optimization_barrier((returned[1], w_q, w_kv, w_out))
         column = lax.all_gather(mixed, "q")
     else:
         asked = lax.all_to_all(ask, ALL, split_axis=0, concat_axis=0, tiled=True)
-        row_hot = hot(asked[:, :capacity].reshape(-1) - me * vocab_dev, vocab_dev)
-        answer = dot(row_hot, table_low).astype(bf16).reshape(devices, capacity, D)
-        returned = lax.all_to_all(answer, ALL, split_axis=0, concat_axis=0, tiled=True).reshape(slots, D)
+        answer = [dot(rows_between(low, high), table_low).astype(bf16).reshape(devices, high - low, D) for low, high in zip(cuts, cuts[1:])]
+        returned = [exchange(blocks) for blocks in answer]
         extra = jnp.zeros((16 * UNIT,), bf16).at[:GAINS].set(flat_low[:GAINS])
         full = lax.all_gather(jnp.concatenate([chunk, extra]).reshape(units + 16, UNIT), ALL)
         gains = full[0, units : units + GAIN_UNITS].astype(f32).reshape(3, D)
@@ -233,7 +250,7 @@
         both = lax.dynamic_index_in_dim(full[edge[1] : edge[2]].reshape(D, 2, 8, UNIT), p_index, 2, False)
         w_gu = both.reshape(D, 2 * SHARE)
         w_down = lax.dynamic_index_in_dim(full[edge[2] :].reshape(8, SHARE, D), p_index, 0, False)
-    x_low = dot(spot, returned).astype(bf16)
+    x_low = sum(dot(spot_between(low, high), rows) for low, high, rows in zip(cuts, cuts[1:], returned)).astype(bf16)
     x_embed = x_low.astype(f32) * emb_mult
 
     pick = hot(loss_rows, tokens)
@@ -244,6 +261,8 @@
     x_pick = dot(pick, x_low) * emb_mult
     query = rotate(dot(h_pick, w_q), cosine_pick, sine_pick).astype(bf16)
     key_value = dot(h_attn, w_kv)
+    if aligned:
+        column, key_value = lax.optimization_barrier((column, key_value))
     key = rotate(key_value[:, :UNIT], cosine, sine).astype(bf16)
     value = key_value[:, UNIT:].astype(bf16)
 
@@ -271,7 +290,6 @@
     x_one = x_pick + dot(attended, w_out)
 
     if aligned:
-        column, x_one = lax.optimization_barrier((column, x_one))
         w_gu = column[1:3].reshape(D, 2 * SHARE)
         w_down = down_unpack(column[3])
     w_gu = jnp.pad(w_gu, ((0, WIDE - D), (0, 0)))
@@ -376,19 +394,17 @@
     rest = (d_x_one - high.astype(f32)).astype(bf16)
     d_x_embed = d_x_attn + dot(pick, high, 0, 0) + dot(pick, rest, 0, 0)
 
-    part = capacity // 2
     scaled = (d_x_embed * emb_mult).astype(bf16)
-    sending = []
-    for side in range(2):
-        inside = (slot >= side * part) & (slot < (side + 1) * part)
-        place_of = jnp.where(inside, owner * part + slot - side * part, -1)
-        sending.append(dot(hot(place_of, devices * part), scaled, 0, 0).astype(bf16).reshape(devices, part, D))
+    sending = [
+        dot(spot_between(low, high), scaled, 0, 0).astype(bf16).reshape(devices, high - low, D)
+        for low, high in zip(cuts_back, cuts_back[1:])
+    ]
     if aligned:
         blocks = jnp.concatenate([jnp.zeros((1, 480, 640), bf16), grad_gu.reshape(2, 480, 640), down_pack(grad_down)[None]])
         share = lax.psum_scatter(blocks, "q", scatter_dimension=0, tiled=False)
         sending, d_q, d_kv, attended = lax.optimization_barrier((sending, d_q, d_kv, attended))
         share, d_q, d_kv, attended = lax.optimization_barrier((share, d_q, d_kv, attended))
-    arrived = [lax.all_to_all(rows, ALL, split_axis=0, concat_axis=0, tiled=True).reshape(-1, D) for rows in sending]
+    arrived = [exchange(blocks) for blocks in sending]
     grad_out = dot(attended, d_branch, 0, 0).astype(bf16)
     grad_q = dot(h_pick, d_q, 0, 0).astype(bf16)
     grad_kv = dot(h_attn, d_kv, 0, 0).astype(bf16)
@@ -414,7 +430,11 @@
         for k in (1, 2, 3):
             piece = lax.dynamic_index_in_dim(own, q_index ^ k, 0, False).astype(bf16)
             quarter = quarter + flip(piece, "q", k, 4).astype(f32)
-        quarter = quarter.astype(bf16)
+        table_grad = head_grad
+        for low, high, rows in zip(cuts_back, cuts_back[1:], arrived):
+            table_grad = table_grad + dot(rows_between(low, high), rows, 0, 0)
+        table_squares = jnp.sum(table_grad * table_grad)
+        quarter, table_squares = lax.optimization_barrier((quarter.astype(bf16), table_squares))
         quarters = [quarter] + [lax.ppermute(quarter, "q", [(k, 0)]) for k in (1, 2, 3)]
         first = jnp.concatenate(quarters)
         gain_out = first[SHARE : SHARE + 3].reshape(-1)
@@ -424,6 +444,10 @@
         mine = jnp.where(q_index == 3, down_unpack(share).reshape(-1), by_share)
         mine = jnp.where(q_index == 0, first, mine)
     else:
+        table_grad = head_grad
+        for low, high, rows in zip(cuts_back, cuts_back[1:], arrived):
+            table_grad = table_grad + dot(rows_between(low, high), rows, 0, 0)
+        table_squares = jnp.sum(table_grad * table_grad)
         both = lax.dynamic_update_index_in_dim(jnp.zeros((D, 2, 8, UNIT), bf16), grad_gu.reshape(D, 2, UNIT), p_index, 2)
         downs = lax.dynamic_update_index_in_dim(jnp.zeros((8, SHARE, D), bf16), grad_down, p_index, 0)
         full = jnp.concatenate([part.reshape(-1, UNIT) for part in (jnp.concatenate([grad_q, grad_kv], axis=1), grad_out, both, downs)]).reshape(devices, units, UNIT)
@@ -437,11 +461,7 @@
     stream = jnp.concatenate([behind, mine, jnp.zeros((tail,), bf16)])
     layer_grad = lax.dynamic_slice(stream, (drift * me,), (shard,)).astype(f32)
 
-    table_grad = head_grad
-    for side in range(2):
-        rows = asked[:, side * part : (side + 1) * part].reshape(-1) - me * vocab_dev
-        table_grad = table_grad + dot(hot(rows, vocab_dev), arrived[side], 0, 0)
-    squares = jnp.sum(layer_grad * layer_grad) + jnp.sum(table_grad * table_grad)
+    squares = jnp.sum(layer_grad * layer_grad) + table_squares
     sums = jnp.broadcast_to(jnp.stack([squares, my_loss])[None], (devices, 2))
     sums = jnp.sum(lax.all_to_all(sums, ALL, split_axis=0, concat_axis=0, tiled=True), axis=0)
     grad_norm = jnp.sqrt(sums[0])

time: 614 us -> 655 us (1.067)
  local copies, waits for them, and re-layouts: 87.5 us -> 111 us
  starting transfers between devices: 78.9 us -> 90.1 us
  waiting for transfers between devices: 182 us -> 175 us
    all_gather x1 -> x0, waiting for transfers between devices: 49.5 us -> none  [local(): level = lax.all_gather(first, PLANE)]
    ppermute x27 -> x31, waiting for transfers between devices: 91.4 us -> 140 us  [flip(): return lax.ppermute(rows, axes, [(i, i ^ bits) for i in range(size)])]
    unnamed x205 -> x221, local copies, waits for them, and re-layouts: 18.9 us -> 30.2 us
    all_to_all x3 -> x4, waiting for transfers between devices: 9.11 us -> 0.01 us  [exchange(): lax.all_to_all(blocks, ALL, split_axis=0, concat_axis=0, tiled=True)]
    ppermute x3, waiting for transfers between devices: 11.7 us -> 3.57 us  [local(): lax.ppermute(quarter, 'q', [(k, 0)])]
    dot_general x37 -> x39, matrix products: 75.2 us -> 82.6 us  [dot(): lax.dot_general(left, right, (((left_dim,), (right_dim,)), ((), ())), pre...]
    all_to_all x3 -> x4, starting transfers between devices: 16.8 us -> 19.9 us  [exchange(): lax.all_to_all(blocks, ALL, split_axis=0, concat_axis=0, tiled=True)]
    ppermute x27 -> x31, starting transfers between devices: 30.2 us -> 33 us  [flip(): return lax.ppermute(rows, axes, [(i, i ^ bits) for i in range(size)])]
  transfers between devices with their start and end apart: 43 -> 47, of which waited for: 24 -> 24; matrix products, arithmetic and copies ran while one was open for 29% -> 26% of each run, Pallas kernels for 0% -> 0%
where the time goes in v6:
time: 655 us; the launch traced here: 643 us
  waiting for transfers between devices  175 us (27%)
  local copies, waits for them, and re-layouts  111 us (17%)
  matrix products  97.8 us (15%)
  starting transfers between devices  90.1 us (14%)
  other arithmetic  81.1 us (12%)
  blocking collectives  67 us (10%)
  between operations  21 us (3%)
    ppermute x31, waiting for transfers between devices, flip(): return lax.ppermute(rows, axes, [(i, i ^ bits) for i in range(size)])  140 us
    dot_general x39, matrix products, dot(): lax.dot_general(left, right, (((left_dim,), (right_dim,)), ((), ())), pre...  82.6 us
    ppermute x31, starting transfers between devices, flip(): return lax.ppermute(rows, axes, [(i, i ^ bits) for i in range(size)])  33 us
    unnamed x221, local copies, waits for them, and re-layouts  30.2 us
    all_gather x2, blocking collectives, spread_plane(): return widen(lax.all_gather(rows, PLANE).reshape(-1, D))  25 us
    all_gather x1, waiting for transfers between devices, local(): column = lax.all_gather(mixed, 'q')  22 us
    all_to_all x4, starting transfers between devices, exchange(): lax.all_to_all(blocks, ALL, split_axis=0, concat_axis=0, tiled=True)  19.9 us
  transfers between devices with their start and end apart: 47, of which 24 were waited for; matrix products, arithmetic and copies ran while one was open for 26% of the time, Pallas kernels for 0%

profile of v6, /device:TPU:1, one launch (start us, length us, event | category | flops | bytes accessed | tf_op | source)
XLA Modules:
  0.0 642.6 jit_solution(6142879536082112966)
XLA Ops:
  18.7 5.7 collective-permute-start.1
  24.4 4.2 all-to-all-start
  28.6 3.7 convert_element_type.298
  36.8 6.5 %all-to-all-start.1 = ((bf16[8,60,640]{2,1,0:T(8,128)(2,1)}), bf16[8,60,640]{2,1,0:T(8,128)(2,1)S(1)}, u32[]{:S(2)}, u32[]{:S(2)}) async-start(bf16[8,60,640]{2,1,0:T(8,128)(2,1)} %reshape.826), calls=%async_computation.1 | async-start | bytes 1310720 | tf_op jit(solution)/shard_map/all_to_all | solution.py:209
  45.3 5.9 collective-permute-start.2
  51.2 4.5 fusion.23
  55.7 2.6 copy.199
  59.0 2.4 convolution_convert_fusion.9
  62.3 3.1 collective-permute-done.2
  65.6 7.5 %all-to-all-start.2 = ((bf16[32,24,960]{2,1,0:T(8,128)(2,1)}), bf16[32,24,960]{2,1,0:T(8,128)(2,1)}, u32[]{:S(2)}, u32[]{:S(2)}) async-start(bf16[32,24,960]{2,1,0:T(8,128)(2,1)} %bitcast.2), calls=%async_computation.2 | async-start | bytes 3145728 | tf_op jit(solution)/shard_map/all_to_all | solution.py:190
  75.8 33.0 %collective-permute-done.5 = bf16[328,960]{1,0:T(8,128)(2,1)S(1)} collective-permute-done((bf16[328,960]{1,0:T(8,128)(2,1)S(1)}, bf16[328,960]{1,0:T(8,128)(2,1)S(1)}, u32[]{:S(2)}, u32[]{:S(2)}) %collective-permute-start.5) | collective-permute-done | bytes 629792 | tf_op jit(solution)/shard_map/ppermute | solution.py:74
  108.8 12.0 %collective-permute-done.4 = bf16[328,960]{1,0:T(8,128)(2,1)S(1)} collective-permute-done((bf16[328,960]{1,0:T(8,128)(2,1)S(1)}, bf16[328,960]{1,0:T(8,128)(2,1)S(1)}, u32[]{:S(2)}, u32[]{:S(2)}) %collective-permute-start.4) | collective-permute-done | bytes 629792 | tf_op jit(solution)/shard_map/ppermute | solution.py:74
  135.6 4.3 all-to-all-start.3
  143.9 3.8 fusion.26
  152.1 2.8 reshape.723
  166.4 2.4 fusion.21
  173.9 22.0 %all-gather.5.cloned.1.call-done = bf16[4,480,640]{2,1,0:T(8,128)(2,1)} async-done(((bf16[1,480,640]{2,1,0:T(8,128)(2,1)}), bf16[4,480,640]{2,1,0:T(8,128)(2,1)}) %all-gather.5.cloned.1.call-update) | async-done | bytes 2457616 | tf_op jit(solution)/shard_map/all_gather | solution.py:237
  197.3 2.8 copy.207
  200.0 2.4 slice.376
  207.1 2.7 fusion.205
  218.9 3.7 fusion.201
  222.6 3.6 convolution_convert_fusion.11
  229.3 11.8 %all-gather = bf16[512,960]{1,0:T(8,128)(2,1)S(1)} all-gather(bf16[64,960]{1,0:T(8,128)(2,1)S(1)} %multiply_convert_fusion.7), channel_id=2, replica_groups=mesh['q'=4,'y'=2,'x'=2,'c'=2] {'y','x','c'}, dimensions={0}, use_global_device_ids=true | all-gather | bytes 1105920 | tf_op jit(solution)/shard_map/all_gather | solution.py:143
  254.7 2.5 collective-permute-done.10
  257.1 3.4 collective-permute-done.9
  262.5 13.0 %all-gather.1 = bf16[256,1024]{1,0:T(8,128)(2,1)S(1)} all-gather(bf16[64,1024]{1,0:T(8,128)(2,1)S(1)} %pad.31), channel_id=3, replica_groups=mesh['q'=4,'y'=2,'x'=2,'c'=2] {'q'}, dimensions={0}, use_global_device_ids=true | all-gather | bytes 655360 | tf_op jit(solution)/shard_map/all_gather | solution.py:307
  277.0 8.3 %collective-permute-done.11 = bf16[4,64,1024]{2,1,0:T(8,128)(2,1)S(1)} collective-permute-done((bf16[4,64,1024]{2,1,0:T(8,128)(2,1)S(1)}, bf16[4,64,1024]{2,1,0:T(8,128)(2,1)S(1)}, u32[]{:S(2)}, u32[]{:S(2)}) %collective-permute-start.11) | collective-permute-done | bytes 524320 | tf_op jit(solution)/shard_map/ppermute | solution.py:74
  289.5 2.7 collective-permute-done.13
  293.7 5.9 collective-permute-start.15
  301.0 4.5 fusion.203
  308.6 3.9 fusion.202
  321.5 9.5 %all_to_all.58 = f32[32,1,256]{2,1,0:T(1,128)} all-to-all(f32[32,1,256]{2,1,0:T(1,128)S(1)} %reshape.837), channel_id=1, replica_groups=mesh['q'=4,'y'=2,'x'=2,'c'=2] {'q','y','x','c'}, dimensions={0} | all-to-all | bytes 65536 | tf_op jit(solution)/shard_map/all_to_all | solution.py:328
  336.6 8.6 %all_to_all.59 = f32[32,1,64]{2,1,0:T(1,128)S(1)} all-to-all(f32[32,1,64]{2,1,0:T(1,128)S(1)} %broadcast_in_dim.103), channel_id=1, replica_groups=mesh['q'=4,'y'=2,'x'=2,'c'=2] {'q','y','x','c'}, dimensions={0} | all-to-all | bytes 16384 | tf_op jit(solution)/shard_map/all_to_all | solution.py:338
  346.6 7.1 %convolution_convert_fusion = bf16[1024,1024]{1,0:T(8,128)(2,1)} fusion(bf16[1000,960]{0,1:T(8,128)(2,1)} %convert_element_type.298, f32[1024,1000]{0,1:T(8,128)} %copy-done.17, f32[1024]{0:T(1024)S(1)} %squeeze.128, f32[1024]{0:T(1024)S(1)} %multiply_add_fusion.2, s32[1024]{0:T(1024)S(1)} %sub.243), kind=kOutput, calls=%fused_computation.61 | convolution fusion | flops 2106392576 | bytes 8125440 | tf_op jit(solution)/shard_map/dot_general | solution.py:52
  354.5 5.6 fusion.175
  360.2 4.8 fusion.204
  367.8 4.3 fusion.176
  372.2 7.4 %collective-permute-done.19 = bf16[4,64,1024]{2,1,0:T(8,128)(2,1)S(1)} collective-permute-done((bf16[4,64,1024]{2,1,0:T(8,128)(2,1)S(1)}, bf16[4,64,1024]{2,1,0:T(8,128)(2,1)S(1)}, u32[]{:S(2)}, u32[]{:S(2)}) %collective-permute-start.19) | collective-permute-done | bytes 524320 | tf_op jit(solution)/shard_map/ppermute | solution.py:74
  379.6 10.4 %collective-permute-done.18 = bf16[4,64,1024]{2,1,0:T(8,128)(2,1)S(1)} collective-permute-done((bf16[4,64,1024]{2,1,0:T(8,128)(2,1)S(1)}, bf16[4,64,1024]{2,1,0:T(8,128)(2,1)S(1)}, u32[]{:S(2)}, u32[]{:S(2)}) %collective-permute-start.18) | collective-permute-done | bytes 524320 | tf_op jit(solution)/shard_map/ppermute | solution.py:74
  394.2 2.9 slice_add_fusion
  397.1 5.7 collective-permute-done.21
  403.8 13.2 %all-gather.2 = bf16[512,960]{1,0:T(8,128)(2,1)S(1)} all-gather(bf16[64,960]{1,0:T(8,128)(2,1)S(1)} %fusion.170), channel_id=4, replica_groups=mesh['q'=4,'y'=2,'x'=2,'c'=2] {'y','x','c'}, dimensions={0}, use_global_device_ids=true | all-gather | bytes 1105920 | tf_op jit(solution)/shard_map/all_gather | solution.py:143
  430.9 3.3 collective-permute-done.25
  446.2 3.9 convolution_convert_fusion.10
  470.6 3.4 all-to-all-start.6
  474.0 3.0 reduce-scatter.2.cloned.1.call-done
  480.7 4.0 reshape.754
  486.1 6.2 fusion.2
  495.5 4.5 all-to-all-start.7
  500.6 4.0 convert_add_fusion
  504.6 2.5 copy-done.5
  510.3 3.8 fusion.53
  514.1 22.8 %collective-permute-done.30 = bf16[352,960]{1,0:T(8,128)(2,1)S(1)} collective-permute-done((bf16[352,960]{1,0:T(8,128)(2,1)S(1)}, bf16[352,960]{1,0:T(8,128)(2,1)S(1)}, u32[]{:S(2)}, u32[]{:S(2)}) %collective-permute-start.30) | collective-permute-done | bytes 675872 | tf_op jit(solution)/shard_map/ppermute | solution.py:74
  536.9 15.2 %collective-permute-done.29 = bf16[352,960]{1,0:T(8,128)(2,1)} collective-permute-done((bf16[352,960]{1,0:T(8,128)(2,1)S(1)}, bf16[352,960]{1,0:T(8,128)(2,1)}, u32[]{:S(2)}, u32[]{:S(2)}) %collective-permute-start.29) | collective-permute-done | bytes 675872 | tf_op jit(solution)/shard_map/ppermute | solution.py:74
  555.4 2.6 collective-permute-start.33
  559.0 3.5 fusion.5
  562.8 4.0 multiply_reduce_fusion
  566.9 7.0 %collective-permute-done.32 = bf16[88,960]{1,0:T(8,128)(2,1)S(1)} collective-permute-done((bf16[88,960]{1,0:T(8,128)(2,1)S(1)}, bf16[88,960]{1,0:T(8,128)(2,1)S(1)}, u32[]{:S(2)}, u32[]{:S(2)}) %collective-permute-start.32) | collective-permute-done | bytes 168992 | tf_op jit(solution)/shard_map/ppermute | solution.py:74
  578.3 4.7 all-to-all-start.8
  587.3 3.6 collective-permute-done.35
  598.9 4.1 collective-permute-start.37
  607.0 11.0 %all_to_all.60 = f32[32,1,2]{2,1,0:T(1,128)S(1)} all-to-all(f32[32,1,2]{2,1,0:T(1,128)S(1)} %broadcast_in_dim.107), channel_id=1, replica_groups=mesh['q'=4,'y'=2,'x'=2,'c'=2] {'q','y','x','c'}, dimensions={0} | all-to-all | bytes 512 | tf_op jit(solution)/shard_map/all_to_all | solution.py:466
  620.1 4.2 add_multiply_fusion.1
  625.4 7.8 %add_multiply_fusion = (f32[1000,960]{0,1:T(8,128)}, f32[1000,960]{0,1:T(8,128)}, f32[1000,960]{0,1:T(8,128)}) fusion(f32[1000,960]{0,1:T(8,128)S(1)} %copy-done.1, f32[1000,960]{0,1:T(8,128)S(1)} %copy-done.3, f32[]{:T(128)S(6)} %div.148, f32[1000,960]{0,1:T(8,128)} %param.23, f32[1000,960]{0,1:T(8,128)} %param.22), kind=kLoop, calls=%fused_computation.23 | loop fusion | flops 14400000 | bytes 26880004 | tf_op jit(solution)/shard_map/mul | solution.py:107
  (511 shorter events, 215.2 us)
Async XLA Ops:
  8.5 5.8 collective-permute-start
  18.7 25.4 %collective-permute-start.1 = (bf16[328,960]{1,0:T(8,128)(2,1)}, bf16[328,960]{1,0:T(8,128)(2,1)}, u32[]{:S(2)}, u32[]{:S(2)}) collective-permute-start(bf16[328,960]{1,0:T(8,128)(2,1)} %maximum_maximum_fusion), channel_id=1, source_target_pairs={{0,16},{1,17},{2,18},{3,19},{4,20},{5,21},{6,22},{7,23}} | collective-permute-start | bytes 1889288 | tf_op jit(solution)/shard_map/ppermute | solution.py:217
  24.4 12.4 %all-to-all-start = ((s32[32,1,96]{2,1,0:T(1,128)}), s32[32,1,96]{2,1,0:T(1,128)S(1)}, u32[]{:S(2)}, u32[]{:S(2)}) async-start(s32[32,1,96]{2,1,0:T(1,128)} %bitcast), calls=%async_computation | async-start | bytes 32768 | tf_op jit(solution)/shard_map/all_to_all | solution.py:215
  36.8 21.5 %copy-start.53 = (s32[32,1,96]{2,1,0:T(1,128)}, s32[32,1,96]{2,1,0:T(1,128)S(1)}, u32[]{:S(2)}) copy-start(s32[32,1,96]{2,1,0:T(1,128)S(1)} %all-to-all-done) | copy-start | bytes 36868
  36.8 28.8 %all-to-all-start.1 = ((bf16[8,60,640]{2,1,0:T(8,128)(2,1)}), bf16[8,60,640]{2,1,0:T(8,128)(2,1)S(1)}, u32[]{:S(2)}, u32[]{:S(2)}) async-start(bf16[8,60,640]{2,1,0:T(8,128)(2,1)} %reshape.826), calls=%async_computation.1 | async-start | bytes 1310720 | tf_op jit(solution)/shard_map/all_to_all | solution.py:209
  45.3 20.2 %collective-permute-start.2 = (bf16[328,960]{1,0:T(8,128)(2,1)S(1)}, bf16[328,960]{1,0:T(8,128)(2,1)S(1)}, u32[]{:S(2)}, u32[]{:S(2)}) collective-permute-start(bf16[328,960]{1,0:T(8,128)(2,1)S(1)} %broadcast_select_fusion), channel_id=1, source_target_pairs={{0,8},{16,24},{1,9},{17,25},{2,10},{18,26},{3,11},{19,27},{4,12},{... | collective-permute-start | bytes 1889288 | tf_op jit(solution)/shard_map/ppermute | solution.py:219
  65.5 57.6 %copy-start.26 = (bf16[328,960]{1,0:T(8,128)(2,1)}, bf16[328,960]{1,0:T(8,128)(2,1)S(1)}, u32[]{:S(2)}) copy-start(bf16[328,960]{1,0:T(8,128)(2,1)S(1)} %broadcast_select_fusion.1) | copy-start | bytes 1889284
  65.6 57.6 %copy-start.28 = (bf16[8,60,640]{2,1,0:T(8,128)(2,1)}, bf16[8,60,640]{2,1,0:T(8,128)(2,1)S(1)}, u32[]{:S(2)}) copy-start(bf16[8,60,640]{2,1,0:T(8,128)(2,1)S(1)} %all-to-all-done.1) | copy-start | bytes 1843204
  65.6 59.4 %all-to-all-start.2 = ((bf16[32,24,960]{2,1,0:T(8,128)(2,1)}), bf16[32,24,960]{2,1,0:T(8,128)(2,1)}, u32[]{:S(2)}, u32[]{:S(2)}) async-start(bf16[32,24,960]{2,1,0:T(8,128)(2,1)} %bitcast.2), calls=%async_computation.2 | async-start | bytes 3145728 | tf_op jit(solution)/shard_map/all_to_all | solution.py:190
  73.1 35.7 %collective-permute-start.5 = (bf16[328,960]{1,0:T(8,128)(2,1)S(1)}, bf16[328,960]{1,0:T(8,128)(2,1)S(1)}, u32[]{:S(2)}, u32[]{:S(2)}) collective-permute-start(bf16[328,960]{1,0:T(8,128)(2,1)S(1)} %broadcast_select_fusion.1), channel_id=1, source_target_pairs={{0,6},{2,4},{4,2},{6,0},{1,7},{3,5},{5,3},{7,1},{8,14},{10,12},{12... | collective-permute-start | bytes 1889288 | tf_op jit(solution)/shard_map/ppermute | solution.py:74
  75.4 45.4 %collective-permute-start.4 = (bf16[328,960]{1,0:T(8,128)(2,1)S(1)}, bf16[328,960]{1,0:T(8,128)(2,1)S(1)}, u32[]{:S(2)}, u32[]{:S(2)}) collective-permute-start(bf16[328,960]{1,0:T(8,128)(2,1)S(1)} %broadcast_select_fusion.1), channel_id=1, source_target_pairs={{0,4},{2,6},{4,0},{6,2},{1,5},{3,7},{5,1},{7,3},{8,12},{10,14},{12... | collective-permute-start | bytes 1889288 | tf_op jit(solution)/shard_map/ppermute | solution.py:74
  75.7 47.4 %collective-permute-start.3 = (bf16[328,960]{1,0:T(8,128)(2,1)S(1)}, bf16[328,960]{1,0:T(8,128)(2,1)S(1)}, u32[]{:S(2)}, u32[]{:S(2)}) collective-permute-start(bf16[328,960]{1,0:T(8,128)(2,1)S(1)} %broadcast_select_fusion.1), channel_id=1, source_target_pairs={{0,2},{2,0},{4,6},{6,4},{1,3},{3,1},{5,7},{7,5},{8,10},{10,8},{12,... | collective-permute-start | bytes 1889288 | tf_op jit(solution)/shard_map/ppermute | solution.py:74
  125.0 22.7 %collective-permute-start.6 = (bf16[4,328,960]{2,1,0:T(8,128)(2,1)S(1)}, bf16[4,328,960]{2,1,0:T(8,128)(2,1)}, u32[]{:S(2)}, u32[]{:S(2)}) collective-permute-start(bf16[4,328,960]{2,1,0:T(8,128)(2,1)S(1)} %pad_maximum_fusion), channel_id=1, source_target_pairs={{0,1},{1,0},{2,3},{3,2},{4,5},{5,4},{6,7},{7,6},{8,9},{9,8},{10,11... | collective-permute-start | bytes 7557128 | tf_op jit(solution)/shard_map/ppermute | solution.py:74
  135.6 30.1 %all-to-all-start.3 = ((bf16[32,8,960]{2,1,0:T(8,128)(2,1)}), bf16[32,8,960]{2,1,0:T(8,128)(2,1)}, u32[]{:S(2)}, u32[]{:S(2)}) async-start(bf16[32,8,960]{2,1,0:T(8,128)(2,1)} %bitcast.298), calls=%async_computation.3 | async-start | bytes 1048576 | tf_op jit(solution)/shard_map/all_to_all | solution.py:190
  140.0 56.0 %all-gather.5.cloned.1.call-start = ((), (), s32[]{:S(2)}) async-start(), calls=%async_computation.11 | async-start | bytes 3072000 | tf_op jit(solution)/shard_map/all_gather | solution.py:237
  143.2 333.8 %reduce-scatter.2.cloned.1.call-start = ((), (), s32[]{:S(2)}) async-start(), calls=%async_computation.12 | async-start | bytes 3072000 | tf_op jit(solution)/shard_map/reduce_scatter | solution.py:404
  170.6 36.6 %copy-start.55 = (bf16[64,960]{1,0:T(8,128)(2,1)}, bf16[64,960]{1,0:T(8,128)(2,1)S(1)}, u32[]{:S(2)}) copy-start(bf16[64,960]{1,0:T(8,128)(2,1)S(1)} %convolution_convert_fusion.12) | copy-start | bytes 368644
  227.5 13.6 %copy-start.32 = (bf16[64,5,3,64]{0,3,2,1:T(8,128)(2,1)}, bf16[64,5,3,64]{0,3,2,1:T(8,128)(2,1)S(1)}, u32[]{:S(2)}) copy-start(bf16[64,5,3,64]{0,3,2,1:T(8,128)(2,1)S(1)} %copy.211) | copy-start | bytes 368644
  227.5 13.6 %copy-start.7 = (bf16[2,480,640]{2,1,0:T(8,128)(2,1)S(1)}, bf16[2,480,640]{2,1,0:T(8,128)(2,1)}, u32[]{:S(2)}) copy-start(bf16[2,480,640]{2,1,0:T(8,128)(2,1)} %slice.376) | copy-start | bytes 3686404
  229.2 12.9 %copy-start.94 = (f32[64]{0:T(128)}, f32[64]{0:T(128)S(1)}, u32[]{:S(2)}) copy-start(f32[64]{0:T(128)S(1)} %add_rsqrt_fusion.2) | copy-start | bytes 772
  245.2 2.3 collective-permute-start.7
  251.1 6.1 collective-permute-start.10
  252.2 8.3 %collective-permute-start.9 = (bf16[64,1024]{1,0:T(8,128)(2,1)}, bf16[64,1024]{1,0:T(8,128)(2,1)S(1)}, u32[]{:S(2)}, u32[]{:S(2)}) collective-permute-start(bf16[64,1024]{1,0:T(8,128)(2,1)} %get-tuple-element.157), channel_id=1, source_target_pairs={{0,4},{2,6},{4,0},{6,2},{1,5},{3,7},{5,1},{7,3},{8,12},{10,14},{12... | collective-permute-start | bytes 393224 | tf_op jit(solution)/shard_map/ppermute | solution.py:74
  253.4 7.7 %collective-permute-start.8 = (bf16[64,1024]{1,0:T(8,128)(2,1)}, bf16[64,1024]{1,0:T(8,128)(2,1)}, u32[]{:S(2)}, u32[]{:S(2)}) collective-permute-start(bf16[64,1024]{1,0:T(8,128)(2,1)} %get-tuple-element.155), channel_id=1, source_target_pairs={{0,2},{2,0},{4,6},{6,4},{1,3},{3,1},{5,7},{7,5},{8,10},{10,8},{12,... | collective-permute-start | bytes 393224 | tf_op jit(solution)/shard_map/ppermute | solution.py:74
  262.4 26.3 %copy-start.90 = (f32[64]{0:T(128)}, f32[64]{0:T(128)S(1)}, u32[]{:S(2)}) copy-start(f32[64]{0:T(128)S(1)} %add_rsqrt_fusion.1) | copy-start | bytes 772
  275.5 9.8 %collective-permute-start.11 = (bf16[4,64,1024]{2,1,0:T(8,128)(2,1)S(1)}, bf16[4,64,1024]{2,1,0:T(8,128)(2,1)S(1)}, u32[]{:S(2)}, u32[]{:S(2)}) collective-permute-start(bf16[4,64,1024]{2,1,0:T(8,128)(2,1)S(1)} %bitcast.295), channel_id=1, source_target_pairs={{0,2},{2,0},{1,3},{3,1},{4,6},{6,4},{5,7},{7,5},{8,10},{10,8},{9,1... | collective-permute-start | bytes 1572872 | tf_op jit(solution)/shard_map/ppermute | solution.py:74
  275.8 10.5 %collective-permute-start.12 = (bf16[4,64,1024]{2,1,0:T(8,128)(2,1)S(1)}, bf16[4,64,1024]{2,1,0:T(8,128)(2,1)S(1)}, u32[]{:S(2)}, u32[]{:S(2)}) collective-permute-start(bf16[4,64,1024]{2,1,0:T(8,128)(2,1)S(1)} %bitcast.296), channel_id=1, source_target_pairs={{0,4},{4,0},{1,5},{5,1},{2,6},{6,2},{3,7},{7,3},{8,12},{12,8},{9,1... | collective-permute-start | bytes 1572872 | tf_op jit(solution)/shard_map/ppermute | solution.py:74
  285.3 6.9 %collective-permute-start.13 = (bf16[2,64,1024]{2,1,0:T(8,128)(2,1)S(1)}, bf16[2,64,1024]{2,1,0:T(8,128)(2,1)S(1)}, u32[]{:S(2)}, u32[]{:S(2)}) collective-permute-start(bf16[2,64,1024]{2,1,0:T(8,128)(2,1)S(1)} %slice.463), channel_id=1, source_target_pairs={{0,4},{4,0},{1,5},{5,1},{2,6},{6,2},{3,7},{7,3},{8,12},{12,8},{9,1... | collective-permute-start | bytes 786440 | tf_op jit(solution)/shard_map/ppermute | solution.py:74
  286.2 13.3 %copy-start.99 = (s32[32]{0:T(128)S(1)}, s32[32]{0:T(128)}, u32[]{:S(2)}) copy-start(s32[32]{0:T(128)} %constant.386.clone) | copy-start | bytes 388
  286.2 13.3 %copy-start.101 = (s32[32]{0:T(128)S(1)}, s32[32]{0:T(128)}, u32[]{:S(2)}) copy-start(s32[32]{0:T(128)} %copy-done.100) | copy-start | bytes 388
  286.2 13.9 %copy-start.54 = (s32[32,1,96]{2,1,0:T(1,128)S(1)}, s32[32,1,96]{2,1,0:T(1,128)}, u32[]{:S(2)}) copy-start(s32[32,1,96]{2,1,0:T(1,128)} %copy-done.53) | copy-start | bytes 36868
  286.3 6.7 %collective-permute-start.14 = (bf16[2,64,1024]{2,1,0:T(8,128)(2,1)S(1)}, bf16[2,64,1024]{2,1,0:T(8,128)(2,1)S(1)}, u32[]{:S(2)}, u32[]{:S(2)}) collective-permute-start(bf16[2,64,1024]{2,1,0:T(8,128)(2,1)S(1)} %slice.464), channel_id=1, source_target_pairs={{0,2},{2,0},{1,3},{3,1},{4,6},{6,4},{5,7},{7,5},{8,10},{10,8},{9,1... | collective-permute-start | bytes 786440 | tf_op jit(solution)/shard_map/ppermute | solution.py:74
  293.7 14.0 %collective-permute-start.15 = (bf16[1024,1024]{1,0:T(8,128)(2,1)}, bf16[1024,1024]{1,0:T(8,128)(2,1)}, u32[]{:S(2)}, u32[]{:S(2)}) collective-permute-start(bf16[1024,1024]{1,0:T(8,128)(2,1)} %bitcast.55), channel_id=1, source_target_pairs={{0,1},{1,0},{2,3},{3,2},{4,5},{5,4},{6,7},{7,6},{8,9},{9,8},{10,11... | collective-permute-start | bytes 6291464 | tf_op jit(solution)/shard_map/ppermute | solution.py:74
  353.8 6.4 collective-permute-start.16
  365.1 14.5 %collective-permute-start.19 = (bf16[4,64,1024]{2,1,0:T(8,128)(2,1)S(1)}, bf16[4,64,1024]{2,1,0:T(8,128)(2,1)S(1)}, u32[]{:S(2)}, u32[]{:S(2)}) collective-permute-start(bf16[4,64,1024]{2,1,0:T(8,128)(2,1)S(1)} %bitcast.326), channel_id=1, source_target_pairs={{0,6},{2,4},{4,2},{6,0},{1,7},{3,5},{5,3},{7,1},{8,14},{10,12},{12... | collective-permute-start | bytes 1572872 | tf_op jit(solution)/shard_map/ppermute | solution.py:74
  365.5 24.5 %collective-permute-start.18 = (bf16[4,64,1024]{2,1,0:T(8,128)(2,1)S(1)}, bf16[4,64,1024]{2,1,0:T(8,128)(2,1)S(1)}, u32[]{:S(2)}, u32[]{:S(2)}) collective-permute-start(bf16[4,64,1024]{2,1,0:T(8,128)(2,1)S(1)} %bitcast.325), channel_id=1, source_target_pairs={{0,4},{2,6},{4,0},{6,2},{1,5},{3,7},{5,1},{7,3},{8,12},{10,14},{12... | collective-permute-start | bytes 1572872 | tf_op jit(solution)/shard_map/ppermute | solution.py:74
  366.6 23.4 %collective-permute-start.17 = (bf16[4,64,1024]{2,1,0:T(8,128)(2,1)S(1)}, bf16[4,64,1024]{2,1,0:T(8,128)(2,1)S(1)}, u32[]{:S(2)}, u32[]{:S(2)}) collective-permute-start(bf16[4,64,1024]{2,1,0:T(8,128)(2,1)S(1)} %bitcast.324), channel_id=1, source_target_pairs={{0,2},{2,0},{4,6},{6,4},{1,3},{3,1},{5,7},{7,5},{8,10},{10,8},{12,... | collective-permute-start | bytes 1572872 | tf_op jit(solution)/shard_map/ppermute | solution.py:74
  390.4 6.7 %collective-permute-start.22 = (bf16[64,1024]{1,0:T(8,128)(2,1)S(1)}, bf16[64,1024]{1,0:T(8,128)(2,1)S(1)}, u32[]{:S(2)}, u32[]{:S(2)}) collective-permute-start(bf16[64,1024]{1,0:T(8,128)(2,1)S(1)} %get-tuple-element.153), channel_id=1, source_target_pairs={{0,24},{8,16},{16,8},{24,0},{1,25},{9,17},{17,9},{25,1},{2,26},{10... | collective-permute-start | bytes 393224 | tf_op jit(solution)/shard_map/ppermute | solution.py:74
  390.8 12.0 %collective-permute-start.21 = (bf16[64,1024]{1,0:T(8,128)(2,1)S(1)}, bf16[64,1024]{1,0:T(8,128)(2,1)S(1)}, u32[]{:S(2)}, u32[]{:S(2)}) collective-permute-start(bf16[64,1024]{1,0:T(8,128)(2,1)S(1)} %get-tuple-element.154), channel_id=1, source_target_pairs={{0,16},{8,24},{16,0},{24,8},{1,17},{9,25},{17,1},{25,9},{2,18},{10... | collective-permute-start | bytes 393224 | tf_op jit(solution)/shard_map/ppermute | solution.py:74
  392.2 10.7 %collective-permute-start.20 = (bf16[64,1024]{1,0:T(8,128)(2,1)S(1)}, bf16[64,1024]{1,0:T(8,128)(2,1)S(1)}, u32[]{:S(2)}, u32[]{:S(2)}) collective-permute-start(bf16[64,1024]{1,0:T(8,128)(2,1)S(1)} %get-tuple-element.152), channel_id=1, source_target_pairs={{0,8},{8,0},{16,24},{24,16},{1,9},{9,1},{17,25},{25,17},{2,10},{10... | collective-permute-start | bytes 393224 | tf_op jit(solution)/shard_map/ppermute | solution.py:74
  397.1 19.9 %copy-start.37 = (f32[512,640]{1,0:T(8,128)S(1)}, f32[512,640]{1,0:T(8,128)}, u32[]{:S(2)}) copy-start(f32[512,640]{1,0:T(8,128)} %copy-done.36) | copy-start | bytes 3932164
  397.1 19.9 %copy-start.58 = (bf16[320,640]{1,0:T(8,128)(2,1)S(1)}, bf16[320,640]{1,0:T(8,128)(2,1)}, u32[]{:S(2)}) copy-start(bf16[320,640]{1,0:T(8,128)(2,1)} %slice_bitcast_fusion.2) | copy-start | bytes 1228804
  397.1 19.9 %copy-start.70 = (bf16[160,320]{1,0:T(8,128)(2,1)S(1)}, bf16[160,320]{1,0:T(8,128)(2,1)}, u32[]{:S(2)}) copy-start(bf16[160,320]{1,0:T(8,128)(2,1)} %copy-done.69) | copy-start | bytes 307204
  397.1 19.9 %copy-start.72 = (bf16[160,320]{1,0:T(8,128)(2,1)S(1)}, bf16[160,320]{1,0:T(8,128)(2,1)}, u32[]{:S(2)}) copy-start(bf16[160,320]{1,0:T(8,128)(2,1)} %copy-done.71) | copy-start | bytes 307204
  418.9 3.4 collective-permute-start.23
  424.7 6.2 collective-permute-start.26
  425.9 8.3 %collective-permute-start.25 = (bf16[64,1024]{1,0:T(8,128)(2,1)}, bf16[64,1024]{1,0:T(8,128)(2,1)}, u32[]{:S(2)}, u32[]{:S(2)}) collective-permute-start(bf16[64,1024]{1,0:T(8,128)(2,1)} %get-tuple-element.151), channel_id=1, source_target_pairs={{0,4},{2,6},{4,0},{6,2},{1,5},{3,7},{5,1},{7,3},{8,12},{10,14},{12... | collective-permute-start | bytes 393224 | tf_op jit(solution)/shard_map/ppermute | solution.py:74
  426.3 7.9 %collective-permute-start.24 = (bf16[64,1024]{1,0:T(8,128)(2,1)}, bf16[64,1024]{1,0:T(8,128)(2,1)}, u32[]{:S(2)}, u32[]{:S(2)}) collective-permute-start(bf16[64,1024]{1,0:T(8,128)(2,1)} %get-tuple-element.149), channel_id=1, source_target_pairs={{0,2},{2,0},{4,6},{6,4},{1,3},{3,1},{5,7},{7,5},{8,10},{10,8},{12,... | collective-permute-start | bytes 393224 | tf_op jit(solution)/shard_map/ppermute | solution.py:74
  470.6 21.7 %all-to-all-start.6 = ((bf16[32,8,960]{2,1,0:T(8,128)(2,1)}), bf16[32,8,960]{2,1,0:T(8,128)(2,1)}, u32[]{:S(2)}, u32[]{:S(2)}) async-start(bf16[32,8,960]{2,1,0:T(8,128)(2,1)} %bitcast.103), calls=%async_computation.7 | async-start | bytes 1048576 | tf_op jit(solution)/shard_map/all_to_all | solution.py:190
  494.4 6.2 collective-permute-start.27
  495.5 59.8 %all-to-all-start.7 = ((bf16[32,24,960]{2,1,0:T(8,128)(2,1)}), bf16[32,24,960]{2,1,0:T(8,128)(2,1)}, u32[]{:S(2)}, u32[]{:S(2)}) async-start(bf16[32,24,960]{2,1,0:T(8,128)(2,1)} %bitcast.104), calls=%async_computation.8 | async-start | bytes 3145728 | tf_op jit(solution)/shard_map/all_to_all | solution.py:190
  507.4 29.5 %collective-permute-start.30 = (bf16[352,960]{1,0:T(8,128)(2,1)S(1)}, bf16[352,960]{1,0:T(8,128)(2,1)S(1)}, u32[]{:S(2)}, u32[]{:S(2)}) collective-permute-start(bf16[352,960]{1,0:T(8,128)(2,1)S(1)} %get-tuple-element.120), channel_id=1, source_target_pairs={{0,6},{2,4},{4,2},{6,0},{1,7},{3,5},{5,3},{7,1},{8,14},{10,12},{12... | collective-permute-start | bytes 2027528 | tf_op jit(solution)/shard_map/ppermute | solution.py:74
  509.5 42.5 %collective-permute-start.29 = (bf16[352,960]{1,0:T(8,128)(2,1)S(1)}, bf16[352,960]{1,0:T(8,128)(2,1)}, u32[]{:S(2)}, u32[]{:S(2)}) collective-permute-start(bf16[352,960]{1,0:T(8,128)(2,1)S(1)} %get-tuple-element.121), channel_id=1, source_target_pairs={{0,4},{2,6},{4,0},{6,2},{1,5},{3,7},{5,1},{7,3},{8,12},{10,14},{12... | collective-permute-start | bytes 2027528 | tf_op jit(solution)/shard_map/ppermute | solution.py:74
  509.8 43.3 %collective-permute-start.28 = (bf16[352,960]{1,0:T(8,128)(2,1)S(1)}, bf16[352,960]{1,0:T(8,128)(2,1)}, u32[]{:S(2)}, u32[]{:S(2)}) collective-permute-start(bf16[352,960]{1,0:T(8,128)(2,1)S(1)} %get-tuple-element.119), channel_id=1, source_target_pairs={{0,2},{2,0},{4,6},{6,4},{1,3},{3,1},{5,7},{7,5},{8,10},{10,8},{12,... | collective-permute-start | bytes 2027528 | tf_op jit(solution)/shard_map/ppermute | solution.py:74
  555.4 11.4 %collective-permute-start.33 = (bf16[88,960]{1,0:T(8,128)(2,1)S(1)}, bf16[88,960]{1,0:T(8,128)(2,1)S(1)}, u32[]{:S(2)}, u32[]{:S(2)}) collective-permute-start(bf16[88,960]{1,0:T(8,128)(2,1)S(1)} %get-tuple-element.131), channel_id=1, source_target_pairs={{0,24},{8,16},{16,8},{24,0},{1,25},{9,17},{17,9},{25,1},{2,26},{10... | collective-permute-start | bytes 506888 | tf_op jit(solution)/shard_map/ppermute | solution.py:74
  558.0 15.9 %collective-permute-start.32 = (bf16[88,960]{1,0:T(8,128)(2,1)S(1)}, bf16[88,960]{1,0:T(8,128)(2,1)S(1)}, u32[]{:S(2)}, u32[]{:S(2)}) collective-permute-start(bf16[88,960]{1,0:T(8,128)(2,1)S(1)} %get-tuple-element.132), channel_id=1, source_target_pairs={{0,16},{8,24},{16,0},{24,8},{1,17},{9,25},{17,1},{25,9},{2,18},{10... | collective-permute-start | bytes 506888 | tf_op jit(solution)/shard_map/ppermute | solution.py:74
  558.0 15.8 %collective-permute-start.31 = (bf16[88,960]{1,0:T(8,128)(2,1)S(1)}, bf16[88,960]{1,0:T(8,128)(2,1)S(1)}, u32[]{:S(2)}, u32[]{:S(2)}) collective-permute-start(bf16[88,960]{1,0:T(8,128)(2,1)S(1)} %get-tuple-element.130), channel_id=1, source_target_pairs={{0,8},{8,0},{16,24},{24,16},{1,9},{9,1},{17,25},{25,17},{2,10},{10... | collective-permute-start | bytes 506888 | tf_op jit(solution)/shard_map/ppermute | solution.py:74
  562.8 13.7 %copy-start.27 = (bf16[1,480,640]{2,1,0:T(8,128)(2,1)S(1)}, bf16[1,480,640]{2,1,0:T(8,128)(2,1)}, u32[]{:S(2)}) copy-start(bf16[1,480,640]{2,1,0:T(8,128)(2,1)} %reduce-scatter.2.cloned.1.call-done) | copy-start | bytes 1843204
  574.0 12.2 %collective-permute-start.36 = (bf16[88,960]{1,0:T(8,128)(2,1)S(1)}, bf16[88,960]{1,0:T(8,128)(2,1)S(1)}, u32[]{:S(2)}, u32[]{:S(2)}) collective-permute-start(bf16[88,960]{1,0:T(8,128)(2,1)S(1)} %fusion.90), channel_id=1, source_target_pairs={{16,0},{17,1},{18,2},{19,3},{20,4},{21,5},{22,6},{23,7}} | collective-permute-start | bytes 506888 | tf_op jit(solution)/shard_map/ppermute | solution.py:438
  575.3 10.9 %collective-permute-start.34 = (bf16[88,960]{1,0:T(8,128)(2,1)S(1)}, bf16[88,960]{1,0:T(8,128)(2,1)S(1)}, u32[]{:S(2)}, u32[]{:S(2)}) collective-permute-start(bf16[88,960]{1,0:T(8,128)(2,1)S(1)} %fusion.90), channel_id=1, source_target_pairs={{24,0},{25,1},{26,2},{27,3},{28,4},{29,5},{30,6},{31,7}} | collective-permute-start | bytes 506888 | tf_op jit(solution)/shard_map/ppermute | solution.py:438
  578.3 16.7 %all-to-all-start.8 = ((bf16[8,60,640]{2,1,0:T(8,128)(2,1)}), bf16[8,60,640]{2,1,0:T(8,128)(2,1)S(1)}, u32[]{:S(2)}, u32[]{:S(2)}) async-start(bf16[8,60,640]{2,1,0:T(8,128)(2,1)} %reshape.765), calls=%async_computation.9 | async-start | bytes 1310720 | tf_op jit(solution)/shard_map/all_to_all | solution.py:428
  583.0 7.9 %collective-permute-start.35 = (bf16[88,960]{1,0:T(8,128)(2,1)S(1)}, bf16[88,960]{1,0:T(8,128)(2,1)S(1)}, u32[]{:S(2)}, u32[]{:S(2)}) collective-permute-start(bf16[88,960]{1,0:T(8,128)(2,1)S(1)} %fusion.90), channel_id=1, source_target_pairs={{8,0},{9,1},{10,2},{11,3},{12,4},{13,5},{14,6},{15,7}} | collective-permute-start | bytes 506888 | tf_op jit(solution)/shard_map/ppermute | solution.py:438
  597.5 22.6 %copy-start.12 = (f32[307290]{0:T(1024)S(1)}, f32[307290]{0:T(1024)}, u32[]{:S(2)}) copy-start(f32[307290]{0:T(1024)} %param.18) | copy-start | bytes 3687484
  598.9 5.0 collective-permute-start.37
  (87 other events, 256.2 us)
Sparse Core Ops, SparseCore 0:
  143.3 52.5 all-gather.4
  429.3 47.7 reduce-scatter.1

commit v7 on v6

--- a/solution.py
+++ b/solution.py
@@ -220,19 +220,20 @@
         first = jnp.where((q_index == 1) | (q_index == 3), stepped, first)
         answer, first, got = lax.optimization_barrier((answer, first, got))
         returned = [exchange(blocks) for blocks in answer]
-        level = jnp.stack([first] + [flip(first, ("y", "x"), k, 4) for k in (1, 2, 3)])
+        level = lax.all_gather(first, ("y", "x"))
         mixed = jnp.where(q_index == 3, down_pack(chunk.reshape(SHARE, D)), got.reshape(480, 2 * UNIT))
+        mixed, level = lax.optimization_barrier((mixed, level))
         level, returned[0] = lax.optimization_barrier((level, returned[0]))
-        level = jnp.concatenate([level, flip(level, "c", 1, 2)])
-
-        def from_place(p):
-            k = p_index ^ p
-            return pick_block(level, (k & 1) * 4 + (k >> 1))
-
-        gains = from_place(0)[SHARE : SHARE + 3].astype(f32)
-        w_q = jnp.concatenate([from_place(p)[:TOP] for p in range(5)])
-        w_kv = jnp.concatenate([from_place(p)[TOP:SHARE] for p in range(5)]).reshape(D, KV)
-        w_out = jnp.concatenate([from_place(p)[:SHARE] for p in range(5, 8)])
+        other = flip(level, "c", 1, 2)
+
+        def from_place(p, low, high):
+            mine, theirs = level[p // 2, low:high], other[p // 2, low:high]
+            return jnp.where(c_index == p % 2, mine, theirs)
+
+        gains = from_place(0, SHARE, SHARE + 3).astype(f32)
+        w_q = jnp.concatenate([from_place(p, 0, TOP) for p in range(5)])
+        w_kv = jnp.concatenate([from_place(p, TOP, SHARE) for p in range(5)]).reshape(D, KV)
+        w_out = jnp.concatenate([from_place(p, 0, SHARE) for p in range(5, 8)])
         returned[1], w_q, w_kv, w_out = lax.optimization_barrier((returned[1], w_q, w_kv, w_out))
         column = lax.all_gather(mixed, "q")
     else:
@@ -261,8 +262,6 @@
     x_pick = dot(pick, x_low) * emb_mult
     query = rotate(dot(h_pick, w_q), cosine_pick, sine_pick).astype(bf16)
     key_value = dot(h_attn, w_kv)
-    if aligned:
-        column, key_value = lax.optimization_barrier((column, key_value))
     key = rotate(key_value[:, :UNIT], cosine, sine).astype(bf16)
     value = key_value[:, UNIT:].astype(bf16)
 
@@ -290,6 +289,7 @@
     x_one = x_pick + dot(attended, w_out)
 
     if aligned:
+        column, x_one = lax.optimization_barrier((column, x_one))
         w_gu = column[1:3].reshape(D, 2 * SHARE)
         w_down = down_unpack(column[3])
     w_gu = jnp.pad(w_gu, ((0, WIDE - D), (0, 0)))
@@ -434,7 +434,9 @@
         for low, high, rows in zip(cuts_back, cuts_back[1:], arrived):
             table_grad = table_grad + dot(rows_between(low, high), rows, 0, 0)
         table_squares = jnp.sum(table_grad * table_grad)
-        quarter, table_squares = lax.optimization_barrier((quarter.astype(bf16), table_squares))
+        quarter = quarter.astype(bf16)
+        squares = jnp.sum(quarter.astype(f32) ** 2) + jnp.sum(share.astype(f32) ** 2) + table_squares
+        quarter, squares = lax.optimization_barrier((quarter, squares))
         quarters = [quarter] + [lax.ppermute(quarter, "q", [(k, 0)]) for k in (1, 2, 3)]
         first = jnp.concatenate(quarters)
         gain_out = first[SHARE : SHARE + 3].reshape(-1)
@@ -461,7 +463,8 @@
     stream = jnp.concatenate([behind, mine, jnp.zeros((tail,), bf16)])
     layer_grad = lax.dynamic_slice(stream, (drift * me,), (shard,)).astype(f32)
 
-    squares = jnp.sum(layer_grad * layer_grad) + table_squares
+    if not aligned:
+        squares = jnp.sum(layer_grad * layer_grad) + table_squares
     sums = jnp.broadcast_to(jnp.stack([squares, my_loss])[None], (devices, 2))
     sums = jnp.sum(lax.all_to_all(sums, ALL, split_axis=0, concat_axis=0, tiled=True), axis=0)
     grad_norm = jnp.sqrt(sums[0])

time: 655 us -> 615 us (0.939)
  local copies, waits for them, and re-layouts: 111 us -> 82.5 us
  waiting for transfers between devices: 175 us -> 158 us
  other arithmetic: 81.1 us -> 96.9 us
  blocking collectives: 67 us -> 59.1 us
    ppermute x31 -> x28, waiting for transfers between devices: 140 us -> 93.3 us  [flip(): return lax.ppermute(rows, axes, [(i, i ^ bits) for i in range(size)])]
    all_gather x0 -> x1, waiting for transfers between devices: none -> 46.8 us  [local(): level = lax.all_gather(first, ('y', 'x'))]
    all_gather x1, waiting for transfers between devices: 22 us -> 0.02 us  [local(): column = lax.all_gather(mixed, 'q')]
    unnamed x0 -> x8, other arithmetic: none -> 11.9 us
    all_to_all x1 -> x0, blocking collectives: 11 us -> none  [local(): lax.all_to_all(sums, ALL, split_axis=0, concat_axis=0, tiled=True)]
    unnamed x221 -> x209, local copies, waits for them, and re-layouts: 30.2 us -> 20.4 us
    ppermute x31 -> x28, starting transfers between devices: 33 us -> 27.9 us  [flip(): return lax.ppermute(rows, axes, [(i, i ^ bits) for i in range(size)])]
  transfers between devices with their start and end apart: 47 -> 46, of which waited for: 24 -> 23; matrix products, arithmetic and copies ran while one was open for 26% -> 33% of each run, Pallas kernels for 0% -> 0%
where the time goes in v7:
time: 615 us; the launch traced here: 603 us
  waiting for transfers between devices  158 us (26%)
  other arithmetic  96.9 us (16%)
  matrix products  93.4 us (15%)
  starting transfers between devices  92.4 us (15%)
  local copies, waits for them, and re-layouts  82.5 us (13%)
  blocking collectives  59.1 us (10%)
  between operations  21.4 us (3%)
    ppermute x28, waiting for transfers between devices, flip(): return lax.ppermute(rows, axes, [(i, i ^ bits) for i in range(size)])  93.3 us
    dot_general x39, matrix products, dot(): lax.dot_general(left, right, (((left_dim,), (right_dim,)), ((), ())), pre...  78.2 us
    all_gather x1, waiting for transfers between devices, local(): level = lax.all_gather(first, ('y', 'x'))  46.8 us
    ppermute x28, starting transfers between devices, flip(): return lax.ppermute(rows, axes, [(i, i ^ bits) for i in range(size)])  27.9 us
    all_gather x2, blocking collectives, spread_plane(): return widen(lax.all_gather(rows, PLANE).reshape(-1, D))  24.7 us
    unnamed x209, local copies, waits for them, and re-layouts  20.4 us
    all_to_all x4, starting transfers between devices, exchange(): lax.all_to_all(blocks, ALL, split_axis=0, concat_axis=0, tiled=True)  19.3 us
    mul x2, other arithmetic, adamw_step(): return (new_one, new_two, -RATE * (ratio + DECAY * param))  14.7 us
  transfers between devices with their start and end apart: 46, of which 23 were waited for; matrix products, arithmetic and copies ran while one was open for 33% of the time, Pallas kernels for 0%

profile of v7, /device:TPU:1, one launch (start us, length us, event | category | flops | bytes accessed | tf_op | source)
XLA Modules:
  0.0 603.5 jit_solution(5773549072251278965)
XLA Ops:
  17.9 5.8 collective-permute-start.1
  23.6 4.2 all-to-all-start
  27.8 3.7 convert_element_type.304
  35.7 6.5 %all-to-all-start.1 = ((bf16[8,60,640]{2,1,0:T(8,128)(2,1)}), bf16[8,60,640]{2,1,0:T(8,128)(2,1)S(1)}, u32[]{:S(2)}, u32[]{:S(2)}) async-start(bf16[8,60,640]{2,1,0:T(8,128)(2,1)} %reshape.806), calls=%async_computation.1 | async-start | bytes 1310720 | tf_op jit(solution)/shard_map/all_to_all | solution.py:209
  43.2 6.0 collective-permute-start.2
  49.2 3.0 fusion.23
  52.2 2.6 copy.199
  55.4 2.4 convolution_convert_fusion.9
  58.8 4.6 collective-permute-done.2
  64.4 7.6 %all-to-all-start.2 = ((bf16[32,24,960]{2,1,0:T(8,128)(2,1)}), bf16[32,24,960]{2,1,0:T(8,128)(2,1)}, u32[]{:S(2)}, u32[]{:S(2)}) async-start(bf16[32,24,960]{2,1,0:T(8,128)(2,1)} %bitcast.2), calls=%async_computation.2 | async-start | bytes 3145728 | tf_op jit(solution)/shard_map/all_to_all | solution.py:190
  73.2 46.8 %all-gather.8.cloned.1.call-done = bf16[1312,960]{1,0:T(8,128)(2,1)} async-done(((bf16[328,960]{1,0:T(8,128)(2,1)}), bf16[1312,960]{1,0:T(8,128)(2,1)}) %all-gather.8.cloned.1.call-update) | async-done | bytes 2519056 | tf_op jit(solution)/shard_map/all_gather | solution.py:223
  124.5 3.8 all-to-all-start.3
  129.5 3.9 fusion.26
  136.4 2.5 fusion.67
  144.9 2.8 reshape.702
  155.3 2.3 fusion.21
  163.3 2.7 fusion.196
  173.2 2.3 copy.241
  177.1 3.7 fusion.192
  180.7 3.6 convolution_convert_fusion.11
  192.5 11.5 %all-gather.2 = bf16[512,960]{1,0:T(8,128)(2,1)S(1)} all-gather(bf16[64,960]{1,0:T(8,128)(2,1)S(1)} %multiply_convert_fusion.7), channel_id=4, replica_groups=mesh['q'=4,'y'=2,'x'=2,'c'=2] {'y','x','c'}, dimensions={0}, use_global_device_ids=true | all-gather | bytes 1105920 | tf_op jit(solution)/shard_map/all_gather | solution.py:143
  216.2 2.4 collective-permute-done.7
  218.6 3.4 collective-permute-done.6
  224.0 14.5 %all-gather.3 = bf16[256,1024]{1,0:T(8,128)(2,1)S(1)} all-gather(bf16[64,1024]{1,0:T(8,128)(2,1)S(1)} %pad.31), channel_id=5, replica_groups=mesh['q'=4,'y'=2,'x'=2,'c'=2] {'q'}, dimensions={0}, use_global_device_ids=true | all-gather | bytes 655360 | tf_op jit(solution)/shard_map/all_gather | solution.py:307
  240.0 10.2 %collective-permute-done.8 = bf16[4,64,1024]{2,1,0:T(8,128)(2,1)S(1)} collective-permute-done((bf16[4,64,1024]{2,1,0:T(8,128)(2,1)S(1)}, bf16[4,64,1024]{2,1,0:T(8,128)(2,1)S(1)}, u32[]{:S(2)}, u32[]{:S(2)}) %collective-permute-start.8) | collective-permute-done | bytes 524320 | tf_op jit(solution)/shard_map/ppermute | solution.py:74
  258.0 4.0 collective-permute-start.12
  263.0 4.5 fusion.194
  270.6 3.9 fusion.193
  281.1 11.3 %all_to_all.58 = f32[32,1,256]{2,1,0:T(1,128)S(1)} all-to-all(f32[32,1,256]{2,1,0:T(1,128)} %reshape.817), channel_id=1, replica_groups=mesh['q'=4,'y'=2,'x'=2,'c'=2] {'q','y','x','c'}, dimensions={0} | all-to-all | bytes 65536 | tf_op jit(solution)/shard_map/all_to_all | solution.py:328
  298.4 8.6 %all_to_all.59 = f32[32,1,64]{2,1,0:T(1,128)S(1)} all-to-all(f32[32,1,64]{2,1,0:T(1,128)S(1)} %broadcast_in_dim.103), channel_id=1, replica_groups=mesh['q'=4,'y'=2,'x'=2,'c'=2] {'q','y','x','c'}, dimensions={0} | all-to-all | bytes 16384 | tf_op jit(solution)/shard_map/all_to_all | solution.py:338
  308.6 7.1 %convolution_convert_fusion = bf16[1024,1024]{1,0:T(8,128)(2,1)} fusion(bf16[1000,960]{0,1:T(8,128)(2,1)} %convert_element_type.304, f32[1024,1000]{0,1:T(8,128)} %copy-done.16, f32[1024]{0:T(1024)S(1)} %squeeze.141, f32[1024]{0:T(1024)S(1)} %multiply_add_fusion.3, s32[1024]{0:T(1024)} %copy-done.83), kind=kOutput, calls=%fused_computation.60 | convolution fusion | flops 2106392576 | bytes 8125440 | tf_op jit(solution)/shard_map/dot_general | solution.py:52
  316.4 5.6 fusion.167
  322.1 4.8 fusion.195
  329.8 4.3 fusion.168
  334.2 7.4 %collective-permute-done.16 = bf16[4,64,1024]{2,1,0:T(8,128)(2,1)S(1)} collective-permute-done((bf16[4,64,1024]{2,1,0:T(8,128)(2,1)S(1)}, bf16[4,64,1024]{2,1,0:T(8,128)(2,1)S(1)}, u32[]{:S(2)}, u32[]{:S(2)}) %collective-permute-start.16) | collective-permute-done | bytes 524320 | tf_op jit(solution)/shard_map/ppermute | solution.py:74
  341.6 10.4 %collective-permute-done.15 = bf16[4,64,1024]{2,1,0:T(8,128)(2,1)S(1)} collective-permute-done((bf16[4,64,1024]{2,1,0:T(8,128)(2,1)S(1)}, bf16[4,64,1024]{2,1,0:T(8,128)(2,1)S(1)}, u32[]{:S(2)}, u32[]{:S(2)}) %collective-permute-start.15) | collective-permute-done | bytes 524320 | tf_op jit(solution)/shard_map/ppermute | solution.py:74
  356.2 2.9 slice_add_fusion
  359.1 5.7 collective-permute-done.18
  365.7 13.2 %all-gather.4 = bf16[512,960]{1,0:T(8,128)(2,1)S(1)} all-gather(bf16[64,960]{1,0:T(8,128)(2,1)S(1)} %fusion.162), channel_id=6, replica_groups=mesh['q'=4,'y'=2,'x'=2,'c'=2] {'y','x','c'}, dimensions={0}, use_global_device_ids=true | all-gather | bytes 1105920 | tf_op jit(solution)/shard_map/all_gather | solution.py:143
  392.8 3.3 collective-permute-done.22
  408.3 3.9 convolution_convert_fusion.10
  427.7 2.3 convolution_convert_fusion.3
  432.5 3.4 all-to-all-start.6
  436.0 3.0 reduce-scatter.2.cloned.1.call-done
  442.7 4.0 reshape.732
  448.0 6.3 %fusion.2 = bf16[8,352,960]{2,1,0:T(8,128)(2,1)} fusion(bf16[1,3,960]{2,1,0:T(4,128)(2,1)S(1)} %convert_element_type.359, bf16[3,320,960]{2,1,0:T(8,128)(2,1)S(1)} %bitcast.252, bf16[5,128,960]{2,1,0:T(8,128)(2,1)S(1)} %copy-done.10, bf16[5,192,960]{2,1,0:T(8,128)(2,1)S(1)} %bitcast.253), kind=kLoop, calls=%fused_computation.10 | loop fusion | flops 27033600 | bytes 10327680 | tf_op jit(solution)/shard_map/concatenate | solution.py:417
  454.3 3.7 dynamic-slice_bitcast_fusion
  459.0 4.5 all-to-all-start.7
  464.3 4.0 convert_add_fusion
  468.3 2.5 copy-done.3
  474.0 3.8 fusion.50
  477.8 22.6 %collective-permute-done.27 = bf16[352,960]{1,0:T(8,128)(2,1)S(1)} collective-permute-done((bf16[352,960]{1,0:T(8,128)(2,1)S(1)}, bf16[352,960]{1,0:T(8,128)(2,1)S(1)}, u32[]{:S(2)}, u32[]{:S(2)}) %collective-permute-start.27) | collective-permute-done | bytes 675872 | tf_op jit(solution)/shard_map/ppermute | solution.py:74
  500.4 15.2 %collective-permute-done.26 = bf16[352,960]{1,0:T(8,128)(2,1)} collective-permute-done((bf16[352,960]{1,0:T(8,128)(2,1)S(1)}, bf16[352,960]{1,0:T(8,128)(2,1)}, u32[]{:S(2)}, u32[]{:S(2)}) %collective-permute-start.26) | collective-permute-done | bytes 675872 | tf_op jit(solution)/shard_map/ppermute | solution.py:74
  519.0 2.5 collective-permute-start.30
  522.6 3.5 fusion.5
  526.4 4.0 multiply_reduce_fusion
  531.5 5.8 collective-permute-done.29
  543.8 6.4 %all-to-all-start.8 = ((f32[32,1,2]{2,1,0:T(1,128)}), f32[32,1,2]{2,1,0:T(1,128)S(1)}, u32[]{:S(2)}, u32[]{:S(2)}) async-start(f32[32,1,2]{2,1,0:T(1,128)} %broadcast_in_dim.107), calls=%async_computation.9 | async-start | bytes 32768 | tf_op jit(solution)/shard_map/all_to_all | solution.py:469
  553.3 3.7 all-to-all-done.8
  557.0 4.3 all-to-all-start.9
  565.7 3.2 all-to-all-done.9
  572.7 5.6 collective-permute-start.34
  578.3 10.3 %add_multiply_fusion = (f32[1000,960]{0,1:T(8,128)}, f32[1000,960]{0,1:T(8,128)}, f32[1000,960]{0,1:T(8,128)}) fusion(f32[1000,960]{0,1:T(8,128)} %param.21, f32[1000,960]{0,1:T(8,128)} %get-tuple-element.109, f32[]{:T(128)S(6)} %div.148, f32[1000,960]{0,1:T(8,128)} %param.23, f32[1000,960]{0,1:T(8,128)} %param.22), kind=kLoop, calls=%fused_computation.23 | loop fusion | flops 14400000 | bytes 26880004 | tf_op jit(solution)/shard_map/mul | solution.py:107
  590.1 4.4 add_multiply_fusion.1
  (502 shorter events, 189.4 us)
Async XLA Ops:
  8.5 5.8 collective-permute-start
  17.9 25.2 %collective-permute-start.1 = (bf16[328,960]{1,0:T(8,128)(2,1)S(1)}, bf16[328,960]{1,0:T(8,128)(2,1)}, u32[]{:S(2)}, u32[]{:S(2)}) collective-permute-start(bf16[328,960]{1,0:T(8,128)(2,1)S(1)} %maximum_maximum_fusion), channel_id=1, source_target_pairs={{0,16},{1,17},{2,18},{3,19},{4,20},{5,21},{6,22},{7,23}} | collective-permute-start | bytes 1889288 | tf_op jit(solution)/shard_map/ppermute | solution.py:217
  23.6 12.1 %all-to-all-start = ((s32[32,1,96]{2,1,0:T(1,128)}), s32[32,1,96]{2,1,0:T(1,128)S(1)}, u32[]{:S(2)}, u32[]{:S(2)}) async-start(s32[32,1,96]{2,1,0:T(1,128)} %bitcast), calls=%async_computation | async-start | bytes 32768 | tf_op jit(solution)/shard_map/all_to_all | solution.py:215
  35.7 28.6 %all-to-all-start.1 = ((bf16[8,60,640]{2,1,0:T(8,128)(2,1)}), bf16[8,60,640]{2,1,0:T(8,128)(2,1)S(1)}, u32[]{:S(2)}, u32[]{:S(2)}) async-start(bf16[8,60,640]{2,1,0:T(8,128)(2,1)} %reshape.806), calls=%async_computation.1 | async-start | bytes 1310720 | tf_op jit(solution)/shard_map/all_to_all | solution.py:209
  42.3 77.7 %all-gather.8.cloned.1.call-start = ((), (), s32[]{:S(2)}) async-start(), calls=%async_computation.12 | async-start | bytes 3358720 | tf_op jit(solution)/shard_map/all_gather | solution.py:223
  43.2 20.3 %collective-permute-start.2 = (bf16[328,960]{1,0:T(8,128)(2,1)S(1)}, bf16[328,960]{1,0:T(8,128)(2,1)S(1)}, u32[]{:S(2)}, u32[]{:S(2)}) collective-permute-start(bf16[328,960]{1,0:T(8,128)(2,1)S(1)} %broadcast_select_fusion), channel_id=1, source_target_pairs={{0,8},{16,24},{1,9},{17,25},{2,10},{18,26},{3,11},{19,27},{4,12},{... | collective-permute-start | bytes 1889288 | tf_op jit(solution)/shard_map/ppermute | solution.py:219
  64.4 55.6 %all-to-all-start.2 = ((bf16[32,24,960]{2,1,0:T(8,128)(2,1)}), bf16[32,24,960]{2,1,0:T(8,128)(2,1)}, u32[]{:S(2)}, u32[]{:S(2)}) async-start(bf16[32,24,960]{2,1,0:T(8,128)(2,1)} %bitcast.2), calls=%async_computation.2 | async-start | bytes 3145728 | tf_op jit(solution)/shard_map/all_to_all | solution.py:190
  72.0 48.6 %copy-start.78 = (s32[64]{0:T(128)S(1)}, s32[64]{0:T(128)}, u32[]{:S(2)}) copy-start(s32[64]{0:T(128)} %param.16) | copy-start | bytes 772
  72.0 48.7 %copy-start = (s32[32]{0:T(128)S(1)}, s32[32]{0:T(128)}, u32[]{:S(2)}) copy-start(s32[32]{0:T(128)} %constant.354.clone) | copy-start | bytes 388
  72.1 49.4 %copy-start.57 = (f32[512,64]{1,0:T(8,128)S(1)}, f32[512,64]{1,0:T(8,128)}, u32[]{:S(2)}) copy-start(f32[512,64]{1,0:T(8,128)} %constant.380) | copy-start | bytes 393220
  72.1 50.0 %copy-start.56 = (f32[512,64]{1,0:T(8,128)S(1)}, f32[512,64]{1,0:T(8,128)}, u32[]{:S(2)}) copy-start(f32[512,64]{1,0:T(8,128)} %constant.379) | copy-start | bytes 393220
  120.0 13.4 %collective-permute-start.3 = (bf16[4,328,960]{2,1,0:T(8,128)(2,1)}, bf16[4,328,960]{2,1,0:T(8,128)(2,1)}, u32[]{:S(2)}, u32[]{:S(2)}) collective-permute-start(bf16[4,328,960]{2,1,0:T(8,128)(2,1)} %bitcast.254), channel_id=1, source_target_pairs={{0,1},{1,0},{2,3},{3,2},{4,5},{5,4},{6,7},{7,6},{8,9},{9,8},{10,11... | collective-permute-start | bytes 7557128 | tf_op jit(solution)/shard_map/ppermute | solution.py:74
  121.4 12.0 %copy-start.98 = (s32[32]{0:T(128)}, s32[32]{0:T(128)S(1)}, u32[]{:S(2)}) copy-start(s32[32]{0:T(128)S(1)} %gather_fusion.2) | copy-start | bytes 388
  122.1 45.3 %copy-start.54 = (f32[64,64]{1,0:T(8,128)}, f32[64,64]{1,0:T(8,128)S(1)}, u32[]{:S(2)}) copy-start(f32[64,64]{1,0:T(8,128)S(1)} %gather_fusion.1) | copy-start | bytes 49156
  124.5 30.8 %all-to-all-start.3 = ((bf16[32,8,960]{2,1,0:T(8,128)(2,1)}), bf16[32,8,960]{2,1,0:T(8,128)(2,1)S(1)}, u32[]{:S(2)}, u32[]{:S(2)}) async-start(bf16[32,8,960]{2,1,0:T(8,128)(2,1)} %bitcast.3), calls=%async_computation.3 | async-start | bytes 1048576 | tf_op jit(solution)/shard_map/all_to_all | solution.py:190
  128.2 60.0 %all-gather.10.cloned.1.call-start = ((), (), s32[]{:S(2)}) async-start(), calls=%async_computation.13 | async-start | bytes 3072000 | tf_op jit(solution)/shard_map/all_gather | solution.py:238
  129.0 310.0 %reduce-scatter.2.cloned.1.call-start = ((), (), s32[]{:S(2)}) async-start(), calls=%async_computation.11 | async-start | bytes 3072000 | tf_op jit(solution)/shard_map/reduce_scatter | solution.py:404
  158.9 33.5 %copy-start.72 = (f32[1,1,960]{2,1,0:T(1,128)}, f32[1,1,960]{2,1,0:T(1,128)S(1)}, u32[]{:S(2)}) copy-start(f32[1,1,960]{2,1,0:T(1,128)S(1)} %get-tuple-element.177) | copy-start | bytes 11524
  158.9 65.0 %copy-start.70 = (f32[1,1,960]{2,1,0:T(1,128)}, f32[1,1,960]{2,1,0:T(1,128)S(1)}, u32[]{:S(2)}) copy-start(f32[1,1,960]{2,1,0:T(1,128)S(1)} %get-tuple-element.176) | copy-start | bytes 11524
  189.6 15.3 %copy-start.4 = (bf16[2,480,640]{2,1,0:T(8,128)(2,1)}, bf16[2,480,640]{2,1,0:T(8,128)(2,1)S(1)}, u32[]{:S(2)}) copy-start(bf16[2,480,640]{2,1,0:T(8,128)(2,1)S(1)} %slice.349) | copy-start | bytes 3686404
  191.0 14.5 %copy-start.51 = (bf16[320,640]{1,0:T(8,128)(2,1)}, bf16[320,640]{1,0:T(8,128)(2,1)S(1)}, u32[]{:S(2)}) copy-start(bf16[320,640]{1,0:T(8,128)(2,1)S(1)} %slice_bitcast_fusion.1) | copy-start | bytes 1228804
  192.4 12.6 %copy-start.93 = (f32[64]{0:T(128)}, f32[64]{0:T(128)S(1)}, u32[]{:S(2)}) copy-start(f32[64]{0:T(128)S(1)} %add_rsqrt_fusion.2) | copy-start | bytes 772
  206.7 2.3 collective-permute-start.4
  212.6 6.1 %collective-permute-start.7 = (bf16[64,1024]{1,0:T(8,128)(2,1)}, bf16[64,1024]{1,0:T(8,128)(2,1)S(1)}, u32[]{:S(2)}, u32[]{:S(2)}) collective-permute-start(bf16[64,1024]{1,0:T(8,128)(2,1)} %get-tuple-element.160), channel_id=1, source_target_pairs={{0,6},{2,4},{4,2},{6,0},{1,7},{3,5},{5,3},{7,1},{8,14},{10,12},{12... | collective-permute-start | bytes 393224 | tf_op jit(solution)/shard_map/ppermute | solution.py:74
  213.7 8.3 %collective-permute-start.6 = (bf16[64,1024]{1,0:T(8,128)(2,1)}, bf16[64,1024]{1,0:T(8,128)(2,1)S(1)}, u32[]{:S(2)}, u32[]{:S(2)}) collective-permute-start(bf16[64,1024]{1,0:T(8,128)(2,1)} %get-tuple-element.161), channel_id=1, source_target_pairs={{0,4},{2,6},{4,0},{6,2},{1,5},{3,7},{5,1},{7,3},{8,12},{10,14},{12... | collective-permute-start | bytes 393224 | tf_op jit(solution)/shard_map/ppermute | solution.py:74
  214.9 7.7 %collective-permute-start.5 = (bf16[64,1024]{1,0:T(8,128)(2,1)}, bf16[64,1024]{1,0:T(8,128)(2,1)}, u32[]{:S(2)}, u32[]{:S(2)}) collective-permute-start(bf16[64,1024]{1,0:T(8,128)(2,1)} %get-tuple-element.159), channel_id=1, source_target_pairs={{0,2},{2,0},{4,6},{6,4},{1,3},{3,1},{5,7},{7,5},{8,10},{10,8},{12,... | collective-permute-start | bytes 393224 | tf_op jit(solution)/shard_map/ppermute | solution.py:74
  223.9 29.6 %copy-start.90 = (f32[64]{0:T(128)}, f32[64]{0:T(128)S(1)}, u32[]{:S(2)}) copy-start(f32[64]{0:T(128)S(1)} %add_rsqrt_fusion.1) | copy-start | bytes 772
  238.5 11.7 %collective-permute-start.8 = (bf16[4,64,1024]{2,1,0:T(8,128)(2,1)S(1)}, bf16[4,64,1024]{2,1,0:T(8,128)(2,1)S(1)}, u32[]{:S(2)}, u32[]{:S(2)}) collective-permute-start(bf16[4,64,1024]{2,1,0:T(8,128)(2,1)S(1)} %bitcast.287), channel_id=1, source_target_pairs={{0,2},{2,0},{1,3},{3,1},{4,6},{6,4},{5,7},{7,5},{8,10},{10,8},{9,1... | collective-permute-start | bytes 1572872 | tf_op jit(solution)/shard_map/ppermute | solution.py:74
  239.4 12.4 %collective-permute-start.9 = (bf16[4,64,1024]{2,1,0:T(8,128)(2,1)S(1)}, bf16[4,64,1024]{2,1,0:T(8,128)(2,1)S(1)}, u32[]{:S(2)}, u32[]{:S(2)}) collective-permute-start(bf16[4,64,1024]{2,1,0:T(8,128)(2,1)S(1)} %bitcast.288), channel_id=1, source_target_pairs={{0,4},{4,0},{1,5},{5,1},{2,6},{6,2},{3,7},{7,3},{8,12},{12,8},{9,1... | collective-permute-start | bytes 1572872 | tf_op jit(solution)/shard_map/ppermute | solution.py:74
  250.2 5.6 collective-permute-start.10
  251.7 5.6 collective-permute-start.11
  258.0 11.6 %collective-permute-start.12 = (bf16[1024,1024]{1,0:T(8,128)(2,1)}, bf16[1024,1024]{1,0:T(8,128)(2,1)}, u32[]{:S(2)}, u32[]{:S(2)}) collective-permute-start(bf16[1024,1024]{1,0:T(8,128)(2,1)} %bitcast.51), channel_id=1, source_target_pairs={{0,1},{1,0},{2,3},{3,2},{4,5},{5,4},{6,7},{7,6},{8,9},{9,8},{10,11... | collective-permute-start | bytes 6291464 | tf_op jit(solution)/shard_map/ppermute | solution.py:74
  315.7 6.4 %collective-permute-start.13 = (bf16[1024,1024]{1,0:T(8,128)(2,1)}, bf16[1024,1024]{1,0:T(8,128)(2,1)}, u32[]{:S(2)}, u32[]{:S(2)}) collective-permute-start(bf16[1024,1024]{1,0:T(8,128)(2,1)} %convolution_convert_fusion), channel_id=1, source_target_pairs={{0,1},{1,0},{2,3},{3,2},{4,5},{5,4},{6,7},{7,6},{8,9},{9,8},{10,11... | collective-permute-start | bytes 6291464 | tf_op jit(solution)/shard_map/ppermute | solution.py:74
  327.1 14.5 %collective-permute-start.16 = (bf16[4,64,1024]{2,1,0:T(8,128)(2,1)S(1)}, bf16[4,64,1024]{2,1,0:T(8,128)(2,1)S(1)}, u32[]{:S(2)}, u32[]{:S(2)}) collective-permute-start(bf16[4,64,1024]{2,1,0:T(8,128)(2,1)S(1)} %bitcast.318), channel_id=1, source_target_pairs={{0,6},{2,4},{4,2},{6,0},{1,7},{3,5},{5,3},{7,1},{8,14},{10,12},{12... | collective-permute-start | bytes 1572872 | tf_op jit(solution)/shard_map/ppermute | solution.py:74
  327.5 24.5 %collective-permute-start.15 = (bf16[4,64,1024]{2,1,0:T(8,128)(2,1)S(1)}, bf16[4,64,1024]{2,1,0:T(8,128)(2,1)S(1)}, u32[]{:S(2)}, u32[]{:S(2)}) collective-permute-start(bf16[4,64,1024]{2,1,0:T(8,128)(2,1)S(1)} %bitcast.317), channel_id=1, source_target_pairs={{0,4},{2,6},{4,0},{6,2},{1,5},{3,7},{5,1},{7,3},{8,12},{10,14},{12... | collective-permute-start | bytes 1572872 | tf_op jit(solution)/shard_map/ppermute | solution.py:74
  328.6 23.4 %collective-permute-start.14 = (bf16[4,64,1024]{2,1,0:T(8,128)(2,1)S(1)}, bf16[4,64,1024]{2,1,0:T(8,128)(2,1)S(1)}, u32[]{:S(2)}, u32[]{:S(2)}) collective-permute-start(bf16[4,64,1024]{2,1,0:T(8,128)(2,1)S(1)} %bitcast.316), channel_id=1, source_target_pairs={{0,2},{2,0},{4,6},{6,4},{1,3},{3,1},{5,7},{7,5},{8,10},{10,8},{12,... | collective-permute-start | bytes 1572872 | tf_op jit(solution)/shard_map/ppermute | solution.py:74
  352.4 6.7 %collective-permute-start.19 = (bf16[64,1024]{1,0:T(8,128)(2,1)S(1)}, bf16[64,1024]{1,0:T(8,128)(2,1)S(1)}, u32[]{:S(2)}, u32[]{:S(2)}) collective-permute-start(bf16[64,1024]{1,0:T(8,128)(2,1)S(1)} %get-tuple-element.157), channel_id=1, source_target_pairs={{0,24},{8,16},{16,8},{24,0},{1,25},{9,17},{17,9},{25,1},{2,26},{10... | collective-permute-start | bytes 393224 | tf_op jit(solution)/shard_map/ppermute | solution.py:74
  352.8 12.0 %collective-permute-start.18 = (bf16[64,1024]{1,0:T(8,128)(2,1)S(1)}, bf16[64,1024]{1,0:T(8,128)(2,1)S(1)}, u32[]{:S(2)}, u32[]{:S(2)}) collective-permute-start(bf16[64,1024]{1,0:T(8,128)(2,1)S(1)} %get-tuple-element.158), channel_id=1, source_target_pairs={{0,16},{8,24},{16,0},{24,8},{1,17},{9,25},{17,1},{25,9},{2,18},{10... | collective-permute-start | bytes 393224 | tf_op jit(solution)/shard_map/ppermute | solution.py:74
  354.1 10.7 %collective-permute-start.17 = (bf16[64,1024]{1,0:T(8,128)(2,1)S(1)}, bf16[64,1024]{1,0:T(8,128)(2,1)S(1)}, u32[]{:S(2)}, u32[]{:S(2)}) collective-permute-start(bf16[64,1024]{1,0:T(8,128)(2,1)S(1)} %get-tuple-element.156), channel_id=1, source_target_pairs={{0,8},{8,0},{16,24},{24,16},{1,9},{9,1},{17,25},{25,17},{2,10},{10... | collective-permute-start | bytes 393224 | tf_op jit(solution)/shard_map/ppermute | solution.py:74
  359.1 19.9 %copy-start.34 = (f32[512,640]{1,0:T(8,128)S(1)}, f32[512,640]{1,0:T(8,128)}, u32[]{:S(2)}) copy-start(f32[512,640]{1,0:T(8,128)} %copy-done.33) | copy-start | bytes 3932164
  359.1 19.9 %copy-start.52 = (bf16[320,640]{1,0:T(8,128)(2,1)S(1)}, bf16[320,640]{1,0:T(8,128)(2,1)}, u32[]{:S(2)}) copy-start(bf16[320,640]{1,0:T(8,128)(2,1)} %copy-done.51) | copy-start | bytes 1228804
  359.1 19.9 %copy-start.67 = (bf16[160,320]{1,0:T(8,128)(2,1)S(1)}, bf16[160,320]{1,0:T(8,128)(2,1)}, u32[]{:S(2)}) copy-start(bf16[160,320]{1,0:T(8,128)(2,1)} %copy-done.66) | copy-start | bytes 307204
  359.1 19.9 %copy-start.69 = (bf16[160,320]{1,0:T(8,128)(2,1)S(1)}, bf16[160,320]{1,0:T(8,128)(2,1)}, u32[]{:S(2)}) copy-start(bf16[160,320]{1,0:T(8,128)(2,1)} %copy-done.68) | copy-start | bytes 307204
  380.9 3.4 collective-permute-start.20
  386.7 6.2 %collective-permute-start.23 = (bf16[64,1024]{1,0:T(8,128)(2,1)}, bf16[64,1024]{1,0:T(8,128)(2,1)}, u32[]{:S(2)}, u32[]{:S(2)}) collective-permute-start(bf16[64,1024]{1,0:T(8,128)(2,1)} %get-tuple-element.154), channel_id=1, source_target_pairs={{0,6},{2,4},{4,2},{6,0},{1,7},{3,5},{5,3},{7,1},{8,14},{10,12},{12... | collective-permute-start | bytes 393224 | tf_op jit(solution)/shard_map/ppermute | solution.py:74
  387.8 8.3 %collective-permute-start.22 = (bf16[64,1024]{1,0:T(8,128)(2,1)}, bf16[64,1024]{1,0:T(8,128)(2,1)}, u32[]{:S(2)}, u32[]{:S(2)}) collective-permute-start(bf16[64,1024]{1,0:T(8,128)(2,1)} %get-tuple-element.155), channel_id=1, source_target_pairs={{0,4},{2,6},{4,0},{6,2},{1,5},{3,7},{5,1},{7,3},{8,12},{10,14},{12... | collective-permute-start | bytes 393224 | tf_op jit(solution)/shard_map/ppermute | solution.py:74
  388.2 7.9 %collective-permute-start.21 = (bf16[64,1024]{1,0:T(8,128)(2,1)}, bf16[64,1024]{1,0:T(8,128)(2,1)}, u32[]{:S(2)}, u32[]{:S(2)}) collective-permute-start(bf16[64,1024]{1,0:T(8,128)(2,1)} %get-tuple-element.153), channel_id=1, source_target_pairs={{0,2},{2,0},{4,6},{6,4},{1,3},{3,1},{5,7},{7,5},{8,10},{10,8},{12,... | collective-permute-start | bytes 393224 | tf_op jit(solution)/shard_map/ppermute | solution.py:74
  432.5 21.7 %all-to-all-start.6 = ((bf16[32,8,960]{2,1,0:T(8,128)(2,1)}), bf16[32,8,960]{2,1,0:T(8,128)(2,1)}, u32[]{:S(2)}, u32[]{:S(2)}) async-start(bf16[32,8,960]{2,1,0:T(8,128)(2,1)} %bitcast.99), calls=%async_computation.7 | async-start | bytes 1048576 | tf_op jit(solution)/shard_map/all_to_all | solution.py:190
  457.9 6.3 %collective-permute-start.24 = (bf16[4,352,960]{2,1,0:T(8,128)(2,1)}, bf16[4,352,960]{2,1,0:T(8,128)(2,1)}, u32[]{:S(2)}, u32[]{:S(2)}) collective-permute-start(bf16[4,352,960]{2,1,0:T(8,128)(2,1)} %dynamic-slice_bitcast_fusion), channel_id=1, source_target_pairs={{0,1},{1,0},{2,3},{3,2},{4,5},{5,4},{6,7},{7,6},{8,9},{9,8},{10,11... | collective-permute-start | bytes 8110088 | tf_op jit(solution)/shard_map/ppermute | solution.py:74
  459.0 59.9 %all-to-all-start.7 = ((bf16[32,24,960]{2,1,0:T(8,128)(2,1)}), bf16[32,24,960]{2,1,0:T(8,128)(2,1)}, u32[]{:S(2)}, u32[]{:S(2)}) async-start(bf16[32,24,960]{2,1,0:T(8,128)(2,1)} %bitcast.100), calls=%async_computation.8 | async-start | bytes 3145728 | tf_op jit(solution)/shard_map/all_to_all | solution.py:190
  471.1 29.3 %collective-permute-start.27 = (bf16[352,960]{1,0:T(8,128)(2,1)S(1)}, bf16[352,960]{1,0:T(8,128)(2,1)S(1)}, u32[]{:S(2)}, u32[]{:S(2)}) collective-permute-start(bf16[352,960]{1,0:T(8,128)(2,1)S(1)} %get-tuple-element.124), channel_id=1, source_target_pairs={{0,6},{2,4},{4,2},{6,0},{1,7},{3,5},{5,3},{7,1},{8,14},{10,12},{12... | collective-permute-start | bytes 2027528 | tf_op jit(solution)/shard_map/ppermute | solution.py:74
  473.3 42.3 %collective-permute-start.26 = (bf16[352,960]{1,0:T(8,128)(2,1)S(1)}, bf16[352,960]{1,0:T(8,128)(2,1)}, u32[]{:S(2)}, u32[]{:S(2)}) collective-permute-start(bf16[352,960]{1,0:T(8,128)(2,1)S(1)} %get-tuple-element.125), channel_id=1, source_target_pairs={{0,4},{2,6},{4,0},{6,2},{1,5},{3,7},{5,1},{7,3},{8,12},{10,14},{12... | collective-permute-start | bytes 2027528 | tf_op jit(solution)/shard_map/ppermute | solution.py:74
  473.5 43.1 %collective-permute-start.25 = (bf16[352,960]{1,0:T(8,128)(2,1)S(1)}, bf16[352,960]{1,0:T(8,128)(2,1)}, u32[]{:S(2)}, u32[]{:S(2)}) collective-permute-start(bf16[352,960]{1,0:T(8,128)(2,1)S(1)} %get-tuple-element.123), channel_id=1, source_target_pairs={{0,2},{2,0},{4,6},{6,4},{1,3},{3,1},{5,7},{7,5},{8,10},{10,8},{12,... | collective-permute-start | bytes 2027528 | tf_op jit(solution)/shard_map/ppermute | solution.py:74
  519.0 12.5 %collective-permute-start.30 = (bf16[88,960]{1,0:T(8,128)(2,1)S(1)}, bf16[88,960]{1,0:T(8,128)(2,1)S(1)}, u32[]{:S(2)}, u32[]{:S(2)}) collective-permute-start(bf16[88,960]{1,0:T(8,128)(2,1)S(1)} %get-tuple-element.135), channel_id=1, source_target_pairs={{0,24},{8,16},{16,8},{24,0},{1,25},{9,17},{17,9},{25,1},{2,26},{10... | collective-permute-start | bytes 506888 | tf_op jit(solution)/shard_map/ppermute | solution.py:74
  521.5 15.8 %collective-permute-start.29 = (bf16[88,960]{1,0:T(8,128)(2,1)S(1)}, bf16[88,960]{1,0:T(8,128)(2,1)S(1)}, u32[]{:S(2)}, u32[]{:S(2)}) collective-permute-start(bf16[88,960]{1,0:T(8,128)(2,1)S(1)} %get-tuple-element.136), channel_id=1, source_target_pairs={{0,16},{8,24},{16,0},{24,8},{1,17},{9,25},{17,1},{25,9},{2,18},{10... | collective-permute-start | bytes 506888 | tf_op jit(solution)/shard_map/ppermute | solution.py:74
  521.5 15.8 %collective-permute-start.28 = (bf16[88,960]{1,0:T(8,128)(2,1)S(1)}, bf16[88,960]{1,0:T(8,128)(2,1)S(1)}, u32[]{:S(2)}, u32[]{:S(2)}) collective-permute-start(bf16[88,960]{1,0:T(8,128)(2,1)S(1)} %get-tuple-element.134), channel_id=1, source_target_pairs={{0,8},{8,0},{16,24},{24,16},{1,9},{9,1},{17,25},{25,17},{2,10},{10... | collective-permute-start | bytes 506888 | tf_op jit(solution)/shard_map/ppermute | solution.py:74
  539.9 22.7 %collective-permute-start.33 = (bf16[88,960]{1,0:T(8,128)(2,1)S(1)}, bf16[88,960]{1,0:T(8,128)(2,1)S(1)}, u32[]{:S(2)}, u32[]{:S(2)}) collective-permute-start(bf16[88,960]{1,0:T(8,128)(2,1)S(1)} %get-tuple-element.87), channel_id=1, source_target_pairs={{16,0},{17,1},{18,2},{19,3},{20,4},{21,5},{22,6},{23,7}} | collective-permute-start | bytes 506888 | tf_op jit(solution)/shard_map/ppermute | solution.py:440
  541.2 21.4 %collective-permute-start.31 = (bf16[88,960]{1,0:T(8,128)(2,1)S(1)}, bf16[88,960]{1,0:T(8,128)(2,1)S(1)}, u32[]{:S(2)}, u32[]{:S(2)}) collective-permute-start(bf16[88,960]{1,0:T(8,128)(2,1)S(1)} %get-tuple-element.87), channel_id=1, source_target_pairs={{24,0},{25,1},{26,2},{27,3},{28,4},{29,5},{30,6},{31,7}} | collective-permute-start | bytes 506888 | tf_op jit(solution)/shard_map/ppermute | solution.py:440
  543.8 13.2 %all-to-all-start.8 = ((f32[32,1,2]{2,1,0:T(1,128)}), f32[32,1,2]{2,1,0:T(1,128)S(1)}, u32[]{:S(2)}, u32[]{:S(2)}) async-start(f32[32,1,2]{2,1,0:T(1,128)} %broadcast_in_dim.107), calls=%async_computation.9 | async-start | bytes 32768 | tf_op jit(solution)/shard_map/all_to_all | solution.py:469
  552.0 11.1 %collective-permute-start.32 = (bf16[88,960]{1,0:T(8,128)(2,1)S(1)}, bf16[88,960]{1,0:T(8,128)(2,1)S(1)}, u32[]{:S(2)}, u32[]{:S(2)}) collective-permute-start(bf16[88,960]{1,0:T(8,128)(2,1)S(1)} %get-tuple-element.87), channel_id=1, source_target_pairs={{8,0},{9,1},{10,2},{11,3},{12,4},{13,5},{14,6},{15,7}} | collective-permute-start | bytes 506888 | tf_op jit(solution)/shard_map/ppermute | solution.py:440
  557.0 11.9 %all-to-all-start.9 = ((bf16[8,60,640]{2,1,0:T(8,128)(2,1)}), bf16[8,60,640]{2,1,0:T(8,128)(2,1)S(1)}, u32[]{:S(2)}, u32[]{:S(2)}) async-start(bf16[8,60,640]{2,1,0:T(8,128)(2,1)} %reshape.743), calls=%async_computation.10 | async-start | bytes 1310720 | tf_op jit(solution)/shard_map/all_to_all | solution.py:428
  572.7 17.4 %collective-permute-start.34 = (bf16[2880]{0:T(1024)(128)(2,1)S(1)}, bf16[2880]{0:T(1024)(128)(2,1)S(1)}, u32[]{:S(2)}, u32[]{:S(2)}) collective-permute-start(bf16[2880]{0:T(1024)(128)(2,1)S(1)} %slice.481), channel_id=1, source_target_pairs={{0,1},{1,2},{2,3},{3,4},{4,5},{5,6},{6,7},{7,8},{8,9},{9,10},{10,1... | collective-permute-start | bytes 17288 | tf_op jit(solution)/shard_map/ppermute | solution.py:460
  578.2 11.8 %copy-start.11 = (f32[307290]{0:T(1024)S(1)}, f32[307290]{0:T(1024)}, u32[]{:S(2)}) copy-start(f32[307290]{0:T(1024)} %param.18) | copy-start | bytes 3687484
  578.3 11.8 %copy-start.40 = (f32[307290]{0:T(1024)S(1)}, f32[307290]{0:T(1024)}, u32[]{:S(2)}) copy-start(f32[307290]{0:T(1024)} %param.20) | copy-start | bytes 3687484
  (84 other events, 286.9 us)
Sparse Core Ops, SparseCore 0:
  64.5 55.4 all-gather.7
  131.2 52.5 all-gather.9
  391.2 47.7 reduce-scatter.1

commit v8 on v7

--- a/solution.py
+++ b/solution.py
@@ -189,7 +189,6 @@
     def exchange(blocks):
         return lax.all_to_all(blocks, ALL, split_axis=0, concat_axis=0, tiled=True).reshape(-1, D)
 
-    cuts = (0, 3 * capacity // 4, capacity)
     cuts_back = (0, capacity // 4, capacity)
     marked = token_ids + 1
     halves = jnp.stack([marked // 256, marked % 256]).astype(bf16)
@@ -213,33 +212,26 @@
         first = jnp.concatenate([first, flat_low[:GAINS].reshape(3, D), jnp.zeros((5, D), bf16)])
         first, ask = lax.optimization_barrier((first, ask))
         asked = lax.all_to_all(ask, ALL, split_axis=0, concat_axis=0, tiled=True)
-        answer = [dot(rows_between(low, high), table_low).astype(bf16).reshape(devices, high - low, D) for low, high in zip(cuts, cuts[1:])]
+        answer = dot(rows_between(0, capacity), table_low).astype(bf16).reshape(devices, capacity, D)
         jumped = lax.ppermute(first, "q", [(0, 2)])
         first = jnp.where(q_index == 2, jumped, first)
         stepped = lax.ppermute(first, "q", [(0, 1), (2, 3)])
         first = jnp.where((q_index == 1) | (q_index == 3), stepped, first)
         answer, first, got = lax.optimization_barrier((answer, first, got))
-        returned = [exchange(blocks) for blocks in answer]
-        level = lax.all_gather(first, ("y", "x"))
+        returned = exchange(answer)
+        level = lax.all_gather(first, PLANE)
         mixed = jnp.where(q_index == 3, down_pack(chunk.reshape(SHARE, D)), got.reshape(480, 2 * UNIT))
         mixed, level = lax.optimization_barrier((mixed, level))
-        level, returned[0] = lax.optimization_barrier((level, returned[0]))
-        other = flip(level, "c", 1, 2)
-
-        def from_place(p, low, high):
-            mine, theirs = level[p // 2, low:high], other[p // 2, low:high]
-            return jnp.where(c_index == p % 2, mine, theirs)
-
-        gains = from_place(0, SHARE, SHARE + 3).astype(f32)
-        w_q = jnp.concatenate([from_place(p, 0, TOP) for p in range(5)])
-        w_kv = jnp.concatenate([from_place(p, TOP, SHARE) for p in range(5)]).reshape(D, KV)
-        w_out = jnp.concatenate([from_place(p, 0, SHARE) for p in range(5, 8)])
-        returned[1], w_q, w_kv, w_out = lax.optimization_barrier((returned[1], w_q, w_kv, w_out))
+        gains = level[0, SHARE : SHARE + 3].astype(f32)
+        w_q = level[:5, :TOP].reshape(D, D)
+        w_kv = level[:5, TOP:SHARE].reshape(D, KV)
+        w_out = level[5:, :SHARE].reshape(D, D)
+        returned, w_q, w_kv, w_out = lax.optimization_barrier((returned, w_q, w_kv, w_out))
         column = lax.all_gather(mixed, "q")
     else:
         asked = lax.all_to_all(ask, ALL, split_axis=0, concat_axis=0, tiled=True)
-        answer = [dot(rows_between(low, high), table_low).astype(bf16).reshape(devices, high - low, D) for low, high in zip(cuts, cuts[1:])]
-        returned = [exchange(blocks) for blocks in answer]
+        answer = dot(rows_between(0, capacity), table_low).astype(bf16).reshape(devices, capacity, D)
+        returned = exchange(answer)
         extra = jnp.zeros((16 * UNIT,), bf16).at[:GAINS].set(flat_low[:GAINS])
         full = lax.all_gather(jnp.concatenate([chunk, extra]).reshape(units + 16, UNIT), ALL)
         gains = full[0, units : units + GAIN_UNITS].astype(f32).reshape(3, D)
@@ -251,7 +243,7 @@
         both = lax.dynamic_index_in_dim(full[edge[1] : edge[2]].reshape(D, 2, 8, UNIT), p_index, 2, False)
         w_gu = both.reshape(D, 2 * SHARE)
         w_down = lax.dynamic_index_in_dim(full[edge[2] :].reshape(8, SHARE, D), p_index, 0, False)
-    x_low = sum(dot(spot_between(low, high), rows) for low, high, rows in zip(cuts, cuts[1:], returned)).astype(bf16)
+    x_low = dot(spot, returned).astype(bf16)
     x_embed = x_low.astype(f32) * emb_mult
 
     pick = hot(loss_rows, tokens)
@@ -288,14 +280,14 @@
     attended = heads_back(mixed_heads.astype(bf16))
     x_one = x_pick + dot(attended, w_out)
 
+    h_mlp = (x_one * scale_of(x_one) * gains[1]).astype(bf16)
+    h_all = spread_plane(h_mlp)
     if aligned:
-        column, x_one = lax.optimization_barrier((column, x_one))
+        column, h_all = lax.optimization_barrier((column, h_all))
         w_gu = column[1:3].reshape(D, 2 * SHARE)
         w_down = down_unpack(column[3])
     w_gu = jnp.pad(w_gu, ((0, WIDE - D), (0, 0)))
     w_down = widen(w_down)
-    h_mlp = (x_one * scale_of(x_one) * gains[1]).astype(bf16)
-    h_all = spread_plane(h_mlp)
     gate_up = dot(h_all, w_gu)
     gate, up = gate_up[:, :SHARE], gate_up[:, SHARE:]
     sig = jax.nn.sigmoid(gate)
@@ -409,6 +401,15 @@
     grad_q = dot(h_pick, d_q, 0, 0).astype(bf16)
     grad_kv = dot(h_attn, d_kv, 0, 0).astype(bf16)
 
+    def finish(squares, table_grad):
+        sums = jnp.broadcast_to(jnp.stack([squares, my_loss])[None], (devices, 2))
+        sums = jnp.sum(lax.all_to_all(sums, ALL, split_axis=0, concat_axis=0, tiled=True), axis=0)
+        grad_norm = jnp.sqrt(sums[0])
+        loss = sums[1] / loss_total
+        limit = CLIP_C / math.sqrt(loss_total)
+        clip_factor = limit / jnp.maximum(grad_norm, limit)
+        return loss, grad_norm, clip_factor, adamw_step(table_master, table_grad, table_m, table_v, clip_factor)
+
     gain_grads = jnp.concatenate([grad_attn, grad_mlp, grad_final]).astype(bf16)
     if aligned:
         lower = jnp.concatenate([grad_q.reshape(5, TOP, D), grad_kv.reshape(5, SHARE - TOP, D)], axis=1)
@@ -419,10 +420,15 @@
         keep = lax.dynamic_index_in_dim(level, c_index, 1, False)
         give = lax.dynamic_index_in_dim(level, 1 - c_index, 1, False)
         level = keep.astype(f32) + flip(give, "c", 1, 2).astype(f32)
-        own = lax.dynamic_index_in_dim(level, yx_index, 0, False)
-        for k in (1, 2, 3):
-            piece = lax.dynamic_index_in_dim(level, yx_index ^ k, 0, False).astype(bf16)
-            own = own + flip(piece, ("y", "x"), k, 4).astype(f32)
+        level = level.reshape(2, 2, SHARE + ROOM, D)
+        middle = (SHARE + ROOM) // 2
+        x_index, y_index = lax.axis_index("x"), lax.axis_index("y")
+        left, right = pick_block(level[:, :, :middle], x_index, 1), pick_block(level[:, :, middle:], y_index, 0)
+        left = left + flip(pick_block(level[:, :, :middle], 1 - x_index, 1).astype(bf16), "x", 1, 2).astype(f32)
+        right = right + flip(pick_block(level[:, :, middle:], 1 - y_index, 0).astype(bf16), "y", 1, 2).astype(f32)
+        left = pick_block(left, y_index) + flip(pick_block(left, 1 - y_index).astype(bf16), "y", 1, 2).astype(f32)
+        right = pick_block(right, x_index) + flip(pick_block(right, 1 - x_index).astype(bf16), "x", 1, 2).astype(f32)
+        own = jnp.concatenate([left, right])
         own = own.reshape(4, (SHARE + ROOM) // 4, D)
         own, share, arrived[1] = lax.optimization_barrier((own, share, arrived[1]))
         got = lax.all_to_all(share.reshape(8, 60, 640), PLANE, split_axis=0, concat_axis=0, tiled=True)
@@ -442,6 +448,8 @@
         gain_out = first[SHARE : SHARE + 3].reshape(-1)
         both = jnp.concatenate([first[:TOP], first[TOP:SHARE].reshape(TOP, KV)], axis=1)
         first = jnp.where(p_index < 5, both.reshape(-1), first[:SHARE].reshape(-1))
+        loss, grad_norm, clip_factor, table_new = finish(squares, table_grad)
+        got, table_new = lax.optimization_barrier((got, table_new))
         by_share = got.reshape(8, 60, 2, UNIT).transpose(1, 2, 0, 3).reshape(-1)
         mine = jnp.where(q_index == 3, down_unpack(share).reshape(-1), by_share)
         mine = jnp.where(q_index == 0, first, mine)
@@ -465,15 +473,9 @@
 
     if not aligned:
         squares = jnp.sum(layer_grad * layer_grad) + table_squares
-    sums = jnp.broadcast_to(jnp.stack([squares, my_loss])[None], (devices, 2))
-    sums = jnp.sum(lax.all_to_all(sums, ALL, split_axis=0, concat_axis=0, tiled=True), axis=0)
-    grad_norm = jnp.sqrt(sums[0])
-    loss = sums[1] / loss_total
-    limit = CLIP_C / math.sqrt(loss_total)
-    clip_factor = limit / jnp.maximum(grad_norm, limit)
-    flat_one, flat_two, flat_update = adamw_step(flat_master, layer_grad, flat_m, flat_v, clip_factor)
-    table_one, table_two, table_update = adamw_step(table_master, table_grad, table_m, table_v, clip_factor)
-    return (loss, grad_norm, flat_one, flat_two, flat_update, table_one, table_two, table_update)
+        loss, grad_norm, clip_factor, table_new = finish(squares, table_grad)
+    flat_new = adamw_step(flat_master, layer_grad, flat_m, flat_v, clip_factor)
+    return (loss, grad_norm) + flat_new + table_new
 
 
 def solution(mesh):

time: 615 us -> 580 us (0.943)
  other arithmetic: 96.9 us -> 80.1 us
  waiting for transfers between devices: 158 us -> 145 us
  local copies, waits for them, and re-layouts: 82.5 us -> 92.6 us
  starting transfers between devices: 92.4 us -> 83.4 us
    unnamed x8 -> x0, other arithmetic: 11.9 us -> none
    ppermute x28, waiting for transfers between devices: 93.3 us -> 81.6 us  [flip(): return lax.ppermute(rows, axes, [(i, i ^ bits) for i in range(size)])]
    all_gather x1, waiting for transfers between devices: 0.02 us -> 8.93 us  [local(): column = lax.all_gather(mixed, 'q')]
    slice x1 -> x5, local copies, waits for them, and re-layouts: 0.58 us -> 9.08 us  [the longest x1 2.97 us: local(): w_out = level[5:, :SHARE].reshape(D, D)]
    dot_general x39 -> x37, matrix products: 78.2 us -> 74.7 us  [dot(): lax.dot_general(left, right, (((left_dim,), (right_dim,)), ((), ())), pre...]
    all_to_all x4 -> x3, starting transfers between devices: 19.3 us -> 17.2 us  [exchange(): lax.all_to_all(blocks, ALL, split_axis=0, concat_axis=0, tiled=True)]
    unnamed x209 -> x207, local copies, waits for them, and re-layouts: 20.4 us -> 18.7 us
  transfers between devices with their start and end apart: 46 -> 45, of which waited for: 23 -> 22; matrix products, arithmetic and copies ran while one was open for 33% -> 32% of each run, Pallas kernels for 0% -> 0%
where the time goes in v8:
time: 580 us; the launch traced here: 569 us
  waiting for transfers between devices  145 us (25%)
  local copies, waits for them, and re-layouts  92.6 us (16%)
  matrix products  90.2 us (16%)
  starting transfers between devices  83.4 us (14%)
  other arithmetic  80.1 us (14%)
  blocking collectives  55.5 us (10%)
  between operations  21.4 us (4%)
    ppermute x28, waiting for transfers between devices, flip(): return lax.ppermute(rows, axes, [(i, i ^ bits) for i in range(size)])  81.6 us
    dot_general x37, matrix products, dot(): lax.dot_general(left, right, (((left_dim,), (right_dim,)), ((), ())), pre...  74.7 us
    all_gather x1, waiting for transfers between devices, local(): level = lax.all_gather(first, PLANE)  49.1 us
    ppermute x28, starting transfers between devices, flip(): return lax.ppermute(rows, axes, [(i, i ^ bits) for i in range(size)])  29.1 us
    all_gather x2, blocking collectives, spread_plane(): return widen(lax.all_gather(rows, PLANE).reshape(-1, D))  24.4 us
    unnamed x207, local copies, waits for them, and re-layouts  18.7 us
    all_to_all x3, starting transfers between devices, exchange(): lax.all_to_all(blocks, ALL, split_axis=0, concat_axis=0, tiled=True)  17.2 us
    mul x2, other arithmetic, adamw_step(): return (new_one, new_two, -RATE * (ratio + DECAY * param))  15 us
  transfers between devices with their start and end apart: 45, of which 22 were waited for; matrix products, arithmetic and copies ran while one was open for 32% of the time, Pallas kernels for 0%

profile of v8, /device:TPU:1, one launch (start us, length us, event | category | flops | bytes accessed | tf_op | source)
XLA Modules:
  0.0 568.6 jit_solution(16693970319854604750)
XLA Ops:
  17.9 5.8 %collective-permute-start.1 = (bf16[328,960]{1,0:T(8,128)(2,1)S(1)}, bf16[328,960]{1,0:T(8,128)(2,1)}, u32[]{:S(2)}, u32[]{:S(2)}) collective-permute-start(bf16[328,960]{1,0:T(8,128)(2,1)S(1)} %maximum_maximum_fusion), channel_id=1, source_target_pairs={{0,16},{1,17},{2,18},{3,19},{4,20},{5,21},{6,22},{7,23}} | collective-permute-start | bytes 1889288 | tf_op jit(solution)/shard_map/ppermute | solution.py:216
  23.6 3.7 convert_element_type.307
  28.0 4.2 all-to-all-start
  36.6 2.1 collective-permute-start.2
  39.1 5.6 all-to-all-start.1
  44.7 5.2 fusion.24
  50.0 3.9 copy.190
  54.9 9.4 %all-to-all-start.2 = ((bf16[32,32,960]{2,1,0:T(8,128)(2,1)}), bf16[32,32,960]{2,1,0:T(8,128)(2,1)}, u32[]{:S(2)}, u32[]{:S(2)}) async-start(bf16[32,32,960]{2,1,0:T(8,128)(2,1)} %bitcast.232), calls=%async_computation.2 | async-start | bytes 4194304 | tf_op jit(solution)/shard_map/all_to_all | solution.py:190
  70.4 49.1 %all-gather.8.cloned.1.call-done = bf16[2624,960]{1,0:T(8,128)(2,1)} async-done(((bf16[328,960]{1,0:T(8,128)(2,1)}), bf16[2624,960]{1,0:T(8,128)(2,1)}) %all-gather.8.cloned.1.call-update) | async-done | bytes 5038096 | tf_op jit(solution)/shard_map/all_gather | solution.py:222
  122.7 3.0 slice.277
  125.7 2.8 reshape.667
  129.2 3.0 fusion.23
  132.9 2.4 fusion.149
  146.9 2.3 copy.230
  150.7 3.7 fusion.178
  154.4 3.6 convolution_convert_fusion.10
  159.8 2.1 multiply_reduce_fusion.9
  162.8 11.2 %all-gather.2 = bf16[512,960]{1,0:T(8,128)(2,1)S(1)} all-gather(bf16[64,960]{1,0:T(8,128)(2,1)S(1)} %multiply_convert_fusion.7), channel_id=4, replica_groups=mesh['q'=4,'y'=2,'x'=2,'c'=2] {'y','x','c'}, dimensions={0}, use_global_device_ids=true | all-gather | bytes 1105920 | tf_op jit(solution)/shard_map/all_gather | solution.py:143
  175.0 8.9 %all-gather.10.cloned.1.call-done = bf16[1920,640]{1,0:T(8,128)(2,1)} async-done(((bf16[480,640]{1,0:T(8,128)(2,1)}), bf16[1920,640]{1,0:T(8,128)(2,1)}) %all-gather.10.cloned.1.call-update) | async-done | bytes 2457616 | tf_op jit(solution)/shard_map/all_gather | solution.py:230
  200.4 2.2 collective-permute-done.6
  202.5 3.7 collective-permute-done.5
  208.3 13.0 %all-gather.3 = bf16[256,1024]{1,0:T(8,128)(2,1)S(1)} all-gather(bf16[64,1024]{1,0:T(8,128)(2,1)S(1)} %pad.31), channel_id=5, replica_groups=mesh['q'=4,'y'=2,'x'=2,'c'=2] {'q'}, dimensions={0}, use_global_device_ids=true | all-gather | bytes 655360 | tf_op jit(solution)/shard_map/all_gather | solution.py:299
  222.5 8.8 %collective-permute-done.7 = bf16[4,64,1024]{2,1,0:T(8,128)(2,1)S(1)} collective-permute-done((bf16[4,64,1024]{2,1,0:T(8,128)(2,1)S(1)}, bf16[4,64,1024]{2,1,0:T(8,128)(2,1)S(1)}, u32[]{:S(2)}, u32[]{:S(2)}) %collective-permute-start.7) | collective-permute-done | bytes 524320 | tf_op jit(solution)/shard_map/ppermute | solution.py:74
  234.9 4.0 collective-permute-done.9
  240.4 6.0 %collective-permute-start.11 = (bf16[1024,1024]{1,0:T(8,128)(2,1)}, bf16[1024,1024]{1,0:T(8,128)(2,1)}, u32[]{:S(2)}, u32[]{:S(2)}) collective-permute-start(bf16[1024,1024]{1,0:T(8,128)(2,1)} %bitcast.38), channel_id=1, source_target_pairs={{0,1},{1,0},{2,3},{3,2},{4,5},{5,4},{6,7},{7,6},{8,9},{9,8},{10,11... | collective-permute-start | bytes 6291464 | tf_op jit(solution)/shard_map/ppermute | solution.py:74
  247.3 4.5 fusion.180
  254.9 3.9 fusion.179
  265.5 9.4 %all_to_all.53 = f32[32,1,256]{2,1,0:T(1,128)S(1)} all-to-all(f32[32,1,256]{2,1,0:T(1,128)} %reshape.784), channel_id=1, replica_groups=mesh['q'=4,'y'=2,'x'=2,'c'=2] {'q','y','x','c'}, dimensions={0} | all-to-all | bytes 65536 | tf_op jit(solution)/shard_map/all_to_all | solution.py:320
  280.9 8.6 %all_to_all.54 = f32[32,1,64]{2,1,0:T(1,128)S(1)} all-to-all(f32[32,1,64]{2,1,0:T(1,128)S(1)} %broadcast_in_dim.101), channel_id=1, replica_groups=mesh['q'=4,'y'=2,'x'=2,'c'=2] {'q','y','x','c'}, dimensions={0} | all-to-all | bytes 16384 | tf_op jit(solution)/shard_map/all_to_all | solution.py:330
  291.0 7.1 %convolution_convert_fusion = bf16[1024,1024]{1,0:T(8,128)(2,1)} fusion(bf16[1000,960]{0,1:T(8,128)(2,1)} %convert_element_type.307, f32[1024,1000]{0,1:T(8,128)} %copy-done.20, f32[1024]{0:T(1024)S(1)} %squeeze.126, f32[1024]{0:T(1024)S(1)} %multiply_add_fusion.3, s32[1024]{0:T(1024)} %copy-done.80), kind=kOutput, calls=%fused_computation.60 | convolution fusion | flops 2106392576 | bytes 8125440 | tf_op jit(solution)/shard_map/dot_general | solution.py:52
  298.9 5.6 fusion.152
  304.6 4.8 fusion.181
  312.3 4.3 fusion.153
  316.6 7.4 %collective-permute-done.15 = bf16[4,64,1024]{2,1,0:T(8,128)(2,1)S(1)} collective-permute-done((bf16[4,64,1024]{2,1,0:T(8,128)(2,1)S(1)}, bf16[4,64,1024]{2,1,0:T(8,128)(2,1)S(1)}, u32[]{:S(2)}, u32[]{:S(2)}) %collective-permute-start.15) | collective-permute-done | bytes 524320 | tf_op jit(solution)/shard_map/ppermute | solution.py:74
  324.0 10.4 %collective-permute-done.14 = bf16[4,64,1024]{2,1,0:T(8,128)(2,1)S(1)} collective-permute-done((bf16[4,64,1024]{2,1,0:T(8,128)(2,1)S(1)}, bf16[4,64,1024]{2,1,0:T(8,128)(2,1)S(1)}, u32[]{:S(2)}, u32[]{:S(2)}) %collective-permute-start.14) | collective-permute-done | bytes 524320 | tf_op jit(solution)/shard_map/ppermute | solution.py:74
  336.6 2.1 collective-permute-start.16
  338.7 2.9 slice_add_fusion
  341.6 5.6 collective-permute-done.17
  348.1 13.3 %all-gather.4 = bf16[512,960]{1,0:T(8,128)(2,1)S(1)} all-gather(bf16[64,960]{1,0:T(8,128)(2,1)S(1)} %fusion.147), channel_id=6, replica_groups=mesh['q'=4,'y'=2,'x'=2,'c'=2] {'y','x','c'}, dimensions={0}, use_global_device_ids=true | all-gather | bytes 1105920 | tf_op jit(solution)/shard_map/all_gather | solution.py:143
  373.9 3.4 collective-permute-done.21
  381.3 2.2 multiply_reduce_fusion.1
  393.1 3.3 convolution_convert_fusion.9
  401.7 2.8 fusion.14
  409.3 2.2 convolution_convert_fusion.3
  411.5 2.6 copy.216
  414.2 3.3 all-to-all-start.5
  417.5 3.1 reduce-scatter.2.cloned.1.call-done
  424.5 3.2 reshape.698
  428.5 6.2 %fusion.2 = bf16[8,352,960]{2,1,0:T(8,128)(2,1)} fusion(bf16[1,3,960]{2,1,0:T(4,128)(2,1)S(1)} %copy-done.73, bf16[3,320,960]{2,1,0:T(8,128)(2,1)S(1)} %bitcast.233, bf16[5,128,960]{2,1,0:T(8,128)(2,1)S(1)} %reshape.698, bf16[5,192,960]{2,1,0:T(8,128)(2,1)S(1)} %bitcast.234), kind=kLoop, calls=%fused_computation.10 | loop fusion | flops 27033600 | bytes 10327680 | tf_op jit(solution)/shard_map/concatenate | solution.py:418
  434.7 3.7 dynamic-slice_bitcast_fusion
  439.4 4.5 all-to-all-start.6
  444.7 4.0 convert_add_fusion
  448.7 2.3 fusion.167
  457.0 23.3 %collective-permute-done.26 = bf16[2,176,960]{2,1,0:T(8,128)(2,1)S(1)} collective-permute-done((bf16[2,176,960]{2,1,0:T(8,128)(2,1)S(1)}, bf16[2,176,960]{2,1,0:T(8,128)(2,1)S(1)}, u32[]{:S(2)}, u32[]{:S(2)}) %collective-permute-start.26) | collective-permute-done | bytes 675872 | tf_op jit(solution)/shard_map/ppermute | solution.py:74
  483.6 3.8 fusion.50
  487.4 4.1 collective-permute-done.27
  496.9 3.5 fusion.5
  500.7 4.0 multiply_reduce_fusion
  506.4 4.5 collective-permute-done.29
  514.9 5.2 all-to-all-start.7
  526.9 4.3 all-to-all-start.8
  532.5 10.2 %add_multiply_fusion = (f32[1000,960]{0,1:T(8,128)}, f32[1000,960]{0,1:T(8,128)}, f32[1000,960]{0,1:T(8,128)}) fusion(f32[1000,960]{0,1:T(8,128)} %param.21, f32[1000,960]{0,1:T(8,128)} %get-tuple-element.111, f32[]{:T(128)S(6)} %div.148, f32[1000,960]{0,1:T(8,128)} %param.23, f32[1000,960]{0,1:T(8,128)} %param.22), kind=kLoop, calls=%fused_computation.25 | loop fusion | flops 14400000 | bytes 26880004 | tf_op jit(solution)/shard_map/mul | solution.py:107
  550.5 3.5 collective-permute-start.34
  554.8 4.8 add_multiply_fusion.1
  (494 shorter events, 169.4 us)
Async XLA Ops:
  8.5 5.8 %collective-permute-start = (bf16[2880]{0:T(1024)(128)(2,1)S(1)}, bf16[2880]{0:T(1024)(128)(2,1)S(1)}, u32[]{:S(2)}, u32[]{:S(2)}) collective-permute-start(bf16[2880]{0:T(1024)(128)(2,1)S(1)} %slice.349), channel_id=1, source_target_pairs={{1,0},{2,1},{3,2},{4,3},{5,4},{6,5},{7,6},{8,7},{9,8},{10,9},{11,1... | collective-permute-start | bytes 17288 | tf_op jit(solution)/shard_map/ppermute | solution.py:200
  17.9 17.6 %collective-permute-start.1 = (bf16[328,960]{1,0:T(8,128)(2,1)S(1)}, bf16[328,960]{1,0:T(8,128)(2,1)}, u32[]{:S(2)}, u32[]{:S(2)}) collective-permute-start(bf16[328,960]{1,0:T(8,128)(2,1)S(1)} %maximum_maximum_fusion), channel_id=1, source_target_pairs={{0,16},{1,17},{2,18},{3,19},{4,20},{5,21},{6,22},{7,23}} | collective-permute-start | bytes 1889288 | tf_op jit(solution)/shard_map/ppermute | solution.py:216
  28.0 11.1 %all-to-all-start = ((s32[32,1,96]{2,1,0:T(1,128)}), s32[32,1,96]{2,1,0:T(1,128)S(1)}, u32[]{:S(2)}, u32[]{:S(2)}) async-start(s32[32,1,96]{2,1,0:T(1,128)} %bitcast), calls=%async_computation | async-start | bytes 32768 | tf_op jit(solution)/shard_map/all_to_all | solution.py:214
  36.6 17.2 %collective-permute-start.2 = (bf16[328,960]{1,0:T(8,128)(2,1)S(1)}, bf16[328,960]{1,0:T(8,128)(2,1)S(1)}, u32[]{:S(2)}, u32[]{:S(2)}) collective-permute-start(bf16[328,960]{1,0:T(8,128)(2,1)S(1)} %broadcast_select_fusion), channel_id=1, source_target_pairs={{0,8},{16,24},{1,9},{17,25},{2,10},{18,26},{3,11},{19,27},{4,12},{... | collective-permute-start | bytes 1889288 | tf_op jit(solution)/shard_map/ppermute | solution.py:218
  39.1 15.7 %all-to-all-start.1 = ((bf16[8,60,640]{2,1,0:T(8,128)(2,1)}), bf16[8,60,640]{2,1,0:T(8,128)(2,1)S(1)}, u32[]{:S(2)}, u32[]{:S(2)}) async-start(bf16[8,60,640]{2,1,0:T(8,128)(2,1)} %reshape.773), calls=%async_computation.1 | async-start | bytes 1310720 | tf_op jit(solution)/shard_map/all_to_all | solution.py:208
  44.7 74.8 %all-gather.8.cloned.1.call-start = ((), (), s32[]{:S(2)}) async-start(), calls=%async_computation.11 | async-start | bytes 6045696 | tf_op jit(solution)/shard_map/all_gather | solution.py:222
  54.8 10.1 %copy-start = (s32[32]{0:T(128)S(1)}, s32[32]{0:T(128)}, u32[]{:S(2)}) copy-start(s32[32]{0:T(128)} %constant.366.clone) | copy-start | bytes 388
  54.8 11.4 %copy-start.56 = (f32[512,64]{1,0:T(8,128)S(1)}, f32[512,64]{1,0:T(8,128)}, u32[]{:S(2)}) copy-start(f32[512,64]{1,0:T(8,128)} %constant.392) | copy-start | bytes 393220
  54.8 12.0 %copy-start.55 = (f32[512,64]{1,0:T(8,128)S(1)}, f32[512,64]{1,0:T(8,128)}, u32[]{:S(2)}) copy-start(f32[512,64]{1,0:T(8,128)} %constant.391) | copy-start | bytes 393220
  54.9 74.3 %all-to-all-start.2 = ((bf16[32,32,960]{2,1,0:T(8,128)(2,1)}), bf16[32,32,960]{2,1,0:T(8,128)(2,1)}, u32[]{:S(2)}, u32[]{:S(2)}) async-start(bf16[32,32,960]{2,1,0:T(8,128)(2,1)} %bitcast.232), calls=%async_computation.2 | async-start | bytes 4194304 | tf_op jit(solution)/shard_map/all_to_all | solution.py:190
  64.2 119.7 %all-gather.10.cloned.1.call-start = ((), (), s32[]{:S(2)}) async-start(), calls=%async_computation.12 | async-start | bytes 3072000 | tf_op jit(solution)/shard_map/all_gather | solution.py:230
  66.8 74.3 %copy-start.53 = (f32[64,64]{1,0:T(8,128)}, f32[64,64]{1,0:T(8,128)S(1)}, u32[]{:S(2)}) copy-start(f32[64,64]{1,0:T(8,128)S(1)} %gather_fusion.1) | copy-start | bytes 49156
  132.1 27.2 %copy-start.4 = (bf16[512,960]{0,1:T(8,128)(2,1)}, bf16[512,960]{0,1:T(8,128)(2,1)S(1)}, u32[]{:S(2)}) copy-start(bf16[512,960]{0,1:T(8,128)(2,1)S(1)} %get-tuple-element.184) | copy-start | bytes 2949124
  132.2 29.8 %copy-start.69 = (f32[1,1,960]{2,1,0:T(1,128)}, f32[1,1,960]{2,1,0:T(1,128)S(1)}, u32[]{:S(2)}) copy-start(f32[1,1,960]{2,1,0:T(1,128)S(1)} %get-tuple-element.171) | copy-start | bytes 11524
  132.2 76.0 %copy-start.67 = (f32[1,1,960]{2,1,0:T(1,128)}, f32[1,1,960]{2,1,0:T(1,128)S(1)}, u32[]{:S(2)}) copy-start(f32[1,1,960]{2,1,0:T(1,128)S(1)} %get-tuple-element.170) | copy-start | bytes 11524
  132.9 287.7 %reduce-scatter.2.cloned.1.call-start = ((), (), s32[]{:S(2)}) async-start(), calls=%async_computation.10 | async-start | bytes 3072000 | tf_op jit(solution)/shard_map/reduce_scatter | solution.py:396
  162.0 23.5 %copy-start.92 = (f32[64]{0:T(128)}, f32[64]{0:T(128)S(1)}, u32[]{:S(2)}) copy-start(f32[64]{0:T(128)S(1)} %add_rsqrt_fusion.2) | copy-start | bytes 772
  190.5 2.8 collective-permute-start.3
  196.8 5.8 %collective-permute-start.6 = (bf16[64,1024]{1,0:T(8,128)(2,1)}, bf16[64,1024]{1,0:T(8,128)(2,1)S(1)}, u32[]{:S(2)}, u32[]{:S(2)}) collective-permute-start(bf16[64,1024]{1,0:T(8,128)(2,1)} %get-tuple-element.158), channel_id=1, source_target_pairs={{0,6},{2,4},{4,2},{6,0},{1,7},{3,5},{5,3},{7,1},{8,14},{10,12},{12... | collective-permute-start | bytes 393224 | tf_op jit(solution)/shard_map/ppermute | solution.py:74
  198.9 7.3 %collective-permute-start.5 = (bf16[64,1024]{1,0:T(8,128)(2,1)}, bf16[64,1024]{1,0:T(8,128)(2,1)S(1)}, u32[]{:S(2)}, u32[]{:S(2)}) collective-permute-start(bf16[64,1024]{1,0:T(8,128)(2,1)} %get-tuple-element.159), channel_id=1, source_target_pairs={{0,4},{2,6},{4,0},{6,2},{1,5},{3,7},{5,1},{7,3},{8,12},{10,14},{12... | collective-permute-start | bytes 393224 | tf_op jit(solution)/shard_map/ppermute | solution.py:74
  199.1 7.7 %collective-permute-start.4 = (bf16[64,1024]{1,0:T(8,128)(2,1)}, bf16[64,1024]{1,0:T(8,128)(2,1)}, u32[]{:S(2)}, u32[]{:S(2)}) collective-permute-start(bf16[64,1024]{1,0:T(8,128)(2,1)} %get-tuple-element.157), channel_id=1, source_target_pairs={{0,2},{2,0},{4,6},{6,4},{1,3},{3,1},{5,7},{7,5},{8,10},{10,8},{12,... | collective-permute-start | bytes 393224 | tf_op jit(solution)/shard_map/ppermute | solution.py:74
  208.2 25.9 %copy-start.89 = (f32[64]{0:T(128)}, f32[64]{0:T(128)S(1)}, u32[]{:S(2)}) copy-start(f32[64]{0:T(128)S(1)} %add_rsqrt_fusion.1) | copy-start | bytes 772
  221.4 9.9 %collective-permute-start.7 = (bf16[4,64,1024]{2,1,0:T(8,128)(2,1)S(1)}, bf16[4,64,1024]{2,1,0:T(8,128)(2,1)S(1)}, u32[]{:S(2)}, u32[]{:S(2)}) collective-permute-start(bf16[4,64,1024]{2,1,0:T(8,128)(2,1)S(1)} %bitcast.259), channel_id=1, source_target_pairs={{0,2},{2,0},{1,3},{3,1},{4,6},{6,4},{5,7},{7,5},{8,10},{10,8},{9,1... | collective-permute-start | bytes 1572872 | tf_op jit(solution)/shard_map/ppermute | solution.py:74
  222.5 9.7 %collective-permute-start.8 = (bf16[4,64,1024]{2,1,0:T(8,128)(2,1)S(1)}, bf16[4,64,1024]{2,1,0:T(8,128)(2,1)S(1)}, u32[]{:S(2)}, u32[]{:S(2)}) collective-permute-start(bf16[4,64,1024]{2,1,0:T(8,128)(2,1)S(1)} %bitcast.260), channel_id=1, source_target_pairs={{0,4},{4,0},{1,5},{5,1},{2,6},{6,2},{3,7},{7,3},{8,12},{12,8},{9,1... | collective-permute-start | bytes 1572872 | tf_op jit(solution)/shard_map/ppermute | solution.py:74
  231.3 7.6 %collective-permute-start.9 = (bf16[2,64,1024]{2,1,0:T(8,128)(2,1)S(1)}, bf16[2,64,1024]{2,1,0:T(8,128)(2,1)S(1)}, u32[]{:S(2)}, u32[]{:S(2)}) collective-permute-start(bf16[2,64,1024]{2,1,0:T(8,128)(2,1)S(1)} %slice.375), channel_id=1, source_target_pairs={{0,4},{4,0},{1,5},{5,1},{2,6},{6,2},{3,7},{7,3},{8,12},{12,8},{9,1... | collective-permute-start | bytes 786440 | tf_op jit(solution)/shard_map/ppermute | solution.py:74
  232.2 14.1 %copy-start.96 = (s32[32]{0:T(128)S(1)}, s32[32]{0:T(128)}, u32[]{:S(2)}) copy-start(s32[32]{0:T(128)} %constant.365.clone) | copy-start | bytes 388
  232.2 14.2 %copy-start.98 = (s32[32]{0:T(128)S(1)}, s32[32]{0:T(128)}, u32[]{:S(2)}) copy-start(s32[32]{0:T(128)} %copy-done.97) | copy-start | bytes 388
  232.2 7.4 %collective-permute-start.10 = (bf16[2,64,1024]{2,1,0:T(8,128)(2,1)S(1)}, bf16[2,64,1024]{2,1,0:T(8,128)(2,1)S(1)}, u32[]{:S(2)}, u32[]{:S(2)}) collective-permute-start(bf16[2,64,1024]{2,1,0:T(8,128)(2,1)S(1)} %slice.376), channel_id=1, source_target_pairs={{0,2},{2,0},{1,3},{3,1},{4,6},{6,4},{5,7},{7,5},{8,10},{10,8},{9,1... | collective-permute-start | bytes 786440 | tf_op jit(solution)/shard_map/ppermute | solution.py:74
  240.4 13.6 %collective-permute-start.11 = (bf16[1024,1024]{1,0:T(8,128)(2,1)}, bf16[1024,1024]{1,0:T(8,128)(2,1)}, u32[]{:S(2)}, u32[]{:S(2)}) collective-permute-start(bf16[1024,1024]{1,0:T(8,128)(2,1)} %bitcast.38), channel_id=1, source_target_pairs={{0,1},{1,0},{2,3},{3,2},{4,5},{5,4},{6,7},{7,6},{8,9},{9,8},{10,11... | collective-permute-start | bytes 6291464 | tf_op jit(solution)/shard_map/ppermute | solution.py:74
  247.2 11.6 %copy-start.80 = (s32[1024]{0:T(1024)}, s32[1024]{0:T(1024)S(1)}, u32[]{:S(2)}) copy-start(s32[1024]{0:T(1024)S(1)} %sub.235) | copy-start | bytes 12292
  298.2 6.4 %collective-permute-start.12 = (bf16[1024,1024]{1,0:T(8,128)(2,1)}, bf16[1024,1024]{1,0:T(8,128)(2,1)}, u32[]{:S(2)}, u32[]{:S(2)}) collective-permute-start(bf16[1024,1024]{1,0:T(8,128)(2,1)} %convolution_convert_fusion), channel_id=1, source_target_pairs={{0,1},{1,0},{2,3},{3,2},{4,5},{5,4},{6,7},{7,6},{8,9},{9,8},{10,11... | collective-permute-start | bytes 6291464 | tf_op jit(solution)/shard_map/ppermute | solution.py:74
  309.6 14.5 %collective-permute-start.15 = (bf16[4,64,1024]{2,1,0:T(8,128)(2,1)S(1)}, bf16[4,64,1024]{2,1,0:T(8,128)(2,1)S(1)}, u32[]{:S(2)}, u32[]{:S(2)}) collective-permute-start(bf16[4,64,1024]{2,1,0:T(8,128)(2,1)S(1)} %bitcast.286), channel_id=1, source_target_pairs={{0,6},{2,4},{4,2},{6,0},{1,7},{3,5},{5,3},{7,1},{8,14},{10,12},{12... | collective-permute-start | bytes 1572872 | tf_op jit(solution)/shard_map/ppermute | solution.py:74
  310.0 24.5 %collective-permute-start.14 = (bf16[4,64,1024]{2,1,0:T(8,128)(2,1)S(1)}, bf16[4,64,1024]{2,1,0:T(8,128)(2,1)S(1)}, u32[]{:S(2)}, u32[]{:S(2)}) collective-permute-start(bf16[4,64,1024]{2,1,0:T(8,128)(2,1)S(1)} %bitcast.285), channel_id=1, source_target_pairs={{0,4},{2,6},{4,0},{6,2},{1,5},{3,7},{5,1},{7,3},{8,12},{10,14},{12... | collective-permute-start | bytes 1572872 | tf_op jit(solution)/shard_map/ppermute | solution.py:74
  311.0 23.5 %collective-permute-start.13 = (bf16[4,64,1024]{2,1,0:T(8,128)(2,1)S(1)}, bf16[4,64,1024]{2,1,0:T(8,128)(2,1)S(1)}, u32[]{:S(2)}, u32[]{:S(2)}) collective-permute-start(bf16[4,64,1024]{2,1,0:T(8,128)(2,1)S(1)} %bitcast.284), channel_id=1, source_target_pairs={{0,2},{2,0},{4,6},{6,4},{1,3},{3,1},{5,7},{7,5},{8,10},{10,8},{12,... | collective-permute-start | bytes 1572872 | tf_op jit(solution)/shard_map/ppermute | solution.py:74
  334.9 6.7 %collective-permute-start.18 = (bf16[64,1024]{1,0:T(8,128)(2,1)S(1)}, bf16[64,1024]{1,0:T(8,128)(2,1)S(1)}, u32[]{:S(2)}, u32[]{:S(2)}) collective-permute-start(bf16[64,1024]{1,0:T(8,128)(2,1)S(1)} %get-tuple-element.155), channel_id=1, source_target_pairs={{0,24},{8,16},{16,8},{24,0},{1,25},{9,17},{17,9},{25,1},{2,26},{10... | collective-permute-start | bytes 393224 | tf_op jit(solution)/shard_map/ppermute | solution.py:74
  335.2 12.0 %collective-permute-start.17 = (bf16[64,1024]{1,0:T(8,128)(2,1)S(1)}, bf16[64,1024]{1,0:T(8,128)(2,1)S(1)}, u32[]{:S(2)}, u32[]{:S(2)}) collective-permute-start(bf16[64,1024]{1,0:T(8,128)(2,1)S(1)} %get-tuple-element.156), channel_id=1, source_target_pairs={{0,16},{8,24},{16,0},{24,8},{1,17},{9,25},{17,1},{25,9},{2,18},{10... | collective-permute-start | bytes 393224 | tf_op jit(solution)/shard_map/ppermute | solution.py:74
  336.6 10.7 %copy-start.68 = (f32[1,1,960]{2,1,0:T(1,128)S(1)}, f32[1,1,960]{2,1,0:T(1,128)}, u32[]{:S(2)}) copy-start(f32[1,1,960]{2,1,0:T(1,128)} %copy-done.67) | copy-start | bytes 11524
  336.6 10.7 %copy-start.90 = (f32[64]{0:T(128)S(1)}, f32[64]{0:T(128)}, u32[]{:S(2)}) copy-start(f32[64]{0:T(128)} %copy-done.89) | copy-start | bytes 772
  336.6 10.7 %collective-permute-start.16 = (bf16[64,1024]{1,0:T(8,128)(2,1)S(1)}, bf16[64,1024]{1,0:T(8,128)(2,1)S(1)}, u32[]{:S(2)}, u32[]{:S(2)}) collective-permute-start(bf16[64,1024]{1,0:T(8,128)(2,1)S(1)} %get-tuple-element.154), channel_id=1, source_target_pairs={{0,8},{8,0},{16,24},{24,16},{1,9},{9,1},{17,25},{25,17},{2,10},{10... | collective-permute-start | bytes 393224 | tf_op jit(solution)/shard_map/ppermute | solution.py:74
  341.5 19.9 %copy-start.38 = (f32[512,640]{1,0:T(8,128)S(1)}, f32[512,640]{1,0:T(8,128)}, u32[]{:S(2)}) copy-start(f32[512,640]{1,0:T(8,128)} %copy-done.37) | copy-start | bytes 3932164
  341.5 19.9 %copy-start.51 = (bf16[320,640]{1,0:T(8,128)(2,1)S(1)}, bf16[320,640]{1,0:T(8,128)(2,1)}, u32[]{:S(2)}) copy-start(bf16[320,640]{1,0:T(8,128)(2,1)} %copy-done.50) | copy-start | bytes 1228804
  341.5 19.9 %copy-start.64 = (bf16[160,320]{1,0:T(8,128)(2,1)S(1)}, bf16[160,320]{1,0:T(8,128)(2,1)}, u32[]{:S(2)}) copy-start(bf16[160,320]{1,0:T(8,128)(2,1)} %copy-done.63) | copy-start | bytes 307204
  341.5 19.9 %copy-start.66 = (bf16[160,320]{1,0:T(8,128)(2,1)S(1)}, bf16[160,320]{1,0:T(8,128)(2,1)}, u32[]{:S(2)}) copy-start(bf16[160,320]{1,0:T(8,128)(2,1)} %copy-done.65) | copy-start | bytes 307204
  363.8 2.5 collective-permute-start.19
  368.0 5.9 %collective-permute-start.22 = (bf16[64,1024]{1,0:T(8,128)(2,1)S(1)}, bf16[64,1024]{1,0:T(8,128)(2,1)}, u32[]{:S(2)}, u32[]{:S(2)}) collective-permute-start(bf16[64,1024]{1,0:T(8,128)(2,1)S(1)} %get-tuple-element.152), channel_id=1, source_target_pairs={{0,6},{2,4},{4,2},{6,0},{1,7},{3,5},{5,3},{7,1},{8,14},{10,12},{12... | collective-permute-start | bytes 393224 | tf_op jit(solution)/shard_map/ppermute | solution.py:74
  369.3 8.1 %collective-permute-start.21 = (bf16[64,1024]{1,0:T(8,128)(2,1)S(1)}, bf16[64,1024]{1,0:T(8,128)(2,1)}, u32[]{:S(2)}, u32[]{:S(2)}) collective-permute-start(bf16[64,1024]{1,0:T(8,128)(2,1)S(1)} %get-tuple-element.153), channel_id=1, source_target_pairs={{0,4},{2,6},{4,0},{6,2},{1,5},{3,7},{5,1},{7,3},{8,12},{10,14},{12... | collective-permute-start | bytes 393224 | tf_op jit(solution)/shard_map/ppermute | solution.py:74
  369.6 7.8 %collective-permute-start.20 = (bf16[64,1024]{1,0:T(8,128)(2,1)S(1)}, bf16[64,1024]{1,0:T(8,128)(2,1)}, u32[]{:S(2)}, u32[]{:S(2)}) collective-permute-start(bf16[64,1024]{1,0:T(8,128)(2,1)S(1)} %get-tuple-element.151), channel_id=1, source_target_pairs={{0,2},{2,0},{4,6},{6,4},{1,3},{3,1},{5,7},{7,5},{8,10},{10,8},{12,... | collective-permute-start | bytes 393224 | tf_op jit(solution)/shard_map/ppermute | solution.py:74
  414.2 20.5 %all-to-all-start.5 = ((bf16[32,8,960]{2,1,0:T(8,128)(2,1)}), bf16[32,8,960]{2,1,0:T(8,128)(2,1)}, u32[]{:S(2)}, u32[]{:S(2)}) async-start(bf16[32,8,960]{2,1,0:T(8,128)(2,1)} %bitcast.86), calls=%async_computation.6 | async-start | bytes 1048576 | tf_op jit(solution)/shard_map/all_to_all | solution.py:190
  438.4 6.3 %collective-permute-start.23 = (bf16[4,352,960]{2,1,0:T(8,128)(2,1)}, bf16[4,352,960]{2,1,0:T(8,128)(2,1)}, u32[]{:S(2)}, u32[]{:S(2)}) collective-permute-start(bf16[4,352,960]{2,1,0:T(8,128)(2,1)} %dynamic-slice_bitcast_fusion), channel_id=1, source_target_pairs={{0,1},{1,0},{2,3},{3,2},{4,5},{5,4},{6,7},{7,6},{8,9},{9,8},{10,11... | collective-permute-start | bytes 8110088 | tf_op jit(solution)/shard_map/ppermute | solution.py:74
  439.4 53.7 %all-to-all-start.6 = ((bf16[32,24,960]{2,1,0:T(8,128)(2,1)}), bf16[32,24,960]{2,1,0:T(8,128)(2,1)}, u32[]{:S(2)}, u32[]{:S(2)}) async-start(bf16[32,24,960]{2,1,0:T(8,128)(2,1)} %bitcast.87), calls=%async_computation.7 | async-start | bytes 3145728 | tf_op jit(solution)/shard_map/all_to_all | solution.py:190
  452.7 27.6 %collective-permute-start.26 = (bf16[2,176,960]{2,1,0:T(8,128)(2,1)S(1)}, bf16[2,176,960]{2,1,0:T(8,128)(2,1)S(1)}, u32[]{:S(2)}, u32[]{:S(2)}) collective-permute-start(bf16[2,176,960]{2,1,0:T(8,128)(2,1)S(1)} %fusion.59), channel_id=1, source_target_pairs={{0,4},{4,0},{1,5},{5,1},{2,6},{6,2},{3,7},{7,3},{8,12},{12,8},{9,1... | collective-permute-start | bytes 2027528 | tf_op jit(solution)/shard_map/ppermute | solution.py:74
  455.4 26.6 %collective-permute-start.24 = (bf16[2,176,960]{2,1,0:T(8,128)(2,1)S(1)}, bf16[2,176,960]{2,1,0:T(8,128)(2,1)}, u32[]{:S(2)}, u32[]{:S(2)}) collective-permute-start(bf16[2,176,960]{2,1,0:T(8,128)(2,1)S(1)} %fusion.58), channel_id=1, source_target_pairs={{0,2},{2,0},{1,3},{3,1},{4,6},{6,4},{5,7},{7,5},{8,10},{10,8},{9,1... | collective-permute-start | bytes 2027528 | tf_op jit(solution)/shard_map/ppermute | solution.py:74
  456.9 25.1 %copy-start.6 = (f32[2,2,176,960]{3,2,1,0:T(8,128)S(1)}, f32[2,2,176,960]{3,2,1,0:T(8,128)}, u32[]{:S(2)}) copy-start(f32[2,2,176,960]{3,2,1,0:T(8,128)} %get-tuple-element.125) | copy-start | bytes 8110084
  481.9 9.5 %collective-permute-start.27 = (bf16[176,960]{1,0:T(8,128)(2,1)S(1)}, bf16[176,960]{1,0:T(8,128)(2,1)S(1)}, u32[]{:S(2)}, u32[]{:S(2)}) collective-permute-start(bf16[176,960]{1,0:T(8,128)(2,1)S(1)} %fusion.76), channel_id=1, source_target_pairs={{0,2},{2,0},{1,3},{3,1},{4,6},{6,4},{5,7},{7,5},{8,10},{10,8},{9,1... | collective-permute-start | bytes 1013768 | tf_op jit(solution)/shard_map/ppermute | solution.py:74
  483.5 9.5 %collective-permute-start.25 = (bf16[176,960]{1,0:T(8,128)(2,1)S(1)}, bf16[176,960]{1,0:T(8,128)(2,1)S(1)}, u32[]{:S(2)}, u32[]{:S(2)}) collective-permute-start(bf16[176,960]{1,0:T(8,128)(2,1)S(1)} %fusion.75), channel_id=1, source_target_pairs={{0,4},{4,0},{1,5},{5,1},{2,6},{6,2},{3,7},{7,3},{8,12},{12,8},{9,1... | collective-permute-start | bytes 1013768 | tf_op jit(solution)/shard_map/ppermute | solution.py:74
  493.3 13.2 %collective-permute-start.30 = (bf16[88,960]{1,0:T(8,128)(2,1)S(1)}, bf16[88,960]{1,0:T(8,128)(2,1)S(1)}, u32[]{:S(2)}, u32[]{:S(2)}) collective-permute-start(bf16[88,960]{1,0:T(8,128)(2,1)S(1)} %get-tuple-element.133), channel_id=1, source_target_pairs={{0,24},{8,16},{16,8},{24,0},{1,25},{9,17},{17,9},{25,1},{2,26},{10... | collective-permute-start | bytes 506888 | tf_op jit(solution)/shard_map/ppermute | solution.py:74
  495.3 15.6 %collective-permute-start.29 = (bf16[88,960]{1,0:T(8,128)(2,1)S(1)}, bf16[88,960]{1,0:T(8,128)(2,1)S(1)}, u32[]{:S(2)}, u32[]{:S(2)}) collective-permute-start(bf16[88,960]{1,0:T(8,128)(2,1)S(1)} %get-tuple-element.134), channel_id=1, source_target_pairs={{0,16},{8,24},{16,0},{24,8},{1,17},{9,25},{17,1},{25,9},{2,18},{10... | collective-permute-start | bytes 506888 | tf_op jit(solution)/shard_map/ppermute | solution.py:74
  495.4 15.4 %collective-permute-start.28 = (bf16[88,960]{1,0:T(8,128)(2,1)S(1)}, bf16[88,960]{1,0:T(8,128)(2,1)S(1)}, u32[]{:S(2)}, u32[]{:S(2)}) collective-permute-start(bf16[88,960]{1,0:T(8,128)(2,1)S(1)} %get-tuple-element.132), channel_id=1, source_target_pairs={{0,8},{8,0},{16,24},{24,16},{1,9},{9,1},{17,25},{25,17},{2,10},{10... | collective-permute-start | bytes 506888 | tf_op jit(solution)/shard_map/ppermute | solution.py:74
  514.9 12.0 %all-to-all-start.7 = ((f32[32,1,2]{2,1,0:T(1,128)}), f32[32,1,2]{2,1,0:T(1,128)S(1)}, u32[]{:S(2)}, u32[]{:S(2)}) async-start(f32[32,1,2]{2,1,0:T(1,128)} %broadcast_in_dim.168), calls=%async_computation.8 | async-start | bytes 32768 | tf_op jit(solution)/shard_map/all_to_all | solution.py:406
  522.8 19.9 %collective-permute-start.33 = (bf16[88,960]{1,0:T(8,128)(2,1)S(1)}, bf16[88,960]{1,0:T(8,128)(2,1)S(1)}, u32[]{:S(2)}, u32[]{:S(2)}) collective-permute-start(bf16[88,960]{1,0:T(8,128)(2,1)S(1)} %get-tuple-element.85), channel_id=1, source_target_pairs={{16,0},{17,1},{18,2},{19,3},{20,4},{21,5},{22,6},{23,7}} | collective-permute-start | bytes 506888 | tf_op jit(solution)/shard_map/ppermute | solution.py:446
  524.1 19.0 %collective-permute-start.32 = (bf16[88,960]{1,0:T(8,128)(2,1)S(1)}, bf16[88,960]{1,0:T(8,128)(2,1)S(1)}, u32[]{:S(2)}, u32[]{:S(2)}) collective-permute-start(bf16[88,960]{1,0:T(8,128)(2,1)S(1)} %get-tuple-element.85), channel_id=1, source_target_pairs={{8,0},{9,1},{10,2},{11,3},{12,4},{13,5},{14,6},{15,7}} | collective-permute-start | bytes 506888 | tf_op jit(solution)/shard_map/ppermute | solution.py:446
  525.4 17.3 %collective-permute-start.31 = (bf16[88,960]{1,0:T(8,128)(2,1)S(1)}, bf16[88,960]{1,0:T(8,128)(2,1)S(1)}, u32[]{:S(2)}, u32[]{:S(2)}) collective-permute-start(bf16[88,960]{1,0:T(8,128)(2,1)S(1)} %get-tuple-element.85), channel_id=1, source_target_pairs={{24,0},{25,1},{26,2},{27,3},{28,4},{29,5},{30,6},{31,7}} | collective-permute-start | bytes 506888 | tf_op jit(solution)/shard_map/ppermute | solution.py:446
  526.9 19.7 %all-to-all-start.8 = ((bf16[8,60,640]{2,1,0:T(8,128)(2,1)}), bf16[8,60,640]{2,1,0:T(8,128)(2,1)S(1)}, u32[]{:S(2)}, u32[]{:S(2)}) async-start(bf16[8,60,640]{2,1,0:T(8,128)(2,1)} %reshape.710), calls=%async_computation.9 | async-start | bytes 1310720 | tf_op jit(solution)/shard_map/all_to_all | solution.py:434
  550.5 4.3 collective-permute-start.34
  (82 other events, 270.7 us)
Sparse Core Ops, SparseCore 0:
  54.9 64.5 all-gather.7
  133.0 50.9 all-gather.9
  372.6 47.8 reduce-scatter.1

commit v9 on v8

--- a/solution.py
+++ b/solution.py
@@ -401,14 +401,12 @@
     grad_q = dot(h_pick, d_q, 0, 0).astype(bf16)
     grad_kv = dot(h_attn, d_kv, 0, 0).astype(bf16)
 
-    def finish(squares, table_grad):
+    def norm_of(squares):
         sums = jnp.broadcast_to(jnp.stack([squares, my_loss])[None], (devices, 2))
         sums = jnp.sum(lax.all_to_all(sums, ALL, split_axis=0, concat_axis=0, tiled=True), axis=0)
         grad_norm = jnp.sqrt(sums[0])
-        loss = sums[1] / loss_total
         limit = CLIP_C / math.sqrt(loss_total)
-        clip_factor = limit / jnp.maximum(grad_norm, limit)
-        return loss, grad_norm, clip_factor, adamw_step(table_master, table_grad, table_m, table_v, clip_factor)
+        return sums[1] / loss_total, grad_norm, limit / jnp.maximum(grad_norm, limit)
 
     gain_grads = jnp.concatenate([grad_attn, grad_mlp, grad_final]).astype(bf16)
     if aligned:
@@ -442,17 +440,17 @@
         table_squares = jnp.sum(table_grad * table_grad)
         quarter = quarter.astype(bf16)
         squares = jnp.sum(quarter.astype(f32) ** 2) + jnp.sum(share.astype(f32) ** 2) + table_squares
-        quarter, squares = lax.optimization_barrier((quarter, squares))
+        quarter, squares, got = lax.optimization_barrier((quarter, squares, got))
         quarters = [quarter] + [lax.ppermute(quarter, "q", [(k, 0)]) for k in (1, 2, 3)]
         first = jnp.concatenate(quarters)
         gain_out = first[SHARE : SHARE + 3].reshape(-1)
         both = jnp.concatenate([first[:TOP], first[TOP:SHARE].reshape(TOP, KV)], axis=1)
         first = jnp.where(p_index < 5, both.reshape(-1), first[:SHARE].reshape(-1))
-        loss, grad_norm, clip_factor, table_new = finish(squares, table_grad)
-        got, table_new = lax.optimization_barrier((got, table_new))
         by_share = got.reshape(8, 60, 2, UNIT).transpose(1, 2, 0, 3).reshape(-1)
         mine = jnp.where(q_index == 3, down_unpack(share).reshape(-1), by_share)
         mine = jnp.where(q_index == 0, first, mine)
+        loss, grad_norm, clip_factor = norm_of(squares)
+        mine, clip_factor = lax.optimization_barrier((mine, clip_factor))
     else:
         table_grad = head_grad
         for low, high, rows in zip(cuts_back, cuts_back[1:], arrived):
@@ -472,9 +470,9 @@
     layer_grad = lax.dynamic_slice(stream, (drift * me,), (shard,)).astype(f32)
 
     if not aligned:
-        squares = jnp.sum(layer_grad * layer_grad) + table_squares
-        loss, grad_norm, clip_factor, table_new = finish(squares, table_grad)
+        loss, grad_norm, clip_factor = norm_of(jnp.sum(layer_grad * layer_grad) + table_squares)
     flat_new = adamw_step(flat_master, layer_grad, flat_m, flat_v, clip_factor)
+    table_new = adamw_step(table_master, table_grad, table_m, table_v, clip_factor)
     return (loss, grad_norm) + flat_new + table_new
 
 

time: 580 us -> 583 us (level)
    unnamed x207 -> x209, local copies, waits for them, and re-layouts: 18.7 us -> 18.7 us
where the time goes in v9:
time: 583 us; the launch traced here: 573 us
  waiting for transfers between devices  143 us (25%)
  local copies, waits for them, and re-layouts  92.5 us (16%)
  matrix products  90.2 us (15%)
  starting transfers between devices  87.3 us (15%)
  other arithmetic  83.4 us (14%)
  blocking collectives  55.5 us (10%)
  between operations  21.4 us (4%)
    ppermute x28, waiting for transfers between devices, flip(): return lax.ppermute(rows, axes, [(i, i ^ bits) for i in range(size)])  77.3 us
    dot_general x37, matrix products, dot(): lax.dot_general(left, right, (((left_dim,), (right_dim,)), ((), ())), pre...  74.8 us
    all_gather x1, waiting for transfers between devices, local(): level = lax.all_gather(first, PLANE)  49.1 us
    ppermute x28, starting transfers between devices, flip(): return lax.ppermute(rows, axes, [(i, i ^ bits) for i in range(size)])  29 us
    all_gather x2, blocking collectives, spread_plane(): return widen(lax.all_gather(rows, PLANE).reshape(-1, D))  24.4 us
    unnamed x209, local copies, waits for them, and re-layouts  18.7 us
    all_to_all x3, starting transfers between devices, exchange(): lax.all_to_all(blocks, ALL, split_axis=0, concat_axis=0, tiled=True)  17.2 us
    mul x2, other arithmetic, adamw_step(): return (new_one, new_two, -RATE * (ratio + DECAY * param))  14.7 us
  transfers between devices with their start and end apart: 45, of which 22 were waited for; matrix products, arithmetic and copies ran while one was open for 32% of the time, Pallas kernels for 0%

profile of v9, /device:TPU:1, one launch (start us, length us, event | category | flops | bytes accessed | tf_op | source)
XLA Modules:
  0.0 573.4 jit_solution(15291992147972210053)
XLA Ops:
  17.9 5.8 %collective-permute-start.1 = (bf16[328,960]{1,0:T(8,128)(2,1)S(1)}, bf16[328,960]{1,0:T(8,128)(2,1)}, u32[]{:S(2)}, u32[]{:S(2)}) collective-permute-start(bf16[328,960]{1,0:T(8,128)(2,1)S(1)} %maximum_maximum_fusion), channel_id=1, source_target_pairs={{0,16},{1,17},{2,18},{3,19},{4,20},{5,21},{6,22},{7,23}} | collective-permute-start | bytes 1889288 | tf_op jit(solution)/shard_map/ppermute | solution.py:216
  23.6 3.7 convert_element_type.307
  28.0 4.2 all-to-all-start
  36.6 2.1 collective-permute-start.2
  39.1 5.6 all-to-all-start.1
  44.8 5.2 fusion.24
  50.0 3.9 copy.190
  54.9 9.4 %all-to-all-start.2 = ((bf16[32,32,960]{2,1,0:T(8,128)(2,1)}), bf16[32,32,960]{2,1,0:T(8,128)(2,1)}, u32[]{:S(2)}, u32[]{:S(2)}) async-start(bf16[32,32,960]{2,1,0:T(8,128)(2,1)} %bitcast.232), calls=%async_computation.2 | async-start | bytes 4194304 | tf_op jit(solution)/shard_map/all_to_all | solution.py:190
  70.4 49.1 %all-gather.8.cloned.1.call-done = bf16[2624,960]{1,0:T(8,128)(2,1)} async-done(((bf16[328,960]{1,0:T(8,128)(2,1)}), bf16[2624,960]{1,0:T(8,128)(2,1)}) %all-gather.8.cloned.1.call-update) | async-done | bytes 5038096 | tf_op jit(solution)/shard_map/all_gather | solution.py:222
  122.7 3.0 slice.277
  125.7 2.8 reshape.667
  129.2 3.0 fusion.23
  132.9 2.4 fusion.149
  146.9 2.3 copy.230
  150.7 3.7 fusion.178
  154.4 3.6 convolution_convert_fusion.10
  159.8 2.1 multiply_reduce_fusion.9
  162.8 11.2 %all-gather.2 = bf16[512,960]{1,0:T(8,128)(2,1)S(1)} all-gather(bf16[64,960]{1,0:T(8,128)(2,1)S(1)} %multiply_convert_fusion.7), channel_id=4, replica_groups=mesh['q'=4,'y'=2,'x'=2,'c'=2] {'y','x','c'}, dimensions={0}, use_global_device_ids=true | all-gather | bytes 1105920 | tf_op jit(solution)/shard_map/all_gather | solution.py:143
  175.0 9.0 %all-gather.10.cloned.1.call-done = bf16[1920,640]{1,0:T(8,128)(2,1)} async-done(((bf16[480,640]{1,0:T(8,128)(2,1)}), bf16[1920,640]{1,0:T(8,128)(2,1)}) %all-gather.10.cloned.1.call-update) | async-done | bytes 2457616 | tf_op jit(solution)/shard_map/all_gather | solution.py:230
  196.8 2.1 collective-permute-start.6
  200.4 2.2 collective-permute-done.6
  202.6 3.6 collective-permute-done.5
  208.4 13.0 %all-gather.3 = bf16[256,1024]{1,0:T(8,128)(2,1)S(1)} all-gather(bf16[64,1024]{1,0:T(8,128)(2,1)S(1)} %pad.31), channel_id=5, replica_groups=mesh['q'=4,'y'=2,'x'=2,'c'=2] {'q'}, dimensions={0}, use_global_device_ids=true | all-gather | bytes 655360 | tf_op jit(solution)/shard_map/all_gather | solution.py:299
  222.5 8.8 %collective-permute-done.7 = bf16[4,64,1024]{2,1,0:T(8,128)(2,1)S(1)} collective-permute-done((bf16[4,64,1024]{2,1,0:T(8,128)(2,1)S(1)}, bf16[4,64,1024]{2,1,0:T(8,128)(2,1)S(1)}, u32[]{:S(2)}, u32[]{:S(2)}) %collective-permute-start.7) | collective-permute-done | bytes 524320 | tf_op jit(solution)/shard_map/ppermute | solution.py:74
  234.9 4.0 collective-permute-done.9
  240.4 5.9 %collective-permute-start.11 = (bf16[1024,1024]{1,0:T(8,128)(2,1)}, bf16[1024,1024]{1,0:T(8,128)(2,1)}, u32[]{:S(2)}, u32[]{:S(2)}) collective-permute-start(bf16[1024,1024]{1,0:T(8,128)(2,1)} %bitcast.38), channel_id=1, source_target_pairs={{0,1},{1,0},{2,3},{3,2},{4,5},{5,4},{6,7},{7,6},{8,9},{9,8},{10,11... | collective-permute-start | bytes 6291464 | tf_op jit(solution)/shard_map/ppermute | solution.py:74
  247.3 4.5 fusion.180
  254.9 3.9 fusion.179
  265.5 9.4 %all_to_all.53 = f32[32,1,256]{2,1,0:T(1,128)S(1)} all-to-all(f32[32,1,256]{2,1,0:T(1,128)} %reshape.784), channel_id=1, replica_groups=mesh['q'=4,'y'=2,'x'=2,'c'=2] {'q','y','x','c'}, dimensions={0} | all-to-all | bytes 65536 | tf_op jit(solution)/shard_map/all_to_all | solution.py:320
  281.0 8.6 %all_to_all.54 = f32[32,1,64]{2,1,0:T(1,128)S(1)} all-to-all(f32[32,1,64]{2,1,0:T(1,128)S(1)} %broadcast_in_dim.101), channel_id=1, replica_groups=mesh['q'=4,'y'=2,'x'=2,'c'=2] {'q','y','x','c'}, dimensions={0} | all-to-all | bytes 16384 | tf_op jit(solution)/shard_map/all_to_all | solution.py:330
  291.1 7.1 %convolution_convert_fusion = bf16[1024,1024]{1,0:T(8,128)(2,1)} fusion(bf16[1000,960]{0,1:T(8,128)(2,1)} %convert_element_type.307, f32[1024,1000]{0,1:T(8,128)} %copy-done.20, f32[1024]{0:T(1024)S(1)} %squeeze.126, f32[1024]{0:T(1024)S(1)} %multiply_add_fusion.3, s32[1024]{0:T(1024)} %copy-done.81), kind=kOutput, calls=%fused_computation.60 | convolution fusion | flops 2106392576 | bytes 8125440 | tf_op jit(solution)/shard_map/dot_general | solution.py:52
  299.0 5.6 fusion.152
  304.7 4.8 fusion.181
  312.4 4.3 fusion.153
  316.7 7.4 %collective-permute-done.15 = bf16[4,64,1024]{2,1,0:T(8,128)(2,1)S(1)} collective-permute-done((bf16[4,64,1024]{2,1,0:T(8,128)(2,1)S(1)}, bf16[4,64,1024]{2,1,0:T(8,128)(2,1)S(1)}, u32[]{:S(2)}, u32[]{:S(2)}) %collective-permute-start.15) | collective-permute-done | bytes 524320 | tf_op jit(solution)/shard_map/ppermute | solution.py:74
  324.1 10.3 %collective-permute-done.14 = bf16[4,64,1024]{2,1,0:T(8,128)(2,1)S(1)} collective-permute-done((bf16[4,64,1024]{2,1,0:T(8,128)(2,1)S(1)}, bf16[4,64,1024]{2,1,0:T(8,128)(2,1)S(1)}, u32[]{:S(2)}, u32[]{:S(2)}) %collective-permute-start.14) | collective-permute-done | bytes 524320 | tf_op jit(solution)/shard_map/ppermute | solution.py:74
  338.7 2.9 slice_add_fusion
  341.6 5.8 %collective-permute-done.17 = bf16[64,1024]{1,0:T(8,128)(2,1)S(1)} collective-permute-done((bf16[64,1024]{1,0:T(8,128)(2,1)S(1)}, bf16[64,1024]{1,0:T(8,128)(2,1)S(1)}, u32[]{:S(2)}, u32[]{:S(2)}) %collective-permute-start.17) | collective-permute-done | bytes 131104 | tf_op jit(solution)/shard_map/ppermute | solution.py:74
  348.3 13.2 %all-gather.4 = bf16[512,960]{1,0:T(8,128)(2,1)S(1)} all-gather(bf16[64,960]{1,0:T(8,128)(2,1)S(1)} %fusion.147), channel_id=6, replica_groups=mesh['q'=4,'y'=2,'x'=2,'c'=2] {'y','x','c'}, dimensions={0}, use_global_device_ids=true | all-gather | bytes 1105920 | tf_op jit(solution)/shard_map/all_gather | solution.py:143
  374.0 3.4 collective-permute-done.21
  381.4 2.2 multiply_reduce_fusion.1
  393.2 3.3 convolution_convert_fusion.9
  401.8 2.8 fusion.14
  409.4 2.2 convolution_convert_fusion.3
  411.6 2.6 copy.216
  414.3 3.3 all-to-all-start.5
  417.6 3.1 reduce-scatter.2.cloned.1.call-done
  424.6 3.2 reshape.698
  428.6 6.2 %fusion.2 = bf16[8,352,960]{2,1,0:T(8,128)(2,1)} fusion(bf16[1,3,960]{2,1,0:T(4,128)(2,1)S(1)} %copy-done.74, bf16[3,320,960]{2,1,0:T(8,128)(2,1)S(1)} %bitcast.233, bf16[5,128,960]{2,1,0:T(8,128)(2,1)S(1)} %reshape.698, bf16[5,192,960]{2,1,0:T(8,128)(2,1)S(1)} %bitcast.234), kind=kLoop, calls=%fused_computation.10 | loop fusion | flops 27033600 | bytes 10327680 | tf_op jit(solution)/shard_map/concatenate | solution.py:416
  434.8 3.7 dynamic-slice_bitcast_fusion
  439.6 4.5 all-to-all-start.6
  444.8 4.0 convert_add_fusion
  448.8 2.3 fusion.167
  457.1 23.3 %collective-permute-done.26 = bf16[2,176,960]{2,1,0:T(8,128)(2,1)S(1)} collective-permute-done((bf16[2,176,960]{2,1,0:T(8,128)(2,1)S(1)}, bf16[2,176,960]{2,1,0:T(8,128)(2,1)S(1)}, u32[]{:S(2)}, u32[]{:S(2)}) %collective-permute-start.26) | collective-permute-done | bytes 675872 | tf_op jit(solution)/shard_map/ppermute | solution.py:74
  483.7 3.8 fusion.50
  487.5 4.1 collective-permute-done.27
  498.6 5.7 all-to-all-start.7
  504.3 3.5 fusion.5
  508.1 4.0 multiply_reduce_fusion
  513.9 2.5 multiply_reduce_fusion.3
  522.2 6.9 %all-to-all-start.8 = ((f32[32,1,2]{2,1,0:T(1,128)}), f32[32,1,2]{2,1,0:T(1,128)S(1)}, u32[]{:S(2)}, u32[]{:S(2)}) async-start(f32[32,1,2]{2,1,0:T(1,128)} %broadcast_in_dim.168), calls=%async_computation.9 | async-start | bytes 32768 | tf_op jit(solution)/shard_map/all_to_all | solution.py:406
  545.3 4.3 collective-permute-start.34
  549.6 10.3 %add_multiply_fusion = (f32[1000,960]{0,1:T(8,128)}, f32[1000,960]{0,1:T(8,128)}, f32[1000,960]{0,1:T(8,128)}) fusion(f32[1000,960]{0,1:T(8,128)} %param.21, f32[1000,960]{0,1:T(8,128)} %get-tuple-element.109, f32[]{:T(128)S(6)} %div.148, f32[1000,960]{0,1:T(8,128)} %param.23, f32[1000,960]{0,1:T(8,128)} %param.22), kind=kLoop, calls=%fused_computation.25 | loop fusion | flops 14400000 | bytes 26880004 | tf_op jit(solution)/shard_map/mul | solution.py:107
  560.0 4.4 add_multiply_fusion.1
  (496 shorter events, 172.6 us)
Async XLA Ops:
  8.5 5.8 %collective-permute-start = (bf16[2880]{0:T(1024)(128)(2,1)S(1)}, bf16[2880]{0:T(1024)(128)(2,1)S(1)}, u32[]{:S(2)}, u32[]{:S(2)}) collective-permute-start(bf16[2880]{0:T(1024)(128)(2,1)S(1)} %slice.349), channel_id=1, source_target_pairs={{1,0},{2,1},{3,2},{4,3},{5,4},{6,5},{7,6},{8,7},{9,8},{10,9},{11,1... | collective-permute-start | bytes 17288 | tf_op jit(solution)/shard_map/ppermute | solution.py:200
  17.9 17.6 %collective-permute-start.1 = (bf16[328,960]{1,0:T(8,128)(2,1)S(1)}, bf16[328,960]{1,0:T(8,128)(2,1)}, u32[]{:S(2)}, u32[]{:S(2)}) collective-permute-start(bf16[328,960]{1,0:T(8,128)(2,1)S(1)} %maximum_maximum_fusion), channel_id=1, source_target_pairs={{0,16},{1,17},{2,18},{3,19},{4,20},{5,21},{6,22},{7,23}} | collective-permute-start | bytes 1889288 | tf_op jit(solution)/shard_map/ppermute | solution.py:216
  28.0 11.1 %all-to-all-start = ((s32[32,1,96]{2,1,0:T(1,128)}), s32[32,1,96]{2,1,0:T(1,128)S(1)}, u32[]{:S(2)}, u32[]{:S(2)}) async-start(s32[32,1,96]{2,1,0:T(1,128)} %bitcast), calls=%async_computation | async-start | bytes 32768 | tf_op jit(solution)/shard_map/all_to_all | solution.py:214
  36.6 17.2 %collective-permute-start.2 = (bf16[328,960]{1,0:T(8,128)(2,1)S(1)}, bf16[328,960]{1,0:T(8,128)(2,1)S(1)}, u32[]{:S(2)}, u32[]{:S(2)}) collective-permute-start(bf16[328,960]{1,0:T(8,128)(2,1)S(1)} %broadcast_select_fusion), channel_id=1, source_target_pairs={{0,8},{16,24},{1,9},{17,25},{2,10},{18,26},{3,11},{19,27},{4,12},{... | collective-permute-start | bytes 1889288 | tf_op jit(solution)/shard_map/ppermute | solution.py:218
  39.1 15.7 %all-to-all-start.1 = ((bf16[8,60,640]{2,1,0:T(8,128)(2,1)}), bf16[8,60,640]{2,1,0:T(8,128)(2,1)S(1)}, u32[]{:S(2)}, u32[]{:S(2)}) async-start(bf16[8,60,640]{2,1,0:T(8,128)(2,1)} %reshape.773), calls=%async_computation.1 | async-start | bytes 1310720 | tf_op jit(solution)/shard_map/all_to_all | solution.py:208
  44.7 74.8 %all-gather.8.cloned.1.call-start = ((), (), s32[]{:S(2)}) async-start(), calls=%async_computation.11 | async-start | bytes 6045696 | tf_op jit(solution)/shard_map/all_gather | solution.py:222
  54.8 11.4 %copy-start.57 = (f32[512,64]{1,0:T(8,128)S(1)}, f32[512,64]{1,0:T(8,128)}, u32[]{:S(2)}) copy-start(f32[512,64]{1,0:T(8,128)} %constant.392) | copy-start | bytes 393220
  54.8 12.0 %copy-start.56 = (f32[512,64]{1,0:T(8,128)S(1)}, f32[512,64]{1,0:T(8,128)}, u32[]{:S(2)}) copy-start(f32[512,64]{1,0:T(8,128)} %constant.391) | copy-start | bytes 393220
  54.9 74.3 %all-to-all-start.2 = ((bf16[32,32,960]{2,1,0:T(8,128)(2,1)}), bf16[32,32,960]{2,1,0:T(8,128)(2,1)}, u32[]{:S(2)}, u32[]{:S(2)}) async-start(bf16[32,32,960]{2,1,0:T(8,128)(2,1)} %bitcast.232), calls=%async_computation.2 | async-start | bytes 4194304 | tf_op jit(solution)/shard_map/all_to_all | solution.py:190
  64.2 119.7 %all-gather.10.cloned.1.call-start = ((), (), s32[]{:S(2)}) async-start(), calls=%async_computation.12 | async-start | bytes 3072000 | tf_op jit(solution)/shard_map/all_gather | solution.py:230
  66.8 74.3 %copy-start.54 = (f32[64,64]{1,0:T(8,128)}, f32[64,64]{1,0:T(8,128)S(1)}, u32[]{:S(2)}) copy-start(f32[64,64]{1,0:T(8,128)S(1)} %gather_fusion.1) | copy-start | bytes 49156
  132.1 27.2 %copy-start.4 = (bf16[512,960]{0,1:T(8,128)(2,1)}, bf16[512,960]{0,1:T(8,128)(2,1)S(1)}, u32[]{:S(2)}) copy-start(bf16[512,960]{0,1:T(8,128)(2,1)S(1)} %get-tuple-element.182) | copy-start | bytes 2949124
  132.2 29.8 %copy-start.70 = (f32[1,1,960]{2,1,0:T(1,128)}, f32[1,1,960]{2,1,0:T(1,128)S(1)}, u32[]{:S(2)}) copy-start(f32[1,1,960]{2,1,0:T(1,128)S(1)} %get-tuple-element.169) | copy-start | bytes 11524
  132.2 76.1 %copy-start.68 = (f32[1,1,960]{2,1,0:T(1,128)}, f32[1,1,960]{2,1,0:T(1,128)S(1)}, u32[]{:S(2)}) copy-start(f32[1,1,960]{2,1,0:T(1,128)S(1)} %get-tuple-element.168) | copy-start | bytes 11524
  132.9 287.8 %reduce-scatter.2.cloned.1.call-start = ((), (), s32[]{:S(2)}) async-start(), calls=%async_computation.10 | async-start | bytes 3072000 | tf_op jit(solution)/shard_map/reduce_scatter | solution.py:396
  162.0 23.5 %copy-start.93 = (f32[64]{0:T(128)}, f32[64]{0:T(128)S(1)}, u32[]{:S(2)}) copy-start(f32[64]{0:T(128)S(1)} %add_rsqrt_fusion.2) | copy-start | bytes 772
  190.5 2.8 collective-permute-start.3
  196.8 5.8 %collective-permute-start.6 = (bf16[64,1024]{1,0:T(8,128)(2,1)}, bf16[64,1024]{1,0:T(8,128)(2,1)S(1)}, u32[]{:S(2)}, u32[]{:S(2)}) collective-permute-start(bf16[64,1024]{1,0:T(8,128)(2,1)} %get-tuple-element.156), channel_id=1, source_target_pairs={{0,6},{2,4},{4,2},{6,0},{1,7},{3,5},{5,3},{7,1},{8,14},{10,12},{12... | collective-permute-start | bytes 393224 | tf_op jit(solution)/shard_map/ppermute | solution.py:74
  198.9 7.4 %collective-permute-start.5 = (bf16[64,1024]{1,0:T(8,128)(2,1)}, bf16[64,1024]{1,0:T(8,128)(2,1)S(1)}, u32[]{:S(2)}, u32[]{:S(2)}) collective-permute-start(bf16[64,1024]{1,0:T(8,128)(2,1)} %get-tuple-element.157), channel_id=1, source_target_pairs={{0,4},{2,6},{4,0},{6,2},{1,5},{3,7},{5,1},{7,3},{8,12},{10,14},{12... | collective-permute-start | bytes 393224 | tf_op jit(solution)/shard_map/ppermute | solution.py:74
  199.2 7.8 %collective-permute-start.4 = (bf16[64,1024]{1,0:T(8,128)(2,1)}, bf16[64,1024]{1,0:T(8,128)(2,1)}, u32[]{:S(2)}, u32[]{:S(2)}) collective-permute-start(bf16[64,1024]{1,0:T(8,128)(2,1)} %get-tuple-element.155), channel_id=1, source_target_pairs={{0,2},{2,0},{4,6},{6,4},{1,3},{3,1},{5,7},{7,5},{8,10},{10,8},{12,... | collective-permute-start | bytes 393224 | tf_op jit(solution)/shard_map/ppermute | solution.py:74
  208.2 25.9 %copy-start.90 = (f32[64]{0:T(128)}, f32[64]{0:T(128)S(1)}, u32[]{:S(2)}) copy-start(f32[64]{0:T(128)S(1)} %add_rsqrt_fusion.1) | copy-start | bytes 772
  221.4 9.9 %collective-permute-start.7 = (bf16[4,64,1024]{2,1,0:T(8,128)(2,1)S(1)}, bf16[4,64,1024]{2,1,0:T(8,128)(2,1)S(1)}, u32[]{:S(2)}, u32[]{:S(2)}) collective-permute-start(bf16[4,64,1024]{2,1,0:T(8,128)(2,1)S(1)} %bitcast.259), channel_id=1, source_target_pairs={{0,2},{2,0},{1,3},{3,1},{4,6},{6,4},{5,7},{7,5},{8,10},{10,8},{9,1... | collective-permute-start | bytes 1572872 | tf_op jit(solution)/shard_map/ppermute | solution.py:74
  222.5 9.8 %collective-permute-start.8 = (bf16[4,64,1024]{2,1,0:T(8,128)(2,1)S(1)}, bf16[4,64,1024]{2,1,0:T(8,128)(2,1)S(1)}, u32[]{:S(2)}, u32[]{:S(2)}) collective-permute-start(bf16[4,64,1024]{2,1,0:T(8,128)(2,1)S(1)} %bitcast.260), channel_id=1, source_target_pairs={{0,4},{4,0},{1,5},{5,1},{2,6},{6,2},{3,7},{7,3},{8,12},{12,8},{9,1... | collective-permute-start | bytes 1572872 | tf_op jit(solution)/shard_map/ppermute | solution.py:74
  231.3 7.6 %collective-permute-start.9 = (bf16[2,64,1024]{2,1,0:T(8,128)(2,1)S(1)}, bf16[2,64,1024]{2,1,0:T(8,128)(2,1)S(1)}, u32[]{:S(2)}, u32[]{:S(2)}) collective-permute-start(bf16[2,64,1024]{2,1,0:T(8,128)(2,1)S(1)} %slice.375), channel_id=1, source_target_pairs={{0,4},{4,0},{1,5},{5,1},{2,6},{6,2},{3,7},{7,3},{8,12},{12,8},{9,1... | collective-permute-start | bytes 786440 | tf_op jit(solution)/shard_map/ppermute | solution.py:74
  232.2 14.1 %copy-start.97 = (s32[32]{0:T(128)S(1)}, s32[32]{0:T(128)}, u32[]{:S(2)}) copy-start(s32[32]{0:T(128)} %constant.365.clone) | copy-start | bytes 388
  232.2 14.1 %copy-start.99 = (s32[32]{0:T(128)S(1)}, s32[32]{0:T(128)}, u32[]{:S(2)}) copy-start(s32[32]{0:T(128)} %copy-done.98) | copy-start | bytes 388
  232.3 7.4 %collective-permute-start.10 = (bf16[2,64,1024]{2,1,0:T(8,128)(2,1)S(1)}, bf16[2,64,1024]{2,1,0:T(8,128)(2,1)S(1)}, u32[]{:S(2)}, u32[]{:S(2)}) collective-permute-start(bf16[2,64,1024]{2,1,0:T(8,128)(2,1)S(1)} %slice.376), channel_id=1, source_target_pairs={{0,2},{2,0},{1,3},{3,1},{4,6},{6,4},{5,7},{7,5},{8,10},{10,8},{9,1... | collective-permute-start | bytes 786440 | tf_op jit(solution)/shard_map/ppermute | solution.py:74
  240.4 13.5 %collective-permute-start.11 = (bf16[1024,1024]{1,0:T(8,128)(2,1)}, bf16[1024,1024]{1,0:T(8,128)(2,1)}, u32[]{:S(2)}, u32[]{:S(2)}) collective-permute-start(bf16[1024,1024]{1,0:T(8,128)(2,1)} %bitcast.38), channel_id=1, source_target_pairs={{0,1},{1,0},{2,3},{3,2},{4,5},{5,4},{6,7},{7,6},{8,9},{9,8},{10,11... | collective-permute-start | bytes 6291464 | tf_op jit(solution)/shard_map/ppermute | solution.py:74
  247.2 11.6 %copy-start.81 = (s32[1024]{0:T(1024)}, s32[1024]{0:T(1024)S(1)}, u32[]{:S(2)}) copy-start(s32[1024]{0:T(1024)S(1)} %sub.235) | copy-start | bytes 12292
  298.3 6.4 %collective-permute-start.12 = (bf16[1024,1024]{1,0:T(8,128)(2,1)}, bf16[1024,1024]{1,0:T(8,128)(2,1)}, u32[]{:S(2)}, u32[]{:S(2)}) collective-permute-start(bf16[1024,1024]{1,0:T(8,128)(2,1)} %convolution_convert_fusion), channel_id=1, source_target_pairs={{0,1},{1,0},{2,3},{3,2},{4,5},{5,4},{6,7},{7,6},{8,9},{9,8},{10,11... | collective-permute-start | bytes 6291464 | tf_op jit(solution)/shard_map/ppermute | solution.py:74
  309.7 14.5 %collective-permute-start.15 = (bf16[4,64,1024]{2,1,0:T(8,128)(2,1)S(1)}, bf16[4,64,1024]{2,1,0:T(8,128)(2,1)S(1)}, u32[]{:S(2)}, u32[]{:S(2)}) collective-permute-start(bf16[4,64,1024]{2,1,0:T(8,128)(2,1)S(1)} %bitcast.286), channel_id=1, source_target_pairs={{0,6},{2,4},{4,2},{6,0},{1,7},{3,5},{5,3},{7,1},{8,14},{10,12},{12... | collective-permute-start | bytes 1572872 | tf_op jit(solution)/shard_map/ppermute | solution.py:74
  310.0 24.4 %collective-permute-start.14 = (bf16[4,64,1024]{2,1,0:T(8,128)(2,1)S(1)}, bf16[4,64,1024]{2,1,0:T(8,128)(2,1)S(1)}, u32[]{:S(2)}, u32[]{:S(2)}) collective-permute-start(bf16[4,64,1024]{2,1,0:T(8,128)(2,1)S(1)} %bitcast.285), channel_id=1, source_target_pairs={{0,4},{2,6},{4,0},{6,2},{1,5},{3,7},{5,1},{7,3},{8,12},{10,14},{12... | collective-permute-start | bytes 1572872 | tf_op jit(solution)/shard_map/ppermute | solution.py:74
  311.1 23.3 %collective-permute-start.13 = (bf16[4,64,1024]{2,1,0:T(8,128)(2,1)S(1)}, bf16[4,64,1024]{2,1,0:T(8,128)(2,1)S(1)}, u32[]{:S(2)}, u32[]{:S(2)}) collective-permute-start(bf16[4,64,1024]{2,1,0:T(8,128)(2,1)S(1)} %bitcast.284), channel_id=1, source_target_pairs={{0,2},{2,0},{4,6},{6,4},{1,3},{3,1},{5,7},{7,5},{8,10},{10,8},{12,... | collective-permute-start | bytes 1572872 | tf_op jit(solution)/shard_map/ppermute | solution.py:74
  334.9 6.7 %collective-permute-start.18 = (bf16[64,1024]{1,0:T(8,128)(2,1)S(1)}, bf16[64,1024]{1,0:T(8,128)(2,1)S(1)}, u32[]{:S(2)}, u32[]{:S(2)}) collective-permute-start(bf16[64,1024]{1,0:T(8,128)(2,1)S(1)} %get-tuple-element.153), channel_id=1, source_target_pairs={{0,24},{8,16},{16,8},{24,0},{1,25},{9,17},{17,9},{25,1},{2,26},{10... | collective-permute-start | bytes 393224 | tf_op jit(solution)/shard_map/ppermute | solution.py:74
  335.3 12.0 %collective-permute-start.17 = (bf16[64,1024]{1,0:T(8,128)(2,1)S(1)}, bf16[64,1024]{1,0:T(8,128)(2,1)S(1)}, u32[]{:S(2)}, u32[]{:S(2)}) collective-permute-start(bf16[64,1024]{1,0:T(8,128)(2,1)S(1)} %get-tuple-element.154), channel_id=1, source_target_pairs={{0,16},{8,24},{16,0},{24,8},{1,17},{9,25},{17,1},{25,9},{2,18},{10... | collective-permute-start | bytes 393224 | tf_op jit(solution)/shard_map/ppermute | solution.py:74
  336.7 10.7 %copy-start.69 = (f32[1,1,960]{2,1,0:T(1,128)S(1)}, f32[1,1,960]{2,1,0:T(1,128)}, u32[]{:S(2)}) copy-start(f32[1,1,960]{2,1,0:T(1,128)} %copy-done.68) | copy-start | bytes 11524
  336.7 10.7 %copy-start.91 = (f32[64]{0:T(128)S(1)}, f32[64]{0:T(128)}, u32[]{:S(2)}) copy-start(f32[64]{0:T(128)} %copy-done.90) | copy-start | bytes 772
  336.7 10.7 %collective-permute-start.16 = (bf16[64,1024]{1,0:T(8,128)(2,1)S(1)}, bf16[64,1024]{1,0:T(8,128)(2,1)S(1)}, u32[]{:S(2)}, u32[]{:S(2)}) collective-permute-start(bf16[64,1024]{1,0:T(8,128)(2,1)S(1)} %get-tuple-element.152), channel_id=1, source_target_pairs={{0,8},{8,0},{16,24},{24,16},{1,9},{9,1},{17,25},{25,17},{2,10},{10... | collective-permute-start | bytes 393224 | tf_op jit(solution)/shard_map/ppermute | solution.py:74
  341.5 20.0 %copy-start.38 = (f32[512,640]{1,0:T(8,128)S(1)}, f32[512,640]{1,0:T(8,128)}, u32[]{:S(2)}) copy-start(f32[512,640]{1,0:T(8,128)} %copy-done.37) | copy-start | bytes 3932164
  341.5 20.0 %copy-start.52 = (bf16[320,640]{1,0:T(8,128)(2,1)S(1)}, bf16[320,640]{1,0:T(8,128)(2,1)}, u32[]{:S(2)}) copy-start(bf16[320,640]{1,0:T(8,128)(2,1)} %copy-done.51) | copy-start | bytes 1228804
  341.5 20.0 %copy-start.65 = (bf16[160,320]{1,0:T(8,128)(2,1)S(1)}, bf16[160,320]{1,0:T(8,128)(2,1)}, u32[]{:S(2)}) copy-start(bf16[160,320]{1,0:T(8,128)(2,1)} %copy-done.64) | copy-start | bytes 307204
  341.5 20.0 %copy-start.67 = (bf16[160,320]{1,0:T(8,128)(2,1)S(1)}, bf16[160,320]{1,0:T(8,128)(2,1)}, u32[]{:S(2)}) copy-start(bf16[160,320]{1,0:T(8,128)(2,1)} %copy-done.66) | copy-start | bytes 307204
  363.9 2.5 collective-permute-start.19
  368.1 5.9 %collective-permute-start.22 = (bf16[64,1024]{1,0:T(8,128)(2,1)S(1)}, bf16[64,1024]{1,0:T(8,128)(2,1)}, u32[]{:S(2)}, u32[]{:S(2)}) collective-permute-start(bf16[64,1024]{1,0:T(8,128)(2,1)S(1)} %get-tuple-element.150), channel_id=1, source_target_pairs={{0,6},{2,4},{4,2},{6,0},{1,7},{3,5},{5,3},{7,1},{8,14},{10,12},{12... | collective-permute-start | bytes 393224 | tf_op jit(solution)/shard_map/ppermute | solution.py:74
  369.4 8.0 %collective-permute-start.21 = (bf16[64,1024]{1,0:T(8,128)(2,1)S(1)}, bf16[64,1024]{1,0:T(8,128)(2,1)}, u32[]{:S(2)}, u32[]{:S(2)}) collective-permute-start(bf16[64,1024]{1,0:T(8,128)(2,1)S(1)} %get-tuple-element.151), channel_id=1, source_target_pairs={{0,4},{2,6},{4,0},{6,2},{1,5},{3,7},{5,1},{7,3},{8,12},{10,14},{12... | collective-permute-start | bytes 393224 | tf_op jit(solution)/shard_map/ppermute | solution.py:74
  369.7 7.7 %collective-permute-start.20 = (bf16[64,1024]{1,0:T(8,128)(2,1)S(1)}, bf16[64,1024]{1,0:T(8,128)(2,1)}, u32[]{:S(2)}, u32[]{:S(2)}) collective-permute-start(bf16[64,1024]{1,0:T(8,128)(2,1)S(1)} %get-tuple-element.149), channel_id=1, source_target_pairs={{0,2},{2,0},{4,6},{6,4},{1,3},{3,1},{5,7},{7,5},{8,10},{10,8},{12,... | collective-permute-start | bytes 393224 | tf_op jit(solution)/shard_map/ppermute | solution.py:74
  414.3 20.5 %all-to-all-start.5 = ((bf16[32,8,960]{2,1,0:T(8,128)(2,1)}), bf16[32,8,960]{2,1,0:T(8,128)(2,1)}, u32[]{:S(2)}, u32[]{:S(2)}) async-start(bf16[32,8,960]{2,1,0:T(8,128)(2,1)} %bitcast.86), calls=%async_computation.6 | async-start | bytes 1048576 | tf_op jit(solution)/shard_map/all_to_all | solution.py:190
  438.5 6.3 %collective-permute-start.23 = (bf16[4,352,960]{2,1,0:T(8,128)(2,1)}, bf16[4,352,960]{2,1,0:T(8,128)(2,1)}, u32[]{:S(2)}, u32[]{:S(2)}) collective-permute-start(bf16[4,352,960]{2,1,0:T(8,128)(2,1)} %dynamic-slice_bitcast_fusion), channel_id=1, source_target_pairs={{0,1},{1,0},{2,3},{3,2},{4,5},{5,4},{6,7},{7,6},{8,9},{9,8},{10,11... | collective-permute-start | bytes 8110088 | tf_op jit(solution)/shard_map/ppermute | solution.py:74
  439.6 53.7 %all-to-all-start.6 = ((bf16[32,24,960]{2,1,0:T(8,128)(2,1)}), bf16[32,24,960]{2,1,0:T(8,128)(2,1)}, u32[]{:S(2)}, u32[]{:S(2)}) async-start(bf16[32,24,960]{2,1,0:T(8,128)(2,1)} %bitcast.87), calls=%async_computation.7 | async-start | bytes 3145728 | tf_op jit(solution)/shard_map/all_to_all | solution.py:190
  452.8 27.6 %collective-permute-start.26 = (bf16[2,176,960]{2,1,0:T(8,128)(2,1)S(1)}, bf16[2,176,960]{2,1,0:T(8,128)(2,1)S(1)}, u32[]{:S(2)}, u32[]{:S(2)}) collective-permute-start(bf16[2,176,960]{2,1,0:T(8,128)(2,1)S(1)} %fusion.59), channel_id=1, source_target_pairs={{0,4},{4,0},{1,5},{5,1},{2,6},{6,2},{3,7},{7,3},{8,12},{12,8},{9,1... | collective-permute-start | bytes 2027528 | tf_op jit(solution)/shard_map/ppermute | solution.py:74
  455.5 26.6 %collective-permute-start.24 = (bf16[2,176,960]{2,1,0:T(8,128)(2,1)S(1)}, bf16[2,176,960]{2,1,0:T(8,128)(2,1)}, u32[]{:S(2)}, u32[]{:S(2)}) collective-permute-start(bf16[2,176,960]{2,1,0:T(8,128)(2,1)S(1)} %fusion.58), channel_id=1, source_target_pairs={{0,2},{2,0},{1,3},{3,1},{4,6},{6,4},{5,7},{7,5},{8,10},{10,8},{9,1... | collective-permute-start | bytes 2027528 | tf_op jit(solution)/shard_map/ppermute | solution.py:74
  457.1 25.1 %copy-start.6 = (f32[2,2,176,960]{3,2,1,0:T(8,128)S(1)}, f32[2,2,176,960]{3,2,1,0:T(8,128)}, u32[]{:S(2)}) copy-start(f32[2,2,176,960]{3,2,1,0:T(8,128)} %get-tuple-element.123) | copy-start | bytes 8110084
  482.1 9.5 %collective-permute-start.27 = (bf16[176,960]{1,0:T(8,128)(2,1)S(1)}, bf16[176,960]{1,0:T(8,128)(2,1)S(1)}, u32[]{:S(2)}, u32[]{:S(2)}) collective-permute-start(bf16[176,960]{1,0:T(8,128)(2,1)S(1)} %fusion.76), channel_id=1, source_target_pairs={{0,2},{2,0},{1,3},{3,1},{4,6},{6,4},{5,7},{7,5},{8,10},{10,8},{9,1... | collective-permute-start | bytes 1013768 | tf_op jit(solution)/shard_map/ppermute | solution.py:74
  483.6 9.5 %collective-permute-start.25 = (bf16[176,960]{1,0:T(8,128)(2,1)S(1)}, bf16[176,960]{1,0:T(8,128)(2,1)S(1)}, u32[]{:S(2)}, u32[]{:S(2)}) collective-permute-start(bf16[176,960]{1,0:T(8,128)(2,1)S(1)} %fusion.75), channel_id=1, source_target_pairs={{0,4},{4,0},{1,5},{5,1},{2,6},{6,2},{3,7},{7,3},{8,12},{12,8},{9,1... | collective-permute-start | bytes 1013768 | tf_op jit(solution)/shard_map/ppermute | solution.py:74
  494.1 19.7 %collective-permute-start.30 = (bf16[88,960]{1,0:T(8,128)(2,1)}, bf16[88,960]{1,0:T(8,128)(2,1)}, u32[]{:S(2)}, u32[]{:S(2)}) collective-permute-start(bf16[88,960]{1,0:T(8,128)(2,1)} %get-tuple-element.131), channel_id=1, source_target_pairs={{0,24},{8,16},{16,8},{24,0},{1,25},{9,17},{17,9},{25,1},{2,26},{10... | collective-permute-start | bytes 506888 | tf_op jit(solution)/shard_map/ppermute | solution.py:74
  496.1 17.8 %collective-permute-start.29 = (bf16[88,960]{1,0:T(8,128)(2,1)}, bf16[88,960]{1,0:T(8,128)(2,1)}, u32[]{:S(2)}, u32[]{:S(2)}) collective-permute-start(bf16[88,960]{1,0:T(8,128)(2,1)} %get-tuple-element.132), channel_id=1, source_target_pairs={{0,16},{8,24},{16,0},{24,8},{1,17},{9,25},{17,1},{25,9},{2,18},{10... | collective-permute-start | bytes 506888 | tf_op jit(solution)/shard_map/ppermute | solution.py:74
  496.2 17.6 %collective-permute-start.28 = (bf16[88,960]{1,0:T(8,128)(2,1)}, bf16[88,960]{1,0:T(8,128)(2,1)}, u32[]{:S(2)}, u32[]{:S(2)}) collective-permute-start(bf16[88,960]{1,0:T(8,128)(2,1)} %get-tuple-element.130), channel_id=1, source_target_pairs={{0,8},{8,0},{16,24},{24,16},{1,9},{9,1},{17,25},{25,17},{2,10},{10... | collective-permute-start | bytes 506888 | tf_op jit(solution)/shard_map/ppermute | solution.py:74
  498.6 19.6 %all-to-all-start.7 = ((bf16[8,60,640]{2,1,0:T(8,128)(2,1)}), bf16[8,60,640]{2,1,0:T(8,128)(2,1)S(1)}, u32[]{:S(2)}, u32[]{:S(2)}) async-start(bf16[8,60,640]{2,1,0:T(8,128)(2,1)} %reshape.705), calls=%async_computation.8 | async-start | bytes 1310720 | tf_op jit(solution)/shard_map/all_to_all | solution.py:432
  518.2 19.7 %collective-permute-start.33 = (bf16[88,960]{1,0:T(8,128)(2,1)}, bf16[88,960]{1,0:T(8,128)(2,1)S(1)}, u32[]{:S(2)}, u32[]{:S(2)}) collective-permute-start(bf16[88,960]{1,0:T(8,128)(2,1)} %get-tuple-element.84), channel_id=1, source_target_pairs={{16,0},{17,1},{18,2},{19,3},{20,4},{21,5},{22,6},{23,7}} | collective-permute-start | bytes 506888 | tf_op jit(solution)/shard_map/ppermute | solution.py:444
  519.5 18.4 %collective-permute-start.31 = (bf16[88,960]{1,0:T(8,128)(2,1)}, bf16[88,960]{1,0:T(8,128)(2,1)S(1)}, u32[]{:S(2)}, u32[]{:S(2)}) collective-permute-start(bf16[88,960]{1,0:T(8,128)(2,1)} %get-tuple-element.84), channel_id=1, source_target_pairs={{24,0},{25,1},{26,2},{27,3},{28,4},{29,5},{30,6},{31,7}} | collective-permute-start | bytes 506888 | tf_op jit(solution)/shard_map/ppermute | solution.py:444
  522.2 13.7 %all-to-all-start.8 = ((f32[32,1,2]{2,1,0:T(1,128)}), f32[32,1,2]{2,1,0:T(1,128)S(1)}, u32[]{:S(2)}, u32[]{:S(2)}) async-start(f32[32,1,2]{2,1,0:T(1,128)} %broadcast_in_dim.168), calls=%async_computation.9 | async-start | bytes 32768 | tf_op jit(solution)/shard_map/all_to_all | solution.py:406
  530.9 8.0 %collective-permute-start.32 = (bf16[88,960]{1,0:T(8,128)(2,1)}, bf16[88,960]{1,0:T(8,128)(2,1)S(1)}, u32[]{:S(2)}, u32[]{:S(2)}) collective-permute-start(bf16[88,960]{1,0:T(8,128)(2,1)} %get-tuple-element.84), channel_id=1, source_target_pairs={{8,0},{9,1},{10,2},{11,3},{12,4},{13,5},{14,6},{15,7}} | collective-permute-start | bytes 506888 | tf_op jit(solution)/shard_map/ppermute | solution.py:444
  545.3 14.7 %collective-permute-start.34 = (bf16[2880]{0:T(1024)(128)(2,1)S(1)}, bf16[2880]{0:T(1024)(128)(2,1)S(1)}, u32[]{:S(2)}, u32[]{:S(2)}) collective-permute-start(bf16[2880]{0:T(1024)(128)(2,1)S(1)} %slice.336), channel_id=1, source_target_pairs={{0,1},{1,2},{2,3},{3,4},{4,5},{5,6},{6,7},{7,8},{8,9},{9,10},{10,1... | collective-permute-start | bytes 17288 | tf_op jit(solution)/shard_map/ppermute | solution.py:466
  549.6 10.4 %copy-start.15 = (f32[307290]{0:T(1024)S(1)}, f32[307290]{0:T(1024)}, u32[]{:S(2)}) copy-start(f32[307290]{0:T(1024)} %param.18) | copy-start | bytes 3687484
  (83 other events, 284.2 us)
Sparse Core Ops, SparseCore 0:
  54.9 64.5 all-gather.7
  133.0 50.9 all-gather.9
  372.7 47.8 reduce-scatter.1

commit v10 on v9

--- a/solution.py
+++ b/solution.py
@@ -189,7 +189,7 @@
     def exchange(blocks):
         return lax.all_to_all(blocks, ALL, split_axis=0, concat_axis=0, tiled=True).reshape(-1, D)
 
-    cuts_back = (0, capacity // 4, capacity)
+    cuts_back = (0, capacity // 2, capacity)
     marked = token_ids + 1
     halves = jnp.stack([marked // 256, marked % 256]).astype(bf16)
     found = dot(halves, spot).astype(jnp.int32)
@@ -417,13 +417,18 @@
         level, arrived[0] = lax.optimization_barrier((level, arrived[0]))
         keep = lax.dynamic_index_in_dim(level, c_index, 1, False)
         give = lax.dynamic_index_in_dim(level, 1 - c_index, 1, False)
-        level = keep.astype(f32) + flip(give, "c", 1, 2).astype(f32)
-        level = level.reshape(2, 2, SHARE + ROOM, D)
+        cores = [rows.reshape(2, 2, SHARE + ROOM, D) for rows in (keep, flip(give, "c", 1, 2))]
         middle = (SHARE + ROOM) // 2
         x_index, y_index = lax.axis_index("x"), lax.axis_index("y")
-        left, right = pick_block(level[:, :, :middle], x_index, 1), pick_block(level[:, :, middle:], y_index, 0)
-        left = left + flip(pick_block(level[:, :, :middle], 1 - x_index, 1).astype(bf16), "x", 1, 2).astype(f32)
-        right = right + flip(pick_block(level[:, :, middle:], 1 - y_index, 0).astype(bf16), "y", 1, 2).astype(f32)
+
+        def upper(index):
+            return sum(pick_block(rows[:, :, :middle], index, 1).astype(f32) for rows in cores)
+
+        def under(index):
+            return sum(pick_block(rows[:, :, middle:], index, 0).astype(f32) for rows in cores)
+
+        left = upper(x_index) + flip(upper(1 - x_index).astype(bf16), "x", 1, 2).astype(f32)
+        right = under(y_index) + flip(under(1 - y_index).astype(bf16), "y", 1, 2).astype(f32)
         left = pick_block(left, y_index) + flip(pick_block(left, 1 - y_index).astype(bf16), "y", 1, 2).astype(f32)
         right = pick_block(right, x_index) + flip(pick_block(right, 1 - x_index).astype(bf16), "x", 1, 2).astype(f32)
         own = jnp.concatenate([left, right])
@@ -442,6 +447,9 @@
         squares = jnp.sum(quarter.astype(f32) ** 2) + jnp.sum(share.astype(f32) ** 2) + table_squares
         quarter, squares, got = lax.optimization_barrier((quarter, squares, got))
         quarters = [quarter] + [lax.ppermute(quarter, "q", [(k, 0)]) for k in (1, 2, 3)]
+        loss, grad_norm, clip_factor = norm_of(squares)
+        table_new = adamw_step(table_master, table_grad, table_m, table_v, clip_factor)
+        quarters, table_new = lax.optimization_barrier((quarters, table_new))
         first = jnp.concatenate(quarters)
         gain_out = first[SHARE : SHARE + 3].reshape(-1)
         both = jnp.concatenate([first[:TOP], first[TOP:SHARE].reshape(TOP, KV)], axis=1)
@@ -449,8 +457,6 @@
         by_share = got.reshape(8, 60, 2, UNIT).transpose(1, 2, 0, 3).reshape(-1)
         mine = jnp.where(q_index == 3, down_unpack(share).reshape(-1), by_share)
         mine = jnp.where(q_index == 0, first, mine)
-        loss, grad_norm, clip_factor = norm_of(squares)
-        mine, clip_factor = lax.optimization_barrier((mine, clip_factor))
     else:
         table_grad = head_grad
         for low, high, rows in zip(cuts_back, cuts_back[1:], arrived):
@@ -471,8 +477,8 @@
 
     if not aligned:
         loss, grad_norm, clip_factor = norm_of(jnp.sum(layer_grad * layer_grad) + table_squares)
+        table_new = adamw_step(table_master, table_grad, table_m, table_v, clip_factor)
     flat_new = adamw_step(flat_master, layer_grad, flat_m, flat_v, clip_factor)
-    table_new = adamw_step(table_master, table_grad, table_m, table_v, clip_factor)
     return (loss, grad_norm) + flat_new + table_new
 
 

time: 583 us -> 586 us (level)
  the two profiles are of different devices: /device:TPU:1 before, /device:TPU:24 now
where the time goes in v10:
time: 586 us; the launch traced here: 576 us
  waiting for transfers between devices  145 us (25%)
  local copies, waits for them, and re-layouts  95.2 us (16%)
  matrix products  90.6 us (15%)
  starting transfers between devices  84.6 us (14%)
  other arithmetic  81.6 us (14%)
  blocking collectives  57.2 us (10%)
  between operations  21.8 us (4%)
    dot_general x37, matrix products, dot(): lax.dot_general(left, right, (((left_dim,), (right_dim,)), ((), ())), pre...  74.5 us
    ppermute x28, waiting for transfers between devices, flip(): return lax.ppermute(rows, axes, [(i, i ^ bits) for i in range(size)])  70.3 us
    all_gather x1, waiting for transfers between devices, local(): level = lax.all_gather(first, PLANE)  48.1 us
    ppermute x28, starting transfers between devices, flip(): return lax.ppermute(rows, axes, [(i, i ^ bits) for i in range(size)])  31.2 us
    all_gather x2, blocking collectives, spread_plane(): return widen(lax.all_gather(rows, PLANE).reshape(-1, D))  22.7 us
    all_to_all x3, starting transfers between devices, exchange(): lax.all_to_all(blocks, ALL, split_axis=0, concat_axis=0, tiled=True)  20 us
    unnamed x211, local copies, waits for them, and re-layouts  17.6 us
    all_gather x1, blocking collectives, local(): across = lax.all_gather(widen(hidden), 'q')  15.4 us
  transfers between devices with their start and end apart: 45, of which 25 were waited for; matrix products, arithmetic and copies ran while one was open for 31% of the time, Pallas kernels for 0%

profile of v10, /device:TPU:24, one launch (start us, length us, event | category | flops | bytes accessed | tf_op | source)
XLA Modules:
  0.0 575.9 jit_solution(8232727284266064630)
XLA Ops:
  8.5 3.7 collective-permute-start
  20.4 3.7 convert_element_type.330
  24.7 6.4 %all-to-all-start = ((s32[32,1,96]{2,1,0:T(1,128)}), s32[32,1,96]{2,1,0:T(1,128)S(1)}, u32[]{:S(2)}, u32[]{:S(2)}) async-start(s32[32,1,96]{2,1,0:T(1,128)} %bitcast), calls=%async_computation | async-start | bytes 32768 | tf_op jit(solution)/shard_map/all_to_all | solution.py:214
  35.6 4.3 all-to-all-done
  39.9 3.5 all-to-all-start.1
  43.6 5.2 fusion.25
  48.8 3.9 copy.201
  54.6 8.4 %all-to-all-start.2 = ((bf16[32,32,960]{2,1,0:T(8,128)(2,1)}), bf16[32,32,960]{2,1,0:T(8,128)(2,1)}, u32[]{:S(2)}, u32[]{:S(2)}) async-start(bf16[32,32,960]{2,1,0:T(8,128)(2,1)} %bitcast.237), calls=%async_computation.2 | async-start | bytes 4194304 | tf_op jit(solution)/shard_map/all_to_all | solution.py:190
  69.0 48.1 %all-gather.8.cloned.1.call-done = bf16[2624,960]{1,0:T(8,128)(2,1)} async-done(((bf16[328,960]{1,0:T(8,128)(2,1)}), bf16[2624,960]{1,0:T(8,128)(2,1)}) %all-gather.8.cloned.1.call-update) | async-done | bytes 5038096 | tf_op jit(solution)/shard_map/all_gather | solution.py:222
  120.3 3.0 slice.285
  123.3 2.8 reshape.681
  126.8 3.0 fusion.24
  130.6 2.4 fusion.150
  144.6 2.3 copy.243
  148.4 3.7 fusion.180
  152.1 3.6 convolution_convert_fusion.10
  160.5 11.5 %all-gather.2 = bf16[512,960]{1,0:T(8,128)(2,1)S(1)} all-gather(bf16[64,960]{1,0:T(8,128)(2,1)S(1)} %multiply_convert_fusion.7), channel_id=4, replica_groups=mesh['q'=4,'y'=2,'x'=2,'c'=2] {'y','x','c'}, dimensions={0}, use_global_device_ids=true | all-gather | bytes 1105920 | tf_op jit(solution)/shard_map/all_gather | solution.py:143
  173.0 7.8 %all-gather.10.cloned.1.call-done = bf16[1920,640]{1,0:T(8,128)(2,1)} async-done(((bf16[480,640]{1,0:T(8,128)(2,1)}), bf16[1920,640]{1,0:T(8,128)(2,1)}) %all-gather.10.cloned.1.call-update) | async-done | bytes 2457616 | tf_op jit(solution)/shard_map/all_gather | solution.py:230
  187.5 2.2 collective-permute-done.3
  193.1 2.4 collective-permute-start.6
  197.6 2.6 collective-permute-done.6
  200.2 2.4 collective-permute-done.5
  204.7 15.4 %all-gather.3 = bf16[256,1024]{1,0:T(8,128)(2,1)S(1)} all-gather(bf16[64,1024]{1,0:T(8,128)(2,1)S(1)} %pad.31), channel_id=5, replica_groups=mesh['q'=4,'y'=2,'x'=2,'c'=2] {'q'}, dimensions={0}, use_global_device_ids=true | all-gather | bytes 655360 | tf_op jit(solution)/shard_map/all_gather | solution.py:299
  221.9 10.3 %collective-permute-done.7 = bf16[4,64,1024]{2,1,0:T(8,128)(2,1)S(1)} collective-permute-done((bf16[4,64,1024]{2,1,0:T(8,128)(2,1)S(1)}, bf16[4,64,1024]{2,1,0:T(8,128)(2,1)S(1)}, u32[]{:S(2)}, u32[]{:S(2)}) %collective-permute-start.7) | collective-permute-done | bytes 524320 | tf_op jit(solution)/shard_map/ppermute | solution.py:74
  236.7 2.3 collective-permute-done.9
  242.7 4.5 fusion.182
  250.3 3.9 fusion.181
  260.9 10.1 %all_to_all.53 = f32[32,1,256]{2,1,0:T(1,128)S(1)} all-to-all(f32[32,1,256]{2,1,0:T(1,128)} %reshape.798), channel_id=1, replica_groups=mesh['q'=4,'y'=2,'x'=2,'c'=2] {'q','y','x','c'}, dimensions={0} | all-to-all | bytes 65536 | tf_op jit(solution)/shard_map/all_to_all | solution.py:320
  277.0 8.9 %all_to_all.54 = f32[32,1,64]{2,1,0:T(1,128)S(1)} all-to-all(f32[32,1,64]{2,1,0:T(1,128)S(1)} %broadcast_in_dim.101), channel_id=1, replica_groups=mesh['q'=4,'y'=2,'x'=2,'c'=2] {'q','y','x','c'}, dimensions={0} | all-to-all | bytes 16384 | tf_op jit(solution)/shard_map/all_to_all | solution.py:330
  287.4 7.1 %convolution_convert_fusion = bf16[1024,1024]{1,0:T(8,128)(2,1)} fusion(bf16[1000,960]{0,1:T(8,128)(2,1)} %convert_element_type.330, f32[1024,1000]{0,1:T(8,128)} %copy-done.17, f32[1024]{0:T(1024)S(1)} %squeeze.126, f32[1024]{0:T(1024)S(1)} %multiply_add_fusion.3, s32[1024]{0:T(1024)} %copy-done.81), kind=kOutput, calls=%fused_computation.61 | convolution fusion | flops 2106392576 | bytes 8125440 | tf_op jit(solution)/shard_map/dot_general | solution.py:52
  294.7 5.6 fusion.153
  300.4 4.8 fusion.183
  308.9 4.3 fusion.154
  313.2 7.9 %collective-permute-done.15 = bf16[4,64,1024]{2,1,0:T(8,128)(2,1)S(1)} collective-permute-done((bf16[4,64,1024]{2,1,0:T(8,128)(2,1)S(1)}, bf16[4,64,1024]{2,1,0:T(8,128)(2,1)S(1)}, u32[]{:S(2)}, u32[]{:S(2)}) %collective-permute-start.15) | collective-permute-done | bytes 524320 | tf_op jit(solution)/shard_map/ppermute | solution.py:74
  321.1 10.0 %collective-permute-done.14 = bf16[4,64,1024]{2,1,0:T(8,128)(2,1)S(1)} collective-permute-done((bf16[4,64,1024]{2,1,0:T(8,128)(2,1)S(1)}, bf16[4,64,1024]{2,1,0:T(8,128)(2,1)S(1)}, u32[]{:S(2)}, u32[]{:S(2)}) %collective-permute-start.14) | collective-permute-done | bytes 524320 | tf_op jit(solution)/shard_map/ppermute | solution.py:74
  331.6 3.8 collective-permute-start.18
  336.4 2.9 slice_add_fusion
  340.2 6.1 %collective-permute-done.17 = bf16[64,1024]{1,0:T(8,128)(2,1)S(1)} collective-permute-done((bf16[64,1024]{1,0:T(8,128)(2,1)S(1)}, bf16[64,1024]{1,0:T(8,128)(2,1)S(1)}, u32[]{:S(2)}, u32[]{:S(2)}) %collective-permute-start.17) | collective-permute-done | bytes 131104 | tf_op jit(solution)/shard_map/ppermute | solution.py:74
  347.2 11.2 %all-gather.4 = bf16[512,960]{1,0:T(8,128)(2,1)S(1)} all-gather(bf16[64,960]{1,0:T(8,128)(2,1)S(1)} %fusion.148), channel_id=6, replica_groups=mesh['q'=4,'y'=2,'x'=2,'c'=2] {'y','x','c'}, dimensions={0}, use_global_device_ids=true | all-gather | bytes 1105920 | tf_op jit(solution)/shard_map/all_gather | solution.py:143
  378.5 2.2 multiply_reduce_fusion.1
  390.4 4.0 convolution_convert_fusion.9
  399.5 2.2 fusion.15
  405.4 2.3 copy.226
  409.4 2.3 copy.227
  411.7 5.5 all-to-all-start.5
  420.6 3.1 reshape.712
  426.1 6.2 %fusion.2 = bf16[8,352,960]{2,1,0:T(8,128)(2,1)} fusion(bf16[1,3,960]{2,1,0:T(4,128)(2,1)S(1)} %copy-done.74, bf16[3,320,960]{2,1,0:T(8,128)(2,1)S(1)} %bitcast.239, bf16[5,128,960]{2,1,0:T(8,128)(2,1)S(1)} %reshape.712, bf16[5,192,960]{2,1,0:T(8,128)(2,1)S(1)} %bitcast.238), kind=kLoop, calls=%fused_computation.10 | loop fusion | flops 27033600 | bytes 10327680 | tf_op jit(solution)/shard_map/concatenate | solution.py:416
  432.3 8.7 %all-to-all-done.5 = bf16[32,16,960]{2,1,0:T(8,128)(2,1)} async-done(((bf16[32,16,960]{2,1,0:T(8,128)(2,1)}), bf16[32,16,960]{2,1,0:T(8,128)(2,1)}, u32[]{:S(2)}, u32[]{:S(2)}) %all-to-all-start.5) | async-done | bytes 983072 | tf_op jit(solution)/shard_map/all_to_all | solution.py:190
  441.1 5.9 %constant_dynamic-slice_fusion = (bf16[4,1,352,960]{3,2,1,0:T(8,128)(2,1)}, bf16[4,352,960]{2,1,0:T(8,128)(2,1)}) fusion(bf16[4,2,352,960]{3,2,1,0:T(8,128)(2,1)} %bitcast.228, s32[]{:T(128)S(6)} %select_n.319, s32[]{:T(128)S(6)} %select_n.320), kind=kLoop, calls=%fused_computation.274 | loop fusion | bytes 10813448 | tf_op jit(solution)/shard_map/jit(dynamic_index_in_dim)/dynamic_slice | solution.py:418
  449.0 3.5 collective-permute-done.23
  460.2 6.0 %all-to-all-start.6 = ((bf16[32,16,960]{2,1,0:T(8,128)(2,1)}), bf16[32,16,960]{2,1,0:T(8,128)(2,1)}, u32[]{:S(2)}, u32[]{:S(2)}) async-start(bf16[32,16,960]{2,1,0:T(8,128)(2,1)} %bitcast.254), calls=%async_computation.7 | async-start | bytes 2097152 | tf_op jit(solution)/shard_map/all_to_all | solution.py:190
  466.5 14.3 %collective-permute-done.26 = bf16[2,176,960]{2,1,0:T(8,128)(2,1)} collective-permute-done((bf16[2,176,960]{2,1,0:T(8,128)(2,1)}, bf16[2,176,960]{2,1,0:T(8,128)(2,1)}, u32[]{:S(2)}, u32[]{:S(2)}) %collective-permute-start.26) | collective-permute-done | bytes 675872 | tf_op jit(solution)/shard_map/ppermute | solution.py:74
  488.6 4.5 fusion.12
  493.1 2.7 collective-permute-done.27
  497.4 2.2 collective-permute-start.30
  499.6 2.2 collective-permute-start.28
  502.7 3.5 all-to-all-start.7
  506.3 2.7 fusion.13
  509.9 4.0 multiply_reduce_fusion
  521.0 6.3 %all-to-all-start.8 = ((f32[32,1,2]{2,1,0:T(1,128)}), f32[32,1,2]{2,1,0:T(1,128)S(1)}, u32[]{:S(2)}, u32[]{:S(2)}) async-start(f32[32,1,2]{2,1,0:T(1,128)} %broadcast_in_dim.168), calls=%async_computation.9 | async-start | bytes 32768 | tf_op jit(solution)/shard_map/all_to_all | solution.py:406
  530.6 3.6 collective-permute-start.33
  537.2 10.2 %add_multiply_fusion = (f32[1000,960]{0,1:T(8,128)}, f32[1000,960]{0,1:T(8,128)}, f32[1000,960]{0,1:T(8,128)}) fusion(f32[1000,960]{0,1:T(8,128)} %param.21, f32[1000,960]{0,1:T(8,128)} %get-tuple-element.119, f32[]{:T(128)S(6)} %div.148, f32[1000,960]{0,1:T(8,128)} %param.23, f32[1000,960]{0,1:T(8,128)} %param.22), kind=kLoop, calls=%fused_computation.24 | loop fusion | flops 14400000 | bytes 26880004 | tf_op jit(solution)/shard_map/mul | solution.py:107
  557.8 4.1 collective-permute-done.34
  561.8 4.8 add_multiply_fusion.1
  (497 shorter events, 180.6 us)
Async XLA Ops:
  8.5 6.8 %collective-permute-start = (bf16[2880]{0:T(1024)(128)(2,1)S(1)}, bf16[2880]{0:T(1024)(128)(2,1)S(1)}, u32[]{:S(2)}, u32[]{:S(2)}) collective-permute-start(bf16[2880]{0:T(1024)(128)(2,1)S(1)} %slice.359), channel_id=1, source_target_pairs={{1,0},{2,1},{3,2},{4,3},{5,4},{6,5},{7,6},{8,7},{9,8},{10,9},{11,1... | collective-permute-start | bytes 17288 | tf_op jit(solution)/shard_map/ppermute | solution.py:200
  18.8 14.3 %collective-permute-start.1 = (bf16[328,960]{1,0:T(8,128)(2,1)S(1)}, bf16[328,960]{1,0:T(8,128)(2,1)}, u32[]{:S(2)}, u32[]{:S(2)}) collective-permute-start(bf16[328,960]{1,0:T(8,128)(2,1)S(1)} %maximum_maximum_fusion), channel_id=1, source_target_pairs={{0,16},{1,17},{2,18},{3,19},{4,20},{5,21},{6,22},{7,23}} | collective-permute-start | bytes 1889288 | tf_op jit(solution)/shard_map/ppermute | solution.py:216
  24.7 15.2 %all-to-all-start = ((s32[32,1,96]{2,1,0:T(1,128)}), s32[32,1,96]{2,1,0:T(1,128)S(1)}, u32[]{:S(2)}, u32[]{:S(2)}) async-start(s32[32,1,96]{2,1,0:T(1,128)} %bitcast), calls=%async_computation | async-start | bytes 32768 | tf_op jit(solution)/shard_map/all_to_all | solution.py:214
  34.3 19.2 %collective-permute-start.2 = (bf16[328,960]{1,0:T(8,128)(2,1)S(1)}, bf16[328,960]{1,0:T(8,128)(2,1)S(1)}, u32[]{:S(2)}, u32[]{:S(2)}) collective-permute-start(bf16[328,960]{1,0:T(8,128)(2,1)S(1)} %broadcast_select_fusion), channel_id=1, source_target_pairs={{0,8},{16,24},{1,9},{17,25},{2,10},{18,26},{3,11},{19,27},{4,12},{... | collective-permute-start | bytes 1889288 | tf_op jit(solution)/shard_map/ppermute | solution.py:218
  39.9 14.6 %all-to-all-start.1 = ((bf16[8,60,640]{2,1,0:T(8,128)(2,1)}), bf16[8,60,640]{2,1,0:T(8,128)(2,1)S(1)}, u32[]{:S(2)}, u32[]{:S(2)}) async-start(bf16[8,60,640]{2,1,0:T(8,128)(2,1)} %reshape.787), calls=%async_computation.1 | async-start | bytes 1310720 | tf_op jit(solution)/shard_map/all_to_all | solution.py:208
  43.5 73.6 %all-gather.8.cloned.1.call-start = ((), (), s32[]{:S(2)}) async-start(), calls=%async_computation.11 | async-start | bytes 6045696 | tf_op jit(solution)/shard_map/all_gather | solution.py:222
  54.6 8.9 %copy-start = (s32[32]{0:T(128)S(1)}, s32[32]{0:T(128)}, u32[]{:S(2)}) copy-start(s32[32]{0:T(128)} %constant.373.clone) | copy-start | bytes 388
  54.6 10.2 %copy-start.55 = (f32[512,64]{1,0:T(8,128)S(1)}, f32[512,64]{1,0:T(8,128)}, u32[]{:S(2)}) copy-start(f32[512,64]{1,0:T(8,128)} %constant.399) | copy-start | bytes 393220
  54.6 10.8 %copy-start.54 = (f32[512,64]{1,0:T(8,128)S(1)}, f32[512,64]{1,0:T(8,128)}, u32[]{:S(2)}) copy-start(f32[512,64]{1,0:T(8,128)} %constant.398) | copy-start | bytes 393220
  54.6 72.2 %all-to-all-start.2 = ((bf16[32,32,960]{2,1,0:T(8,128)(2,1)}), bf16[32,32,960]{2,1,0:T(8,128)(2,1)}, u32[]{:S(2)}, u32[]{:S(2)}) async-start(bf16[32,32,960]{2,1,0:T(8,128)(2,1)} %bitcast.237), calls=%async_computation.2 | async-start | bytes 4194304 | tf_op jit(solution)/shard_map/all_to_all | solution.py:190
  63.0 117.8 %all-gather.10.cloned.1.call-start = ((), (), s32[]{:S(2)}) async-start(), calls=%async_computation.12 | async-start | bytes 3072000 | tf_op jit(solution)/shard_map/all_gather | solution.py:230
  65.4 73.4 %copy-start.52 = (f32[64,64]{1,0:T(8,128)}, f32[64,64]{1,0:T(8,128)S(1)}, u32[]{:S(2)}) copy-start(f32[64,64]{1,0:T(8,128)S(1)} %gather_fusion.1) | copy-start | bytes 49156
  129.7 27.3 %copy-start.3 = (bf16[512,960]{0,1:T(8,128)(2,1)}, bf16[512,960]{0,1:T(8,128)(2,1)S(1)}, u32[]{:S(2)}) copy-start(bf16[512,960]{0,1:T(8,128)(2,1)S(1)} %get-tuple-element.198) | copy-start | bytes 2949124
  129.8 29.9 %copy-start.69 = (f32[1,1,960]{2,1,0:T(1,128)}, f32[1,1,960]{2,1,0:T(1,128)S(1)}, u32[]{:S(2)}) copy-start(f32[1,1,960]{2,1,0:T(1,128)S(1)} %get-tuple-element.185) | copy-start | bytes 11524
  129.8 74.8 %copy-start.67 = (f32[1,1,960]{2,1,0:T(1,128)}, f32[1,1,960]{2,1,0:T(1,128)S(1)}, u32[]{:S(2)}) copy-start(f32[1,1,960]{2,1,0:T(1,128)S(1)} %get-tuple-element.184) | copy-start | bytes 11524
  130.5 288.1 %reduce-scatter.2.cloned.1.call-start = ((), (), s32[]{:S(2)}) async-start(), calls=%async_computation.10 | async-start | bytes 3072000 | tf_op jit(solution)/shard_map/reduce_scatter | solution.py:396
  159.7 22.6 %copy-start.93 = (f32[64]{0:T(128)}, f32[64]{0:T(128)S(1)}, u32[]{:S(2)}) copy-start(f32[64]{0:T(128)S(1)} %add_rsqrt_fusion.2) | copy-start | bytes 772
  187.4 2.3 collective-permute-start.3
  193.1 7.1 %collective-permute-start.6 = (bf16[64,1024]{1,0:T(8,128)(2,1)}, bf16[64,1024]{1,0:T(8,128)(2,1)S(1)}, u32[]{:S(2)}, u32[]{:S(2)}) collective-permute-start(bf16[64,1024]{1,0:T(8,128)(2,1)} %get-tuple-element.170), channel_id=1, source_target_pairs={{0,6},{2,4},{4,2},{6,0},{1,7},{3,5},{5,3},{7,1},{8,14},{10,12},{12... | collective-permute-start | bytes 393224 | tf_op jit(solution)/shard_map/ppermute | solution.py:74
  195.5 7.0 %collective-permute-start.5 = (bf16[64,1024]{1,0:T(8,128)(2,1)}, bf16[64,1024]{1,0:T(8,128)(2,1)S(1)}, u32[]{:S(2)}, u32[]{:S(2)}) collective-permute-start(bf16[64,1024]{1,0:T(8,128)(2,1)} %get-tuple-element.171), channel_id=1, source_target_pairs={{0,4},{2,6},{4,0},{6,2},{1,5},{3,7},{5,1},{7,3},{8,12},{10,14},{12... | collective-permute-start | bytes 393224 | tf_op jit(solution)/shard_map/ppermute | solution.py:74
  196.1 7.2 %collective-permute-start.4 = (bf16[64,1024]{1,0:T(8,128)(2,1)}, bf16[64,1024]{1,0:T(8,128)(2,1)}, u32[]{:S(2)}, u32[]{:S(2)}) collective-permute-start(bf16[64,1024]{1,0:T(8,128)(2,1)} %get-tuple-element.169), channel_id=1, source_target_pairs={{0,2},{2,0},{4,6},{6,4},{1,3},{3,1},{5,7},{7,5},{8,10},{10,8},{12,... | collective-permute-start | bytes 393224 | tf_op jit(solution)/shard_map/ppermute | solution.py:74
  204.6 31.3 %copy-start.89 = (f32[64]{0:T(128)}, f32[64]{0:T(128)S(1)}, u32[]{:S(2)}) copy-start(f32[64]{0:T(128)S(1)} %add_rsqrt_fusion.1) | copy-start | bytes 772
  220.1 12.1 %collective-permute-start.7 = (bf16[4,64,1024]{2,1,0:T(8,128)(2,1)S(1)}, bf16[4,64,1024]{2,1,0:T(8,128)(2,1)S(1)}, u32[]{:S(2)}, u32[]{:S(2)}) collective-permute-start(bf16[4,64,1024]{2,1,0:T(8,128)(2,1)S(1)} %bitcast.265), channel_id=1, source_target_pairs={{0,2},{2,0},{1,3},{3,1},{4,6},{6,4},{5,7},{7,5},{8,10},{10,8},{9,1... | collective-permute-start | bytes 1572872 | tf_op jit(solution)/shard_map/ppermute | solution.py:74
  221.7 12.8 %collective-permute-start.8 = (bf16[4,64,1024]{2,1,0:T(8,128)(2,1)S(1)}, bf16[4,64,1024]{2,1,0:T(8,128)(2,1)S(1)}, u32[]{:S(2)}, u32[]{:S(2)}) collective-permute-start(bf16[4,64,1024]{2,1,0:T(8,128)(2,1)S(1)} %bitcast.266), channel_id=1, source_target_pairs={{0,4},{4,0},{1,5},{5,1},{2,6},{6,2},{3,7},{7,3},{8,12},{12,8},{9,1... | collective-permute-start | bytes 1572872 | tf_op jit(solution)/shard_map/ppermute | solution.py:74
  232.2 6.8 %collective-permute-start.9 = (bf16[2,64,1024]{2,1,0:T(8,128)(2,1)S(1)}, bf16[2,64,1024]{2,1,0:T(8,128)(2,1)S(1)}, u32[]{:S(2)}, u32[]{:S(2)}) collective-permute-start(bf16[2,64,1024]{2,1,0:T(8,128)(2,1)S(1)} %slice.385), channel_id=1, source_target_pairs={{0,4},{4,0},{1,5},{5,1},{2,6},{6,2},{3,7},{7,3},{8,12},{12,8},{9,1... | collective-permute-start | bytes 786440 | tf_op jit(solution)/shard_map/ppermute | solution.py:74
  234.6 6.4 %collective-permute-start.10 = (bf16[2,64,1024]{2,1,0:T(8,128)(2,1)S(1)}, bf16[2,64,1024]{2,1,0:T(8,128)(2,1)S(1)}, u32[]{:S(2)}, u32[]{:S(2)}) collective-permute-start(bf16[2,64,1024]{2,1,0:T(8,128)(2,1)S(1)} %slice.386), channel_id=1, source_target_pairs={{0,2},{2,0},{1,3},{3,1},{4,6},{6,4},{5,7},{7,5},{8,10},{10,8},{9,1... | collective-permute-start | bytes 786440 | tf_op jit(solution)/shard_map/ppermute | solution.py:74
  241.7 7.6 %collective-permute-start.11 = (bf16[1024,1024]{1,0:T(8,128)(2,1)}, bf16[1024,1024]{1,0:T(8,128)(2,1)}, u32[]{:S(2)}, u32[]{:S(2)}) collective-permute-start(bf16[1024,1024]{1,0:T(8,128)(2,1)} %bitcast.38), channel_id=1, source_target_pairs={{0,1},{1,0},{2,3},{3,2},{4,5},{5,4},{6,7},{7,6},{8,9},{9,8},{10,11... | collective-permute-start | bytes 6291464 | tf_op jit(solution)/shard_map/ppermute | solution.py:74
  242.6 11.6 %copy-start.81 = (s32[1024]{0:T(1024)}, s32[1024]{0:T(1024)S(1)}, u32[]{:S(2)}) copy-start(s32[1024]{0:T(1024)S(1)} %sub.233) | copy-start | bytes 12292
  294.5 5.8 %collective-permute-start.12 = (bf16[1024,1024]{1,0:T(8,128)(2,1)}, bf16[1024,1024]{1,0:T(8,128)(2,1)}, u32[]{:S(2)}, u32[]{:S(2)}) collective-permute-start(bf16[1024,1024]{1,0:T(8,128)(2,1)} %convolution_convert_fusion), channel_id=1, source_target_pairs={{0,1},{1,0},{2,3},{3,2},{4,5},{5,4},{6,7},{7,6},{8,9},{9,8},{10,11... | collective-permute-start | bytes 6291464 | tf_op jit(solution)/shard_map/ppermute | solution.py:74
  305.3 15.8 %collective-permute-start.15 = (bf16[4,64,1024]{2,1,0:T(8,128)(2,1)S(1)}, bf16[4,64,1024]{2,1,0:T(8,128)(2,1)S(1)}, u32[]{:S(2)}, u32[]{:S(2)}) collective-permute-start(bf16[4,64,1024]{2,1,0:T(8,128)(2,1)S(1)} %bitcast.292), channel_id=1, source_target_pairs={{0,6},{2,4},{4,2},{6,0},{1,7},{3,5},{5,3},{7,1},{8,14},{10,12},{12... | collective-permute-start | bytes 1572872 | tf_op jit(solution)/shard_map/ppermute | solution.py:74
  305.9 25.3 %collective-permute-start.14 = (bf16[4,64,1024]{2,1,0:T(8,128)(2,1)S(1)}, bf16[4,64,1024]{2,1,0:T(8,128)(2,1)S(1)}, u32[]{:S(2)}, u32[]{:S(2)}) collective-permute-start(bf16[4,64,1024]{2,1,0:T(8,128)(2,1)S(1)} %bitcast.291), channel_id=1, source_target_pairs={{0,4},{2,6},{4,0},{6,2},{1,5},{3,7},{5,1},{7,3},{8,12},{10,14},{12... | collective-permute-start | bytes 1572872 | tf_op jit(solution)/shard_map/ppermute | solution.py:74
  307.3 23.8 %collective-permute-start.13 = (bf16[4,64,1024]{2,1,0:T(8,128)(2,1)S(1)}, bf16[4,64,1024]{2,1,0:T(8,128)(2,1)S(1)}, u32[]{:S(2)}, u32[]{:S(2)}) collective-permute-start(bf16[4,64,1024]{2,1,0:T(8,128)(2,1)S(1)} %bitcast.290), channel_id=1, source_target_pairs={{0,2},{2,0},{4,6},{6,4},{1,3},{3,1},{5,7},{7,5},{8,10},{10,8},{12,... | collective-permute-start | bytes 1572872 | tf_op jit(solution)/shard_map/ppermute | solution.py:74
  331.6 8.6 %collective-permute-start.18 = (bf16[64,1024]{1,0:T(8,128)(2,1)S(1)}, bf16[64,1024]{1,0:T(8,128)(2,1)S(1)}, u32[]{:S(2)}, u32[]{:S(2)}) collective-permute-start(bf16[64,1024]{1,0:T(8,128)(2,1)S(1)} %get-tuple-element.167), channel_id=1, source_target_pairs={{0,24},{8,16},{16,8},{24,0},{1,25},{9,17},{17,9},{25,1},{2,26},{10... | collective-permute-start | bytes 393224 | tf_op jit(solution)/shard_map/ppermute | solution.py:74
  335.4 10.9 %collective-permute-start.17 = (bf16[64,1024]{1,0:T(8,128)(2,1)S(1)}, bf16[64,1024]{1,0:T(8,128)(2,1)S(1)}, u32[]{:S(2)}, u32[]{:S(2)}) collective-permute-start(bf16[64,1024]{1,0:T(8,128)(2,1)S(1)} %get-tuple-element.168), channel_id=1, source_target_pairs={{0,16},{8,24},{16,0},{24,8},{1,17},{9,25},{17,1},{25,9},{2,18},{10... | collective-permute-start | bytes 393224 | tf_op jit(solution)/shard_map/ppermute | solution.py:74
  335.4 10.9 %copy-start.68 = (f32[1,1,960]{2,1,0:T(1,128)S(1)}, f32[1,1,960]{2,1,0:T(1,128)}, u32[]{:S(2)}) copy-start(f32[1,1,960]{2,1,0:T(1,128)} %copy-done.67) | copy-start | bytes 11524
  335.4 10.9 %copy-start.90 = (f32[64]{0:T(128)S(1)}, f32[64]{0:T(128)}, u32[]{:S(2)}) copy-start(f32[64]{0:T(128)} %copy-done.89) | copy-start | bytes 772
  335.4 10.9 %collective-permute-start.16 = (bf16[64,1024]{1,0:T(8,128)(2,1)S(1)}, bf16[64,1024]{1,0:T(8,128)(2,1)S(1)}, u32[]{:S(2)}, u32[]{:S(2)}) collective-permute-start(bf16[64,1024]{1,0:T(8,128)(2,1)S(1)} %get-tuple-element.166), channel_id=1, source_target_pairs={{0,8},{8,0},{16,24},{24,16},{1,9},{9,1},{17,25},{25,17},{2,10},{10... | collective-permute-start | bytes 393224 | tf_op jit(solution)/shard_map/ppermute | solution.py:74
  339.3 19.2 %copy-start.36 = (f32[512,640]{1,0:T(8,128)S(1)}, f32[512,640]{1,0:T(8,128)}, u32[]{:S(2)}) copy-start(f32[512,640]{1,0:T(8,128)} %copy-done.35) | copy-start | bytes 3932164
  339.3 19.2 %copy-start.50 = (bf16[320,640]{1,0:T(8,128)(2,1)S(1)}, bf16[320,640]{1,0:T(8,128)(2,1)}, u32[]{:S(2)}) copy-start(bf16[320,640]{1,0:T(8,128)(2,1)} %copy-done.49) | copy-start | bytes 1228804
  339.3 19.2 %copy-start.64 = (bf16[160,320]{1,0:T(8,128)(2,1)S(1)}, bf16[160,320]{1,0:T(8,128)(2,1)}, u32[]{:S(2)}) copy-start(bf16[160,320]{1,0:T(8,128)(2,1)} %copy-done.63) | copy-start | bytes 307204
  339.3 19.2 %copy-start.66 = (bf16[160,320]{1,0:T(8,128)(2,1)S(1)}, bf16[160,320]{1,0:T(8,128)(2,1)}, u32[]{:S(2)}) copy-start(bf16[160,320]{1,0:T(8,128)(2,1)} %copy-done.65) | copy-start | bytes 307204
  360.9 2.6 collective-permute-start.19
  365.2 7.5 %collective-permute-start.22 = (bf16[64,1024]{1,0:T(8,128)(2,1)S(1)}, bf16[64,1024]{1,0:T(8,128)(2,1)}, u32[]{:S(2)}, u32[]{:S(2)}) collective-permute-start(bf16[64,1024]{1,0:T(8,128)(2,1)S(1)} %get-tuple-element.164), channel_id=1, source_target_pairs={{0,6},{2,4},{4,2},{6,0},{1,7},{3,5},{5,3},{7,1},{8,14},{10,12},{12... | collective-permute-start | bytes 393224 | tf_op jit(solution)/shard_map/ppermute | solution.py:74
  366.7 8.0 %collective-permute-start.21 = (bf16[64,1024]{1,0:T(8,128)(2,1)S(1)}, bf16[64,1024]{1,0:T(8,128)(2,1)}, u32[]{:S(2)}, u32[]{:S(2)}) collective-permute-start(bf16[64,1024]{1,0:T(8,128)(2,1)S(1)} %get-tuple-element.165), channel_id=1, source_target_pairs={{0,4},{2,6},{4,0},{6,2},{1,5},{3,7},{5,1},{7,3},{8,12},{10,14},{12... | collective-permute-start | bytes 393224 | tf_op jit(solution)/shard_map/ppermute | solution.py:74
  367.3 7.4 %collective-permute-start.20 = (bf16[64,1024]{1,0:T(8,128)(2,1)S(1)}, bf16[64,1024]{1,0:T(8,128)(2,1)}, u32[]{:S(2)}, u32[]{:S(2)}) collective-permute-start(bf16[64,1024]{1,0:T(8,128)(2,1)S(1)} %get-tuple-element.163), channel_id=1, source_target_pairs={{0,2},{2,0},{4,6},{6,4},{1,3},{3,1},{5,7},{7,5},{8,10},{10,8},{12,... | collective-permute-start | bytes 393224 | tf_op jit(solution)/shard_map/ppermute | solution.py:74
  411.7 29.4 %all-to-all-start.5 = ((bf16[32,16,960]{2,1,0:T(8,128)(2,1)}), bf16[32,16,960]{2,1,0:T(8,128)(2,1)}, u32[]{:S(2)}, u32[]{:S(2)}) async-start(bf16[32,16,960]{2,1,0:T(8,128)(2,1)} %bitcast.86), calls=%async_computation.6 | async-start | bytes 2097152 | tf_op jit(solution)/shard_map/all_to_all | solution.py:190
  446.9 5.6 collective-permute-start.23
  456.0 24.8 %collective-permute-start.26 = (bf16[2,176,960]{2,1,0:T(8,128)(2,1)}, bf16[2,176,960]{2,1,0:T(8,128)(2,1)}, u32[]{:S(2)}, u32[]{:S(2)}) collective-permute-start(bf16[2,176,960]{2,1,0:T(8,128)(2,1)} %fusion.59), channel_id=1, source_target_pairs={{0,4},{4,0},{1,5},{5,1},{2,6},{6,2},{3,7},{7,3},{8,12},{12,8},{9,1... | collective-permute-start | bytes 2027528 | tf_op jit(solution)/shard_map/ppermute | solution.py:74
  458.8 26.4 %collective-permute-start.24 = (bf16[2,176,960]{2,1,0:T(8,128)(2,1)}, bf16[2,176,960]{2,1,0:T(8,128)(2,1)}, u32[]{:S(2)}, u32[]{:S(2)}) collective-permute-start(bf16[2,176,960]{2,1,0:T(8,128)(2,1)} %fusion.58), channel_id=1, source_target_pairs={{0,2},{2,0},{1,3},{3,1},{4,6},{6,4},{5,7},{7,5},{8,10},{10,8},{9,1... | collective-permute-start | bytes 2027528 | tf_op jit(solution)/shard_map/ppermute | solution.py:74
  460.2 36.4 %all-to-all-start.6 = ((bf16[32,16,960]{2,1,0:T(8,128)(2,1)}), bf16[32,16,960]{2,1,0:T(8,128)(2,1)}, u32[]{:S(2)}, u32[]{:S(2)}) async-start(bf16[32,16,960]{2,1,0:T(8,128)(2,1)} %bitcast.254), calls=%async_computation.7 | async-start | bytes 2097152 | tf_op jit(solution)/shard_map/all_to_all | solution.py:190
  482.8 13.1 %collective-permute-start.27 = (bf16[176,960]{1,0:T(8,128)(2,1)S(1)}, bf16[176,960]{1,0:T(8,128)(2,1)S(1)}, u32[]{:S(2)}, u32[]{:S(2)}) collective-permute-start(bf16[176,960]{1,0:T(8,128)(2,1)S(1)} %fusion.77), channel_id=1, source_target_pairs={{0,2},{2,0},{1,3},{3,1},{4,6},{6,4},{5,7},{7,5},{8,10},{10,8},{9,1... | collective-permute-start | bytes 1013768 | tf_op jit(solution)/shard_map/ppermute | solution.py:74
  486.7 9.7 %collective-permute-start.25 = (bf16[176,960]{1,0:T(8,128)(2,1)S(1)}, bf16[176,960]{1,0:T(8,128)(2,1)S(1)}, u32[]{:S(2)}, u32[]{:S(2)}) collective-permute-start(bf16[176,960]{1,0:T(8,128)(2,1)S(1)} %fusion.76), channel_id=1, source_target_pairs={{0,4},{4,0},{1,5},{5,1},{2,6},{6,2},{3,7},{7,3},{8,12},{12,8},{9,1... | collective-permute-start | bytes 1013768 | tf_op jit(solution)/shard_map/ppermute | solution.py:74
  497.4 18.6 %collective-permute-start.30 = (bf16[88,960]{1,0:T(8,128)(2,1)}, bf16[88,960]{1,0:T(8,128)(2,1)}, u32[]{:S(2)}, u32[]{:S(2)}) collective-permute-start(bf16[88,960]{1,0:T(8,128)(2,1)} %get-tuple-element.145), channel_id=1, source_target_pairs={{0,24},{8,16},{16,8},{24,0},{1,25},{9,17},{17,9},{25,1},{2,26},{10... | collective-permute-start | bytes 506888 | tf_op jit(solution)/shard_map/ppermute | solution.py:74
  499.6 16.4 %collective-permute-start.29 = (bf16[88,960]{1,0:T(8,128)(2,1)}, bf16[88,960]{1,0:T(8,128)(2,1)}, u32[]{:S(2)}, u32[]{:S(2)}) collective-permute-start(bf16[88,960]{1,0:T(8,128)(2,1)} %get-tuple-element.146), channel_id=1, source_target_pairs={{0,16},{8,24},{16,0},{24,8},{1,17},{9,25},{17,1},{25,9},{2,18},{10... | collective-permute-start | bytes 506888 | tf_op jit(solution)/shard_map/ppermute | solution.py:74
  499.6 16.4 %collective-permute-start.28 = (bf16[88,960]{1,0:T(8,128)(2,1)}, bf16[88,960]{1,0:T(8,128)(2,1)}, u32[]{:S(2)}, u32[]{:S(2)}) collective-permute-start(bf16[88,960]{1,0:T(8,128)(2,1)} %get-tuple-element.144), channel_id=1, source_target_pairs={{0,8},{8,0},{16,24},{24,16},{1,9},{9,1},{17,25},{25,17},{2,10},{10... | collective-permute-start | bytes 506888 | tf_op jit(solution)/shard_map/ppermute | solution.py:74
  502.7 17.0 %all-to-all-start.7 = ((bf16[8,60,640]{2,1,0:T(8,128)(2,1)}), bf16[8,60,640]{2,1,0:T(8,128)(2,1)S(1)}, u32[]{:S(2)}, u32[]{:S(2)}) async-start(bf16[8,60,640]{2,1,0:T(8,128)(2,1)} %reshape.720), calls=%async_computation.8 | async-start | bytes 1310720 | tf_op jit(solution)/shard_map/all_to_all | solution.py:437
  517.8 17.2 %copy-start.38 = (bf16[88,960]{1,0:T(8,128)(2,1)}, bf16[88,960]{1,0:T(8,128)(2,1)S(1)}, u32[]{:S(2)}) copy-start(bf16[88,960]{1,0:T(8,128)(2,1)S(1)} %get-tuple-element.91) | copy-start | bytes 506884
  521.0 14.8 %all-to-all-start.8 = ((f32[32,1,2]{2,1,0:T(1,128)}), f32[32,1,2]{2,1,0:T(1,128)S(1)}, u32[]{:S(2)}, u32[]{:S(2)}) async-start(f32[32,1,2]{2,1,0:T(1,128)} %broadcast_in_dim.168), calls=%async_computation.9 | async-start | bytes 32768 | tf_op jit(solution)/shard_map/all_to_all | solution.py:406
  529.2 18.3 %collective-permute-start.31 = (bf16[88,960]{1,0:T(8,128)(2,1)S(1)}, bf16[88,960]{1,0:T(8,128)(2,1)S(1)}, u32[]{:S(2)}, u32[]{:S(2)}) collective-permute-start(bf16[88,960]{1,0:T(8,128)(2,1)S(1)} %get-tuple-element.91), channel_id=1, source_target_pairs={{8,0},{9,1},{10,2},{11,3},{12,4},{13,5},{14,6},{15,7}} | collective-permute-start | bytes 506888 | tf_op jit(solution)/shard_map/ppermute | solution.py:449
  529.9 17.6 %collective-permute-start.32 = (bf16[88,960]{1,0:T(8,128)(2,1)S(1)}, bf16[88,960]{1,0:T(8,128)(2,1)S(1)}, u32[]{:S(2)}, u32[]{:S(2)}) collective-permute-start(bf16[88,960]{1,0:T(8,128)(2,1)S(1)} %get-tuple-element.91), channel_id=1, source_target_pairs={{16,0},{17,1},{18,2},{19,3},{20,4},{21,5},{22,6},{23,7}} | collective-permute-start | bytes 506888 | tf_op jit(solution)/shard_map/ppermute | solution.py:449
  530.6 16.9 %collective-permute-start.33 = (bf16[88,960]{1,0:T(8,128)(2,1)S(1)}, bf16[88,960]{1,0:T(8,128)(2,1)S(1)}, u32[]{:S(2)}, u32[]{:S(2)}) collective-permute-start(bf16[88,960]{1,0:T(8,128)(2,1)S(1)} %get-tuple-element.91), channel_id=1, source_target_pairs={{24,0},{25,1},{26,2},{27,3},{28,4},{29,5},{30,6},{31,7}} | collective-permute-start | bytes 506888 | tf_op jit(solution)/shard_map/ppermute | solution.py:449
  537.2 11.3 %copy-start.39 = (bf16[88,960]{1,0:T(8,128)(2,1)S(1)}, bf16[88,960]{1,0:T(8,128)(2,1)}, u32[]{:S(2)}) copy-start(bf16[88,960]{1,0:T(8,128)(2,1)} %copy-done.38) | copy-start | bytes 506884
  552.3 9.6 %copy-start.12 = (f32[307290]{0:T(1024)S(1)}, f32[307290]{0:T(1024)}, u32[]{:S(2)}) copy-start(f32[307290]{0:T(1024)} %param.18) | copy-start | bytes 3687484
  555.1 6.7 %collective-permute-start.34 = (bf16[2880]{0:T(1024)(128)(2,1)S(1)}, bf16[2880]{0:T(1024)(128)(2,1)S(1)}, u32[]{:S(2)}, u32[]{:S(2)}) collective-permute-start(bf16[2880]{0:T(1024)(128)(2,1)S(1)} %slice.424), channel_id=1, source_target_pairs={{0,1},{1,2},{2,3},{3,4},{4,5},{5,6},{6,7},{7,8},{8,9},{9,10},{10,1... | collective-permute-start | bytes 17288 | tf_op jit(solution)/shard_map/ppermute | solution.py:472
  (84 other events, 284.7 us)
Sparse Core Ops, SparseCore 0:
  54.7 62.3 all-gather.7
  130.6 50.1 all-gather.9
  370.6 47.9 reduce-scatter.1

commit v11 on v10

--- a/solution.py
+++ b/solution.py
@@ -105,6 +105,12 @@
     new_two = BETA2 * moment_two + (1.0 - BETA2) * gradient * gradient
     ratio = new_one / (1.0 - BETA1**STEP) / (jnp.sqrt(new_two / (1.0 - BETA2**STEP)) + ADAM_EPS)
     return (new_one, new_two, -RATE * (ratio + DECAY * param))
+
+
+def merge_stats(one, two):
+    peak = jnp.maximum(one[0], two[0])
+    total = one[1] * jnp.exp(one[0] - peak) + two[1] * jnp.exp(two[0] - peak)
+    return jnp.stack([peak, total, one[2] + two[2], one[3] + two[3]])
 
 
 def pick_block(blocks, index, axis=0):
@@ -168,9 +174,7 @@
     aligned = devices == 32
 
     place = np.array([q * 8 + kyx * 2 + kc for kc in range(2) for kyx in range(4) for q in range(rows_q)])
-    rank_of = np.argsort(place)
     source_of = p_index ^ jnp.asarray(place, jnp.int32)
-    order_of = jnp.take(jnp.asarray(rank_of, jnp.int32), p_index ^ jnp.arange(devices, dtype=jnp.int32))
 
     table_low = table_master.astype(bf16)
     owner = token_ids // vocab_dev
@@ -189,7 +193,7 @@
     def exchange(blocks):
         return lax.all_to_all(blocks, ALL, split_axis=0, concat_axis=0, tiled=True).reshape(-1, D)
 
-    cuts_back = (0, capacity // 2, capacity)
+    cuts_back = (0, capacity // 4, capacity)
     marked = token_ids + 1
     halves = jnp.stack([marked // 256, marked % 256]).astype(bf16)
     found = dot(halves, spot).astype(jnp.int32)
@@ -315,20 +319,21 @@
         logits.append(z)
         hits.append(hit)
         stats.append(jnp.stack([local_peak, local_total, local_target, local_sum]))
-    stats = jnp.concatenate(stats, axis=1).reshape(4, devices, loss_dev)
-    stats = jnp.take(stats, order_of, axis=1).transpose(1, 0, 2)
-    stats = lax.all_to_all(stats, ALL, split_axis=0, concat_axis=0, tiled=True)
-    peak = jnp.max(stats[:, 0], axis=0)
-    total = jnp.sum(stats[:, 1] * jnp.exp(stats[:, 0] - peak[None]), axis=0)
-    my_log = peak + jnp.log(total)
-    my_loss = jnp.sum(
-        my_log
-        - (1.0 - SMOOTH) * jnp.sum(stats[:, 2], axis=0)
-        - SMOOTH / V * jnp.sum(stats[:, 3], axis=0)
-        + ZCOEF * my_log * my_log
-    )
-    logs = lax.all_to_all(jnp.broadcast_to(my_log[None, None], (devices, 1, loss_dev)), ALL, split_axis=0, concat_axis=0, tiled=True)
-    log_total = jnp.take(logs[:, 0], source_of, axis=0).reshape(2, loss_total // 2, 1)
+    stats = jnp.concatenate(stats, axis=1)
+    block = rows_q * loss_dev
+    for axis, bit in (("c", 4), ("x", 1), ("y", 2)):
+        other = flip(stats, axis, 1, 2)
+        other = jnp.concatenate([other[:, (k ^ bit) * block : ((k ^ bit) + 1) * block] for k in range(8)], axis=1)
+        stats = merge_stats(stats, other)
+    bit = 1
+    while bit < rows_q:
+        stats = merge_stats(stats, flip(stats, "q", bit, rows_q))
+        bit *= 2
+    log_total = stats[0] + jnp.log(stats[1])
+    mine_at = q_index * loss_dev
+    my_log, my_target, my_sum = (lax.dynamic_slice(row, (mine_at,), (loss_dev,)) for row in (log_total, stats[2], stats[3]))
+    my_loss = jnp.sum(my_log - (1.0 - SMOOTH) * my_target - SMOOTH / V * my_sum + ZCOEF * my_log * my_log)
+    log_total = log_total.reshape(2, loss_total // 2, 1)
     d_logits = [
         (
             (

time: 586 us -> 571 us (0.974)
  blocking collectives: 57.2 us -> 37.9 us
  waiting for transfers between devices: 145 us -> 160 us
  local copies, waits for them, and re-layouts: 95.2 us -> 88.7 us
    ppermute x28 -> x33, waiting for transfers between devices: 70.3 us -> 91.2 us  [flip(): return lax.ppermute(rows, axes, [(i, i ^ bits) for i in range(size)])]
    all_to_all x2 -> x0, blocking collectives: 19 us -> none  [the longest x1 10.1 us: local(): stats = lax.all_to_all(stats, ALL, split_axis=0, concat_axis=0, tiled=True)]
    all_to_all x3, waiting for transfers between devices: 8.75 us -> 0.01 us  [exchange(): lax.all_to_all(blocks, ALL, split_axis=0, concat_axis=0, tiled=True)]
    ppermute x28 -> x33, starting transfers between devices: 31.2 us -> 34.1 us  [flip(): return lax.ppermute(rows, axes, [(i, i ^ bits) for i in range(size)])]
    unnamed x211 -> x206, local copies, waits for them, and re-layouts: 17.6 us -> 15.6 us
  transfers between devices with their start and end apart: 45 -> 50, of which waited for: 25 -> 27; matrix products, arithmetic and copies ran while one was open for 31% -> 33% of each run, Pallas kernels for 0% -> 0%
where the time goes in v11:
time: 571 us; the launch traced here: 561 us
  waiting for transfers between devices  160 us (28%)
  local copies, waits for them, and re-layouts  88.7 us (16%)
  matrix products  88.5 us (15%)
  starting transfers between devices  87.4 us (15%)
  other arithmetic  76.6 us (13%)
  blocking collectives  37.9 us (7%)
  between operations  21.6 us (4%)
    ppermute x33, waiting for transfers between devices, flip(): return lax.ppermute(rows, axes, [(i, i ^ bits) for i in range(size)])  91.2 us
    dot_general x37, matrix products, dot(): lax.dot_general(left, right, (((left_dim,), (right_dim,)), ((), ())), pre...  73 us
    all_gather x1, waiting for transfers between devices, local(): level = lax.all_gather(first, PLANE)  49.5 us
    ppermute x33, starting transfers between devices, flip(): return lax.ppermute(rows, axes, [(i, i ^ bits) for i in range(size)])  34.1 us
    all_gather x2, blocking collectives, spread_plane(): return widen(lax.all_gather(rows, PLANE).reshape(-1, D))  22.1 us
    all_to_all x3, starting transfers between devices, exchange(): lax.all_to_all(blocks, ALL, split_axis=0, concat_axis=0, tiled=True)  20 us
    all_gather x1, blocking collectives, local(): across = lax.all_gather(widen(hidden), 'q')  15.8 us
    unnamed x206, local copies, waits for them, and re-layouts  15.6 us
  transfers between devices with their start and end apart: 50, of which 27 were waited for; matrix products, arithmetic and copies ran while one was open for 33% of the time, Pallas kernels for 0%

profile of v11, /device:TPU:24, one launch (start us, length us, event | category | flops | bytes accessed | tf_op | source)
XLA Modules:
  0.0 560.8 jit_solution(8898759447045065091)
XLA Ops:
  8.5 3.7 collective-permute-start
  20.4 3.7 convert_element_type.330
  24.7 6.4 %all-to-all-start = ((s32[32,1,96]{2,1,0:T(1,128)}), s32[32,1,96]{2,1,0:T(1,128)S(1)}, u32[]{:S(2)}, u32[]{:S(2)}) async-start(s32[32,1,96]{2,1,0:T(1,128)} %bitcast), calls=%async_computation | async-start | bytes 32768 | tf_op jit(solution)/shard_map/all_to_all | solution.py:218
  35.6 4.3 all-to-all-done
  39.9 3.5 all-to-all-start.1
  43.6 5.2 fusion.24
  48.8 3.9 copy.190
  54.6 8.4 %all-to-all-start.2 = ((bf16[32,32,960]{2,1,0:T(8,128)(2,1)}), bf16[32,32,960]{2,1,0:T(8,128)(2,1)}, u32[]{:S(2)}, u32[]{:S(2)}) async-start(bf16[32,32,960]{2,1,0:T(8,128)(2,1)} %bitcast.248), calls=%async_computation.2 | async-start | bytes 4194304 | tf_op jit(solution)/shard_map/all_to_all | solution.py:194
  67.6 49.5 %all-gather.8.cloned.1.call-done = bf16[2624,960]{1,0:T(8,128)(2,1)} async-done(((bf16[328,960]{1,0:T(8,128)(2,1)}), bf16[2624,960]{1,0:T(8,128)(2,1)}) %all-gather.8.cloned.1.call-update) | async-done | bytes 5038096 | tf_op jit(solution)/shard_map/all_gather | solution.py:226
  120.3 3.0 slice.408
  123.3 2.8 reshape.612
  126.8 3.0 fusion.23
  130.5 2.4 fusion.166
  144.5 2.3 copy.230
  148.4 3.7 fusion.200
  152.1 3.6 convolution_convert_fusion.10
  160.4 11.1 %all-gather.2 = bf16[512,960]{1,0:T(8,128)(2,1)S(1)} all-gather(bf16[64,960]{1,0:T(8,128)(2,1)S(1)} %multiply_convert_fusion.7), channel_id=4, replica_groups=mesh['q'=4,'y'=2,'x'=2,'c'=2] {'y','x','c'}, dimensions={0}, use_global_device_ids=true | all-gather | bytes 1105920 | tf_op jit(solution)/shard_map/all_gather | solution.py:149
  172.6 8.1 %all-gather.10.cloned.1.call-done = bf16[1920,640]{1,0:T(8,128)(2,1)} async-done(((bf16[480,640]{1,0:T(8,128)(2,1)}), bf16[1920,640]{1,0:T(8,128)(2,1)}) %all-gather.10.cloned.1.call-update) | async-done | bytes 2457616 | tf_op jit(solution)/shard_map/all_gather | solution.py:234
  187.4 2.2 collective-permute-done.3
  193.1 2.4 collective-permute-start.6
  197.5 2.6 collective-permute-done.6
  200.1 2.4 collective-permute-done.5
  204.7 15.8 %all-gather.3 = bf16[256,1024]{1,0:T(8,128)(2,1)S(1)} all-gather(bf16[64,1024]{1,0:T(8,128)(2,1)S(1)} %pad.31), channel_id=5, replica_groups=mesh['q'=4,'y'=2,'x'=2,'c'=2] {'q'}, dimensions={0}, use_global_device_ids=true | all-gather | bytes 655360 | tf_op jit(solution)/shard_map/all_gather | solution.py:303
  222.2 10.3 %collective-permute-done.7 = bf16[4,64,1024]{2,1,0:T(8,128)(2,1)S(1)} collective-permute-done((bf16[4,64,1024]{2,1,0:T(8,128)(2,1)S(1)}, bf16[4,64,1024]{2,1,0:T(8,128)(2,1)S(1)}, u32[]{:S(2)}, u32[]{:S(2)}) %collective-permute-start.7) | collective-permute-done | bytes 524320 | tf_op jit(solution)/shard_map/ppermute | solution.py:74
  237.1 2.3 collective-permute-done.9
  243.0 4.5 fusion.202
  250.6 3.9 fusion.201
  258.1 3.5 collective-permute-done.13
  262.4 3.3 collective-permute-done.14
  269.9 2.2 collective-permute-start.16
  272.1 2.7 collective-permute-done.16
  275.5 5.2 convolution_convert_fusion
  280.9 5.6 %fusion.169 = f32[1000,1024]{0,1:T(8,128)S(1)} fusion(bf16[1024,1024]{1,0:T(8,128)(2,1)} %bitcast.37, f32[1024,1000]{0,1:T(8,128)} %copy-done.21, f32[1024]{0:T(1024)S(1)} %get-tuple-element.216, f32[1024]{0:T(1024)S(1)} %get-tuple-element.213, s32[1024]{0:T(1024)S(1)} %copy-done.84), kind=kOutput, calls=%fused_computation.425 | convolution fusion | flops 2105344000 | bytes 10301440 | tf_op jit(solution)/shard_map/dot_general | solution.py:52
  286.5 4.8 fusion.203
  295.1 4.3 fusion.170
  299.4 7.9 %collective-permute-done.20 = bf16[4,64,1024]{2,1,0:T(8,128)(2,1)S(1)} collective-permute-done((bf16[4,64,1024]{2,1,0:T(8,128)(2,1)S(1)}, bf16[4,64,1024]{2,1,0:T(8,128)(2,1)S(1)}, u32[]{:S(2)}, u32[]{:S(2)}) %collective-permute-start.20) | collective-permute-done | bytes 524320 | tf_op jit(solution)/shard_map/ppermute | solution.py:74
  307.3 10.7 %collective-permute-done.19 = bf16[4,64,1024]{2,1,0:T(8,128)(2,1)S(1)} collective-permute-done((bf16[4,64,1024]{2,1,0:T(8,128)(2,1)S(1)}, bf16[4,64,1024]{2,1,0:T(8,128)(2,1)S(1)}, u32[]{:S(2)}, u32[]{:S(2)}) %collective-permute-start.19) | collective-permute-done | bytes 524320 | tf_op jit(solution)/shard_map/ppermute | solution.py:74
  318.4 3.0 collective-permute-start.23
  322.8 2.9 slice_add_fusion
  326.7 5.9 %collective-permute-done.22 = bf16[64,1024]{1,0:T(8,128)(2,1)S(1)} collective-permute-done((bf16[64,1024]{1,0:T(8,128)(2,1)S(1)}, bf16[64,1024]{1,0:T(8,128)(2,1)S(1)}, u32[]{:S(2)}, u32[]{:S(2)}) %collective-permute-start.22) | collective-permute-done | bytes 131104 | tf_op jit(solution)/shard_map/ppermute | solution.py:74
  333.5 11.0 %all-gather.4 = bf16[512,960]{1,0:T(8,128)(2,1)S(1)} all-gather(bf16[64,960]{1,0:T(8,128)(2,1)S(1)} %fusion.164), channel_id=6, replica_groups=mesh['q'=4,'y'=2,'x'=2,'c'=2] {'y','x','c'}, dimensions={0}, use_global_device_ids=true | all-gather | bytes 1105920 | tf_op jit(solution)/shard_map/all_gather | solution.py:149
  376.5 3.3 convolution_convert_fusion.9
  385.1 3.0 fusion.14
  392.9 2.2 convolution_convert_fusion.3
  395.1 2.7 copy.214
  397.9 4.9 all-to-all-start.3
  408.7 3.2 reshape.642
  412.7 6.3 %fusion.2 = bf16[8,352,960]{2,1,0:T(8,128)(2,1)} fusion(bf16[1,3,960]{2,1,0:T(4,128)(2,1)S(1)} %copy-done.74, bf16[3,320,960]{2,1,0:T(8,128)(2,1)S(1)} %bitcast.249, bf16[5,128,960]{2,1,0:T(8,128)(2,1)S(1)} %reshape.642, bf16[5,192,960]{2,1,0:T(8,128)(2,1)S(1)} %bitcast.250), kind=kLoop, calls=%fused_computation.7 | loop fusion | flops 27033600 | bytes 10327680 | tf_op jit(solution)/shard_map/concatenate | solution.py:421
  419.0 5.9 %constant_dynamic-slice_fusion.4 = (bf16[4,1,352,960]{3,2,1,0:T(8,128)(2,1)}, bf16[4,352,960]{2,1,0:T(8,128)(2,1)}) fusion(bf16[4,2,352,960]{3,2,1,0:T(8,128)(2,1)} %bitcast.239, s32[]{:T(128)S(6)} %select_n.259, s32[]{:T(128)S(6)} %select_n.260), kind=kLoop, calls=%fused_computation.290 | loop fusion | bytes 10813448 | tf_op jit(solution)/shard_map/jit(dynamic_index_in_dim)/dynamic_slice | solution.py:423
  424.8 6.6 %all-to-all-start.4 = ((bf16[32,24,960]{2,1,0:T(8,128)(2,1)}), bf16[32,24,960]{2,1,0:T(8,128)(2,1)}, u32[]{:S(2)}, u32[]{:S(2)}) async-start(bf16[32,24,960]{2,1,0:T(8,128)(2,1)} %bitcast.93), calls=%async_computation.5 | async-start | bytes 3145728 | tf_op jit(solution)/shard_map/all_to_all | solution.py:194
  433.6 2.6 fusion.187
  443.3 23.2 %collective-permute-done.31 = bf16[2,176,960]{2,1,0:T(8,128)(2,1)} collective-permute-done((bf16[2,176,960]{2,1,0:T(8,128)(2,1)}, bf16[2,176,960]{2,1,0:T(8,128)(2,1)}, u32[]{:S(2)}, u32[]{:S(2)}) %collective-permute-start.31) | collective-permute-done | bytes 675872 | tf_op jit(solution)/shard_map/ppermute | solution.py:74
  471.3 3.8 fusion.50
  475.1 3.8 collective-permute-done.32
  479.0 2.4 collective-permute-done.30
  483.9 2.9 collective-permute-start.33
  487.8 3.5 all-to-all-start.5
  491.4 3.5 fusion.5
  495.1 4.0 multiply_reduce_fusion
  506.2 6.3 %all-to-all-start.6 = ((f32[32,1,2]{2,1,0:T(1,128)}), f32[32,1,2]{2,1,0:T(1,128)S(1)}, u32[]{:S(2)}, u32[]{:S(2)}) async-start(f32[32,1,2]{2,1,0:T(1,128)} %broadcast_in_dim.71), calls=%async_computation.7 | async-start | bytes 32768 | tf_op jit(solution)/shard_map/all_to_all | solution.py:411
  515.8 3.6 collective-permute-start.38
  522.4 10.2 %add_multiply_fusion = (f32[1000,960]{0,1:T(8,128)}, f32[1000,960]{0,1:T(8,128)}, f32[1000,960]{0,1:T(8,128)}) fusion(f32[1000,960]{0,1:T(8,128)} %param.20, f32[1000,960]{0,1:T(8,128)} %get-tuple-element.117, f32[]{:T(128)S(6)} %div.148, f32[1000,960]{0,1:T(8,128)} %param.22, f32[1000,960]{0,1:T(8,128)} %param.21), kind=kLoop, calls=%fused_computation.21 | loop fusion | flops 14400000 | bytes 26880004 | tf_op jit(solution)/shard_map/mul | solution.py:107
  542.9 4.1 collective-permute-done.39
  547.0 4.8 add_multiply_fusion.1
  (494 shorter events, 174.2 us)
Async XLA Ops:
  8.5 6.8 %collective-permute-start = (bf16[2880]{0:T(1024)(128)(2,1)S(1)}, bf16[2880]{0:T(1024)(128)(2,1)S(1)}, u32[]{:S(2)}, u32[]{:S(2)}) collective-permute-start(bf16[2880]{0:T(1024)(128)(2,1)S(1)} %slice.510), channel_id=1, source_target_pairs={{1,0},{2,1},{3,2},{4,3},{5,4},{6,5},{7,6},{8,7},{9,8},{10,9},{11,1... | collective-permute-start | bytes 17288 | tf_op jit(solution)/shard_map/ppermute | solution.py:204
  18.8 14.3 %collective-permute-start.1 = (bf16[328,960]{1,0:T(8,128)(2,1)S(1)}, bf16[328,960]{1,0:T(8,128)(2,1)}, u32[]{:S(2)}, u32[]{:S(2)}) collective-permute-start(bf16[328,960]{1,0:T(8,128)(2,1)S(1)} %maximum_maximum_fusion), channel_id=1, source_target_pairs={{0,16},{1,17},{2,18},{3,19},{4,20},{5,21},{6,22},{7,23}} | collective-permute-start | bytes 1889288 | tf_op jit(solution)/shard_map/ppermute | solution.py:220
  24.7 15.2 %all-to-all-start = ((s32[32,1,96]{2,1,0:T(1,128)}), s32[32,1,96]{2,1,0:T(1,128)S(1)}, u32[]{:S(2)}, u32[]{:S(2)}) async-start(s32[32,1,96]{2,1,0:T(1,128)} %bitcast), calls=%async_computation | async-start | bytes 32768 | tf_op jit(solution)/shard_map/all_to_all | solution.py:218
  34.3 19.2 %collective-permute-start.2 = (bf16[328,960]{1,0:T(8,128)(2,1)S(1)}, bf16[328,960]{1,0:T(8,128)(2,1)S(1)}, u32[]{:S(2)}, u32[]{:S(2)}) collective-permute-start(bf16[328,960]{1,0:T(8,128)(2,1)S(1)} %broadcast_select_fusion), channel_id=1, source_target_pairs={{0,8},{16,24},{1,9},{17,25},{2,10},{18,26},{3,11},{19,27},{4,12},{... | collective-permute-start | bytes 1889288 | tf_op jit(solution)/shard_map/ppermute | solution.py:222
  39.9 14.6 %all-to-all-start.1 = ((bf16[8,60,640]{2,1,0:T(8,128)(2,1)}), bf16[8,60,640]{2,1,0:T(8,128)(2,1)S(1)}, u32[]{:S(2)}, u32[]{:S(2)}) async-start(bf16[8,60,640]{2,1,0:T(8,128)(2,1)} %reshape.700), calls=%async_computation.1 | async-start | bytes 1310720 | tf_op jit(solution)/shard_map/all_to_all | solution.py:212
  43.5 73.6 %all-gather.8.cloned.1.call-start = ((), (), s32[]{:S(2)}) async-start(), calls=%async_computation.9 | async-start | bytes 6045696 | tf_op jit(solution)/shard_map/all_gather | solution.py:226
  54.6 72.2 %all-to-all-start.2 = ((bf16[32,32,960]{2,1,0:T(8,128)(2,1)}), bf16[32,32,960]{2,1,0:T(8,128)(2,1)}, u32[]{:S(2)}, u32[]{:S(2)}) async-start(bf16[32,32,960]{2,1,0:T(8,128)(2,1)} %bitcast.248), calls=%async_computation.2 | async-start | bytes 4194304 | tf_op jit(solution)/shard_map/all_to_all | solution.py:194
  63.0 117.7 %all-gather.10.cloned.1.call-start = ((), (), s32[]{:S(2)}) async-start(), calls=%async_computation.10 | async-start | bytes 3072000 | tf_op jit(solution)/shard_map/all_gather | solution.py:234
  64.0 74.7 %copy-start.55 = (f32[64,64]{1,0:T(8,128)}, f32[64,64]{1,0:T(8,128)S(1)}, u32[]{:S(2)}) copy-start(f32[64,64]{1,0:T(8,128)S(1)} %gather_fusion.1) | copy-start | bytes 49156
  129.7 27.3 %copy-start.3 = (bf16[512,960]{0,1:T(8,128)(2,1)}, bf16[512,960]{0,1:T(8,128)(2,1)S(1)}, u32[]{:S(2)}) copy-start(bf16[512,960]{0,1:T(8,128)(2,1)S(1)} %get-tuple-element.228) | copy-start | bytes 2949124
  130.4 274.3 %reduce-scatter.2.cloned.1.call-start = ((), (), s32[]{:S(2)}) async-start(), calls=%async_computation.8 | async-start | bytes 3072000 | tf_op jit(solution)/shard_map/reduce_scatter | solution.py:401
  159.7 22.5 %copy-start.92 = (f32[64]{0:T(128)}, f32[64]{0:T(128)S(1)}, u32[]{:S(2)}) copy-start(f32[64]{0:T(128)S(1)} %add_rsqrt_fusion.2) | copy-start | bytes 772
  187.3 2.3 collective-permute-start.3
  193.1 7.1 %collective-permute-start.6 = (bf16[64,1024]{1,0:T(8,128)(2,1)}, bf16[64,1024]{1,0:T(8,128)(2,1)S(1)}, u32[]{:S(2)}, u32[]{:S(2)}) collective-permute-start(bf16[64,1024]{1,0:T(8,128)(2,1)} %get-tuple-element.174), channel_id=1, source_target_pairs={{0,6},{2,4},{4,2},{6,0},{1,7},{3,5},{5,3},{7,1},{8,14},{10,12},{12... | collective-permute-start | bytes 393224 | tf_op jit(solution)/shard_map/ppermute | solution.py:74
  195.5 7.0 %collective-permute-start.5 = (bf16[64,1024]{1,0:T(8,128)(2,1)}, bf16[64,1024]{1,0:T(8,128)(2,1)S(1)}, u32[]{:S(2)}, u32[]{:S(2)}) collective-permute-start(bf16[64,1024]{1,0:T(8,128)(2,1)} %get-tuple-element.175), channel_id=1, source_target_pairs={{0,4},{2,6},{4,0},{6,2},{1,5},{3,7},{5,1},{7,3},{8,12},{10,14},{12... | collective-permute-start | bytes 393224 | tf_op jit(solution)/shard_map/ppermute | solution.py:74
  196.1 7.2 %collective-permute-start.4 = (bf16[64,1024]{1,0:T(8,128)(2,1)}, bf16[64,1024]{1,0:T(8,128)(2,1)}, u32[]{:S(2)}, u32[]{:S(2)}) collective-permute-start(bf16[64,1024]{1,0:T(8,128)(2,1)} %get-tuple-element.173), channel_id=1, source_target_pairs={{0,2},{2,0},{4,6},{6,4},{1,3},{3,1},{5,7},{7,5},{8,10},{10,8},{12,... | collective-permute-start | bytes 393224 | tf_op jit(solution)/shard_map/ppermute | solution.py:74
  204.5 31.7 %copy-start.90 = (f32[64]{0:T(128)}, f32[64]{0:T(128)S(1)}, u32[]{:S(2)}) copy-start(f32[64]{0:T(128)S(1)} %add_rsqrt_fusion.1) | copy-start | bytes 772
  220.5 12.1 %collective-permute-start.7 = (bf16[4,64,1024]{2,1,0:T(8,128)(2,1)S(1)}, bf16[4,64,1024]{2,1,0:T(8,128)(2,1)S(1)}, u32[]{:S(2)}, u32[]{:S(2)}) collective-permute-start(bf16[4,64,1024]{2,1,0:T(8,128)(2,1)S(1)} %bitcast.275), channel_id=1, source_target_pairs={{0,2},{2,0},{1,3},{3,1},{4,6},{6,4},{5,7},{7,5},{8,10},{10,8},{9,1... | collective-permute-start | bytes 1572872 | tf_op jit(solution)/shard_map/ppermute | solution.py:74
  222.1 12.8 %collective-permute-start.8 = (bf16[4,64,1024]{2,1,0:T(8,128)(2,1)S(1)}, bf16[4,64,1024]{2,1,0:T(8,128)(2,1)S(1)}, u32[]{:S(2)}, u32[]{:S(2)}) collective-permute-start(bf16[4,64,1024]{2,1,0:T(8,128)(2,1)S(1)} %bitcast.276), channel_id=1, source_target_pairs={{0,4},{4,0},{1,5},{5,1},{2,6},{6,2},{3,7},{7,3},{8,12},{12,8},{9,1... | collective-permute-start | bytes 1572872 | tf_op jit(solution)/shard_map/ppermute | solution.py:74
  232.6 6.8 %collective-permute-start.9 = (bf16[2,64,1024]{2,1,0:T(8,128)(2,1)S(1)}, bf16[2,64,1024]{2,1,0:T(8,128)(2,1)S(1)}, u32[]{:S(2)}, u32[]{:S(2)}) collective-permute-start(bf16[2,64,1024]{2,1,0:T(8,128)(2,1)S(1)} %slice.536), channel_id=1, source_target_pairs={{0,4},{4,0},{1,5},{5,1},{2,6},{6,2},{3,7},{7,3},{8,12},{12,8},{9,1... | collective-permute-start | bytes 786440 | tf_op jit(solution)/shard_map/ppermute | solution.py:74
  234.9 6.4 %collective-permute-start.10 = (bf16[2,64,1024]{2,1,0:T(8,128)(2,1)S(1)}, bf16[2,64,1024]{2,1,0:T(8,128)(2,1)S(1)}, u32[]{:S(2)}, u32[]{:S(2)}) collective-permute-start(bf16[2,64,1024]{2,1,0:T(8,128)(2,1)S(1)} %slice.537), channel_id=1, source_target_pairs={{0,2},{2,0},{1,3},{3,1},{4,6},{6,4},{5,7},{7,5},{8,10},{10,8},{9,1... | collective-permute-start | bytes 786440 | tf_op jit(solution)/shard_map/ppermute | solution.py:74
  242.1 7.5 %collective-permute-start.11 = (bf16[1024,1024]{1,0:T(8,128)(2,1)}, bf16[1024,1024]{1,0:T(8,128)(2,1)}, u32[]{:S(2)}, u32[]{:S(2)}) collective-permute-start(bf16[1024,1024]{1,0:T(8,128)(2,1)} %bitcast.37), channel_id=1, source_target_pairs={{0,1},{1,0},{2,3},{3,2},{4,5},{5,4},{6,7},{7,6},{8,9},{9,8},{10,11... | collective-permute-start | bytes 6291464 | tf_op jit(solution)/shard_map/ppermute | solution.py:74
  242.9 11.6 %copy-start.81 = (s32[1024]{0:T(1024)}, s32[1024]{0:T(1024)S(1)}, u32[]{:S(2)}) copy-start(s32[1024]{0:T(1024)S(1)} %sub.293) | copy-start | bytes 12292
  254.5 21.0 %copy-start.19 = (f32[1024,1000]{0,1:T(8,128)}, f32[1024,1000]{0,1:T(8,128)S(1)}, u32[]{:S(2)}) copy-start(f32[1024,1000]{0,1:T(8,128)S(1)} %get-tuple-element.234) | copy-start | bytes 12288004
  256.0 1.4 collective-permute-start.12
  257.6 4.0 collective-permute-start.13
  261.7 4.0 collective-permute-start.14
  265.8 4.0 collective-permute-start.15
  269.9 10.8 %copy-start.71 = (f32[1,2048]{1,0:T(1,128)}, f32[1,2048]{1,0:T(1,128)S(1)}, u32[]{:S(2)}) copy-start(f32[1,2048]{1,0:T(1,128)S(1)} %get-tuple-element.196) | copy-start | bytes 24580
  269.9 4.9 collective-permute-start.16
  280.7 5.8 %collective-permute-start.17 = (bf16[1024,1024]{1,0:T(8,128)(2,1)}, bf16[1024,1024]{1,0:T(8,128)(2,1)}, u32[]{:S(2)}, u32[]{:S(2)}) collective-permute-start(bf16[1024,1024]{1,0:T(8,128)(2,1)} %convolution_convert_fusion), channel_id=1, source_target_pairs={{0,1},{1,0},{2,3},{3,2},{4,5},{5,4},{6,7},{7,6},{8,9},{9,8},{10,11... | collective-permute-start | bytes 6291464 | tf_op jit(solution)/shard_map/ppermute | solution.py:74
  291.5 15.8 %collective-permute-start.20 = (bf16[4,64,1024]{2,1,0:T(8,128)(2,1)S(1)}, bf16[4,64,1024]{2,1,0:T(8,128)(2,1)S(1)}, u32[]{:S(2)}, u32[]{:S(2)}) collective-permute-start(bf16[4,64,1024]{2,1,0:T(8,128)(2,1)S(1)} %bitcast.301), channel_id=1, source_target_pairs={{0,6},{2,4},{4,2},{6,0},{1,7},{3,5},{5,3},{7,1},{8,14},{10,12},{12... | collective-permute-start | bytes 1572872 | tf_op jit(solution)/shard_map/ppermute | solution.py:74
  293.1 24.9 %collective-permute-start.19 = (bf16[4,64,1024]{2,1,0:T(8,128)(2,1)S(1)}, bf16[4,64,1024]{2,1,0:T(8,128)(2,1)S(1)}, u32[]{:S(2)}, u32[]{:S(2)}) collective-permute-start(bf16[4,64,1024]{2,1,0:T(8,128)(2,1)S(1)} %bitcast.300), channel_id=1, source_target_pairs={{0,4},{2,6},{4,0},{6,2},{1,5},{3,7},{5,1},{7,3},{8,12},{10,14},{12... | collective-permute-start | bytes 1572872 | tf_op jit(solution)/shard_map/ppermute | solution.py:74
  293.5 24.5 %collective-permute-start.18 = (bf16[4,64,1024]{2,1,0:T(8,128)(2,1)S(1)}, bf16[4,64,1024]{2,1,0:T(8,128)(2,1)S(1)}, u32[]{:S(2)}, u32[]{:S(2)}) collective-permute-start(bf16[4,64,1024]{2,1,0:T(8,128)(2,1)S(1)} %bitcast.299), channel_id=1, source_target_pairs={{0,2},{2,0},{4,6},{6,4},{1,3},{3,1},{5,7},{7,5},{8,10},{10,8},{12,... | collective-permute-start | bytes 1572872 | tf_op jit(solution)/shard_map/ppermute | solution.py:74
  318.4 8.4 %collective-permute-start.23 = (bf16[64,1024]{1,0:T(8,128)(2,1)S(1)}, bf16[64,1024]{1,0:T(8,128)(2,1)S(1)}, u32[]{:S(2)}, u32[]{:S(2)}) collective-permute-start(bf16[64,1024]{1,0:T(8,128)(2,1)S(1)} %get-tuple-element.171), channel_id=1, source_target_pairs={{0,24},{8,16},{16,8},{24,0},{1,25},{9,17},{17,9},{25,1},{2,26},{10... | collective-permute-start | bytes 393224 | tf_op jit(solution)/shard_map/ppermute | solution.py:74
  321.4 11.2 %collective-permute-start.22 = (bf16[64,1024]{1,0:T(8,128)(2,1)S(1)}, bf16[64,1024]{1,0:T(8,128)(2,1)S(1)}, u32[]{:S(2)}, u32[]{:S(2)}) collective-permute-start(bf16[64,1024]{1,0:T(8,128)(2,1)S(1)} %get-tuple-element.172), channel_id=1, source_target_pairs={{0,16},{8,24},{16,0},{24,8},{1,17},{9,25},{17,1},{25,9},{2,18},{10... | collective-permute-start | bytes 393224 | tf_op jit(solution)/shard_map/ppermute | solution.py:74
  321.4 11.3 %copy-start.91 = (f32[64]{0:T(128)S(1)}, f32[64]{0:T(128)}, u32[]{:S(2)}) copy-start(f32[64]{0:T(128)} %copy-done.90) | copy-start | bytes 772
  321.4 11.2 %collective-permute-start.21 = (bf16[64,1024]{1,0:T(8,128)(2,1)S(1)}, bf16[64,1024]{1,0:T(8,128)(2,1)S(1)}, u32[]{:S(2)}, u32[]{:S(2)}) collective-permute-start(bf16[64,1024]{1,0:T(8,128)(2,1)S(1)} %get-tuple-element.170), channel_id=1, source_target_pairs={{0,8},{8,0},{16,24},{24,16},{1,9},{9,1},{17,25},{25,17},{2,10},{10... | collective-permute-start | bytes 393224 | tf_op jit(solution)/shard_map/ppermute | solution.py:74
  325.7 18.9 %copy-start.37 = (f32[512,640]{1,0:T(8,128)S(1)}, f32[512,640]{1,0:T(8,128)}, u32[]{:S(2)}) copy-start(f32[512,640]{1,0:T(8,128)} %copy-done.36) | copy-start | bytes 3932164
  325.7 18.9 %copy-start.53 = (bf16[320,640]{1,0:T(8,128)(2,1)S(1)}, bf16[320,640]{1,0:T(8,128)(2,1)}, u32[]{:S(2)}) copy-start(bf16[320,640]{1,0:T(8,128)(2,1)} %copy-done.52) | copy-start | bytes 1228804
  325.7 18.9 %copy-start.66 = (bf16[160,320]{1,0:T(8,128)(2,1)S(1)}, bf16[160,320]{1,0:T(8,128)(2,1)}, u32[]{:S(2)}) copy-start(bf16[160,320]{1,0:T(8,128)(2,1)} %copy-done.65) | copy-start | bytes 307204
  325.7 18.9 %copy-start.68 = (bf16[160,320]{1,0:T(8,128)(2,1)S(1)}, bf16[160,320]{1,0:T(8,128)(2,1)}, u32[]{:S(2)}) copy-start(bf16[160,320]{1,0:T(8,128)(2,1)} %copy-done.67) | copy-start | bytes 307204
  347.0 2.6 collective-permute-start.24
  351.3 7.5 %collective-permute-start.27 = (bf16[64,1024]{1,0:T(8,128)(2,1)S(1)}, bf16[64,1024]{1,0:T(8,128)(2,1)}, u32[]{:S(2)}, u32[]{:S(2)}) collective-permute-start(bf16[64,1024]{1,0:T(8,128)(2,1)S(1)} %get-tuple-element.168), channel_id=1, source_target_pairs={{0,6},{2,4},{4,2},{6,0},{1,7},{3,5},{5,3},{7,1},{8,14},{10,12},{12... | collective-permute-start | bytes 393224 | tf_op jit(solution)/shard_map/ppermute | solution.py:74
  352.8 8.0 %collective-permute-start.26 = (bf16[64,1024]{1,0:T(8,128)(2,1)S(1)}, bf16[64,1024]{1,0:T(8,128)(2,1)}, u32[]{:S(2)}, u32[]{:S(2)}) collective-permute-start(bf16[64,1024]{1,0:T(8,128)(2,1)S(1)} %get-tuple-element.169), channel_id=1, source_target_pairs={{0,4},{2,6},{4,0},{6,2},{1,5},{3,7},{5,1},{7,3},{8,12},{10,14},{12... | collective-permute-start | bytes 393224 | tf_op jit(solution)/shard_map/ppermute | solution.py:74
  353.6 7.2 %collective-permute-start.25 = (bf16[64,1024]{1,0:T(8,128)(2,1)S(1)}, bf16[64,1024]{1,0:T(8,128)(2,1)}, u32[]{:S(2)}, u32[]{:S(2)}) collective-permute-start(bf16[64,1024]{1,0:T(8,128)(2,1)S(1)} %get-tuple-element.167), channel_id=1, source_target_pairs={{0,2},{2,0},{4,6},{6,4},{1,3},{3,1},{5,7},{7,5},{8,10},{10,8},{12,... | collective-permute-start | bytes 393224 | tf_op jit(solution)/shard_map/ppermute | solution.py:74
  397.9 21.1 %all-to-all-start.3 = ((bf16[32,8,960]{2,1,0:T(8,128)(2,1)}), bf16[32,8,960]{2,1,0:T(8,128)(2,1)}, u32[]{:S(2)}, u32[]{:S(2)}) async-start(bf16[32,8,960]{2,1,0:T(8,128)(2,1)} %bitcast.92), calls=%async_computation.4 | async-start | bytes 1048576 | tf_op jit(solution)/shard_map/all_to_all | solution.py:194
  424.8 8.7 %collective-permute-start.28 = (bf16[4,352,960]{2,1,0:T(8,128)(2,1)}, bf16[4,352,960]{2,1,0:T(8,128)(2,1)}, u32[]{:S(2)}, u32[]{:S(2)}) collective-permute-start(bf16[4,352,960]{2,1,0:T(8,128)(2,1)} %get-tuple-element.138), channel_id=1, source_target_pairs={{0,1},{1,0},{2,3},{3,2},{4,5},{5,4},{6,7},{7,6},{8,9},{9,8},{10,11... | collective-permute-start | bytes 8110088 | tf_op jit(solution)/shard_map/ppermute | solution.py:74
  424.8 56.8 %all-to-all-start.4 = ((bf16[32,24,960]{2,1,0:T(8,128)(2,1)}), bf16[32,24,960]{2,1,0:T(8,128)(2,1)}, u32[]{:S(2)}, u32[]{:S(2)}) async-start(bf16[32,24,960]{2,1,0:T(8,128)(2,1)} %bitcast.93), calls=%async_computation.5 | async-start | bytes 3145728 | tf_op jit(solution)/shard_map/all_to_all | solution.py:194
  437.5 28.9 %collective-permute-start.31 = (bf16[2,176,960]{2,1,0:T(8,128)(2,1)}, bf16[2,176,960]{2,1,0:T(8,128)(2,1)}, u32[]{:S(2)}, u32[]{:S(2)}) collective-permute-start(bf16[2,176,960]{2,1,0:T(8,128)(2,1)} %fusion.59), channel_id=1, source_target_pairs={{0,4},{4,0},{1,5},{5,1},{2,6},{6,2},{3,7},{7,3},{8,12},{12,8},{9,1... | collective-permute-start | bytes 2027528 | tf_op jit(solution)/shard_map/ppermute | solution.py:74
  440.2 29.5 %collective-permute-start.29 = (bf16[2,176,960]{2,1,0:T(8,128)(2,1)}, bf16[2,176,960]{2,1,0:T(8,128)(2,1)}, u32[]{:S(2)}, u32[]{:S(2)}) collective-permute-start(bf16[2,176,960]{2,1,0:T(8,128)(2,1)} %fusion.58), channel_id=1, source_target_pairs={{0,2},{2,0},{1,3},{3,1},{4,6},{6,4},{5,7},{7,5},{8,10},{10,8},{9,1... | collective-permute-start | bytes 2027528 | tf_op jit(solution)/shard_map/ppermute | solution.py:74
  468.4 10.4 %collective-permute-start.32 = (bf16[176,960]{1,0:T(8,128)(2,1)S(1)}, bf16[176,960]{1,0:T(8,128)(2,1)S(1)}, u32[]{:S(2)}, u32[]{:S(2)}) collective-permute-start(bf16[176,960]{1,0:T(8,128)(2,1)S(1)} %fusion.76), channel_id=1, source_target_pairs={{0,2},{2,0},{1,3},{3,1},{4,6},{6,4},{5,7},{7,5},{8,10},{10,8},{9,1... | collective-permute-start | bytes 1013768 | tf_op jit(solution)/shard_map/ppermute | solution.py:74
  471.2 10.2 %collective-permute-start.30 = (bf16[176,960]{1,0:T(8,128)(2,1)S(1)}, bf16[176,960]{1,0:T(8,128)(2,1)S(1)}, u32[]{:S(2)}, u32[]{:S(2)}) collective-permute-start(bf16[176,960]{1,0:T(8,128)(2,1)S(1)} %fusion.75), channel_id=1, source_target_pairs={{0,4},{4,0},{1,5},{5,1},{2,6},{6,2},{3,7},{7,3},{8,12},{12,8},{9,1... | collective-permute-start | bytes 1013768 | tf_op jit(solution)/shard_map/ppermute | solution.py:74
  482.5 18.7 %collective-permute-start.35 = (bf16[88,960]{1,0:T(8,128)(2,1)}, bf16[88,960]{1,0:T(8,128)(2,1)}, u32[]{:S(2)}, u32[]{:S(2)}) collective-permute-start(bf16[88,960]{1,0:T(8,128)(2,1)} %get-tuple-element.149), channel_id=1, source_target_pairs={{0,24},{8,16},{16,8},{24,0},{1,25},{9,17},{17,9},{25,1},{2,26},{10... | collective-permute-start | bytes 506888 | tf_op jit(solution)/shard_map/ppermute | solution.py:74
  482.5 18.7 %collective-permute-start.34 = (bf16[88,960]{1,0:T(8,128)(2,1)}, bf16[88,960]{1,0:T(8,128)(2,1)}, u32[]{:S(2)}, u32[]{:S(2)}) collective-permute-start(bf16[88,960]{1,0:T(8,128)(2,1)} %get-tuple-element.150), channel_id=1, source_target_pairs={{0,16},{8,24},{16,0},{24,8},{1,17},{9,25},{17,1},{25,9},{2,18},{10... | collective-permute-start | bytes 506888 | tf_op jit(solution)/shard_map/ppermute | solution.py:74
  483.9 17.3 %collective-permute-start.33 = (bf16[88,960]{1,0:T(8,128)(2,1)}, bf16[88,960]{1,0:T(8,128)(2,1)}, u32[]{:S(2)}, u32[]{:S(2)}) collective-permute-start(bf16[88,960]{1,0:T(8,128)(2,1)} %get-tuple-element.148), channel_id=1, source_target_pairs={{0,8},{8,0},{16,24},{24,16},{1,9},{9,1},{17,25},{25,17},{2,10},{10... | collective-permute-start | bytes 506888 | tf_op jit(solution)/shard_map/ppermute | solution.py:74
  487.8 17.1 %all-to-all-start.5 = ((bf16[8,60,640]{2,1,0:T(8,128)(2,1)}), bf16[8,60,640]{2,1,0:T(8,128)(2,1)S(1)}, u32[]{:S(2)}, u32[]{:S(2)}) async-start(bf16[8,60,640]{2,1,0:T(8,128)(2,1)} %reshape.650), calls=%async_computation.6 | async-start | bytes 1310720 | tf_op jit(solution)/shard_map/all_to_all | solution.py:442
  503.0 17.1 %copy-start.39 = (bf16[88,960]{1,0:T(8,128)(2,1)}, bf16[88,960]{1,0:T(8,128)(2,1)S(1)}, u32[]{:S(2)}) copy-start(bf16[88,960]{1,0:T(8,128)(2,1)S(1)} %get-tuple-element.91) | copy-start | bytes 506884
  506.2 14.8 %all-to-all-start.6 = ((f32[32,1,2]{2,1,0:T(1,128)}), f32[32,1,2]{2,1,0:T(1,128)S(1)}, u32[]{:S(2)}, u32[]{:S(2)}) async-start(f32[32,1,2]{2,1,0:T(1,128)} %broadcast_in_dim.71), calls=%async_computation.7 | async-start | bytes 32768 | tf_op jit(solution)/shard_map/all_to_all | solution.py:411
  514.4 18.2 %collective-permute-start.36 = (bf16[88,960]{1,0:T(8,128)(2,1)S(1)}, bf16[88,960]{1,0:T(8,128)(2,1)S(1)}, u32[]{:S(2)}, u32[]{:S(2)}) collective-permute-start(bf16[88,960]{1,0:T(8,128)(2,1)S(1)} %get-tuple-element.91), channel_id=1, source_target_pairs={{8,0},{9,1},{10,2},{11,3},{12,4},{13,5},{14,6},{15,7}} | collective-permute-start | bytes 506888 | tf_op jit(solution)/shard_map/ppermute | solution.py:454
  515.1 17.5 %collective-permute-start.37 = (bf16[88,960]{1,0:T(8,128)(2,1)S(1)}, bf16[88,960]{1,0:T(8,128)(2,1)S(1)}, u32[]{:S(2)}, u32[]{:S(2)}) collective-permute-start(bf16[88,960]{1,0:T(8,128)(2,1)S(1)} %get-tuple-element.91), channel_id=1, source_target_pairs={{16,0},{17,1},{18,2},{19,3},{20,4},{21,5},{22,6},{23,7}} | collective-permute-start | bytes 506888 | tf_op jit(solution)/shard_map/ppermute | solution.py:454
  515.8 16.9 %collective-permute-start.38 = (bf16[88,960]{1,0:T(8,128)(2,1)S(1)}, bf16[88,960]{1,0:T(8,128)(2,1)S(1)}, u32[]{:S(2)}, u32[]{:S(2)}) collective-permute-start(bf16[88,960]{1,0:T(8,128)(2,1)S(1)} %get-tuple-element.91), channel_id=1, source_target_pairs={{24,0},{25,1},{26,2},{27,3},{28,4},{29,5},{30,6},{31,7}} | collective-permute-start | bytes 506888 | tf_op jit(solution)/shard_map/ppermute | solution.py:454
  522.4 11.3 %copy-start.40 = (bf16[88,960]{1,0:T(8,128)(2,1)S(1)}, bf16[88,960]{1,0:T(8,128)(2,1)}, u32[]{:S(2)}) copy-start(bf16[88,960]{1,0:T(8,128)(2,1)} %copy-done.39) | copy-start | bytes 506884
  540.2 6.7 %collective-permute-start.39 = (bf16[2880]{0:T(1024)(128)(2,1)S(1)}, bf16[2880]{0:T(1024)(128)(2,1)S(1)}, u32[]{:S(2)}, u32[]{:S(2)}) collective-permute-start(bf16[2880]{0:T(1024)(128)(2,1)S(1)} %slice.611), channel_id=1, source_target_pairs={{0,1},{1,2},{2,3},{3,4},{4,5},{5,6},{6,7},{7,8},{8,9},{9,10},{10,1... | collective-permute-start | bytes 17288 | tf_op jit(solution)/shard_map/ppermute | solution.py:477
  (84 other events, 295.6 us)
Sparse Core Ops, SparseCore 0:
  54.7 62.3 all-gather.7
  130.6 50.1 all-gather.9
  356.8 47.9 reduce-scatter.1

commit v12 on v11

--- a/solution.py
+++ b/solution.py
@@ -407,8 +407,9 @@
     grad_kv = dot(h_attn, d_kv, 0, 0).astype(bf16)
 
     def norm_of(squares):
-        sums = jnp.broadcast_to(jnp.stack([squares, my_loss])[None], (devices, 2))
-        sums = jnp.sum(lax.all_to_all(sums, ALL, split_axis=0, concat_axis=0, tiled=True), axis=0)
+        sums = jnp.stack([squares, my_loss])
+        for axis, bit, size in [("c", 1, 2), ("x", 1, 2), ("y", 1, 2)] + [("q", 1 << k, rows_q) for k in range(rows_q.bit_length() - 1)]:
+            sums = sums + flip(sums, axis, bit, size)
         grad_norm = jnp.sqrt(sums[0])
         limit = CLIP_C / math.sqrt(loss_total)
         return sums[1] / loss_total, grad_norm, limit / jnp.maximum(grad_norm, limit)
@@ -450,11 +451,7 @@
         table_squares = jnp.sum(table_grad * table_grad)
         quarter = quarter.astype(bf16)
         squares = jnp.sum(quarter.astype(f32) ** 2) + jnp.sum(share.astype(f32) ** 2) + table_squares
-        quarter, squares, got = lax.optimization_barrier((quarter, squares, got))
         quarters = [quarter] + [lax.ppermute(quarter, "q", [(k, 0)]) for k in (1, 2, 3)]
-        loss, grad_norm, clip_factor = norm_of(squares)
-        table_new = adamw_step(table_master, table_grad, table_m, table_v, clip_factor)
-        quarters, table_new = lax.optimization_barrier((quarters, table_new))
         first = jnp.concatenate(quarters)
         gain_out = first[SHARE : SHARE + 3].reshape(-1)
         both = jnp.concatenate([first[:TOP], first[TOP:SHARE].reshape(TOP, KV)], axis=1)
@@ -462,6 +459,8 @@
         by_share = got.reshape(8, 60, 2, UNIT).transpose(1, 2, 0, 3).reshape(-1)
         mine = jnp.where(q_index == 3, down_unpack(share).reshape(-1), by_share)
         mine = jnp.where(q_index == 0, first, mine)
+        loss, grad_norm, clip_factor = norm_of(squares)
+        mine, clip_factor = lax.optimization_barrier((mine, clip_factor))
     else:
         table_grad = head_grad
         for low, high, rows in zip(cuts_back, cuts_back[1:], arrived):
@@ -482,8 +481,8 @@
 
     if not aligned:
         loss, grad_norm, clip_factor = norm_of(jnp.sum(layer_grad * layer_grad) + table_squares)
-        table_new = adamw_step(table_master, table_grad, table_m, table_v, clip_factor)
     flat_new = adamw_step(flat_master, layer_grad, flat_m, flat_v, clip_factor)
+    table_new = adamw_step(table_master, table_grad, table_m, table_v, clip_factor)
     return (loss, grad_norm) + flat_new + table_new
 
 

time: 571 us -> 573 us (level)
  the two profiles are of different devices: /device:TPU:24 before, /device:TPU:1 now
where the time goes in v12:
time: 573 us; the launch traced here: 562 us
  waiting for transfers between devices  161 us (28%)
  starting transfers between devices  96.9 us (17%)
  matrix products  88.4 us (15%)
  local copies, waits for them, and re-layouts  86.3 us (15%)
  other arithmetic  72.6 us (13%)
  blocking collectives  35.9 us (6%)
  between operations  21.5 us (4%)
    ppermute x38, waiting for transfers between devices, flip(): return lax.ppermute(rows, axes, [(i, i ^ bits) for i in range(size)])  95.3 us
    dot_general x37, matrix products, dot(): lax.dot_general(left, right, (((left_dim,), (right_dim,)), ((), ())), pre...  73 us
    all_gather x1, waiting for transfers between devices, local(): level = lax.all_gather(first, PLANE)  50.7 us
    ppermute x38, starting transfers between devices, flip(): return lax.ppermute(rows, axes, [(i, i ^ bits) for i in range(size)])  42.1 us
    all_gather x2, blocking collectives, spread_plane(): return widen(lax.all_gather(rows, PLANE).reshape(-1, D))  22.4 us
    all_to_all x3, starting transfers between devices, exchange(): lax.all_to_all(blocks, ALL, split_axis=0, concat_axis=0, tiled=True)  17.6 us
    unnamed x206, local copies, waits for them, and re-layouts  15.1 us
    mul x2, other arithmetic, adamw_step(): return (new_one, new_two, -RATE * (ratio + DECAY * param))  13.5 us
  transfers between devices with their start and end apart: 54, of which 29 were waited for; matrix products, arithmetic and copies ran while one was open for 33% of the time, Pallas kernels for 0%

profile of v12, /device:TPU:1, one launch (start us, length us, event | category | flops | bytes accessed | tf_op | source)
XLA Modules:
  0.0 562.3 jit_solution(12853183217683830188)
XLA Ops:
  17.9 5.8 %collective-permute-start.1 = (bf16[328,960]{1,0:T(8,128)(2,1)S(1)}, bf16[328,960]{1,0:T(8,128)(2,1)}, u32[]{:S(2)}, u32[]{:S(2)}) collective-permute-start(bf16[328,960]{1,0:T(8,128)(2,1)S(1)} %maximum_maximum_fusion), channel_id=1, source_target_pairs={{0,16},{1,17},{2,18},{3,19},{4,20},{5,21},{6,22},{7,23}} | collective-permute-start | bytes 1889288 | tf_op jit(solution)/shard_map/ppermute | solution.py:220
  23.6 3.7 convert_element_type.330
  28.0 4.2 all-to-all-start
  39.1 5.6 all-to-all-start.1
  44.8 5.2 fusion.24
  50.0 3.9 copy.125
  54.8 9.4 %all-to-all-start.2 = ((bf16[32,32,960]{2,1,0:T(8,128)(2,1)}), bf16[32,32,960]{2,1,0:T(8,128)(2,1)}, u32[]{:S(2)}, u32[]{:S(2)}) async-start(bf16[32,32,960]{2,1,0:T(8,128)(2,1)} %bitcast.248), calls=%async_computation.2 | async-start | bytes 4194304 | tf_op jit(solution)/shard_map/all_to_all | solution.py:194
  68.8 50.7 %all-gather.8.cloned.1.call-done = bf16[2624,960]{1,0:T(8,128)(2,1)} async-done(((bf16[328,960]{1,0:T(8,128)(2,1)}), bf16[2624,960]{1,0:T(8,128)(2,1)}) %all-gather.8.cloned.1.call-update) | async-done | bytes 5038096 | tf_op jit(solution)/shard_map/all_gather | solution.py:226
  122.7 3.0 slice.408
  125.7 2.8 reshape.606
  129.2 3.0 fusion.23
  132.9 2.4 fusion.166
  146.9 2.3 copy.163
  150.7 3.7 fusion.200
  154.4 3.6 convolution_convert_fusion.10
  162.8 11.0 %all-gather.2 = bf16[512,960]{1,0:T(8,128)(2,1)S(1)} all-gather(bf16[64,960]{1,0:T(8,128)(2,1)S(1)} %multiply_convert_fusion.7), channel_id=4, replica_groups=mesh['q'=4,'y'=2,'x'=2,'c'=2] {'y','x','c'}, dimensions={0}, use_global_device_ids=true | all-gather | bytes 1105920 | tf_op jit(solution)/shard_map/all_gather | solution.py:149
  174.9 9.1 %all-gather.10.cloned.1.call-done = bf16[1920,640]{1,0:T(8,128)(2,1)} async-done(((bf16[480,640]{1,0:T(8,128)(2,1)}), bf16[1920,640]{1,0:T(8,128)(2,1)}) %all-gather.10.cloned.1.call-update) | async-done | bytes 2457616 | tf_op jit(solution)/shard_map/all_gather | solution.py:234
  200.4 2.2 collective-permute-done.6
  202.6 3.7 collective-permute-done.5
  208.3 13.4 %all-gather.3 = bf16[256,1024]{1,0:T(8,128)(2,1)S(1)} all-gather(bf16[64,1024]{1,0:T(8,128)(2,1)S(1)} %pad.31), channel_id=5, replica_groups=mesh['q'=4,'y'=2,'x'=2,'c'=2] {'q'}, dimensions={0}, use_global_device_ids=true | all-gather | bytes 655360 | tf_op jit(solution)/shard_map/all_gather | solution.py:303
  222.9 8.8 %collective-permute-done.7 = bf16[4,64,1024]{2,1,0:T(8,128)(2,1)S(1)} collective-permute-done((bf16[4,64,1024]{2,1,0:T(8,128)(2,1)S(1)}, bf16[4,64,1024]{2,1,0:T(8,128)(2,1)S(1)}, u32[]{:S(2)}, u32[]{:S(2)}) %collective-permute-start.7) | collective-permute-done | bytes 524320 | tf_op jit(solution)/shard_map/ppermute | solution.py:74
  235.3 4.0 collective-permute-done.9
  240.8 6.0 %collective-permute-start.11 = (bf16[1024,1024]{1,0:T(8,128)(2,1)}, bf16[1024,1024]{1,0:T(8,128)(2,1)}, u32[]{:S(2)}, u32[]{:S(2)}) collective-permute-start(bf16[1024,1024]{1,0:T(8,128)(2,1)} %bitcast.37), channel_id=1, source_target_pairs={{0,1},{1,0},{2,3},{3,2},{4,5},{5,4},{6,7},{7,6},{8,9},{9,8},{10,11... | collective-permute-start | bytes 6291464 | tf_op jit(solution)/shard_map/ppermute | solution.py:74
  247.6 4.5 fusion.202
  255.2 3.9 fusion.201
  262.1 2.8 collective-permute-done.13
  265.2 2.8 collective-permute-done.14
  268.1 2.8 collective-permute-done.15
  271.7 3.2 collective-permute-done.16
  275.6 5.2 convolution_convert_fusion
  280.7 4.7 collective-permute-start.17
  285.4 5.6 %fusion.169 = f32[1000,1024]{0,1:T(8,128)S(1)} fusion(bf16[1024,1024]{1,0:T(8,128)(2,1)} %bitcast.37, f32[1024,1000]{0,1:T(8,128)} %copy-done.21, f32[1024]{0:T(1024)S(1)} %get-tuple-element.200, f32[1024]{0:T(1024)S(1)} %get-tuple-element.197, s32[1024]{0:T(1024)S(1)} %copy-done.84), kind=kOutput, calls=%fused_computation.425 | convolution fusion | flops 2105344000 | bytes 10301440 | tf_op jit(solution)/shard_map/dot_general | solution.py:52
  291.1 4.8 fusion.203
  298.8 4.3 fusion.170
  303.2 7.3 %collective-permute-done.20 = bf16[4,64,1024]{2,1,0:T(8,128)(2,1)S(1)} collective-permute-done((bf16[4,64,1024]{2,1,0:T(8,128)(2,1)S(1)}, bf16[4,64,1024]{2,1,0:T(8,128)(2,1)S(1)}, u32[]{:S(2)}, u32[]{:S(2)}) %collective-permute-start.20) | collective-permute-done | bytes 524320 | tf_op jit(solution)/shard_map/ppermute | solution.py:74
  310.5 10.7 %collective-permute-done.19 = bf16[4,64,1024]{2,1,0:T(8,128)(2,1)S(1)} collective-permute-done((bf16[4,64,1024]{2,1,0:T(8,128)(2,1)S(1)}, bf16[4,64,1024]{2,1,0:T(8,128)(2,1)S(1)}, u32[]{:S(2)}, u32[]{:S(2)}) %collective-permute-start.19) | collective-permute-done | bytes 524320 | tf_op jit(solution)/shard_map/ppermute | solution.py:74
  322.7 2.5 collective-permute-start.21
  325.3 2.9 slice_add_fusion
  328.2 6.6 %collective-permute-done.22 = bf16[64,1024]{1,0:T(8,128)(2,1)S(1)} collective-permute-done((bf16[64,1024]{1,0:T(8,128)(2,1)S(1)}, bf16[64,1024]{1,0:T(8,128)(2,1)S(1)}, u32[]{:S(2)}, u32[]{:S(2)}) %collective-permute-start.22) | collective-permute-done | bytes 131104 | tf_op jit(solution)/shard_map/ppermute | solution.py:74
  335.7 11.4 %all-gather.4 = bf16[512,960]{1,0:T(8,128)(2,1)S(1)} all-gather(bf16[64,960]{1,0:T(8,128)(2,1)S(1)} %fusion.164), channel_id=6, replica_groups=mesh['q'=4,'y'=2,'x'=2,'c'=2] {'y','x','c'}, dimensions={0}, use_global_device_ids=true | all-gather | bytes 1105920 | tf_op jit(solution)/shard_map/all_gather | solution.py:149
  359.6 3.4 collective-permute-done.26
  366.9 2.2 multiply_reduce_fusion.1
  378.7 3.3 convolution_convert_fusion.9
  387.3 3.0 fusion.14
  395.1 2.2 convolution_convert_fusion.3
  397.3 2.7 copy.149
  400.1 3.9 all-to-all-start.3
  404.0 3.2 reduce-scatter.2.cloned.1.call-done
  411.1 3.2 reshape.636
  415.1 6.2 %fusion.2 = bf16[8,352,960]{2,1,0:T(8,128)(2,1)} fusion(bf16[1,3,960]{2,1,0:T(4,128)(2,1)S(1)} %copy-done.74, bf16[3,320,960]{2,1,0:T(8,128)(2,1)S(1)} %bitcast.249, bf16[5,128,960]{2,1,0:T(8,128)(2,1)S(1)} %reshape.636, bf16[5,192,960]{2,1,0:T(8,128)(2,1)S(1)} %bitcast.250), kind=kLoop, calls=%fused_computation.7 | loop fusion | flops 27033600 | bytes 10327680 | tf_op jit(solution)/shard_map/concatenate | solution.py:422
  421.3 5.9 %constant_dynamic-slice_fusion.4 = (bf16[4,1,352,960]{3,2,1,0:T(8,128)(2,1)}, bf16[4,352,960]{2,1,0:T(8,128)(2,1)}) fusion(bf16[4,2,352,960]{3,2,1,0:T(8,128)(2,1)} %bitcast.239, s32[]{:T(128)S(6)} %select_n.259, s32[]{:T(128)S(6)} %select_n.260), kind=kLoop, calls=%fused_computation.290 | loop fusion | bytes 10813448 | tf_op jit(solution)/shard_map/jit(dynamic_index_in_dim)/dynamic_slice | solution.py:424
  428.2 4.3 all-to-all-start.4
  434.6 2.6 fusion.187
  443.9 23.4 %collective-permute-done.31 = bf16[2,176,960]{2,1,0:T(8,128)(2,1)} collective-permute-done((bf16[2,176,960]{2,1,0:T(8,128)(2,1)}, bf16[2,176,960]{2,1,0:T(8,128)(2,1)}, u32[]{:S(2)}, u32[]{:S(2)}) %collective-permute-start.31) | collective-permute-done | bytes 675872 | tf_op jit(solution)/shard_map/ppermute | solution.py:74
  471.1 3.8 fusion.50
  474.9 3.1 collective-permute-done.32
  481.8 4.9 collective-permute-start.35
  488.5 5.6 all-to-all-start.5
  494.1 3.5 fusion.5
  497.9 4.0 multiply_reduce_fusion
  521.8 2.4 collective-permute-start.40
  532.1 7.6 %collective-permute-start.44 = (bf16[2880]{0:T(1024)(128)(2,1)S(1)}, bf16[2880]{0:T(1024)(128)(2,1)S(1)}, u32[]{:S(2)}, u32[]{:S(2)}) collective-permute-start(bf16[2880]{0:T(1024)(128)(2,1)S(1)} %slice.503), channel_id=1, source_target_pairs={{0,1},{1,2},{2,3},{3,4},{4,5},{5,6},{6,7},{7,8},{8,9},{9,10},{10,1... | collective-permute-start | bytes 17288 | tf_op jit(solution)/shard_map/ppermute | solution.py:476
  539.8 10.3 %add_multiply_fusion = (f32[1000,960]{0,1:T(8,128)}, f32[1000,960]{0,1:T(8,128)}, f32[1000,960]{0,1:T(8,128)}) fusion(f32[1000,960]{0,1:T(8,128)} %param.20, f32[1000,960]{0,1:T(8,128)} %get-tuple-element.101, f32[]{:T(128)S(6)} %div.148, f32[1000,960]{0,1:T(8,128)} %param.22, f32[1000,960]{0,1:T(8,128)} %param.21), kind=kLoop, calls=%fused_computation.21 | loop fusion | flops 14400000 | bytes 26880004 | tf_op jit(solution)/shard_map/mul | solution.py:107
  550.1 3.2 add_multiply_fusion.1
  (505 shorter events, 169.7 us)
Async XLA Ops:
  8.5 5.8 %collective-permute-start = (bf16[2880]{0:T(1024)(128)(2,1)S(1)}, bf16[2880]{0:T(1024)(128)(2,1)S(1)}, u32[]{:S(2)}, u32[]{:S(2)}) collective-permute-start(bf16[2880]{0:T(1024)(128)(2,1)S(1)} %slice.510), channel_id=1, source_target_pairs={{1,0},{2,1},{3,2},{4,3},{5,4},{6,5},{7,6},{8,7},{9,8},{10,9},{11,1... | collective-permute-start | bytes 17288 | tf_op jit(solution)/shard_map/ppermute | solution.py:204
  17.9 17.6 %collective-permute-start.1 = (bf16[328,960]{1,0:T(8,128)(2,1)S(1)}, bf16[328,960]{1,0:T(8,128)(2,1)}, u32[]{:S(2)}, u32[]{:S(2)}) collective-permute-start(bf16[328,960]{1,0:T(8,128)(2,1)S(1)} %maximum_maximum_fusion), channel_id=1, source_target_pairs={{0,16},{1,17},{2,18},{3,19},{4,20},{5,21},{6,22},{7,23}} | collective-permute-start | bytes 1889288 | tf_op jit(solution)/shard_map/ppermute | solution.py:220
  28.0 11.1 %all-to-all-start = ((s32[32,1,96]{2,1,0:T(1,128)}), s32[32,1,96]{2,1,0:T(1,128)S(1)}, u32[]{:S(2)}, u32[]{:S(2)}) async-start(s32[32,1,96]{2,1,0:T(1,128)} %bitcast), calls=%async_computation | async-start | bytes 32768 | tf_op jit(solution)/shard_map/all_to_all | solution.py:218
  36.6 17.2 %collective-permute-start.2 = (bf16[328,960]{1,0:T(8,128)(2,1)S(1)}, bf16[328,960]{1,0:T(8,128)(2,1)S(1)}, u32[]{:S(2)}, u32[]{:S(2)}) collective-permute-start(bf16[328,960]{1,0:T(8,128)(2,1)S(1)} %broadcast_select_fusion), channel_id=1, source_target_pairs={{0,8},{16,24},{1,9},{17,25},{2,10},{18,26},{3,11},{19,27},{4,12},{... | collective-permute-start | bytes 1889288 | tf_op jit(solution)/shard_map/ppermute | solution.py:222
  39.1 15.7 %all-to-all-start.1 = ((bf16[8,60,640]{2,1,0:T(8,128)(2,1)}), bf16[8,60,640]{2,1,0:T(8,128)(2,1)S(1)}, u32[]{:S(2)}, u32[]{:S(2)}) async-start(bf16[8,60,640]{2,1,0:T(8,128)(2,1)} %reshape.694), calls=%async_computation.1 | async-start | bytes 1310720 | tf_op jit(solution)/shard_map/all_to_all | solution.py:212
  44.7 74.8 %all-gather.8.cloned.1.call-start = ((), (), s32[]{:S(2)}) async-start(), calls=%async_computation.8 | async-start | bytes 6045696 | tf_op jit(solution)/shard_map/all_gather | solution.py:226
  54.8 74.3 %all-to-all-start.2 = ((bf16[32,32,960]{2,1,0:T(8,128)(2,1)}), bf16[32,32,960]{2,1,0:T(8,128)(2,1)}, u32[]{:S(2)}, u32[]{:S(2)}) async-start(bf16[32,32,960]{2,1,0:T(8,128)(2,1)} %bitcast.248), calls=%async_computation.2 | async-start | bytes 4194304 | tf_op jit(solution)/shard_map/all_to_all | solution.py:194
  64.2 119.7 %all-gather.10.cloned.1.call-start = ((), (), s32[]{:S(2)}) async-start(), calls=%async_computation.9 | async-start | bytes 3072000 | tf_op jit(solution)/shard_map/all_gather | solution.py:234
  65.2 75.9 %copy-start.55 = (f32[64,64]{1,0:T(8,128)}, f32[64,64]{1,0:T(8,128)S(1)}, u32[]{:S(2)}) copy-start(f32[64,64]{1,0:T(8,128)S(1)} %gather_fusion.1) | copy-start | bytes 49156
  132.1 27.2 %copy-start.3 = (bf16[512,960]{0,1:T(8,128)(2,1)}, bf16[512,960]{0,1:T(8,128)(2,1)S(1)}, u32[]{:S(2)}) copy-start(bf16[512,960]{0,1:T(8,128)(2,1)S(1)} %get-tuple-element.212) | copy-start | bytes 2949124
  132.9 274.3 %reduce-scatter.2.cloned.1.call-start = ((), (), s32[]{:S(2)}) async-start(), calls=%async_computation.7 | async-start | bytes 3072000 | tf_op jit(solution)/shard_map/reduce_scatter | solution.py:401
  162.0 23.5 %copy-start.92 = (f32[64]{0:T(128)}, f32[64]{0:T(128)S(1)}, u32[]{:S(2)}) copy-start(f32[64]{0:T(128)S(1)} %add_rsqrt_fusion.2) | copy-start | bytes 772
  190.5 2.8 collective-permute-start.3
  196.8 5.8 %collective-permute-start.6 = (bf16[64,1024]{1,0:T(8,128)(2,1)}, bf16[64,1024]{1,0:T(8,128)(2,1)S(1)}, u32[]{:S(2)}, u32[]{:S(2)}) collective-permute-start(bf16[64,1024]{1,0:T(8,128)(2,1)} %get-tuple-element.158), channel_id=1, source_target_pairs={{0,6},{2,4},{4,2},{6,0},{1,7},{3,5},{5,3},{7,1},{8,14},{10,12},{12... | collective-permute-start | bytes 393224 | tf_op jit(solution)/shard_map/ppermute | solution.py:74
  198.9 7.3 %collective-permute-start.5 = (bf16[64,1024]{1,0:T(8,128)(2,1)}, bf16[64,1024]{1,0:T(8,128)(2,1)S(1)}, u32[]{:S(2)}, u32[]{:S(2)}) collective-permute-start(bf16[64,1024]{1,0:T(8,128)(2,1)} %get-tuple-element.159), channel_id=1, source_target_pairs={{0,4},{2,6},{4,0},{6,2},{1,5},{3,7},{5,1},{7,3},{8,12},{10,14},{12... | collective-permute-start | bytes 393224 | tf_op jit(solution)/shard_map/ppermute | solution.py:74
  199.1 7.7 %collective-permute-start.4 = (bf16[64,1024]{1,0:T(8,128)(2,1)}, bf16[64,1024]{1,0:T(8,128)(2,1)}, u32[]{:S(2)}, u32[]{:S(2)}) collective-permute-start(bf16[64,1024]{1,0:T(8,128)(2,1)} %get-tuple-element.157), channel_id=1, source_target_pairs={{0,2},{2,0},{4,6},{6,4},{1,3},{3,1},{5,7},{7,5},{8,10},{10,8},{12,... | collective-permute-start | bytes 393224 | tf_op jit(solution)/shard_map/ppermute | solution.py:74
  208.2 26.3 %copy-start.90 = (f32[64]{0:T(128)}, f32[64]{0:T(128)S(1)}, u32[]{:S(2)}) copy-start(f32[64]{0:T(128)S(1)} %add_rsqrt_fusion.1) | copy-start | bytes 772
  221.8 9.9 %collective-permute-start.7 = (bf16[4,64,1024]{2,1,0:T(8,128)(2,1)S(1)}, bf16[4,64,1024]{2,1,0:T(8,128)(2,1)S(1)}, u32[]{:S(2)}, u32[]{:S(2)}) collective-permute-start(bf16[4,64,1024]{2,1,0:T(8,128)(2,1)S(1)} %bitcast.275), channel_id=1, source_target_pairs={{0,2},{2,0},{1,3},{3,1},{4,6},{6,4},{5,7},{7,5},{8,10},{10,8},{9,1... | collective-permute-start | bytes 1572872 | tf_op jit(solution)/shard_map/ppermute | solution.py:74
  222.9 9.7 %collective-permute-start.8 = (bf16[4,64,1024]{2,1,0:T(8,128)(2,1)S(1)}, bf16[4,64,1024]{2,1,0:T(8,128)(2,1)S(1)}, u32[]{:S(2)}, u32[]{:S(2)}) collective-permute-start(bf16[4,64,1024]{2,1,0:T(8,128)(2,1)S(1)} %bitcast.276), channel_id=1, source_target_pairs={{0,4},{4,0},{1,5},{5,1},{2,6},{6,2},{3,7},{7,3},{8,12},{12,8},{9,1... | collective-permute-start | bytes 1572872 | tf_op jit(solution)/shard_map/ppermute | solution.py:74
  231.7 7.6 %collective-permute-start.9 = (bf16[2,64,1024]{2,1,0:T(8,128)(2,1)S(1)}, bf16[2,64,1024]{2,1,0:T(8,128)(2,1)S(1)}, u32[]{:S(2)}, u32[]{:S(2)}) collective-permute-start(bf16[2,64,1024]{2,1,0:T(8,128)(2,1)S(1)} %slice.536), channel_id=1, source_target_pairs={{0,4},{4,0},{1,5},{5,1},{2,6},{6,2},{3,7},{7,3},{8,12},{12,8},{9,1... | collective-permute-start | bytes 786440 | tf_op jit(solution)/shard_map/ppermute | solution.py:74
  232.6 14.2 %copy-start.95 = (s32[32]{0:T(128)S(1)}, s32[32]{0:T(128)}, u32[]{:S(2)}) copy-start(s32[32]{0:T(128)} %constant.338.clone) | copy-start | bytes 388
  232.6 7.4 %collective-permute-start.10 = (bf16[2,64,1024]{2,1,0:T(8,128)(2,1)S(1)}, bf16[2,64,1024]{2,1,0:T(8,128)(2,1)S(1)}, u32[]{:S(2)}, u32[]{:S(2)}) collective-permute-start(bf16[2,64,1024]{2,1,0:T(8,128)(2,1)S(1)} %slice.537), channel_id=1, source_target_pairs={{0,2},{2,0},{1,3},{3,1},{4,6},{6,4},{5,7},{7,5},{8,10},{10,8},{9,1... | collective-permute-start | bytes 786440 | tf_op jit(solution)/shard_map/ppermute | solution.py:74
  240.8 13.5 %collective-permute-start.11 = (bf16[1024,1024]{1,0:T(8,128)(2,1)}, bf16[1024,1024]{1,0:T(8,128)(2,1)}, u32[]{:S(2)}, u32[]{:S(2)}) collective-permute-start(bf16[1024,1024]{1,0:T(8,128)(2,1)} %bitcast.37), channel_id=1, source_target_pairs={{0,1},{1,0},{2,3},{3,2},{4,5},{5,4},{6,7},{7,6},{8,9},{9,8},{10,11... | collective-permute-start | bytes 6291464 | tf_op jit(solution)/shard_map/ppermute | solution.py:74
  259.2 16.4 %copy-start.19 = (f32[1024,1000]{0,1:T(8,128)}, f32[1024,1000]{0,1:T(8,128)S(1)}, u32[]{:S(2)}) copy-start(f32[1024,1000]{0,1:T(8,128)S(1)} %get-tuple-element.218) | copy-start | bytes 12288004
  260.7 1.3 collective-permute-start.12
  262.1 2.8 collective-permute-start.13
  265.1 2.8 collective-permute-start.14
  268.0 2.8 collective-permute-start.15
  271.0 3.9 collective-permute-start.16
  280.7 10.3 %collective-permute-start.17 = (bf16[1024,1024]{1,0:T(8,128)(2,1)}, bf16[1024,1024]{1,0:T(8,128)(2,1)}, u32[]{:S(2)}, u32[]{:S(2)}) collective-permute-start(bf16[1024,1024]{1,0:T(8,128)(2,1)} %convolution_convert_fusion), channel_id=1, source_target_pairs={{0,1},{1,0},{2,3},{3,2},{4,5},{5,4},{6,7},{7,6},{8,9},{9,8},{10,11... | collective-permute-start | bytes 6291464 | tf_op jit(solution)/shard_map/ppermute | solution.py:74
  296.1 14.4 %collective-permute-start.20 = (bf16[4,64,1024]{2,1,0:T(8,128)(2,1)S(1)}, bf16[4,64,1024]{2,1,0:T(8,128)(2,1)S(1)}, u32[]{:S(2)}, u32[]{:S(2)}) collective-permute-start(bf16[4,64,1024]{2,1,0:T(8,128)(2,1)S(1)} %bitcast.301), channel_id=1, source_target_pairs={{0,6},{2,4},{4,2},{6,0},{1,7},{3,5},{5,3},{7,1},{8,14},{10,12},{12... | collective-permute-start | bytes 1572872 | tf_op jit(solution)/shard_map/ppermute | solution.py:74
  296.6 24.6 %collective-permute-start.19 = (bf16[4,64,1024]{2,1,0:T(8,128)(2,1)S(1)}, bf16[4,64,1024]{2,1,0:T(8,128)(2,1)S(1)}, u32[]{:S(2)}, u32[]{:S(2)}) collective-permute-start(bf16[4,64,1024]{2,1,0:T(8,128)(2,1)S(1)} %bitcast.300), channel_id=1, source_target_pairs={{0,4},{2,6},{4,0},{6,2},{1,5},{3,7},{5,1},{7,3},{8,12},{10,14},{12... | collective-permute-start | bytes 1572872 | tf_op jit(solution)/shard_map/ppermute | solution.py:74
  297.1 24.1 %collective-permute-start.18 = (bf16[4,64,1024]{2,1,0:T(8,128)(2,1)S(1)}, bf16[4,64,1024]{2,1,0:T(8,128)(2,1)S(1)}, u32[]{:S(2)}, u32[]{:S(2)}) collective-permute-start(bf16[4,64,1024]{2,1,0:T(8,128)(2,1)S(1)} %bitcast.299), channel_id=1, source_target_pairs={{0,2},{2,0},{4,6},{6,4},{1,3},{3,1},{5,7},{7,5},{8,10},{10,8},{12,... | collective-permute-start | bytes 1572872 | tf_op jit(solution)/shard_map/ppermute | solution.py:74
  321.7 6.5 %collective-permute-start.23 = (bf16[64,1024]{1,0:T(8,128)(2,1)S(1)}, bf16[64,1024]{1,0:T(8,128)(2,1)S(1)}, u32[]{:S(2)}, u32[]{:S(2)}) collective-permute-start(bf16[64,1024]{1,0:T(8,128)(2,1)S(1)} %get-tuple-element.155), channel_id=1, source_target_pairs={{0,24},{8,16},{16,8},{24,0},{1,25},{9,17},{17,9},{25,1},{2,26},{10... | collective-permute-start | bytes 393224 | tf_op jit(solution)/shard_map/ppermute | solution.py:74
  322.7 12.0 %collective-permute-start.22 = (bf16[64,1024]{1,0:T(8,128)(2,1)S(1)}, bf16[64,1024]{1,0:T(8,128)(2,1)S(1)}, u32[]{:S(2)}, u32[]{:S(2)}) collective-permute-start(bf16[64,1024]{1,0:T(8,128)(2,1)S(1)} %get-tuple-element.156), channel_id=1, source_target_pairs={{0,16},{8,24},{16,0},{24,8},{1,17},{9,25},{17,1},{25,9},{2,18},{10... | collective-permute-start | bytes 393224 | tf_op jit(solution)/shard_map/ppermute | solution.py:74
  322.7 12.0 %collective-permute-start.21 = (bf16[64,1024]{1,0:T(8,128)(2,1)S(1)}, bf16[64,1024]{1,0:T(8,128)(2,1)S(1)}, u32[]{:S(2)}, u32[]{:S(2)}) collective-permute-start(bf16[64,1024]{1,0:T(8,128)(2,1)S(1)} %get-tuple-element.154), channel_id=1, source_target_pairs={{0,8},{8,0},{16,24},{24,16},{1,9},{9,1},{17,25},{25,17},{2,10},{10... | collective-permute-start | bytes 393224 | tf_op jit(solution)/shard_map/ppermute | solution.py:74
  328.1 19.0 %copy-start.38 = (f32[512,640]{1,0:T(8,128)S(1)}, f32[512,640]{1,0:T(8,128)}, u32[]{:S(2)}) copy-start(f32[512,640]{1,0:T(8,128)} %copy-done.37) | copy-start | bytes 3932164
  328.1 19.0 %copy-start.53 = (bf16[320,640]{1,0:T(8,128)(2,1)S(1)}, bf16[320,640]{1,0:T(8,128)(2,1)}, u32[]{:S(2)}) copy-start(bf16[320,640]{1,0:T(8,128)(2,1)} %copy-done.52) | copy-start | bytes 1228804
  328.2 19.0 %copy-start.66 = (bf16[160,320]{1,0:T(8,128)(2,1)S(1)}, bf16[160,320]{1,0:T(8,128)(2,1)}, u32[]{:S(2)}) copy-start(bf16[160,320]{1,0:T(8,128)(2,1)} %copy-done.65) | copy-start | bytes 307204
  328.2 19.0 %copy-start.68 = (bf16[160,320]{1,0:T(8,128)(2,1)S(1)}, bf16[160,320]{1,0:T(8,128)(2,1)}, u32[]{:S(2)}) copy-start(bf16[160,320]{1,0:T(8,128)(2,1)} %copy-done.67) | copy-start | bytes 307204
  349.5 2.5 collective-permute-start.24
  353.7 5.9 %collective-permute-start.27 = (bf16[64,1024]{1,0:T(8,128)(2,1)S(1)}, bf16[64,1024]{1,0:T(8,128)(2,1)}, u32[]{:S(2)}, u32[]{:S(2)}) collective-permute-start(bf16[64,1024]{1,0:T(8,128)(2,1)S(1)} %get-tuple-element.152), channel_id=1, source_target_pairs={{0,6},{2,4},{4,2},{6,0},{1,7},{3,5},{5,3},{7,1},{8,14},{10,12},{12... | collective-permute-start | bytes 393224 | tf_op jit(solution)/shard_map/ppermute | solution.py:74
  355.0 8.0 %collective-permute-start.26 = (bf16[64,1024]{1,0:T(8,128)(2,1)S(1)}, bf16[64,1024]{1,0:T(8,128)(2,1)}, u32[]{:S(2)}, u32[]{:S(2)}) collective-permute-start(bf16[64,1024]{1,0:T(8,128)(2,1)S(1)} %get-tuple-element.153), channel_id=1, source_target_pairs={{0,4},{2,6},{4,0},{6,2},{1,5},{3,7},{5,1},{7,3},{8,12},{10,14},{12... | collective-permute-start | bytes 393224 | tf_op jit(solution)/shard_map/ppermute | solution.py:74
  355.8 7.3 %collective-permute-start.25 = (bf16[64,1024]{1,0:T(8,128)(2,1)S(1)}, bf16[64,1024]{1,0:T(8,128)(2,1)}, u32[]{:S(2)}, u32[]{:S(2)}) collective-permute-start(bf16[64,1024]{1,0:T(8,128)(2,1)S(1)} %get-tuple-element.151), channel_id=1, source_target_pairs={{0,2},{2,0},{4,6},{6,4},{1,3},{3,1},{5,7},{7,5},{8,10},{10,8},{12,... | collective-permute-start | bytes 393224 | tf_op jit(solution)/shard_map/ppermute | solution.py:74
  400.1 21.2 %all-to-all-start.3 = ((bf16[32,8,960]{2,1,0:T(8,128)(2,1)}), bf16[32,8,960]{2,1,0:T(8,128)(2,1)}, u32[]{:S(2)}, u32[]{:S(2)}) async-start(bf16[32,8,960]{2,1,0:T(8,128)(2,1)} %bitcast.92), calls=%async_computation.4 | async-start | bytes 1048576 | tf_op jit(solution)/shard_map/all_to_all | solution.py:194
  427.1 7.5 %collective-permute-start.28 = (bf16[4,352,960]{2,1,0:T(8,128)(2,1)}, bf16[4,352,960]{2,1,0:T(8,128)(2,1)}, u32[]{:S(2)}, u32[]{:S(2)}) collective-permute-start(bf16[4,352,960]{2,1,0:T(8,128)(2,1)} %get-tuple-element.122), channel_id=1, source_target_pairs={{0,1},{1,0},{2,3},{3,2},{4,5},{5,4},{6,7},{7,6},{8,9},{9,8},{10,11... | collective-permute-start | bytes 8110088 | tf_op jit(solution)/shard_map/ppermute | solution.py:74
  428.2 51.6 %all-to-all-start.4 = ((bf16[32,24,960]{2,1,0:T(8,128)(2,1)}), bf16[32,24,960]{2,1,0:T(8,128)(2,1)}, u32[]{:S(2)}, u32[]{:S(2)}) async-start(bf16[32,24,960]{2,1,0:T(8,128)(2,1)} %bitcast.93), calls=%async_computation.5 | async-start | bytes 3145728 | tf_op jit(solution)/shard_map/all_to_all | solution.py:194
  438.6 28.7 %collective-permute-start.31 = (bf16[2,176,960]{2,1,0:T(8,128)(2,1)}, bf16[2,176,960]{2,1,0:T(8,128)(2,1)}, u32[]{:S(2)}, u32[]{:S(2)}) collective-permute-start(bf16[2,176,960]{2,1,0:T(8,128)(2,1)} %fusion.59), channel_id=1, source_target_pairs={{0,4},{4,0},{1,5},{5,1},{2,6},{6,2},{3,7},{7,3},{8,12},{12,8},{9,1... | collective-permute-start | bytes 2027528 | tf_op jit(solution)/shard_map/ppermute | solution.py:74
  441.1 28.3 %collective-permute-start.29 = (bf16[2,176,960]{2,1,0:T(8,128)(2,1)}, bf16[2,176,960]{2,1,0:T(8,128)(2,1)}, u32[]{:S(2)}, u32[]{:S(2)}) collective-permute-start(bf16[2,176,960]{2,1,0:T(8,128)(2,1)} %fusion.58), channel_id=1, source_target_pairs={{0,2},{2,0},{1,3},{3,1},{4,6},{6,4},{5,7},{7,5},{8,10},{10,8},{9,1... | collective-permute-start | bytes 2027528 | tf_op jit(solution)/shard_map/ppermute | solution.py:74
  469.3 8.8 %collective-permute-start.32 = (bf16[176,960]{1,0:T(8,128)(2,1)S(1)}, bf16[176,960]{1,0:T(8,128)(2,1)S(1)}, u32[]{:S(2)}, u32[]{:S(2)}) collective-permute-start(bf16[176,960]{1,0:T(8,128)(2,1)S(1)} %fusion.76), channel_id=1, source_target_pairs={{0,2},{2,0},{1,3},{3,1},{4,6},{6,4},{5,7},{7,5},{8,10},{10,8},{9,1... | collective-permute-start | bytes 1013768 | tf_op jit(solution)/shard_map/ppermute | solution.py:74
  470.9 8.7 %collective-permute-start.30 = (bf16[176,960]{1,0:T(8,128)(2,1)S(1)}, bf16[176,960]{1,0:T(8,128)(2,1)S(1)}, u32[]{:S(2)}, u32[]{:S(2)}) collective-permute-start(bf16[176,960]{1,0:T(8,128)(2,1)S(1)} %fusion.75), channel_id=1, source_target_pairs={{0,4},{4,0},{1,5},{5,1},{2,6},{6,2},{3,7},{7,3},{8,12},{12,8},{9,1... | collective-permute-start | bytes 1013768 | tf_op jit(solution)/shard_map/ppermute | solution.py:74
  481.8 21.1 %collective-permute-start.35 = (bf16[88,960]{1,0:T(8,128)(2,1)}, bf16[88,960]{1,0:T(8,128)(2,1)}, u32[]{:S(2)}, u32[]{:S(2)}) collective-permute-start(bf16[88,960]{1,0:T(8,128)(2,1)} %get-tuple-element.133), channel_id=1, source_target_pairs={{0,24},{8,16},{16,8},{24,0},{1,25},{9,17},{17,9},{25,1},{2,26},{10... | collective-permute-start | bytes 506888 | tf_op jit(solution)/shard_map/ppermute | solution.py:74
  486.6 16.2 %collective-permute-start.34 = (bf16[88,960]{1,0:T(8,128)(2,1)}, bf16[88,960]{1,0:T(8,128)(2,1)}, u32[]{:S(2)}, u32[]{:S(2)}) collective-permute-start(bf16[88,960]{1,0:T(8,128)(2,1)} %get-tuple-element.134), channel_id=1, source_target_pairs={{0,16},{8,24},{16,0},{24,8},{1,17},{9,25},{17,1},{25,9},{2,18},{10... | collective-permute-start | bytes 506888 | tf_op jit(solution)/shard_map/ppermute | solution.py:74
  486.6 16.2 %collective-permute-start.33 = (bf16[88,960]{1,0:T(8,128)(2,1)}, bf16[88,960]{1,0:T(8,128)(2,1)}, u32[]{:S(2)}, u32[]{:S(2)}) collective-permute-start(bf16[88,960]{1,0:T(8,128)(2,1)} %get-tuple-element.132), channel_id=1, source_target_pairs={{0,8},{8,0},{16,24},{24,16},{1,9},{9,1},{17,25},{25,17},{2,10},{10... | collective-permute-start | bytes 506888 | tf_op jit(solution)/shard_map/ppermute | solution.py:74
  488.5 41.7 %all-to-all-start.5 = ((bf16[8,60,640]{2,1,0:T(8,128)(2,1)}), bf16[8,60,640]{2,1,0:T(8,128)(2,1)S(1)}, u32[]{:S(2)}, u32[]{:S(2)}) async-start(bf16[8,60,640]{2,1,0:T(8,128)(2,1)} %reshape.649), calls=%async_computation.6 | async-start | bytes 1310720 | tf_op jit(solution)/shard_map/all_to_all | solution.py:443
  504.7 22.4 %collective-permute-start.43 = (bf16[88,960]{1,0:T(8,128)(2,1)S(1)}, bf16[88,960]{1,0:T(8,128)(2,1)S(1)}, u32[]{:S(2)}, u32[]{:S(2)}) collective-permute-start(bf16[88,960]{1,0:T(8,128)(2,1)S(1)} %get-tuple-element.103), channel_id=1, source_target_pairs={{16,0},{17,1},{18,2},{19,3},{20,4},{21,5},{22,6},{23,7}} | collective-permute-start | bytes 506888 | tf_op jit(solution)/shard_map/ppermute | solution.py:454
  506.0 21.6 %collective-permute-start.42 = (bf16[88,960]{1,0:T(8,128)(2,1)S(1)}, bf16[88,960]{1,0:T(8,128)(2,1)S(1)}, u32[]{:S(2)}, u32[]{:S(2)}) collective-permute-start(bf16[88,960]{1,0:T(8,128)(2,1)S(1)} %get-tuple-element.103), channel_id=1, source_target_pairs={{8,0},{9,1},{10,2},{11,3},{12,4},{13,5},{14,6},{15,7}} | collective-permute-start | bytes 506888 | tf_op jit(solution)/shard_map/ppermute | solution.py:454
  507.3 19.9 %collective-permute-start.41 = (bf16[88,960]{1,0:T(8,128)(2,1)S(1)}, bf16[88,960]{1,0:T(8,128)(2,1)S(1)}, u32[]{:S(2)}, u32[]{:S(2)}) collective-permute-start(bf16[88,960]{1,0:T(8,128)(2,1)S(1)} %get-tuple-element.103), channel_id=1, source_target_pairs={{24,0},{25,1},{26,2},{27,3},{28,4},{29,5},{30,6},{31,7}} | collective-permute-start | bytes 506888 | tf_op jit(solution)/shard_map/ppermute | solution.py:454
  511.4 1.2 collective-permute-start.36
  513.2 2.7 collective-permute-start.37
  516.7 2.7 collective-permute-start.38
  519.4 2.4 collective-permute-start.39
  521.8 3.3 collective-permute-start.40
  532.1 18.0 %collective-permute-start.44 = (bf16[2880]{0:T(1024)(128)(2,1)S(1)}, bf16[2880]{0:T(1024)(128)(2,1)S(1)}, u32[]{:S(2)}, u32[]{:S(2)}) collective-permute-start(bf16[2880]{0:T(1024)(128)(2,1)S(1)} %slice.503), channel_id=1, source_target_pairs={{0,1},{1,2},{2,3},{3,4},{4,5},{5,6},{6,7},{7,8},{8,9},{9,10},{10,1... | collective-permute-start | bytes 17288 | tf_op jit(solution)/shard_map/ppermute | solution.py:476
  (88 other events, 351.1 us)
Sparse Core Ops, SparseCore 0:
  54.9 64.4 all-gather.7
  133.0 50.9 all-gather.9
  358.4 48.7 reduce-scatter.1

commit v13 on v11

--- a/solution.py
+++ b/solution.py
@@ -146,7 +146,7 @@
 
 
 def spread_plane(rows):
-    return widen(lax.all_gather(rows, PLANE).reshape(-1, D))
+    return lax.all_gather(rows, PLANE).reshape(-1, D)
 
 
 def local(
@@ -290,13 +290,12 @@
         column, h_all = lax.optimization_barrier((column, h_all))
         w_gu = column[1:3].reshape(D, 2 * SHARE)
         w_down = down_unpack(column[3])
-    w_gu = jnp.pad(w_gu, ((0, WIDE - D), (0, 0)))
-    w_down = widen(w_down)
+    wide_gu = jnp.pad(w_gu, ((0, WIDE - D), (0, 0)))
     gate_up = dot(h_all, w_gu)
     gate, up = gate_up[:, :SHARE], gate_up[:, SHARE:]
     sig = jax.nn.sigmoid(gate)
     act = (gate * sig * up).astype(bf16)
-    x_two = x_one + fold_plane(act, w_down, 0)
+    x_two = x_one + fold_plane(act, widen(w_down), 0)
 
     hidden = (x_two * scale_of(x_two) * gains[2]).astype(bf16)
     wide_table = widen(table_low)
@@ -364,9 +363,9 @@
     d_act = dot(d_down, w_down, 1, 1)
     d_gate = d_act * up * sig * (1.0 + gate * (1.0 - sig))
     d_gu = jnp.concatenate([d_gate, d_act * gate * sig], axis=1).astype(bf16)
-    d_h_mlp = fold_plane(d_gu, w_gu, 1)
-    grad_down = dot(act, d_down, 0, 0)[:, :D].astype(bf16)
-    grad_gu = dot(h_all, d_gu, 0, 0)[:D].astype(bf16)
+    d_h_mlp = fold_plane(d_gu, wide_gu, 1)
+    grad_down = dot(act, d_down, 0, 0).astype(bf16)
+    grad_gu = dot(h_all, d_gu, 0, 0).astype(bf16)
     d_x_mlp, grad_mlp = norm_back(x_one, gains[1], d_h_mlp)
     d_x_one = d_x_two + d_x_mlp
 

time: 571 us -> 571 us (level)
  transfers between devices with their start and end apart: 50 -> 50, of which waited for: 27 -> 28; matrix products, arithmetic and copies ran while one was open for 33% -> 33% of each run, Pallas kernels for 0% -> 0%
where the time goes in v13:
time: 571 us; the launch traced here: 561 us
  waiting for transfers between devices  161 us (28%)
  matrix products  88.4 us (15%)
  local copies, waits for them, and re-layouts  88.1 us (15%)
  starting transfers between devices  87.3 us (15%)
  other arithmetic  76.7 us (13%)
  blocking collectives  38.8 us (7%)
  between operations  21.5 us (4%)
    ppermute x33, waiting for transfers between devices, flip(): return lax.ppermute(rows, axes, [(i, i ^ bits) for i in range(size)])  91.7 us
    dot_general x37, matrix products, dot(): lax.dot_general(left, right, (((left_dim,), (right_dim,)), ((), ())), pre...  73 us
    all_gather x1, waiting for transfers between devices, local(): level = lax.all_gather(first, PLANE)  49.5 us
    ppermute x33, starting transfers between devices, flip(): return lax.ppermute(rows, axes, [(i, i ^ bits) for i in range(size)])  34 us
    all_gather x2, blocking collectives, spread_plane(): return lax.all_gather(rows, PLANE).reshape(-1, D)  22.9 us
    all_to_all x3, starting transfers between devices, exchange(): lax.all_to_all(blocks, ALL, split_axis=0, concat_axis=0, tiled=True)  20 us
    unnamed x206, local copies, waits for them, and re-layouts  16.2 us
    all_gather x1, blocking collectives, local(): across = lax.all_gather(widen(hidden), 'q')  15.8 us
  transfers between devices with their start and end apart: 50, of which 28 were waited for; matrix products, arithmetic and copies ran while one was open for 33% of the time, Pallas kernels for 0%

profile of v13, /device:TPU:24, one launch (start us, length us, event | category | flops | bytes accessed | tf_op | source)
XLA Modules:
  0.0 561.5 jit_solution(12907140646548136551)
XLA Ops:
  8.5 3.7 collective-permute-start
  20.3 3.7 convert_element_type.331
  24.7 6.4 %all-to-all-start = ((s32[32,1,96]{2,1,0:T(1,128)}), s32[32,1,96]{2,1,0:T(1,128)S(1)}, u32[]{:S(2)}, u32[]{:S(2)}) async-start(s32[32,1,96]{2,1,0:T(1,128)} %bitcast), calls=%async_computation | async-start | bytes 32768 | tf_op jit(solution)/shard_map/all_to_all | solution.py:218
  35.6 4.3 all-to-all-done
  39.9 3.5 all-to-all-start.1
  43.6 5.2 fusion.24
  48.8 3.9 copy.190
  54.6 8.4 %all-to-all-start.2 = ((bf16[32,32,960]{2,1,0:T(8,128)(2,1)}), bf16[32,32,960]{2,1,0:T(8,128)(2,1)}, u32[]{:S(2)}, u32[]{:S(2)}) async-start(bf16[32,32,960]{2,1,0:T(8,128)(2,1)} %bitcast.251), calls=%async_computation.2 | async-start | bytes 4194304 | tf_op jit(solution)/shard_map/all_to_all | solution.py:194
  67.6 49.5 %all-gather.8.cloned.1.call-done = bf16[2624,960]{1,0:T(8,128)(2,1)} async-done(((bf16[328,960]{1,0:T(8,128)(2,1)}), bf16[2624,960]{1,0:T(8,128)(2,1)}) %all-gather.8.cloned.1.call-update) | async-done | bytes 5038096 | tf_op jit(solution)/shard_map/all_gather | solution.py:226
  120.3 3.0 slice.399
  123.3 2.8 reshape.612
  126.8 3.0 fusion.23
  130.5 2.4 fusion.160
  144.5 2.3 copy.230
  148.4 3.7 fusion.188
  152.1 3.6 convolution_convert_fusion.11
  160.4 11.9 %all-gather.2 = bf16[512,960]{1,0:T(8,128)(2,1)} all-gather(bf16[64,960]{1,0:T(8,128)(2,1)S(1)} %multiply_convert_fusion.7), channel_id=4, replica_groups=mesh['q'=4,'y'=2,'x'=2,'c'=2] {'y','x','c'}, dimensions={0}, use_global_device_ids=true | all-gather | bytes 1105920 | tf_op jit(solution)/shard_map/all_gather | solution.py:149
  172.4 8.4 %all-gather.10.cloned.1.call-done = bf16[1920,640]{1,0:T(8,128)(2,1)} async-done(((bf16[480,640]{1,0:T(8,128)(2,1)}), bf16[1920,640]{1,0:T(8,128)(2,1)}) %all-gather.10.cloned.1.call-update) | async-done | bytes 2457616 | tf_op jit(solution)/shard_map/all_gather | solution.py:234
  188.8 2.2 collective-permute-done.3
  194.5 2.4 collective-permute-start.6
  199.0 2.6 collective-permute-done.6
  201.5 2.4 collective-permute-done.5
  206.1 15.8 %all-gather.3 = bf16[256,1024]{1,0:T(8,128)(2,1)S(1)} all-gather(bf16[64,1024]{1,0:T(8,128)(2,1)S(1)} %pad.22), channel_id=5, replica_groups=mesh['q'=4,'y'=2,'x'=2,'c'=2] {'q'}, dimensions={0}, use_global_device_ids=true | all-gather | bytes 655360 | tf_op jit(solution)/shard_map/all_gather | solution.py:302
  223.6 10.3 %collective-permute-done.7 = bf16[4,64,1024]{2,1,0:T(8,128)(2,1)S(1)} collective-permute-done((bf16[4,64,1024]{2,1,0:T(8,128)(2,1)S(1)}, bf16[4,64,1024]{2,1,0:T(8,128)(2,1)S(1)}, u32[]{:S(2)}, u32[]{:S(2)}) %collective-permute-start.7) | collective-permute-done | bytes 524320 | tf_op jit(solution)/shard_map/ppermute | solution.py:74
  238.5 2.3 collective-permute-done.9
  244.4 4.5 fusion.190
  251.9 3.9 fusion.189
  259.5 3.4 collective-permute-done.13
  263.8 3.3 collective-permute-done.14
  273.3 2.9 collective-permute-done.16
  276.9 5.2 convolution_convert_fusion
  282.2 5.6 %fusion.163 = f32[1000,1024]{0,1:T(8,128)S(1)} fusion(bf16[1024,1024]{1,0:T(8,128)(2,1)} %bitcast.37, f32[1024,1000]{0,1:T(8,128)} %copy-done.22, f32[1024]{0:T(1024)S(1)} %get-tuple-element.216, f32[1024]{0:T(1024)S(1)} %get-tuple-element.213, s32[1024]{0:T(1024)S(1)} %copy-done.84), kind=kOutput, calls=%fused_computation.417 | convolution fusion | flops 2105344000 | bytes 10301440 | tf_op jit(solution)/shard_map/dot_general | solution.py:52
  287.9 4.8 fusion.191
  296.4 4.3 fusion.164
  300.8 7.9 %collective-permute-done.20 = bf16[4,64,1024]{2,1,0:T(8,128)(2,1)S(1)} collective-permute-done((bf16[4,64,1024]{2,1,0:T(8,128)(2,1)S(1)}, bf16[4,64,1024]{2,1,0:T(8,128)(2,1)S(1)}, u32[]{:S(2)}, u32[]{:S(2)}) %collective-permute-start.20) | collective-permute-done | bytes 524320 | tf_op jit(solution)/shard_map/ppermute | solution.py:74
  308.7 10.7 %collective-permute-done.19 = bf16[4,64,1024]{2,1,0:T(8,128)(2,1)S(1)} collective-permute-done((bf16[4,64,1024]{2,1,0:T(8,128)(2,1)S(1)}, bf16[4,64,1024]{2,1,0:T(8,128)(2,1)S(1)}, u32[]{:S(2)}, u32[]{:S(2)}) %collective-permute-start.19) | collective-permute-done | bytes 524320 | tf_op jit(solution)/shard_map/ppermute | solution.py:74
  319.8 3.1 collective-permute-start.23
  324.2 2.9 slice_add_fusion
  328.1 5.9 %collective-permute-done.22 = bf16[64,1024]{1,0:T(8,128)(2,1)S(1)} collective-permute-done((bf16[64,1024]{1,0:T(8,128)(2,1)S(1)}, bf16[64,1024]{1,0:T(8,128)(2,1)S(1)}, u32[]{:S(2)}, u32[]{:S(2)}) %collective-permute-start.22) | collective-permute-done | bytes 131104 | tf_op jit(solution)/shard_map/ppermute | solution.py:74
  335.0 11.0 %all-gather.4 = bf16[512,960]{1,0:T(8,128)(2,1)S(1)} all-gather(bf16[64,960]{1,0:T(8,128)(2,1)S(1)} %fusion.157), channel_id=6, replica_groups=mesh['q'=4,'y'=2,'x'=2,'c'=2] {'y','x','c'}, dimensions={0}, use_global_device_ids=true | all-gather | bytes 1105920 | tf_op jit(solution)/shard_map/all_gather | solution.py:149
  365.5 2.2 multiply_reduce_fusion.1
  377.4 3.3 convolution_convert_fusion.10
  386.0 3.0 fusion.14
  393.8 2.2 convolution_convert_fusion.3
  396.0 2.7 copy.214
  398.7 4.9 all-to-all-start.3
  409.4 3.2 reshape.642
  413.4 6.3 %fusion.2 = bf16[8,352,960]{2,1,0:T(8,128)(2,1)} fusion(bf16[1,3,960]{2,1,0:T(4,128)(2,1)S(1)} %copy-done.74, bf16[3,320,960]{2,1,0:T(8,128)(2,1)S(1)} %bitcast.252, bf16[5,128,960]{2,1,0:T(8,128)(2,1)S(1)} %reshape.642, bf16[5,192,960]{2,1,0:T(8,128)(2,1)S(1)} %bitcast.253), kind=kLoop, calls=%fused_computation.7 | loop fusion | flops 27033600 | bytes 10327680 | tf_op jit(solution)/shard_map/concatenate | solution.py:420
  419.7 5.9 %constant_dynamic-slice_fusion.4 = (bf16[4,1,352,960]{3,2,1,0:T(8,128)(2,1)}, bf16[4,352,960]{2,1,0:T(8,128)(2,1)}) fusion(bf16[4,2,352,960]{3,2,1,0:T(8,128)(2,1)} %bitcast.242, s32[]{:T(128)S(6)} %select_n.259, s32[]{:T(128)S(6)} %select_n.260), kind=kLoop, calls=%fused_computation.282 | loop fusion | bytes 10813448 | tf_op jit(solution)/shard_map/jit(dynamic_index_in_dim)/dynamic_slice | solution.py:422
  425.5 6.6 %all-to-all-start.4 = ((bf16[32,24,960]{2,1,0:T(8,128)(2,1)}), bf16[32,24,960]{2,1,0:T(8,128)(2,1)}, u32[]{:S(2)}, u32[]{:S(2)}) async-start(bf16[32,24,960]{2,1,0:T(8,128)(2,1)} %bitcast.93), calls=%async_computation.5 | async-start | bytes 3145728 | tf_op jit(solution)/shard_map/all_to_all | solution.py:194
  434.2 2.6 fusion.175
  443.9 23.2 %collective-permute-done.31 = bf16[2,176,960]{2,1,0:T(8,128)(2,1)} collective-permute-done((bf16[2,176,960]{2,1,0:T(8,128)(2,1)}, bf16[2,176,960]{2,1,0:T(8,128)(2,1)}, u32[]{:S(2)}, u32[]{:S(2)}) %collective-permute-start.31) | collective-permute-done | bytes 675872 | tf_op jit(solution)/shard_map/ppermute | solution.py:74
  472.0 3.8 fusion.45
  475.8 3.8 collective-permute-done.32
  479.6 2.4 collective-permute-done.30
  484.6 2.9 collective-permute-start.33
  488.5 3.5 all-to-all-start.5
  492.0 3.5 fusion.5
  495.8 4.0 multiply_reduce_fusion
  506.9 6.3 %all-to-all-start.6 = ((f32[32,1,2]{2,1,0:T(1,128)}), f32[32,1,2]{2,1,0:T(1,128)S(1)}, u32[]{:S(2)}, u32[]{:S(2)}) async-start(f32[32,1,2]{2,1,0:T(1,128)} %broadcast_in_dim.71), calls=%async_computation.7 | async-start | bytes 32768 | tf_op jit(solution)/shard_map/all_to_all | solution.py:410
  516.5 3.6 collective-permute-start.38
  523.1 10.2 %add_multiply_fusion = (f32[1000,960]{0,1:T(8,128)}, f32[1000,960]{0,1:T(8,128)}, f32[1000,960]{0,1:T(8,128)}) fusion(f32[1000,960]{0,1:T(8,128)} %param.20, f32[1000,960]{0,1:T(8,128)} %get-tuple-element.117, f32[]{:T(128)S(6)} %div.148, f32[1000,960]{0,1:T(8,128)} %param.22, f32[1000,960]{0,1:T(8,128)} %param.21), kind=kLoop, calls=%fused_computation.21 | loop fusion | flops 14400000 | bytes 26880004 | tf_op jit(solution)/shard_map/mul | solution.py:107
  543.6 4.1 collective-permute-done.39
  547.7 4.8 add_multiply_fusion.1
  (492 shorter events, 173.8 us)
Async XLA Ops:
  8.5 6.8 %collective-permute-start = (bf16[2880]{0:T(1024)(128)(2,1)S(1)}, bf16[2880]{0:T(1024)(128)(2,1)S(1)}, u32[]{:S(2)}, u32[]{:S(2)}) collective-permute-start(bf16[2880]{0:T(1024)(128)(2,1)S(1)} %slice.500), channel_id=1, source_target_pairs={{1,0},{2,1},{3,2},{4,3},{5,4},{6,5},{7,6},{8,7},{9,8},{10,9},{11,1... | collective-permute-start | bytes 17288 | tf_op jit(solution)/shard_map/ppermute | solution.py:204
  18.8 14.3 %collective-permute-start.1 = (bf16[328,960]{1,0:T(8,128)(2,1)S(1)}, bf16[328,960]{1,0:T(8,128)(2,1)}, u32[]{:S(2)}, u32[]{:S(2)}) collective-permute-start(bf16[328,960]{1,0:T(8,128)(2,1)S(1)} %maximum_maximum_fusion), channel_id=1, source_target_pairs={{0,16},{1,17},{2,18},{3,19},{4,20},{5,21},{6,22},{7,23}} | collective-permute-start | bytes 1889288 | tf_op jit(solution)/shard_map/ppermute | solution.py:220
  24.7 15.2 %all-to-all-start = ((s32[32,1,96]{2,1,0:T(1,128)}), s32[32,1,96]{2,1,0:T(1,128)S(1)}, u32[]{:S(2)}, u32[]{:S(2)}) async-start(s32[32,1,96]{2,1,0:T(1,128)} %bitcast), calls=%async_computation | async-start | bytes 32768 | tf_op jit(solution)/shard_map/all_to_all | solution.py:218
  34.3 19.2 %collective-permute-start.2 = (bf16[328,960]{1,0:T(8,128)(2,1)S(1)}, bf16[328,960]{1,0:T(8,128)(2,1)S(1)}, u32[]{:S(2)}, u32[]{:S(2)}) collective-permute-start(bf16[328,960]{1,0:T(8,128)(2,1)S(1)} %broadcast_select_fusion), channel_id=1, source_target_pairs={{0,8},{16,24},{1,9},{17,25},{2,10},{18,26},{3,11},{19,27},{4,12},{... | collective-permute-start | bytes 1889288 | tf_op jit(solution)/shard_map/ppermute | solution.py:222
  39.9 14.6 %all-to-all-start.1 = ((bf16[8,60,640]{2,1,0:T(8,128)(2,1)}), bf16[8,60,640]{2,1,0:T(8,128)(2,1)S(1)}, u32[]{:S(2)}, u32[]{:S(2)}) async-start(bf16[8,60,640]{2,1,0:T(8,128)(2,1)} %reshape.700), calls=%async_computation.1 | async-start | bytes 1310720 | tf_op jit(solution)/shard_map/all_to_all | solution.py:212
  43.5 73.6 %all-gather.8.cloned.1.call-start = ((), (), s32[]{:S(2)}) async-start(), calls=%async_computation.9 | async-start | bytes 6045696 | tf_op jit(solution)/shard_map/all_gather | solution.py:226
  54.6 72.2 %all-to-all-start.2 = ((bf16[32,32,960]{2,1,0:T(8,128)(2,1)}), bf16[32,32,960]{2,1,0:T(8,128)(2,1)}, u32[]{:S(2)}, u32[]{:S(2)}) async-start(bf16[32,32,960]{2,1,0:T(8,128)(2,1)} %bitcast.251), calls=%async_computation.2 | async-start | bytes 4194304 | tf_op jit(solution)/shard_map/all_to_all | solution.py:194
  63.0 117.7 %all-gather.10.cloned.1.call-start = ((), (), s32[]{:S(2)}) async-start(), calls=%async_computation.10 | async-start | bytes 3072000 | tf_op jit(solution)/shard_map/all_gather | solution.py:234
  64.0 74.7 %copy-start.59 = (f32[64,64]{1,0:T(8,128)}, f32[64,64]{1,0:T(8,128)S(1)}, u32[]{:S(2)}) copy-start(f32[64,64]{1,0:T(8,128)S(1)} %gather_fusion.1) | copy-start | bytes 49156
  129.7 27.3 %copy-start.3 = (bf16[512,960]{0,1:T(8,128)(2,1)}, bf16[512,960]{0,1:T(8,128)(2,1)S(1)}, u32[]{:S(2)}) copy-start(bf16[512,960]{0,1:T(8,128)(2,1)S(1)} %get-tuple-element.228) | copy-start | bytes 2949124
  130.4 275.0 %reduce-scatter.2.cloned.1.call-start = ((), (), s32[]{:S(2)}) async-start(), calls=%async_computation.8 | async-start | bytes 3072000 | tf_op jit(solution)/shard_map/reduce_scatter | solution.py:400
  159.6 22.6 %copy-start.92 = (f32[64]{0:T(128)}, f32[64]{0:T(128)S(1)}, u32[]{:S(2)}) copy-start(f32[64]{0:T(128)S(1)} %add_rsqrt_fusion.2) | copy-start | bytes 772
  188.8 2.3 collective-permute-start.3
  194.5 7.0 %collective-permute-start.6 = (bf16[64,1024]{1,0:T(8,128)(2,1)}, bf16[64,1024]{1,0:T(8,128)(2,1)S(1)}, u32[]{:S(2)}, u32[]{:S(2)}) collective-permute-start(bf16[64,1024]{1,0:T(8,128)(2,1)} %get-tuple-element.174), channel_id=1, source_target_pairs={{0,6},{2,4},{4,2},{6,0},{1,7},{3,5},{5,3},{7,1},{8,14},{10,12},{12... | collective-permute-start | bytes 393224 | tf_op jit(solution)/shard_map/ppermute | solution.py:74
  196.9 7.0 %collective-permute-start.5 = (bf16[64,1024]{1,0:T(8,128)(2,1)}, bf16[64,1024]{1,0:T(8,128)(2,1)S(1)}, u32[]{:S(2)}, u32[]{:S(2)}) collective-permute-start(bf16[64,1024]{1,0:T(8,128)(2,1)} %get-tuple-element.175), channel_id=1, source_target_pairs={{0,4},{2,6},{4,0},{6,2},{1,5},{3,7},{5,1},{7,3},{8,12},{10,14},{12... | collective-permute-start | bytes 393224 | tf_op jit(solution)/shard_map/ppermute | solution.py:74
  197.5 7.2 %collective-permute-start.4 = (bf16[64,1024]{1,0:T(8,128)(2,1)}, bf16[64,1024]{1,0:T(8,128)(2,1)}, u32[]{:S(2)}, u32[]{:S(2)}) collective-permute-start(bf16[64,1024]{1,0:T(8,128)(2,1)} %get-tuple-element.173), channel_id=1, source_target_pairs={{0,2},{2,0},{4,6},{6,4},{1,3},{3,1},{5,7},{7,5},{8,10},{10,8},{12,... | collective-permute-start | bytes 393224 | tf_op jit(solution)/shard_map/ppermute | solution.py:74
  206.0 31.7 %copy-start.90 = (f32[64]{0:T(128)}, f32[64]{0:T(128)S(1)}, u32[]{:S(2)}) copy-start(f32[64]{0:T(128)S(1)} %add_rsqrt_fusion.1) | copy-start | bytes 772
  221.9 12.1 %collective-permute-start.7 = (bf16[4,64,1024]{2,1,0:T(8,128)(2,1)S(1)}, bf16[4,64,1024]{2,1,0:T(8,128)(2,1)S(1)}, u32[]{:S(2)}, u32[]{:S(2)}) collective-permute-start(bf16[4,64,1024]{2,1,0:T(8,128)(2,1)S(1)} %bitcast.279), channel_id=1, source_target_pairs={{0,2},{2,0},{1,3},{3,1},{4,6},{6,4},{5,7},{7,5},{8,10},{10,8},{9,1... | collective-permute-start | bytes 1572872 | tf_op jit(solution)/shard_map/ppermute | solution.py:74
  223.5 12.8 %collective-permute-start.8 = (bf16[4,64,1024]{2,1,0:T(8,128)(2,1)S(1)}, bf16[4,64,1024]{2,1,0:T(8,128)(2,1)S(1)}, u32[]{:S(2)}, u32[]{:S(2)}) collective-permute-start(bf16[4,64,1024]{2,1,0:T(8,128)(2,1)S(1)} %bitcast.280), channel_id=1, source_target_pairs={{0,4},{4,0},{1,5},{5,1},{2,6},{6,2},{3,7},{7,3},{8,12},{12,8},{9,1... | collective-permute-start | bytes 1572872 | tf_op jit(solution)/shard_map/ppermute | solution.py:74
  234.0 6.8 %collective-permute-start.9 = (bf16[2,64,1024]{2,1,0:T(8,128)(2,1)S(1)}, bf16[2,64,1024]{2,1,0:T(8,128)(2,1)S(1)}, u32[]{:S(2)}, u32[]{:S(2)}) collective-permute-start(bf16[2,64,1024]{2,1,0:T(8,128)(2,1)S(1)} %slice.526), channel_id=1, source_target_pairs={{0,4},{4,0},{1,5},{5,1},{2,6},{6,2},{3,7},{7,3},{8,12},{12,8},{9,1... | collective-permute-start | bytes 786440 | tf_op jit(solution)/shard_map/ppermute | solution.py:74
  236.3 6.4 %collective-permute-start.10 = (bf16[2,64,1024]{2,1,0:T(8,128)(2,1)S(1)}, bf16[2,64,1024]{2,1,0:T(8,128)(2,1)S(1)}, u32[]{:S(2)}, u32[]{:S(2)}) collective-permute-start(bf16[2,64,1024]{2,1,0:T(8,128)(2,1)S(1)} %slice.527), channel_id=1, source_target_pairs={{0,2},{2,0},{1,3},{3,1},{4,6},{6,4},{5,7},{7,5},{8,10},{10,8},{9,1... | collective-permute-start | bytes 786440 | tf_op jit(solution)/shard_map/ppermute | solution.py:74
  243.5 7.5 %collective-permute-start.11 = (bf16[1024,1024]{1,0:T(8,128)(2,1)}, bf16[1024,1024]{1,0:T(8,128)(2,1)}, u32[]{:S(2)}, u32[]{:S(2)}) collective-permute-start(bf16[1024,1024]{1,0:T(8,128)(2,1)} %bitcast.37), channel_id=1, source_target_pairs={{0,1},{1,0},{2,3},{3,2},{4,5},{5,4},{6,7},{7,6},{8,9},{9,8},{10,11... | collective-permute-start | bytes 6291464 | tf_op jit(solution)/shard_map/ppermute | solution.py:74
  244.3 11.6 %copy-start.81 = (s32[1024]{0:T(1024)}, s32[1024]{0:T(1024)S(1)}, u32[]{:S(2)}) copy-start(s32[1024]{0:T(1024)S(1)} %sub.293) | copy-start | bytes 12292
  255.9 21.0 %copy-start.20 = (f32[1024,1000]{0,1:T(8,128)}, f32[1024,1000]{0,1:T(8,128)S(1)}, u32[]{:S(2)}) copy-start(f32[1024,1000]{0,1:T(8,128)S(1)} %get-tuple-element.234) | copy-start | bytes 12288004
  257.4 1.4 collective-permute-start.12
  258.9 4.0 collective-permute-start.13
  263.1 4.0 collective-permute-start.14
  267.2 4.0 collective-permute-start.15
  271.3 10.8 %copy-start.71 = (f32[1,2048]{1,0:T(1,128)}, f32[1,2048]{1,0:T(1,128)S(1)}, u32[]{:S(2)}) copy-start(f32[1,2048]{1,0:T(1,128)S(1)} %get-tuple-element.196) | copy-start | bytes 24580
  271.3 4.9 collective-permute-start.16
  282.1 5.8 %collective-permute-start.17 = (bf16[1024,1024]{1,0:T(8,128)(2,1)}, bf16[1024,1024]{1,0:T(8,128)(2,1)}, u32[]{:S(2)}, u32[]{:S(2)}) collective-permute-start(bf16[1024,1024]{1,0:T(8,128)(2,1)} %convolution_convert_fusion), channel_id=1, source_target_pairs={{0,1},{1,0},{2,3},{3,2},{4,5},{5,4},{6,7},{7,6},{8,9},{9,8},{10,11... | collective-permute-start | bytes 6291464 | tf_op jit(solution)/shard_map/ppermute | solution.py:74
  292.9 15.8 %collective-permute-start.20 = (bf16[4,64,1024]{2,1,0:T(8,128)(2,1)S(1)}, bf16[4,64,1024]{2,1,0:T(8,128)(2,1)S(1)}, u32[]{:S(2)}, u32[]{:S(2)}) collective-permute-start(bf16[4,64,1024]{2,1,0:T(8,128)(2,1)S(1)} %bitcast.306), channel_id=1, source_target_pairs={{0,6},{2,4},{4,2},{6,0},{1,7},{3,5},{5,3},{7,1},{8,14},{10,12},{12... | collective-permute-start | bytes 1572872 | tf_op jit(solution)/shard_map/ppermute | solution.py:74
  294.5 24.8 %collective-permute-start.19 = (bf16[4,64,1024]{2,1,0:T(8,128)(2,1)S(1)}, bf16[4,64,1024]{2,1,0:T(8,128)(2,1)S(1)}, u32[]{:S(2)}, u32[]{:S(2)}) collective-permute-start(bf16[4,64,1024]{2,1,0:T(8,128)(2,1)S(1)} %bitcast.305), channel_id=1, source_target_pairs={{0,4},{2,6},{4,0},{6,2},{1,5},{3,7},{5,1},{7,3},{8,12},{10,14},{12... | collective-permute-start | bytes 1572872 | tf_op jit(solution)/shard_map/ppermute | solution.py:74
  294.9 24.4 %collective-permute-start.18 = (bf16[4,64,1024]{2,1,0:T(8,128)(2,1)S(1)}, bf16[4,64,1024]{2,1,0:T(8,128)(2,1)S(1)}, u32[]{:S(2)}, u32[]{:S(2)}) collective-permute-start(bf16[4,64,1024]{2,1,0:T(8,128)(2,1)S(1)} %bitcast.304), channel_id=1, source_target_pairs={{0,2},{2,0},{4,6},{6,4},{1,3},{3,1},{5,7},{7,5},{8,10},{10,8},{12,... | collective-permute-start | bytes 1572872 | tf_op jit(solution)/shard_map/ppermute | solution.py:74
  319.8 8.3 %collective-permute-start.23 = (bf16[64,1024]{1,0:T(8,128)(2,1)S(1)}, bf16[64,1024]{1,0:T(8,128)(2,1)S(1)}, u32[]{:S(2)}, u32[]{:S(2)}) collective-permute-start(bf16[64,1024]{1,0:T(8,128)(2,1)S(1)} %get-tuple-element.171), channel_id=1, source_target_pairs={{0,24},{8,16},{16,8},{24,0},{1,25},{9,17},{17,9},{25,1},{2,26},{10... | collective-permute-start | bytes 393224 | tf_op jit(solution)/shard_map/ppermute | solution.py:74
  322.8 11.2 %collective-permute-start.22 = (bf16[64,1024]{1,0:T(8,128)(2,1)S(1)}, bf16[64,1024]{1,0:T(8,128)(2,1)S(1)}, u32[]{:S(2)}, u32[]{:S(2)}) collective-permute-start(bf16[64,1024]{1,0:T(8,128)(2,1)S(1)} %get-tuple-element.172), channel_id=1, source_target_pairs={{0,16},{8,24},{16,0},{24,8},{1,17},{9,25},{17,1},{25,9},{2,18},{10... | collective-permute-start | bytes 393224 | tf_op jit(solution)/shard_map/ppermute | solution.py:74
  322.8 11.3 %copy-start.91 = (f32[64]{0:T(128)S(1)}, f32[64]{0:T(128)}, u32[]{:S(2)}) copy-start(f32[64]{0:T(128)} %copy-done.90) | copy-start | bytes 772
  322.8 11.2 %collective-permute-start.21 = (bf16[64,1024]{1,0:T(8,128)(2,1)S(1)}, bf16[64,1024]{1,0:T(8,128)(2,1)S(1)}, u32[]{:S(2)}, u32[]{:S(2)}) collective-permute-start(bf16[64,1024]{1,0:T(8,128)(2,1)S(1)} %get-tuple-element.170), channel_id=1, source_target_pairs={{0,8},{8,0},{16,24},{24,16},{1,9},{9,1},{17,25},{25,17},{2,10},{10... | collective-permute-start | bytes 393224 | tf_op jit(solution)/shard_map/ppermute | solution.py:74
  327.1 18.9 %copy-start.38 = (f32[512,640]{1,0:T(8,128)S(1)}, f32[512,640]{1,0:T(8,128)}, u32[]{:S(2)}) copy-start(f32[512,640]{1,0:T(8,128)} %copy-done.37) | copy-start | bytes 3932164
  327.1 18.9 %copy-start.40 = (bf16[320,640]{1,0:T(8,128)(2,1)S(1)}, bf16[320,640]{1,0:T(8,128)(2,1)}, u32[]{:S(2)}) copy-start(bf16[320,640]{1,0:T(8,128)(2,1)} %copy-done.39) | copy-start | bytes 1228804
  327.1 18.9 %copy-start.55 = (bf16[160,320]{1,0:T(8,128)(2,1)S(1)}, bf16[160,320]{1,0:T(8,128)(2,1)}, u32[]{:S(2)}) copy-start(bf16[160,320]{1,0:T(8,128)(2,1)} %copy-done.54) | copy-start | bytes 307204
  327.1 18.9 %copy-start.57 = (bf16[160,320]{1,0:T(8,128)(2,1)S(1)}, bf16[160,320]{1,0:T(8,128)(2,1)}, u32[]{:S(2)}) copy-start(bf16[160,320]{1,0:T(8,128)(2,1)} %copy-done.56) | copy-start | bytes 307204
  348.3 2.0 collective-permute-start.24
  352.0 7.5 %collective-permute-start.27 = (bf16[64,1024]{1,0:T(8,128)(2,1)S(1)}, bf16[64,1024]{1,0:T(8,128)(2,1)}, u32[]{:S(2)}, u32[]{:S(2)}) collective-permute-start(bf16[64,1024]{1,0:T(8,128)(2,1)S(1)} %get-tuple-element.168), channel_id=1, source_target_pairs={{0,6},{2,4},{4,2},{6,0},{1,7},{3,5},{5,3},{7,1},{8,14},{10,12},{12... | collective-permute-start | bytes 393224 | tf_op jit(solution)/shard_map/ppermute | solution.py:74
  353.6 8.1 %collective-permute-start.26 = (bf16[64,1024]{1,0:T(8,128)(2,1)S(1)}, bf16[64,1024]{1,0:T(8,128)(2,1)}, u32[]{:S(2)}, u32[]{:S(2)}) collective-permute-start(bf16[64,1024]{1,0:T(8,128)(2,1)S(1)} %get-tuple-element.169), channel_id=1, source_target_pairs={{0,4},{2,6},{4,0},{6,2},{1,5},{3,7},{5,1},{7,3},{8,12},{10,14},{12... | collective-permute-start | bytes 393224 | tf_op jit(solution)/shard_map/ppermute | solution.py:74
  354.4 7.3 %collective-permute-start.25 = (bf16[64,1024]{1,0:T(8,128)(2,1)S(1)}, bf16[64,1024]{1,0:T(8,128)(2,1)}, u32[]{:S(2)}, u32[]{:S(2)}) collective-permute-start(bf16[64,1024]{1,0:T(8,128)(2,1)S(1)} %get-tuple-element.167), channel_id=1, source_target_pairs={{0,2},{2,0},{4,6},{6,4},{1,3},{3,1},{5,7},{7,5},{8,10},{10,8},{12,... | collective-permute-start | bytes 393224 | tf_op jit(solution)/shard_map/ppermute | solution.py:74
  398.7 20.9 %all-to-all-start.3 = ((bf16[32,8,960]{2,1,0:T(8,128)(2,1)}), bf16[32,8,960]{2,1,0:T(8,128)(2,1)}, u32[]{:S(2)}, u32[]{:S(2)}) async-start(bf16[32,8,960]{2,1,0:T(8,128)(2,1)} %bitcast.92), calls=%async_computation.4 | async-start | bytes 1048576 | tf_op jit(solution)/shard_map/all_to_all | solution.py:194
  425.5 8.7 %collective-permute-start.28 = (bf16[4,352,960]{2,1,0:T(8,128)(2,1)}, bf16[4,352,960]{2,1,0:T(8,128)(2,1)}, u32[]{:S(2)}, u32[]{:S(2)}) collective-permute-start(bf16[4,352,960]{2,1,0:T(8,128)(2,1)} %get-tuple-element.138), channel_id=1, source_target_pairs={{0,1},{1,0},{2,3},{3,2},{4,5},{5,4},{6,7},{7,6},{8,9},{9,8},{10,11... | collective-permute-start | bytes 8110088 | tf_op jit(solution)/shard_map/ppermute | solution.py:74
  425.5 56.8 %all-to-all-start.4 = ((bf16[32,24,960]{2,1,0:T(8,128)(2,1)}), bf16[32,24,960]{2,1,0:T(8,128)(2,1)}, u32[]{:S(2)}, u32[]{:S(2)}) async-start(bf16[32,24,960]{2,1,0:T(8,128)(2,1)} %bitcast.93), calls=%async_computation.5 | async-start | bytes 3145728 | tf_op jit(solution)/shard_map/all_to_all | solution.py:194
  438.2 28.9 %collective-permute-start.31 = (bf16[2,176,960]{2,1,0:T(8,128)(2,1)}, bf16[2,176,960]{2,1,0:T(8,128)(2,1)}, u32[]{:S(2)}, u32[]{:S(2)}) collective-permute-start(bf16[2,176,960]{2,1,0:T(8,128)(2,1)} %fusion.51), channel_id=1, source_target_pairs={{0,4},{4,0},{1,5},{5,1},{2,6},{6,2},{3,7},{7,3},{8,12},{12,8},{9,1... | collective-permute-start | bytes 2027528 | tf_op jit(solution)/shard_map/ppermute | solution.py:74
  440.8 29.5 %collective-permute-start.29 = (bf16[2,176,960]{2,1,0:T(8,128)(2,1)}, bf16[2,176,960]{2,1,0:T(8,128)(2,1)}, u32[]{:S(2)}, u32[]{:S(2)}) collective-permute-start(bf16[2,176,960]{2,1,0:T(8,128)(2,1)} %fusion.50), channel_id=1, source_target_pairs={{0,2},{2,0},{1,3},{3,1},{4,6},{6,4},{5,7},{7,5},{8,10},{10,8},{9,1... | collective-permute-start | bytes 2027528 | tf_op jit(solution)/shard_map/ppermute | solution.py:74
  469.1 10.4 %collective-permute-start.32 = (bf16[176,960]{1,0:T(8,128)(2,1)S(1)}, bf16[176,960]{1,0:T(8,128)(2,1)S(1)}, u32[]{:S(2)}, u32[]{:S(2)}) collective-permute-start(bf16[176,960]{1,0:T(8,128)(2,1)S(1)} %fusion.70), channel_id=1, source_target_pairs={{0,2},{2,0},{1,3},{3,1},{4,6},{6,4},{5,7},{7,5},{8,10},{10,8},{9,1... | collective-permute-start | bytes 1013768 | tf_op jit(solution)/shard_map/ppermute | solution.py:74
  471.9 10.2 %collective-permute-start.30 = (bf16[176,960]{1,0:T(8,128)(2,1)S(1)}, bf16[176,960]{1,0:T(8,128)(2,1)S(1)}, u32[]{:S(2)}, u32[]{:S(2)}) collective-permute-start(bf16[176,960]{1,0:T(8,128)(2,1)S(1)} %fusion.69), channel_id=1, source_target_pairs={{0,4},{4,0},{1,5},{5,1},{2,6},{6,2},{3,7},{7,3},{8,12},{12,8},{9,1... | collective-permute-start | bytes 1013768 | tf_op jit(solution)/shard_map/ppermute | solution.py:74
  483.1 18.7 %collective-permute-start.35 = (bf16[88,960]{1,0:T(8,128)(2,1)}, bf16[88,960]{1,0:T(8,128)(2,1)}, u32[]{:S(2)}, u32[]{:S(2)}) collective-permute-start(bf16[88,960]{1,0:T(8,128)(2,1)} %get-tuple-element.149), channel_id=1, source_target_pairs={{0,24},{8,16},{16,8},{24,0},{1,25},{9,17},{17,9},{25,1},{2,26},{10... | collective-permute-start | bytes 506888 | tf_op jit(solution)/shard_map/ppermute | solution.py:74
  483.1 18.7 %collective-permute-start.34 = (bf16[88,960]{1,0:T(8,128)(2,1)}, bf16[88,960]{1,0:T(8,128)(2,1)}, u32[]{:S(2)}, u32[]{:S(2)}) collective-permute-start(bf16[88,960]{1,0:T(8,128)(2,1)} %get-tuple-element.150), channel_id=1, source_target_pairs={{0,16},{8,24},{16,0},{24,8},{1,17},{9,25},{17,1},{25,9},{2,18},{10... | collective-permute-start | bytes 506888 | tf_op jit(solution)/shard_map/ppermute | solution.py:74
  484.6 17.3 %collective-permute-start.33 = (bf16[88,960]{1,0:T(8,128)(2,1)}, bf16[88,960]{1,0:T(8,128)(2,1)}, u32[]{:S(2)}, u32[]{:S(2)}) collective-permute-start(bf16[88,960]{1,0:T(8,128)(2,1)} %get-tuple-element.148), channel_id=1, source_target_pairs={{0,8},{8,0},{16,24},{24,16},{1,9},{9,1},{17,25},{25,17},{2,10},{10... | collective-permute-start | bytes 506888 | tf_op jit(solution)/shard_map/ppermute | solution.py:74
  488.5 17.1 %all-to-all-start.5 = ((bf16[8,60,640]{2,1,0:T(8,128)(2,1)}), bf16[8,60,640]{2,1,0:T(8,128)(2,1)S(1)}, u32[]{:S(2)}, u32[]{:S(2)}) async-start(bf16[8,60,640]{2,1,0:T(8,128)(2,1)} %reshape.650), calls=%async_computation.6 | async-start | bytes 1310720 | tf_op jit(solution)/shard_map/all_to_all | solution.py:441
  503.7 17.1 %copy-start.41 = (bf16[88,960]{1,0:T(8,128)(2,1)}, bf16[88,960]{1,0:T(8,128)(2,1)S(1)}, u32[]{:S(2)}) copy-start(bf16[88,960]{1,0:T(8,128)(2,1)S(1)} %get-tuple-element.91) | copy-start | bytes 506884
  506.9 14.8 %all-to-all-start.6 = ((f32[32,1,2]{2,1,0:T(1,128)}), f32[32,1,2]{2,1,0:T(1,128)S(1)}, u32[]{:S(2)}, u32[]{:S(2)}) async-start(f32[32,1,2]{2,1,0:T(1,128)} %broadcast_in_dim.71), calls=%async_computation.7 | async-start | bytes 32768 | tf_op jit(solution)/shard_map/all_to_all | solution.py:410
  515.1 18.2 %collective-permute-start.36 = (bf16[88,960]{1,0:T(8,128)(2,1)S(1)}, bf16[88,960]{1,0:T(8,128)(2,1)S(1)}, u32[]{:S(2)}, u32[]{:S(2)}) collective-permute-start(bf16[88,960]{1,0:T(8,128)(2,1)S(1)} %get-tuple-element.91), channel_id=1, source_target_pairs={{8,0},{9,1},{10,2},{11,3},{12,4},{13,5},{14,6},{15,7}} | collective-permute-start | bytes 506888 | tf_op jit(solution)/shard_map/ppermute | solution.py:453
  515.8 17.5 %collective-permute-start.37 = (bf16[88,960]{1,0:T(8,128)(2,1)S(1)}, bf16[88,960]{1,0:T(8,128)(2,1)S(1)}, u32[]{:S(2)}, u32[]{:S(2)}) collective-permute-start(bf16[88,960]{1,0:T(8,128)(2,1)S(1)} %get-tuple-element.91), channel_id=1, source_target_pairs={{16,0},{17,1},{18,2},{19,3},{20,4},{21,5},{22,6},{23,7}} | collective-permute-start | bytes 506888 | tf_op jit(solution)/shard_map/ppermute | solution.py:453
  516.5 16.9 %collective-permute-start.38 = (bf16[88,960]{1,0:T(8,128)(2,1)S(1)}, bf16[88,960]{1,0:T(8,128)(2,1)S(1)}, u32[]{:S(2)}, u32[]{:S(2)}) collective-permute-start(bf16[88,960]{1,0:T(8,128)(2,1)S(1)} %get-tuple-element.91), channel_id=1, source_target_pairs={{24,0},{25,1},{26,2},{27,3},{28,4},{29,5},{30,6},{31,7}} | collective-permute-start | bytes 506888 | tf_op jit(solution)/shard_map/ppermute | solution.py:453
  523.0 11.3 %copy-start.42 = (bf16[88,960]{1,0:T(8,128)(2,1)S(1)}, bf16[88,960]{1,0:T(8,128)(2,1)}, u32[]{:S(2)}) copy-start(bf16[88,960]{1,0:T(8,128)(2,1)} %copy-done.41) | copy-start | bytes 506884
  540.9 6.7 %collective-permute-start.39 = (bf16[2880]{0:T(1024)(128)(2,1)S(1)}, bf16[2880]{0:T(1024)(128)(2,1)S(1)}, u32[]{:S(2)}, u32[]{:S(2)}) collective-permute-start(bf16[2880]{0:T(1024)(128)(2,1)S(1)} %slice.600), channel_id=1, source_target_pairs={{0,1},{1,2},{2,3},{3,4},{4,5},{5,6},{6,7},{7,8},{8,9},{9,10},{10,1... | collective-permute-start | bytes 17288 | tf_op jit(solution)/shard_map/ppermute | solution.py:476
  (83 other events, 289.9 us)
Sparse Core Ops, SparseCore 0:
  54.7 62.3 all-gather.7
  130.6 50.1 all-gather.9
  357.5 47.9 reduce-scatter.1

commit v14 on v12

--- a/solution.py
+++ b/solution.py
@@ -406,9 +406,14 @@
     grad_q = dot(h_pick, d_q, 0, 0).astype(bf16)
     grad_kv = dot(h_attn, d_kv, 0, 0).astype(bf16)
 
-    def norm_of(squares):
+    def begun(squares):
         sums = jnp.stack([squares, my_loss])
-        for axis, bit, size in [("c", 1, 2), ("x", 1, 2), ("y", 1, 2)] + [("q", 1 << k, rows_q) for k in range(rows_q.bit_length() - 1)]:
+        for axis in ("c", "x"):
+            sums = sums + flip(sums, axis, 1, 2)
+        return sums
+
+    def norm_of(sums):
+        for axis, bit, size in [("y", 1, 2)] + [("q", 1 << k, rows_q) for k in range(rows_q.bit_length() - 1)]:
             sums = sums + flip(sums, axis, bit, size)
         grad_norm = jnp.sqrt(sums[0])
         limit = CLIP_C / math.sqrt(loss_total)
@@ -451,6 +456,7 @@
         table_squares = jnp.sum(table_grad * table_grad)
         quarter = quarter.astype(bf16)
         squares = jnp.sum(quarter.astype(f32) ** 2) + jnp.sum(share.astype(f32) ** 2) + table_squares
+        quarter, sums = lax.optimization_barrier((quarter, begun(squares)))
         quarters = [quarter] + [lax.ppermute(quarter, "q", [(k, 0)]) for k in (1, 2, 3)]
         first = jnp.concatenate(quarters)
         gain_out = first[SHARE : SHARE + 3].reshape(-1)
@@ -459,7 +465,7 @@
         by_share = got.reshape(8, 60, 2, UNIT).transpose(1, 2, 0, 3).reshape(-1)
         mine = jnp.where(q_index == 3, down_unpack(share).reshape(-1), by_share)
         mine = jnp.where(q_index == 0, first, mine)
-        loss, grad_norm, clip_factor = norm_of(squares)
+        loss, grad_norm, clip_factor = norm_of(sums)
         mine, clip_factor = lax.optimization_barrier((mine, clip_factor))
     else:
         table_grad = head_grad
@@ -480,7 +486,7 @@
     layer_grad = lax.dynamic_slice(stream, (drift * me,), (shard,)).astype(f32)
 
     if not aligned:
-        loss, grad_norm, clip_factor = norm_of(jnp.sum(layer_grad * layer_grad) + table_squares)
+        loss, grad_norm, clip_factor = norm_of(begun(jnp.sum(layer_grad * layer_grad) + table_squares))
     flat_new = adamw_step(flat_master, layer_grad, flat_m, flat_v, clip_factor)
     table_new = adamw_step(table_master, table_grad, table_m, table_v, clip_factor)
     return (loss, grad_norm) + flat_new + table_new

time: 573 us -> 581 us (1.014)
    ppermute x38, waiting for transfers between devices: 95.3 us -> 103 us  [flip(): return lax.ppermute(rows, axes, [(i, i ^ bits) for i in range(size)])]
  transfers between devices with their start and end apart: 54 -> 54, of which waited for: 29 -> 30; matrix products, arithmetic and copies ran while one was open for 33% -> 33% of each run, Pallas kernels for 0% -> 0%
where the time goes in v14:
time: 581 us; the launch traced here: 571 us
  waiting for transfers between devices  164 us (28%)
  starting transfers between devices  97.5 us (17%)
  local copies, waits for them, and re-layouts  88.9 us (15%)
  matrix products  88.4 us (15%)
  other arithmetic  74.4 us (13%)
  blocking collectives  36.1 us (6%)
  between operations  21.5 us (4%)
    ppermute x38, waiting for transfers between devices, flip(): return lax.ppermute(rows, axes, [(i, i ^ bits) for i in range(size)])  103 us
    dot_general x37, matrix products, dot(): lax.dot_general(left, right, (((left_dim,), (right_dim,)), ((), ())), pre...  73 us
    all_gather x1, waiting for transfers between devices, local(): level = lax.all_gather(first, PLANE)  50.7 us
    ppermute x38, starting transfers between devices, flip(): return lax.ppermute(rows, axes, [(i, i ^ bits) for i in range(size)])  43.7 us
    all_gather x2, blocking collectives, spread_plane(): return widen(lax.all_gather(rows, PLANE).reshape(-1, D))  22.8 us
    all_to_all x3, starting transfers between devices, exchange(): lax.all_to_all(blocks, ALL, split_axis=0, concat_axis=0, tiled=True)  17.4 us
    unnamed x206, local copies, waits for them, and re-layouts  15.6 us
    mul x2, other arithmetic, adamw_step(): return (new_one, new_two, -RATE * (ratio + DECAY * param))  13.5 us
  transfers between devices with their start and end apart: 54, of which 30 were waited for; matrix products, arithmetic and copies ran while one was open for 33% of the time, Pallas kernels for 0%

profile of v14, /device:TPU:1, one launch (start us, length us, event | category | flops | bytes accessed | tf_op | source)
XLA Modules:
  0.0 571.4 jit_solution(17349850543810838871)
XLA Ops:
  17.9 5.8 %collective-permute-start.1 = (bf16[328,960]{1,0:T(8,128)(2,1)S(1)}, bf16[328,960]{1,0:T(8,128)(2,1)}, u32[]{:S(2)}, u32[]{:S(2)}) collective-permute-start(bf16[328,960]{1,0:T(8,128)(2,1)S(1)} %maximum_maximum_fusion), channel_id=1, source_target_pairs={{0,16},{1,17},{2,18},{3,19},{4,20},{5,21},{6,22},{7,23}} | collective-permute-start | bytes 1889288 | tf_op jit(solution)/shard_map/ppermute | solution.py:220
  23.6 3.7 convert_element_type.330
  28.0 4.2 all-to-all-start
  39.1 5.6 all-to-all-start.1
  44.8 5.2 fusion.24
  50.0 3.9 copy.125
  54.8 9.4 %all-to-all-start.2 = ((bf16[32,32,960]{2,1,0:T(8,128)(2,1)}), bf16[32,32,960]{2,1,0:T(8,128)(2,1)}, u32[]{:S(2)}, u32[]{:S(2)}) async-start(bf16[32,32,960]{2,1,0:T(8,128)(2,1)} %bitcast.248), calls=%async_computation.2 | async-start | bytes 4194304 | tf_op jit(solution)/shard_map/all_to_all | solution.py:194
  68.8 50.7 %all-gather.8.cloned.1.call-done = bf16[2624,960]{1,0:T(8,128)(2,1)} async-done(((bf16[328,960]{1,0:T(8,128)(2,1)}), bf16[2624,960]{1,0:T(8,128)(2,1)}) %all-gather.8.cloned.1.call-update) | async-done | bytes 5038096 | tf_op jit(solution)/shard_map/all_gather | solution.py:226
  122.7 3.0 slice.408
  125.7 2.8 reshape.606
  129.2 3.0 fusion.23
  132.9 2.4 fusion.166
  149.0 2.2 copy.163
  154.5 3.7 fusion.200
  158.2 3.6 convolution_convert_fusion.10
  166.6 11.0 %all-gather.2 = bf16[512,960]{1,0:T(8,128)(2,1)S(1)} all-gather(bf16[64,960]{1,0:T(8,128)(2,1)S(1)} %multiply_convert_fusion.7), channel_id=4, replica_groups=mesh['q'=4,'y'=2,'x'=2,'c'=2] {'y','x','c'}, dimensions={0}, use_global_device_ids=true | all-gather | bytes 1105920 | tf_op jit(solution)/shard_map/all_gather | solution.py:149
  178.7 5.2 all-gather.10.cloned.1.call-done
  202.5 3.7 collective-permute-done.5
  208.3 13.3 %all-gather.3 = bf16[256,1024]{1,0:T(8,128)(2,1)S(1)} all-gather(bf16[64,1024]{1,0:T(8,128)(2,1)S(1)} %pad.31), channel_id=5, replica_groups=mesh['q'=4,'y'=2,'x'=2,'c'=2] {'q'}, dimensions={0}, use_global_device_ids=true | all-gather | bytes 655360 | tf_op jit(solution)/shard_map/all_gather | solution.py:303
  222.8 8.6 %collective-permute-done.7 = bf16[4,64,1024]{2,1,0:T(8,128)(2,1)S(1)} collective-permute-done((bf16[4,64,1024]{2,1,0:T(8,128)(2,1)S(1)}, bf16[4,64,1024]{2,1,0:T(8,128)(2,1)S(1)}, u32[]{:S(2)}, u32[]{:S(2)}) %collective-permute-start.7) | collective-permute-done | bytes 524320 | tf_op jit(solution)/shard_map/ppermute | solution.py:74
  235.2 4.1 collective-permute-done.9
  240.7 6.1 %collective-permute-start.11 = (bf16[1024,1024]{1,0:T(8,128)(2,1)}, bf16[1024,1024]{1,0:T(8,128)(2,1)}, u32[]{:S(2)}, u32[]{:S(2)}) collective-permute-start(bf16[1024,1024]{1,0:T(8,128)(2,1)} %bitcast.37), channel_id=1, source_target_pairs={{0,1},{1,0},{2,3},{3,2},{4,5},{5,4},{6,7},{7,6},{8,9},{9,8},{10,11... | collective-permute-start | bytes 6291464 | tf_op jit(solution)/shard_map/ppermute | solution.py:74
  247.8 4.5 fusion.202
  255.4 3.9 fusion.201
  262.3 2.8 collective-permute-done.13
  265.3 2.8 collective-permute-done.14
  268.2 2.8 collective-permute-done.15
  271.7 3.3 collective-permute-done.16
  275.6 5.1 convolution_convert_fusion
  280.8 4.8 collective-permute-start.17
  285.6 5.6 fusion.169
  291.3 4.8 fusion.203
  298.9 4.3 fusion.170
  303.3 7.3 %collective-permute-done.20 = bf16[4,64,1024]{2,1,0:T(8,128)(2,1)S(1)} collective-permute-done((bf16[4,64,1024]{2,1,0:T(8,128)(2,1)S(1)}, bf16[4,64,1024]{2,1,0:T(8,128)(2,1)S(1)}, u32[]{:S(2)}, u32[]{:S(2)}) %collective-permute-start.20) | collective-permute-done | bytes 524320 | tf_op jit(solution)/shard_map/ppermute | solution.py:74
  310.6 10.4 %collective-permute-done.19 = bf16[4,64,1024]{2,1,0:T(8,128)(2,1)S(1)} collective-permute-done((bf16[4,64,1024]{2,1,0:T(8,128)(2,1)S(1)}, bf16[4,64,1024]{2,1,0:T(8,128)(2,1)S(1)}, u32[]{:S(2)}, u32[]{:S(2)}) %collective-permute-start.19) | collective-permute-done | bytes 524320 | tf_op jit(solution)/shard_map/ppermute | solution.py:74
  322.7 2.3 collective-permute-start.21
  325.0 2.9 slice_add_fusion
  327.9 6.6 %collective-permute-done.22 = bf16[64,1024]{1,0:T(8,128)(2,1)S(1)} collective-permute-done((bf16[64,1024]{1,0:T(8,128)(2,1)S(1)}, bf16[64,1024]{1,0:T(8,128)(2,1)S(1)}, u32[]{:S(2)}, u32[]{:S(2)}) %collective-permute-start.22) | collective-permute-done | bytes 131104 | tf_op jit(solution)/shard_map/ppermute | solution.py:74
  335.4 11.8 %all-gather.4 = bf16[512,960]{1,0:T(8,128)(2,1)S(1)} all-gather(bf16[64,960]{1,0:T(8,128)(2,1)S(1)} %fusion.164), channel_id=6, replica_groups=mesh['q'=4,'y'=2,'x'=2,'c'=2] {'y','x','c'}, dimensions={0}, use_global_device_ids=true | all-gather | bytes 1105920 | tf_op jit(solution)/shard_map/all_gather | solution.py:149
  359.7 3.4 collective-permute-done.26
  378.8 3.3 convolution_convert_fusion.9
  387.4 3.0 fusion.14
  397.4 2.7 copy.149
  400.2 3.8 all-to-all-start.3
  403.9 3.2 reduce-scatter.2.cloned.1.call-done
  411.1 3.2 reshape.636
  415.1 6.2 %fusion.2 = bf16[8,352,960]{2,1,0:T(8,128)(2,1)} fusion(bf16[1,3,960]{2,1,0:T(4,128)(2,1)S(1)} %copy-done.74, bf16[3,320,960]{2,1,0:T(8,128)(2,1)S(1)} %bitcast.249, bf16[5,128,960]{2,1,0:T(8,128)(2,1)S(1)} %reshape.636, bf16[5,192,960]{2,1,0:T(8,128)(2,1)S(1)} %bitcast.250), kind=kLoop, calls=%fused_computation.7 | loop fusion | flops 27033600 | bytes 10327680 | tf_op jit(solution)/shard_map/concatenate | solution.py:427
  421.3 5.9 %constant_dynamic-slice_fusion.4 = (bf16[4,1,352,960]{3,2,1,0:T(8,128)(2,1)}, bf16[4,352,960]{2,1,0:T(8,128)(2,1)}) fusion(bf16[4,2,352,960]{3,2,1,0:T(8,128)(2,1)} %bitcast.239, s32[]{:T(128)S(6)} %select_n.259, s32[]{:T(128)S(6)} %select_n.260), kind=kLoop, calls=%fused_computation.290 | loop fusion | bytes 10813448 | tf_op jit(solution)/shard_map/jit(dynamic_index_in_dim)/dynamic_slice | solution.py:429
  428.2 4.3 all-to-all-start.4
  434.6 2.6 fusion.187
  443.9 23.4 %collective-permute-done.31 = bf16[2,176,960]{2,1,0:T(8,128)(2,1)} collective-permute-done((bf16[2,176,960]{2,1,0:T(8,128)(2,1)}, bf16[2,176,960]{2,1,0:T(8,128)(2,1)}, u32[]{:S(2)}, u32[]{:S(2)}) %collective-permute-start.31) | collective-permute-done | bytes 675872 | tf_op jit(solution)/shard_map/ppermute | solution.py:74
  471.1 3.8 fusion.50
  474.9 3.1 collective-permute-done.32
  479.9 4.9 collective-permute-start.35
  485.2 3.5 fusion.5
  489.0 4.1 multiply_reduce_fusion
  494.7 3.7 collective-permute-done.34
  513.8 4.9 all-to-all-start.5
  521.7 4.3 collective-permute-done.38
  526.0 2.7 collective-permute-done.39
  528.8 3.0 collective-permute-start.40
  541.3 7.5 %collective-permute-start.44 = (bf16[2880]{0:T(1024)(128)(2,1)S(1)}, bf16[2880]{0:T(1024)(128)(2,1)S(1)}, u32[]{:S(2)}, u32[]{:S(2)}) collective-permute-start(bf16[2880]{0:T(1024)(128)(2,1)S(1)} %slice.503), channel_id=1, source_target_pairs={{0,1},{1,2},{2,3},{3,4},{4,5},{5,6},{6,7},{7,8},{8,9},{9,10},{10,1... | collective-permute-start | bytes 17288 | tf_op jit(solution)/shard_map/ppermute | solution.py:482
  548.8 10.3 %add_multiply_fusion = (f32[1000,960]{0,1:T(8,128)}, f32[1000,960]{0,1:T(8,128)}, f32[1000,960]{0,1:T(8,128)}) fusion(f32[1000,960]{0,1:T(8,128)} %param.20, f32[1000,960]{0,1:T(8,128)} %get-tuple-element.105, f32[]{:T(128)S(6)} %div.148, f32[1000,960]{0,1:T(8,128)} %param.22, f32[1000,960]{0,1:T(8,128)} %param.21), kind=kLoop, calls=%fused_computation.21 | loop fusion | flops 14400000 | bytes 26880004 | tf_op jit(solution)/shard_map/mul | solution.py:107
  559.2 3.2 add_multiply_fusion.1
  (505 shorter events, 178.8 us)
Async XLA Ops:
  8.5 5.8 %collective-permute-start = (bf16[2880]{0:T(1024)(128)(2,1)S(1)}, bf16[2880]{0:T(1024)(128)(2,1)S(1)}, u32[]{:S(2)}, u32[]{:S(2)}) collective-permute-start(bf16[2880]{0:T(1024)(128)(2,1)S(1)} %slice.510), channel_id=1, source_target_pairs={{1,0},{2,1},{3,2},{4,3},{5,4},{6,5},{7,6},{8,7},{9,8},{10,9},{11,1... | collective-permute-start | bytes 17288 | tf_op jit(solution)/shard_map/ppermute | solution.py:204
  17.9 17.6 %collective-permute-start.1 = (bf16[328,960]{1,0:T(8,128)(2,1)S(1)}, bf16[328,960]{1,0:T(8,128)(2,1)}, u32[]{:S(2)}, u32[]{:S(2)}) collective-permute-start(bf16[328,960]{1,0:T(8,128)(2,1)S(1)} %maximum_maximum_fusion), channel_id=1, source_target_pairs={{0,16},{1,17},{2,18},{3,19},{4,20},{5,21},{6,22},{7,23}} | collective-permute-start | bytes 1889288 | tf_op jit(solution)/shard_map/ppermute | solution.py:220
  28.0 11.1 %all-to-all-start = ((s32[32,1,96]{2,1,0:T(1,128)}), s32[32,1,96]{2,1,0:T(1,128)S(1)}, u32[]{:S(2)}, u32[]{:S(2)}) async-start(s32[32,1,96]{2,1,0:T(1,128)} %bitcast), calls=%async_computation | async-start | bytes 32768 | tf_op jit(solution)/shard_map/all_to_all | solution.py:218
  36.6 17.2 %collective-permute-start.2 = (bf16[328,960]{1,0:T(8,128)(2,1)S(1)}, bf16[328,960]{1,0:T(8,128)(2,1)S(1)}, u32[]{:S(2)}, u32[]{:S(2)}) collective-permute-start(bf16[328,960]{1,0:T(8,128)(2,1)S(1)} %broadcast_select_fusion), channel_id=1, source_target_pairs={{0,8},{16,24},{1,9},{17,25},{2,10},{18,26},{3,11},{19,27},{4,12},{... | collective-permute-start | bytes 1889288 | tf_op jit(solution)/shard_map/ppermute | solution.py:222
  39.1 15.7 %all-to-all-start.1 = ((bf16[8,60,640]{2,1,0:T(8,128)(2,1)}), bf16[8,60,640]{2,1,0:T(8,128)(2,1)S(1)}, u32[]{:S(2)}, u32[]{:S(2)}) async-start(bf16[8,60,640]{2,1,0:T(8,128)(2,1)} %reshape.694), calls=%async_computation.1 | async-start | bytes 1310720 | tf_op jit(solution)/shard_map/all_to_all | solution.py:212
  44.7 74.8 %all-gather.8.cloned.1.call-start = ((), (), s32[]{:S(2)}) async-start(), calls=%async_computation.8 | async-start | bytes 6045696 | tf_op jit(solution)/shard_map/all_gather | solution.py:226
  54.8 74.3 %all-to-all-start.2 = ((bf16[32,32,960]{2,1,0:T(8,128)(2,1)}), bf16[32,32,960]{2,1,0:T(8,128)(2,1)}, u32[]{:S(2)}, u32[]{:S(2)}) async-start(bf16[32,32,960]{2,1,0:T(8,128)(2,1)} %bitcast.248), calls=%async_computation.2 | async-start | bytes 4194304 | tf_op jit(solution)/shard_map/all_to_all | solution.py:194
  64.2 119.7 %all-gather.10.cloned.1.call-start = ((), (), s32[]{:S(2)}) async-start(), calls=%async_computation.9 | async-start | bytes 3072000 | tf_op jit(solution)/shard_map/all_gather | solution.py:234
  65.2 75.7 %copy-start.56 = (f32[64,64]{1,0:T(8,128)}, f32[64,64]{1,0:T(8,128)S(1)}, u32[]{:S(2)}) copy-start(f32[64,64]{1,0:T(8,128)S(1)} %gather_fusion.1) | copy-start | bytes 49156
  132.1 31.0 %copy-start.3 = (bf16[512,960]{0,1:T(8,128)(2,1)}, bf16[512,960]{0,1:T(8,128)(2,1)S(1)}, u32[]{:S(2)}) copy-start(bf16[512,960]{0,1:T(8,128)(2,1)S(1)} %get-tuple-element.216) | copy-start | bytes 2949124
  132.9 274.3 %reduce-scatter.2.cloned.1.call-start = ((), (), s32[]{:S(2)}) async-start(), calls=%async_computation.7 | async-start | bytes 3072000 | tf_op jit(solution)/shard_map/reduce_scatter | solution.py:401
  165.8 19.6 %copy-start.92 = (f32[64]{0:T(128)}, f32[64]{0:T(128)S(1)}, u32[]{:S(2)}) copy-start(f32[64]{0:T(128)S(1)} %add_rsqrt_fusion.2) | copy-start | bytes 772
  190.5 2.8 collective-permute-start.3
  196.7 5.8 %collective-permute-start.6 = (bf16[64,1024]{1,0:T(8,128)(2,1)}, bf16[64,1024]{1,0:T(8,128)(2,1)S(1)}, u32[]{:S(2)}, u32[]{:S(2)}) collective-permute-start(bf16[64,1024]{1,0:T(8,128)(2,1)} %get-tuple-element.162), channel_id=1, source_target_pairs={{0,6},{2,4},{4,2},{6,0},{1,7},{3,5},{5,3},{7,1},{8,14},{10,12},{12... | collective-permute-start | bytes 393224 | tf_op jit(solution)/shard_map/ppermute | solution.py:74
  198.8 7.3 %collective-permute-start.5 = (bf16[64,1024]{1,0:T(8,128)(2,1)}, bf16[64,1024]{1,0:T(8,128)(2,1)S(1)}, u32[]{:S(2)}, u32[]{:S(2)}) collective-permute-start(bf16[64,1024]{1,0:T(8,128)(2,1)} %get-tuple-element.163), channel_id=1, source_target_pairs={{0,4},{2,6},{4,0},{6,2},{1,5},{3,7},{5,1},{7,3},{8,12},{10,14},{12... | collective-permute-start | bytes 393224 | tf_op jit(solution)/shard_map/ppermute | solution.py:74
  199.1 7.7 %collective-permute-start.4 = (bf16[64,1024]{1,0:T(8,128)(2,1)}, bf16[64,1024]{1,0:T(8,128)(2,1)}, u32[]{:S(2)}, u32[]{:S(2)}) collective-permute-start(bf16[64,1024]{1,0:T(8,128)(2,1)} %get-tuple-element.161), channel_id=1, source_target_pairs={{0,2},{2,0},{4,6},{6,4},{1,3},{3,1},{5,7},{7,5},{8,10},{10,8},{12,... | collective-permute-start | bytes 393224 | tf_op jit(solution)/shard_map/ppermute | solution.py:74
  208.1 26.3 %copy-start.90 = (f32[64]{0:T(128)}, f32[64]{0:T(128)S(1)}, u32[]{:S(2)}) copy-start(f32[64]{0:T(128)S(1)} %add_rsqrt_fusion.1) | copy-start | bytes 772
  221.6 9.8 %collective-permute-start.7 = (bf16[4,64,1024]{2,1,0:T(8,128)(2,1)S(1)}, bf16[4,64,1024]{2,1,0:T(8,128)(2,1)S(1)}, u32[]{:S(2)}, u32[]{:S(2)}) collective-permute-start(bf16[4,64,1024]{2,1,0:T(8,128)(2,1)S(1)} %bitcast.275), channel_id=1, source_target_pairs={{0,2},{2,0},{1,3},{3,1},{4,6},{6,4},{5,7},{7,5},{8,10},{10,8},{9,1... | collective-permute-start | bytes 1572872 | tf_op jit(solution)/shard_map/ppermute | solution.py:74
  222.8 9.5 %collective-permute-start.8 = (bf16[4,64,1024]{2,1,0:T(8,128)(2,1)S(1)}, bf16[4,64,1024]{2,1,0:T(8,128)(2,1)S(1)}, u32[]{:S(2)}, u32[]{:S(2)}) collective-permute-start(bf16[4,64,1024]{2,1,0:T(8,128)(2,1)S(1)} %bitcast.276), channel_id=1, source_target_pairs={{0,4},{4,0},{1,5},{5,1},{2,6},{6,2},{3,7},{7,3},{8,12},{12,8},{9,1... | collective-permute-start | bytes 1572872 | tf_op jit(solution)/shard_map/ppermute | solution.py:74
  231.4 7.9 %collective-permute-start.9 = (bf16[2,64,1024]{2,1,0:T(8,128)(2,1)S(1)}, bf16[2,64,1024]{2,1,0:T(8,128)(2,1)S(1)}, u32[]{:S(2)}, u32[]{:S(2)}) collective-permute-start(bf16[2,64,1024]{2,1,0:T(8,128)(2,1)S(1)} %slice.536), channel_id=1, source_target_pairs={{0,4},{4,0},{1,5},{5,1},{2,6},{6,2},{3,7},{7,3},{8,12},{12,8},{9,1... | collective-permute-start | bytes 786440 | tf_op jit(solution)/shard_map/ppermute | solution.py:74
  232.3 14.5 %copy-start.95 = (s32[32]{0:T(128)S(1)}, s32[32]{0:T(128)}, u32[]{:S(2)}) copy-start(s32[32]{0:T(128)} %constant.338.clone) | copy-start | bytes 388
  232.3 7.7 %collective-permute-start.10 = (bf16[2,64,1024]{2,1,0:T(8,128)(2,1)S(1)}, bf16[2,64,1024]{2,1,0:T(8,128)(2,1)S(1)}, u32[]{:S(2)}, u32[]{:S(2)}) collective-permute-start(bf16[2,64,1024]{2,1,0:T(8,128)(2,1)S(1)} %slice.537), channel_id=1, source_target_pairs={{0,2},{2,0},{1,3},{3,1},{4,6},{6,4},{5,7},{7,5},{8,10},{10,8},{9,1... | collective-permute-start | bytes 786440 | tf_op jit(solution)/shard_map/ppermute | solution.py:74
  240.7 13.7 %collective-permute-start.11 = (bf16[1024,1024]{1,0:T(8,128)(2,1)}, bf16[1024,1024]{1,0:T(8,128)(2,1)}, u32[]{:S(2)}, u32[]{:S(2)}) collective-permute-start(bf16[1024,1024]{1,0:T(8,128)(2,1)} %bitcast.37), channel_id=1, source_target_pairs={{0,1},{1,0},{2,3},{3,2},{4,5},{5,4},{6,7},{7,6},{8,9},{9,8},{10,11... | collective-permute-start | bytes 6291464 | tf_op jit(solution)/shard_map/ppermute | solution.py:74
  259.3 16.3 %copy-start.19 = (f32[1024,1000]{0,1:T(8,128)}, f32[1024,1000]{0,1:T(8,128)S(1)}, u32[]{:S(2)}) copy-start(f32[1024,1000]{0,1:T(8,128)S(1)} %get-tuple-element.222) | copy-start | bytes 12288004
  260.8 1.3 collective-permute-start.12
  262.2 2.8 collective-permute-start.13
  265.2 2.8 collective-permute-start.14
  268.2 2.8 collective-permute-start.15
  271.1 3.8 collective-permute-start.16
  280.8 10.4 %collective-permute-start.17 = (bf16[1024,1024]{1,0:T(8,128)(2,1)}, bf16[1024,1024]{1,0:T(8,128)(2,1)}, u32[]{:S(2)}, u32[]{:S(2)}) collective-permute-start(bf16[1024,1024]{1,0:T(8,128)(2,1)} %convolution_convert_fusion), channel_id=1, source_target_pairs={{0,1},{1,0},{2,3},{3,2},{4,5},{5,4},{6,7},{7,6},{8,9},{9,8},{10,11... | collective-permute-start | bytes 6291464 | tf_op jit(solution)/shard_map/ppermute | solution.py:74
  296.2 14.4 %collective-permute-start.20 = (bf16[4,64,1024]{2,1,0:T(8,128)(2,1)S(1)}, bf16[4,64,1024]{2,1,0:T(8,128)(2,1)S(1)}, u32[]{:S(2)}, u32[]{:S(2)}) collective-permute-start(bf16[4,64,1024]{2,1,0:T(8,128)(2,1)S(1)} %bitcast.301), channel_id=1, source_target_pairs={{0,6},{2,4},{4,2},{6,0},{1,7},{3,5},{5,3},{7,1},{8,14},{10,12},{12... | collective-permute-start | bytes 1572872 | tf_op jit(solution)/shard_map/ppermute | solution.py:74
  296.5 24.4 %collective-permute-start.19 = (bf16[4,64,1024]{2,1,0:T(8,128)(2,1)S(1)}, bf16[4,64,1024]{2,1,0:T(8,128)(2,1)S(1)}, u32[]{:S(2)}, u32[]{:S(2)}) collective-permute-start(bf16[4,64,1024]{2,1,0:T(8,128)(2,1)S(1)} %bitcast.300), channel_id=1, source_target_pairs={{0,4},{2,6},{4,0},{6,2},{1,5},{3,7},{5,1},{7,3},{8,12},{10,14},{12... | collective-permute-start | bytes 1572872 | tf_op jit(solution)/shard_map/ppermute | solution.py:74
  297.2 23.8 %collective-permute-start.18 = (bf16[4,64,1024]{2,1,0:T(8,128)(2,1)S(1)}, bf16[4,64,1024]{2,1,0:T(8,128)(2,1)S(1)}, u32[]{:S(2)}, u32[]{:S(2)}) collective-permute-start(bf16[4,64,1024]{2,1,0:T(8,128)(2,1)S(1)} %bitcast.299), channel_id=1, source_target_pairs={{0,2},{2,0},{4,6},{6,4},{1,3},{3,1},{5,7},{7,5},{8,10},{10,8},{12,... | collective-permute-start | bytes 1572872 | tf_op jit(solution)/shard_map/ppermute | solution.py:74
  321.4 6.5 %collective-permute-start.23 = (bf16[64,1024]{1,0:T(8,128)(2,1)S(1)}, bf16[64,1024]{1,0:T(8,128)(2,1)S(1)}, u32[]{:S(2)}, u32[]{:S(2)}) collective-permute-start(bf16[64,1024]{1,0:T(8,128)(2,1)S(1)} %get-tuple-element.159), channel_id=1, source_target_pairs={{0,24},{8,16},{16,8},{24,0},{1,25},{9,17},{17,9},{25,1},{2,26},{10... | collective-permute-start | bytes 393224 | tf_op jit(solution)/shard_map/ppermute | solution.py:74
  322.7 11.8 %collective-permute-start.22 = (bf16[64,1024]{1,0:T(8,128)(2,1)S(1)}, bf16[64,1024]{1,0:T(8,128)(2,1)S(1)}, u32[]{:S(2)}, u32[]{:S(2)}) collective-permute-start(bf16[64,1024]{1,0:T(8,128)(2,1)S(1)} %get-tuple-element.160), channel_id=1, source_target_pairs={{0,16},{8,24},{16,0},{24,8},{1,17},{9,25},{17,1},{25,9},{2,18},{10... | collective-permute-start | bytes 393224 | tf_op jit(solution)/shard_map/ppermute | solution.py:74
  322.7 11.8 %collective-permute-start.21 = (bf16[64,1024]{1,0:T(8,128)(2,1)S(1)}, bf16[64,1024]{1,0:T(8,128)(2,1)S(1)}, u32[]{:S(2)}, u32[]{:S(2)}) collective-permute-start(bf16[64,1024]{1,0:T(8,128)(2,1)S(1)} %get-tuple-element.158), channel_id=1, source_target_pairs={{0,8},{8,0},{16,24},{24,16},{1,9},{9,1},{17,25},{25,17},{2,10},{10... | collective-permute-start | bytes 393224 | tf_op jit(solution)/shard_map/ppermute | solution.py:74
  327.9 19.4 %copy-start.37 = (f32[512,640]{1,0:T(8,128)S(1)}, f32[512,640]{1,0:T(8,128)}, u32[]{:S(2)}) copy-start(f32[512,640]{1,0:T(8,128)} %copy-done.36) | copy-start | bytes 3932164
  327.9 19.4 %copy-start.54 = (bf16[320,640]{1,0:T(8,128)(2,1)S(1)}, bf16[320,640]{1,0:T(8,128)(2,1)}, u32[]{:S(2)}) copy-start(bf16[320,640]{1,0:T(8,128)(2,1)} %copy-done.53) | copy-start | bytes 1228804
  327.9 19.4 %copy-start.66 = (bf16[160,320]{1,0:T(8,128)(2,1)S(1)}, bf16[160,320]{1,0:T(8,128)(2,1)}, u32[]{:S(2)}) copy-start(bf16[160,320]{1,0:T(8,128)(2,1)} %copy-done.65) | copy-start | bytes 307204
  327.9 19.4 %copy-start.68 = (bf16[160,320]{1,0:T(8,128)(2,1)S(1)}, bf16[160,320]{1,0:T(8,128)(2,1)}, u32[]{:S(2)}) copy-start(bf16[160,320]{1,0:T(8,128)(2,1)} %copy-done.67) | copy-start | bytes 307204
  349.7 2.5 collective-permute-start.24
  353.8 5.9 %collective-permute-start.27 = (bf16[64,1024]{1,0:T(8,128)(2,1)S(1)}, bf16[64,1024]{1,0:T(8,128)(2,1)}, u32[]{:S(2)}, u32[]{:S(2)}) collective-permute-start(bf16[64,1024]{1,0:T(8,128)(2,1)S(1)} %get-tuple-element.156), channel_id=1, source_target_pairs={{0,6},{2,4},{4,2},{6,0},{1,7},{3,5},{5,3},{7,1},{8,14},{10,12},{12... | collective-permute-start | bytes 393224 | tf_op jit(solution)/shard_map/ppermute | solution.py:74
  355.1 8.0 %collective-permute-start.26 = (bf16[64,1024]{1,0:T(8,128)(2,1)S(1)}, bf16[64,1024]{1,0:T(8,128)(2,1)}, u32[]{:S(2)}, u32[]{:S(2)}) collective-permute-start(bf16[64,1024]{1,0:T(8,128)(2,1)S(1)} %get-tuple-element.157), channel_id=1, source_target_pairs={{0,4},{2,6},{4,0},{6,2},{1,5},{3,7},{5,1},{7,3},{8,12},{10,14},{12... | collective-permute-start | bytes 393224 | tf_op jit(solution)/shard_map/ppermute | solution.py:74
  355.7 7.5 %collective-permute-start.25 = (bf16[64,1024]{1,0:T(8,128)(2,1)S(1)}, bf16[64,1024]{1,0:T(8,128)(2,1)}, u32[]{:S(2)}, u32[]{:S(2)}) collective-permute-start(bf16[64,1024]{1,0:T(8,128)(2,1)S(1)} %get-tuple-element.155), channel_id=1, source_target_pairs={{0,2},{2,0},{4,6},{6,4},{1,3},{3,1},{5,7},{7,5},{8,10},{10,8},{12,... | collective-permute-start | bytes 393224 | tf_op jit(solution)/shard_map/ppermute | solution.py:74
  400.2 21.1 %all-to-all-start.3 = ((bf16[32,8,960]{2,1,0:T(8,128)(2,1)}), bf16[32,8,960]{2,1,0:T(8,128)(2,1)}, u32[]{:S(2)}, u32[]{:S(2)}) async-start(bf16[32,8,960]{2,1,0:T(8,128)(2,1)} %bitcast.92), calls=%async_computation.4 | async-start | bytes 1048576 | tf_op jit(solution)/shard_map/all_to_all | solution.py:194
  427.1 7.5 %collective-permute-start.28 = (bf16[4,352,960]{2,1,0:T(8,128)(2,1)}, bf16[4,352,960]{2,1,0:T(8,128)(2,1)}, u32[]{:S(2)}, u32[]{:S(2)}) collective-permute-start(bf16[4,352,960]{2,1,0:T(8,128)(2,1)} %get-tuple-element.126), channel_id=1, source_target_pairs={{0,1},{1,0},{2,3},{3,2},{4,5},{5,4},{6,7},{7,6},{8,9},{9,8},{10,11... | collective-permute-start | bytes 8110088 | tf_op jit(solution)/shard_map/ppermute | solution.py:74
  428.2 51.6 %all-to-all-start.4 = ((bf16[32,24,960]{2,1,0:T(8,128)(2,1)}), bf16[32,24,960]{2,1,0:T(8,128)(2,1)}, u32[]{:S(2)}, u32[]{:S(2)}) async-start(bf16[32,24,960]{2,1,0:T(8,128)(2,1)} %bitcast.93), calls=%async_computation.5 | async-start | bytes 3145728 | tf_op jit(solution)/shard_map/all_to_all | solution.py:194
  438.6 28.7 %collective-permute-start.31 = (bf16[2,176,960]{2,1,0:T(8,128)(2,1)}, bf16[2,176,960]{2,1,0:T(8,128)(2,1)}, u32[]{:S(2)}, u32[]{:S(2)}) collective-permute-start(bf16[2,176,960]{2,1,0:T(8,128)(2,1)} %fusion.59), channel_id=1, source_target_pairs={{0,4},{4,0},{1,5},{5,1},{2,6},{6,2},{3,7},{7,3},{8,12},{12,8},{9,1... | collective-permute-start | bytes 2027528 | tf_op jit(solution)/shard_map/ppermute | solution.py:74
  441.0 28.3 %collective-permute-start.29 = (bf16[2,176,960]{2,1,0:T(8,128)(2,1)}, bf16[2,176,960]{2,1,0:T(8,128)(2,1)}, u32[]{:S(2)}, u32[]{:S(2)}) collective-permute-start(bf16[2,176,960]{2,1,0:T(8,128)(2,1)} %fusion.58), channel_id=1, source_target_pairs={{0,2},{2,0},{1,3},{3,1},{4,6},{6,4},{5,7},{7,5},{8,10},{10,8},{9,1... | collective-permute-start | bytes 2027528 | tf_op jit(solution)/shard_map/ppermute | solution.py:74
  469.3 8.8 %collective-permute-start.32 = (bf16[176,960]{1,0:T(8,128)(2,1)S(1)}, bf16[176,960]{1,0:T(8,128)(2,1)S(1)}, u32[]{:S(2)}, u32[]{:S(2)}) collective-permute-start(bf16[176,960]{1,0:T(8,128)(2,1)S(1)} %fusion.76), channel_id=1, source_target_pairs={{0,2},{2,0},{1,3},{3,1},{4,6},{6,4},{5,7},{7,5},{8,10},{10,8},{9,1... | collective-permute-start | bytes 1013768 | tf_op jit(solution)/shard_map/ppermute | solution.py:74
  470.9 8.7 %collective-permute-start.30 = (bf16[176,960]{1,0:T(8,128)(2,1)S(1)}, bf16[176,960]{1,0:T(8,128)(2,1)S(1)}, u32[]{:S(2)}, u32[]{:S(2)}) collective-permute-start(bf16[176,960]{1,0:T(8,128)(2,1)S(1)} %fusion.75), channel_id=1, source_target_pairs={{0,4},{4,0},{1,5},{5,1},{2,6},{6,2},{3,7},{7,3},{8,12},{12,8},{9,1... | collective-permute-start | bytes 1013768 | tf_op jit(solution)/shard_map/ppermute | solution.py:74
  479.9 14.8 %collective-permute-start.35 = (bf16[88,960]{1,0:T(8,128)(2,1)S(1)}, bf16[88,960]{1,0:T(8,128)(2,1)S(1)}, u32[]{:S(2)}, u32[]{:S(2)}) collective-permute-start(bf16[88,960]{1,0:T(8,128)(2,1)S(1)} %get-tuple-element.137), channel_id=1, source_target_pairs={{0,24},{8,16},{16,8},{24,0},{1,25},{9,17},{17,9},{25,1},{2,26},{10... | collective-permute-start | bytes 506888 | tf_op jit(solution)/shard_map/ppermute | solution.py:74
  484.8 13.6 %collective-permute-start.34 = (bf16[88,960]{1,0:T(8,128)(2,1)S(1)}, bf16[88,960]{1,0:T(8,128)(2,1)S(1)}, u32[]{:S(2)}, u32[]{:S(2)}) collective-permute-start(bf16[88,960]{1,0:T(8,128)(2,1)S(1)} %get-tuple-element.138), channel_id=1, source_target_pairs={{0,16},{8,24},{16,0},{24,8},{1,17},{9,25},{17,1},{25,9},{2,18},{10... | collective-permute-start | bytes 506888 | tf_op jit(solution)/shard_map/ppermute | solution.py:74
  484.8 13.6 %collective-permute-start.33 = (bf16[88,960]{1,0:T(8,128)(2,1)S(1)}, bf16[88,960]{1,0:T(8,128)(2,1)S(1)}, u32[]{:S(2)}, u32[]{:S(2)}) collective-permute-start(bf16[88,960]{1,0:T(8,128)(2,1)S(1)} %get-tuple-element.136), channel_id=1, source_target_pairs={{0,8},{8,0},{16,24},{24,16},{1,9},{9,1},{17,25},{25,17},{2,10},{10... | collective-permute-start | bytes 506888 | tf_op jit(solution)/shard_map/ppermute | solution.py:74
  501.9 2.8 collective-permute-start.36
  505.4 2.4 collective-permute-start.37
  508.5 26.2 %collective-permute-start.43 = (bf16[88,960]{1,0:T(8,128)(2,1)S(1)}, bf16[88,960]{1,0:T(8,128)(2,1)S(1)}, u32[]{:S(2)}, u32[]{:S(2)}) collective-permute-start(bf16[88,960]{1,0:T(8,128)(2,1)S(1)} %get-tuple-element.83), channel_id=1, source_target_pairs={{16,0},{17,1},{18,2},{19,3},{20,4},{21,5},{22,6},{23,7}} | collective-permute-start | bytes 506888 | tf_op jit(solution)/shard_map/ppermute | solution.py:460
  509.8 24.9 %collective-permute-start.41 = (bf16[88,960]{1,0:T(8,128)(2,1)S(1)}, bf16[88,960]{1,0:T(8,128)(2,1)S(1)}, u32[]{:S(2)}, u32[]{:S(2)}) collective-permute-start(bf16[88,960]{1,0:T(8,128)(2,1)S(1)} %get-tuple-element.83), channel_id=1, source_target_pairs={{24,0},{25,1},{26,2},{27,3},{28,4},{29,5},{30,6},{31,7}} | collective-permute-start | bytes 506888 | tf_op jit(solution)/shard_map/ppermute | solution.py:460
  513.8 25.5 %all-to-all-start.5 = ((bf16[8,60,640]{2,1,0:T(8,128)(2,1)}), bf16[8,60,640]{2,1,0:T(8,128)(2,1)S(1)}, u32[]{:S(2)}, u32[]{:S(2)}) async-start(bf16[8,60,640]{2,1,0:T(8,128)(2,1)} %reshape.649), calls=%async_computation.6 | async-start | bytes 1310720 | tf_op jit(solution)/shard_map/all_to_all | solution.py:448
  518.8 16.3 %collective-permute-start.42 = (bf16[88,960]{1,0:T(8,128)(2,1)S(1)}, bf16[88,960]{1,0:T(8,128)(2,1)S(1)}, u32[]{:S(2)}, u32[]{:S(2)}) collective-permute-start(bf16[88,960]{1,0:T(8,128)(2,1)S(1)} %get-tuple-element.83), channel_id=1, source_target_pairs={{8,0},{9,1},{10,2},{11,3},{12,4},{13,5},{14,6},{15,7}} | collective-permute-start | bytes 506888 | tf_op jit(solution)/shard_map/ppermute | solution.py:460
  520.3 5.7 %collective-permute-start.38 = (f32[2]{0:T(128)S(1)}, f32[2]{0:T(128)S(1)}, u32[]{:S(2)}, u32[]{:S(2)}) collective-permute-start(f32[2]{0:T(128)S(1)} %fusion.255), channel_id=1, source_target_pairs={{0,4},{4,0},{1,5},{5,1},{2,6},{6,2},{3,7},{7,3},{8,12},{12,8},{9,1... | collective-permute-start | bytes 32 | tf_op jit(solution)/shard_map/ppermute | solution.py:74
  526.0 2.7 collective-permute-start.39
  528.8 3.9 collective-permute-start.40
  541.3 17.9 %collective-permute-start.44 = (bf16[2880]{0:T(1024)(128)(2,1)S(1)}, bf16[2880]{0:T(1024)(128)(2,1)S(1)}, u32[]{:S(2)}, u32[]{:S(2)}) collective-permute-start(bf16[2880]{0:T(1024)(128)(2,1)S(1)} %slice.503), channel_id=1, source_target_pairs={{0,1},{1,2},{2,3},{3,4},{4,5},{5,6},{6,7},{7,8},{8,9},{9,10},{10,1... | collective-permute-start | bytes 17288 | tf_op jit(solution)/shard_map/ppermute | solution.py:482
  (88 other events, 351.9 us)
Sparse Core Ops, SparseCore 0:
  54.9 64.4 all-gather.7
  133.0 50.8 all-gather.9
  358.5 48.6 reduce-scatter.1
